TPU v7x, 32 devices: a whole 2x2x4 slice. The times are simulated.
32 devices in a mesh: seq: 8 (over z, x), exp: 4 (over y, core).
Axes of the slice: x: 2, y: 2, z: 4, core: 2. Of those that a mesh axis runs over, the one named last changes fastest.
Arguments:
- block_in: bfloat16 [16, 2048, 1024], P('exp', 'seq'), may hold values from -6 to 6
- cotangent: bfloat16 [16, 2048, 1024], P('exp', 'seq'), may hold values from -6 to 6
- segment_ids: int32 [16, 2048], P('exp'), may hold values from 0 to 3, never falling along the last dimension, each value on 1 to 1024 neighbouring positions
- expert_routes: int32 [16, 2048, 2], P('exp', 'seq'), may hold values from 0 to 3, all different within a row
- pair_priority: int32 [4, 8, 2048], P('exp', 'seq'), may hold values from 0 to 2047, each once within a row
- gain_attention: float32 [1024], P(('seq', 'exp')), may hold values from 0.5 to 1.5
- w_query: float32 [1024, 1024], P(('seq', 'exp')), may hold values from -0.1875 to 0.1875
- w_key: float32 [1024, 1024], P(('seq', 'exp')), may hold values from -0.1875 to 0.1875
- w_value: float32 [1024, 1024], P(('seq', 'exp')), may hold values from -0.1875 to 0.1875
- w_out: float32 [1024, 1024], P(('seq', 'exp')), may hold values from -2.5 to 2.5
- bias_table: float32 [512], P(('seq', 'exp')), may hold values from -3 to 3
- gain_experts: float32 [1024], P(('seq', 'exp')), may hold values from 0.5 to 1.5
- w_router: float32 [1024, 4], P(('seq', 'exp')), may hold values from -0.09375 to 0.09375
- w_gate: float32 [4, 1024, 2816], P('exp', 'seq'), may hold values from -0.1875 to 0.1875
- w_up: float32 [4, 1024, 2816], P('exp', 'seq'), may hold values from -0.1875 to 0.1875
- w_down: float32 [4, 2816, 1024], P('exp', 'seq'), may hold values from -0.109375 to 0.109375
Outputs:
- block_out: bfloat16 [16, 2048, 1024], P('exp', 'seq')
- block_in_grad: float32 [16, 2048, 1024], P('exp', 'seq')
- gain_attention_grad: float32 [1024], P(('seq', 'exp'))
- query_grad: float32 [1024, 1024], P(('seq', 'exp'))
- key_grad: float32 [1024, 1024], P(('seq', 'exp'))
- value_grad: float32 [1024, 1024], P(('seq', 'exp'))
- out_weight_grad: float32 [1024, 1024], P(('seq', 'exp'))
- bias_grad: float32 [512], P(('seq', 'exp'))
- gain_experts_grad: float32 [1024], P(('seq', 'exp'))
- router_grad: float32 [1024, 4], P(('seq', 'exp'))
- gate_grad: float32 [4, 1024, 2816], P('exp', 'seq')
- up_grad: float32 [4, 1024, 2816], P('exp', 'seq')
- down_grad: float32 [4, 2816, 1024], P('exp', 'seq')
Inputs may be any that keep to these rules, and one draw needn't show every extreme that they name: `segment_ids`: document ids never fall along a sequence; no document is longer than 1024 tokens. `expert_routes`: the two experts of a token differ. `pair_priority`: each row is a permutation of the 2048 pairs of one device.
All inputs are finite; a program needn't handle non-finite values.
Results may differ from a plain program's by a relative error of at most 0.017.
The roundings to bfloat16 on the way count: a program that leaves them out, or rounds other values in their place, can miss the bound.
Values may be sent and summed in bfloat16 or wider, within the bound.
A program may use at most 320 MiB of HBM per device.

v0:
```python
from functools import partial

import jax
import jax.numpy as jnp
from jax import lax
from jax.sharding import PartitionSpec as P

HEAD_DIM = 64
BUCKETS = 32


EPS = 1e-06
NEG = -1e30
THRESHOLDS = (12, 16, 23, 32, 46, 64, 91)
FULL_PRECISION = lax.Precision.HIGHEST


def bucket_of(offsets):
    distance = jnp.abs(offsets)
    extra = jnp.zeros_like(distance)
    for threshold in THRESHOLDS:
        extra = extra + (distance >= threshold).astype(jnp.int32)
    nearby = jnp.where(distance < 8, distance, 8 + extra)
    return nearby + 16 * (offsets > 0).astype(jnp.int32)


def gelu_tanh(value_entries):
    return (
        0.5
        * value_entries
        * (
            1.0
            + jnp.tanh(
                0.7978845608028654
                * (value_entries + 0.044715 * value_entries * value_entries * value_entries)
            )
        )
    )


def geglu_product(gate_part, up_part):
    return gelu_tanh(gate_part) * up_part


def rms_scale(value_entries, gain_row):
    return (
        value_entries
        * lax.rsqrt(jnp.mean(value_entries * value_entries, axis=-1, keepdims=True) + EPS)
        * gain_row
    )


def gate_values(routes, normed, router):
    logits = jnp.dot(normed, router, precision=FULL_PRECISION)
    row_peak = jnp.max(logits, axis=-1, keepdims=True)
    exponent = jnp.exp(logits - row_peak)
    probabilities = exponent / jnp.sum(exponent, axis=-1, keepdims=True)
    choose = (routes[..., None] == jnp.arange(router.shape[1], dtype=jnp.int32)).astype(
        probabilities.dtype
    )
    chosen = jnp.sum(probabilities[..., None, :] * choose, axis=-1)
    return chosen / jnp.sum(chosen, axis=-1, keepdims=True)


def split_heads(value_entries):
    return value_entries.reshape(
        value_entries.shape[0], value_entries.shape[1], value_entries.shape[2] // HEAD_DIM, HEAD_DIM
    )


def join_blocks(blocks):
    moved = jnp.moveaxis(blocks, 0, 1)
    return moved.reshape(
        moved.shape[0], moved.shape[1] * moved.shape[2], moved.shape[3] * moved.shape[4]
    )


def block_buckets(query_rows, key_rows, first_row):
    query_pos = first_row + jnp.arange(query_rows, dtype=jnp.int32)
    key_pos = jnp.arange(key_rows, dtype=jnp.int32)
    return bucket_of(key_pos[None, :] - query_pos[:, None])


def bias_lookup(table_rows, bucket_ids):
    total = jnp.zeros((table_rows.shape[0],) + bucket_ids.shape, jnp.float32)
    for bucket in range(BUCKETS):
        total = total + jnp.where(
            bucket_ids[None] == bucket, table_rows[:, bucket][:, None, None], 0.0
        )
    return total


def scores_block(query_block, key_heads, table_rows, segment_query, segments, first_row):
    raw_scores = jnp.einsum(
        "gqhd,gkhd->ghqk", query_block, key_heads, preferred_element_type=jnp.float32
    )
    bucket_ids = block_buckets(query_block.shape[1], key_heads.shape[1], first_row)
    bias_rows = bias_lookup(table_rows, bucket_ids)
    same_doc = segment_query[:, None, :, None] == segments[:, None, None, :]
    return jnp.where(same_doc, raw_scores * HEAD_DIM ** (-0.5) + bias_rows[None], NEG)


def bucket_totals(summed, first_row):
    bucket_ids = block_buckets(summed.shape[1], summed.shape[2], first_row)
    columns = [
        jnp.sum(jnp.where(bucket_ids[None] == bucket, summed, 0.0), axis=(1, 2))
        for bucket in range(BUCKETS)
    ]
    return jnp.stack(columns, axis=1)


def attend_forward(query_heads, key_heads, value_heads, table_rows, segments):
    length = key_heads.shape[1]
    block_rows = min(512, length)

    def one_block(block_index):
        first_row = block_index * block_rows
        query_block = lax.dynamic_slice_in_dim(query_heads, first_row, block_rows, 1)
        segment_query = lax.dynamic_slice_in_dim(segments, first_row, block_rows, 1)
        logits = scores_block(
            query_block, key_heads, table_rows, segment_query, segments, first_row
        )
        row_peak = jnp.max(logits, axis=-1, keepdims=True)
        exponent = jnp.exp(logits - row_peak)
        row_total = jnp.sum(exponent, axis=-1, keepdims=True)
        weights_low = (exponent / row_total).astype(jnp.bfloat16)
        context = jnp.einsum(
            "ghqk,gkhd->gqhd", weights_low, value_heads, preferred_element_type=jnp.float32
        )
        return (context.astype(jnp.bfloat16), (row_peak + jnp.log(row_total))[..., 0])

    contexts, log_totals = lax.map(one_block, jnp.arange(length // block_rows, dtype=jnp.int32))
    return (join_blocks(contexts), log_totals)


def attend_backward(
    query_heads, key_heads, value_heads, table_rows, segments, log_totals, grad_heads
):
    length = key_heads.shape[1]
    block_rows = min(512, length)

    def one_block(running, block_index):
        key_sum, value_sum, table_sum = running
        first_row = block_index * block_rows
        query_block = lax.dynamic_slice_in_dim(query_heads, first_row, block_rows, 1)
        grad_block = lax.dynamic_slice_in_dim(grad_heads, first_row, block_rows, 1)
        segment_query = lax.dynamic_slice_in_dim(segments, first_row, block_rows, 1)
        logits = scores_block(
            query_block, key_heads, table_rows, segment_query, segments, first_row
        )
        probabilities = jnp.exp(logits - log_totals[block_index][..., None])
        weights_low = probabilities.astype(jnp.bfloat16)
        value_sum = value_sum + jnp.einsum(
            "ghqk,gqhd->gkhd", weights_low, grad_block, preferred_element_type=jnp.float32
        )
        prob_grad = jnp.einsum(
            "gqhd,gkhd->ghqk", grad_block, value_heads, preferred_element_type=jnp.float32
        )
        score_grad = probabilities * (
            prob_grad - jnp.sum(probabilities * prob_grad, axis=-1, keepdims=True)
        )
        table_sum = table_sum + bucket_totals(jnp.sum(score_grad, axis=0), first_row)
        raw_grad = (score_grad * HEAD_DIM ** (-0.5)).astype(jnp.bfloat16)
        query_grad = jnp.einsum(
            "ghqk,gkhd->gqhd", raw_grad, key_heads, preferred_element_type=jnp.float32
        ).astype(jnp.bfloat16)
        key_sum = key_sum + jnp.einsum(
            "ghqk,gqhd->gkhd", raw_grad, query_block, preferred_element_type=jnp.float32
        )
        return ((key_sum, value_sum, table_sum), query_grad)

    zero_heads = jnp.zeros(key_heads.shape, jnp.float32)
    zero_table = jnp.zeros(table_rows.shape, jnp.float32)
    (key_sum, value_sum, table_sum), query_grads = lax.scan(
        one_block,
        (zero_heads, zero_heads, zero_table),
        jnp.arange(length // block_rows, dtype=jnp.int32),
    )
    flat_shape = (key_sum.shape[0], length, key_sum.shape[2] * HEAD_DIM)
    return (
        join_blocks(query_grads),
        key_sum.reshape(flat_shape).astype(jnp.bfloat16),
        value_sum.reshape(flat_shape).astype(jnp.bfloat16),
        table_sum,
    )


def per_device(
    block_in,
    cotangent,
    segment_ids,
    expert_routes,
    pair_priority,
    gain_attention,
    w_query,
    w_key,
    w_value,
    w_out,
    bias_table,
    gain_experts,
    w_router,
    w_gate,
    w_up,
    w_down,
):
    low_type = jnp.bfloat16
    gain_a, query_w, key_w, value_w, out_w, table_all, gain_b, router_w = (
        lax.all_gather(gain_attention.astype(low_type), ("seq", "exp"), axis=0, tiled=True),
        lax.all_gather(w_query.astype(low_type), ("seq", "exp"), axis=0, tiled=True),
        lax.all_gather(w_key.astype(low_type), ("seq", "exp"), axis=0, tiled=True),
        lax.all_gather(w_value.astype(low_type), ("seq", "exp"), axis=0, tiled=True),
        lax.all_gather(w_out.astype(low_type), ("seq", "exp"), axis=0, tiled=True),
        lax.all_gather(bias_table.astype(low_type), ("seq", "exp"), axis=0, tiled=True),
        lax.all_gather(gain_experts.astype(low_type), ("seq", "exp"), axis=0, tiled=True),
        lax.all_gather(w_router.astype(low_type), ("seq", "exp"), axis=0, tiled=True),
    )
    gate_w, up_w, down_w = (
        lax.all_gather(w_gate.astype(low_type), "seq", axis=1, tiled=True),
        lax.all_gather(w_up.astype(low_type), "seq", axis=1, tiled=True),
        lax.all_gather(w_down.astype(low_type), "seq", axis=1, tiled=True),
    )
    groups, local_len, model_width = block_in.shape
    tokens = groups * local_len
    inputs = block_in.astype(jnp.float32).reshape(tokens, model_width)
    gain_one = gain_a.astype(jnp.float32)
    gain_two = gain_b.astype(jnp.float32)
    normed_full, norm_one_back = jax.vjp(rms_scale, inputs, gain_one)
    normed_one = normed_full.astype(low_type)
    queries = (
        jnp.dot(normed_one, query_w, preferred_element_type=jnp.float32)
        .astype(low_type)
        .reshape(groups, local_len, -1)
    )
    key_local = (
        jnp.dot(normed_one, key_w, preferred_element_type=jnp.float32)
        .astype(low_type)
        .reshape(groups, local_len, -1)
    )
    value_local = (
        jnp.dot(normed_one, value_w, preferred_element_type=jnp.float32)
        .astype(low_type)
        .reshape(groups, local_len, -1)
    )
    head_q, head_k, head_v = (
        lax.all_to_all(queries, "seq", split_axis=2, concat_axis=1, tiled=True),
        lax.all_to_all(key_local, "seq", split_axis=2, concat_axis=1, tiled=True),
        lax.all_to_all(value_local, "seq", split_axis=2, concat_axis=1, tiled=True),
    )
    query_heads = split_heads(head_q)
    key_heads = split_heads(head_k)
    value_heads = split_heads(head_v)
    heads_here = query_heads.shape[2]
    first_head = lax.axis_index("seq") * heads_here
    table_full = table_all.astype(jnp.float32).reshape(-1, BUCKETS)
    table_rows = lax.dynamic_slice_in_dim(table_full, first_head, heads_here, 0)
    contexts, log_totals = attend_forward(
        query_heads, key_heads, value_heads, table_rows, segment_ids
    )
    context_local = lax.all_to_all(
        contexts, "seq", split_axis=1, concat_axis=2, tiled=True
    ).reshape(tokens, -1)
    mid = inputs + jnp.dot(context_local, out_w, preferred_element_type=jnp.float32)
    normed_two_full, norm_two_back = jax.vjp(rms_scale, mid, gain_two)
    normed_two = normed_two_full.astype(low_type)
    routes_local = expert_routes.reshape(tokens, -1)
    top_count = routes_local.shape[1]
    gates, gates_back = jax.vjp(
        partial(gate_values, routes_local),
        normed_two.astype(jnp.float32),
        router_w.astype(jnp.float32),
    )
    experts_all = router_w.shape[1]
    pair_experts = routes_local.reshape(-1)
    priority = pair_priority.reshape(-1)
    expert_table = (
        pair_experts[:, None] == jnp.arange(experts_all, dtype=jnp.int32)[None, :]
    ).astype(jnp.float32)
    earlier = (priority[None, :] < priority[:, None]).astype(jnp.float32)
    ahead_counts = jnp.dot(earlier, expert_table, precision=FULL_PRECISION)
    slots = jnp.sum(ahead_counts * expert_table, axis=1).astype(jnp.int32)
    capacity = (5 * top_count * tokens + 4 * experts_all - 1) // (4 * experts_all)
    slot_index = jnp.where(
        slots < capacity, pair_experts * capacity + slots, experts_all * capacity
    )
    exp_count = lax.axis_size("exp")
    local_experts = gate_w.shape[0]
    slot_table = (
        slot_index[:, None] == jnp.arange(experts_all * capacity, dtype=jnp.int32)[None, :]
    ).astype(low_type)
    slot_table = slot_table.reshape(tokens, top_count, experts_all * capacity)
    token_table = jnp.sum(slot_table, axis=1, dtype=jnp.float32).astype(low_type)
    buffer = jnp.einsum(
        "ts,td->sd", token_table, normed_two, preferred_element_type=jnp.float32
    ).astype(low_type)
    arrived = lax.all_to_all(
        buffer.reshape(exp_count, -1, model_width), "exp", split_axis=0, concat_axis=0, tiled=True
    )
    arrived = arrived.reshape(exp_count, local_experts, capacity, model_width)
    gate_hidden = jnp.einsum("necd,edf->necf", arrived, gate_w, preferred_element_type=jnp.float32)
    up_hidden = jnp.einsum("necd,edf->necf", arrived, up_w, preferred_element_type=jnp.float32)
    hidden_pair, geglu_back = jax.vjp(geglu_product, gate_hidden, up_hidden)
    hidden = hidden_pair.astype(low_type)
    expert_out = jnp.einsum(
        "necf,efd->necd", hidden, down_w, preferred_element_type=jnp.float32
    ).astype(low_type)
    returned = lax.all_to_all(
        expert_out.reshape(exp_count, -1, model_width),
        "exp",
        split_axis=0,
        concat_axis=0,
        tiled=True,
    )
    picked = jnp.einsum(
        "tks,sd->tkd",
        slot_table,
        returned.reshape(-1, model_width),
        preferred_element_type=jnp.float32,
    )
    mixture = jnp.sum(picked * gates[..., None], axis=1)
    block_out = (mid + mixture).astype(low_type).reshape(groups, local_len, model_width)
    query_w, key_w, value_w, out_w = (
        lax.all_gather(w_query.astype(low_type), ("seq", "exp"), axis=0, tiled=True),
        lax.all_gather(w_key.astype(low_type), ("seq", "exp"), axis=0, tiled=True),
        lax.all_gather(w_value.astype(low_type), ("seq", "exp"), axis=0, tiled=True),
        lax.all_gather(w_out.astype(low_type), ("seq", "exp"), axis=0, tiled=True),
    )
    gate_w, up_w, down_w = (
        lax.all_gather(w_gate.astype(low_type), "seq", axis=1, tiled=True),
        lax.all_gather(w_up.astype(low_type), "seq", axis=1, tiled=True),
        lax.all_gather(w_down.astype(low_type), "seq", axis=1, tiled=True),
    )
    grad_out = cotangent.astype(jnp.float32).reshape(tokens, model_width)
    gate_grad_pairs = jnp.sum(picked * grad_out[:, None, :], axis=-1)
    pair_grad = (gates[..., None] * grad_out[:, None, :]).astype(low_type)
    slot_grad = jnp.einsum(
        "tks,tkd->sd", slot_table, pair_grad, preferred_element_type=jnp.float32
    ).astype(low_type)
    expert_grad_in = lax.all_to_all(
        slot_grad.reshape(exp_count, -1, model_width),
        "exp",
        split_axis=0,
        concat_axis=0,
        tiled=True,
    )
    expert_grad_in = expert_grad_in.reshape(exp_count, local_experts, capacity, model_width)
    hidden_grad = jnp.einsum(
        "necd,efd->necf", expert_grad_in, down_w, preferred_element_type=jnp.float32
    )
    gate_hidden_grad, up_hidden_grad = geglu_back(hidden_grad)
    gate_low = gate_hidden_grad.astype(low_type)
    up_low = up_hidden_grad.astype(low_type)
    arrived_grad = jnp.einsum(
        "necf,edf->necd", gate_low, gate_w, preferred_element_type=jnp.float32
    )
    arrived_grad = (
        arrived_grad
        + jnp.einsum("necf,edf->necd", up_low, up_w, preferred_element_type=jnp.float32)
    ).astype(low_type)
    back_rows = lax.all_to_all(
        arrived_grad.reshape(exp_count, -1, model_width),
        "exp",
        split_axis=0,
        concat_axis=0,
        tiled=True,
    )
    down_sum = jnp.einsum(
        "necf,necd->efd", hidden, expert_grad_in, preferred_element_type=jnp.float32
    )
    gate_sum = jnp.einsum("necd,necf->edf", arrived, gate_low, preferred_element_type=jnp.float32)
    up_sum = jnp.einsum("necd,necf->edf", arrived, up_low, preferred_element_type=jnp.float32)
    gate_owned, up_owned, down_owned = (
        lax.psum_scatter(
            gate_sum.astype(jnp.bfloat16), "seq", scatter_dimension=1, tiled=True
        ).astype(jnp.float32),
        lax.psum_scatter(
            up_sum.astype(jnp.bfloat16), "seq", scatter_dimension=1, tiled=True
        ).astype(jnp.float32),
        lax.psum_scatter(
            down_sum.astype(jnp.bfloat16), "seq", scatter_dimension=1, tiled=True
        ).astype(jnp.float32),
    )
    row_grad = jnp.einsum(
        "ts,sd->td",
        token_table,
        back_rows.reshape(-1, model_width),
        preferred_element_type=jnp.float32,
    )
    normed_two_grad, router_sum = gates_back(gate_grad_pairs)
    mid_part, gain_two_sum = norm_two_back(normed_two_grad + row_grad)
    mid_grad = grad_out + mid_part
    attention_grad = mid_grad.astype(low_type)
    out_w_sum = jnp.einsum(
        "tk,td->kd", context_local, attention_grad, preferred_element_type=jnp.float32
    )
    context_grad = jnp.einsum(
        "td,kd->tk", attention_grad, out_w, preferred_element_type=jnp.float32
    ).astype(low_type)
    context_heads = lax.all_to_all(
        context_grad.reshape(groups, local_len, -1), "seq", split_axis=2, concat_axis=1, tiled=True
    )
    query_back, key_back, value_back, table_local = attend_backward(
        query_heads,
        key_heads,
        value_heads,
        table_rows,
        segment_ids,
        log_totals,
        split_heads(context_heads),
    )
    query_pos, key_pos, value_pos = (
        lax.all_to_all(query_back, "seq", split_axis=1, concat_axis=2, tiled=True),
        lax.all_to_all(key_back, "seq", split_axis=1, concat_axis=2, tiled=True),
        lax.all_to_all(value_back, "seq", split_axis=1, concat_axis=2, tiled=True),
    )
    query_pos = query_pos.reshape(tokens, -1)
    key_pos = key_pos.reshape(tokens, -1)
    value_pos = value_pos.reshape(tokens, -1)
    normed_one_grad = jnp.einsum(
        "tk,dk->td", query_pos, query_w, preferred_element_type=jnp.float32
    )
    normed_one_grad = normed_one_grad + jnp.einsum(
        "tk,dk->td", key_pos, key_w, preferred_element_type=jnp.float32
    )
    normed_one_grad = normed_one_grad + jnp.einsum(
        "tk,dk->td", value_pos, value_w, preferred_element_type=jnp.float32
    )
    query_sum = jnp.einsum("td,tk->dk", normed_one, query_pos, preferred_element_type=jnp.float32)
    key_sum = jnp.einsum("td,tk->dk", normed_one, key_pos, preferred_element_type=jnp.float32)
    value_sum = jnp.einsum("td,tk->dk", normed_one, value_pos, preferred_element_type=jnp.float32)
    input_part, gain_one_sum = norm_one_back(normed_one_grad)
    block_in_grad = (mid_grad + input_part).reshape(groups, local_len, model_width)
    table_sum = lax.dynamic_update_slice_in_dim(
        jnp.zeros(table_full.shape, jnp.float32), table_local, first_head, 0
    ).reshape(-1)
    gain_one_out, query_out, key_out, value_out, out_w_out, table_out, gain_two_out, router_out = (
        lax.psum_scatter(gain_one_sum, ("seq", "exp"), scatter_dimension=0, tiled=True),
        lax.psum_scatter(query_sum, ("seq", "exp"), scatter_dimension=0, tiled=True),
        lax.psum_scatter(key_sum, ("seq", "exp"), scatter_dimension=0, tiled=True),
        lax.psum_scatter(value_sum, ("seq", "exp"), scatter_dimension=0, tiled=True),
        lax.psum_scatter(out_w_sum, ("seq", "exp"), scatter_dimension=0, tiled=True),
        lax.psum_scatter(table_sum, ("seq", "exp"), scatter_dimension=0, tiled=True),
        lax.psum_scatter(gain_two_sum, ("seq", "exp"), scatter_dimension=0, tiled=True),
        lax.psum_scatter(router_sum, ("seq", "exp"), scatter_dimension=0, tiled=True),
    )
    return (
        block_out,
        block_in_grad,
        gain_one_out,
        query_out,
        key_out,
        value_out,
        out_w_out,
        table_out,
        gain_two_out,
        router_out,
        gate_owned,
        up_owned,
        down_owned,
    )


def solution(mesh):
    placed = (
        P("exp", "seq", None),
        P("exp", "seq", None),
        P("exp", None),
        P("exp", "seq", None),
        P("exp", "seq", None),
        P(("seq", "exp")),
        P(("seq", "exp"), None),
        P(("seq", "exp"), None),
        P(("seq", "exp"), None),
        P(("seq", "exp"), None),
        P(("seq", "exp")),
        P(("seq", "exp")),
        P(("seq", "exp"), None),
        P("exp", "seq", None),
        P("exp", "seq", None),
        P("exp", "seq", None),
    )
    return jax.shard_map(
        per_device,
        mesh=mesh,
        in_specs=placed,
        out_specs=(
            P("exp", "seq", None),
            P("exp", "seq", None),
            P(("seq", "exp")),
            P(("seq", "exp"), None),
            P(("seq", "exp"), None),
            P(("seq", "exp"), None),
            P(("seq", "exp"), None),
            P(("seq", "exp")),
            P(("seq", "exp")),
            P(("seq", "exp"), None),
            P("exp", "seq", None),
            P("exp", "seq", None),
            P("exp", "seq", None),
        ),
        check_vma=False,
    )
```

profile of v0, /device:TPU:0, one launch (start us, length us, event | category | flops | bytes accessed | tf_op | source)
XLA Modules:
  0.0 3056.6 jit_solution(3866187155260220145)
XLA Ops:
  16.4 42.2 %all-reduce.7 = (bf16[1024]{0:T(1024)(128)(2,1)S(1)}, bf16[512]{0:T(512)(128)(2,1)S(1)}, bf16[1024]{0:T(1024)(128)(2,1)}) all-reduce(bf16[1024]{0:T(1024)(128)(2,1)S(1)} %dynamic-update-slice, bf16[512]{0:T(512)(128)(2,1)S(1)} %dynamic-update-slice.1, bf16[1024]{0:T(1024)(128)(2,1)S(1)} %dynamic-update-slice.2), channel_id=1, replica_groups=mesh['seq'=8,'exp'=4] {'seq','exp'}, use_global_device_ids=true, to_apply=%add | all-reduce | flops 2560 | bytes 10240
  83.2 71.3 %all-gather.11.cloned.1.call-done = bf16[1024,1024]{1,0:T(8,128)(2,1)} async-done(((bf16[32,1024]{1,0:T(8,128)(2,1)}), bf16[1024,1024]{1,0:T(8,128)(2,1)}) %all-gather.11.cloned.1.call-update) | async-done | bytes 2097168 | tf_op jit(solution)/shard_map/all_gather | solution.py:210
  169.0 67.3 %all-gather.13.cloned.1.call-done = bf16[1024,1024]{1,0:T(8,128)(2,1)} async-done(((bf16[32,1024]{1,0:T(8,128)(2,1)}), bf16[1024,1024]{1,0:T(8,128)(2,1)}) %all-gather.13.cloned.1.call-update) | async-done | bytes 2097168 | tf_op jit(solution)/shard_map/all_gather | solution.py:211
  310.1 496.4 %while.29 = (s32[]{:T(128)}, bf16[4,4,512,2,64]{2,4,3,1,0:T(8,128)(2,1)}, f32[4,4,2,512]{3,2,1,0:T(2,128)S(1)}, s32[4]{0:T(128)S(1)}, s32[4,2048]{1,0:T(4,128)S(...) while((s32[]{:T(128)}, ...), condition=%wide.region_4.5_spmd, body=%wide.region_1.4_spmd.sunk | while | flops 2472800768 | bytes 265483792 | solution.py:132
  830.6 69.5 %all-gather = bf16[32,32,4]{1,2,0:T(4,128)(2,1)S(1)} all-gather(bf16[1,32,4]{1,2,0:T(4,128)(2,1)S(1)} %convert_bitcast_fusion), channel_id=1, replica_groups=mesh['seq'=8,'exp'=4] {'seq','exp'}, dimensions={0}, use_global_device_ids=true | all-gather | bytes 8448 | tf_op jit(solution)/shard_map/all_gather | solution.py:215
  961.7 43.4 %all-to-all-done.6 = bf16[4,640,1024]{2,1,0:T(8,128)(2,1)} async-done(((bf16[4,640,1024]{2,1,0:T(8,128)(2,1)}), bf16[4,640,1024]{2,1,0:T(8,128)(2,1)}, u32[]{:S(2)}, u32[]{:S(2)}) %all-to-all-start.6) | async-done | bytes 5242912 | tf_op jit(solution)/shard_map/all_to_all | solution.py:338
  1032.9 36.9 %all-to-all-done.4 = bf16[4,640,1024]{2,1,0:T(8,128)(2,1)} async-done(((bf16[4,640,1024]{2,1,0:T(8,128)(2,1)}), bf16[4,640,1024]{2,1,0:T(8,128)(2,1)}, u32[]{:S(2)}, u32[]{:S(2)}) %all-to-all-start.4) | async-done | bytes 5242912 | tf_op jit(solution)/shard_map/all_to_all | solution.py:295
  1092.3 50.4 %fusion.132 = (bf16[4,640,2816]{2,1,0:T(8,128)(2,1)}, bf16[4,1,640,2816]{3,2,0,1:T(8,128)(2,1)}, bf16[4,640,2816]{2,1,0:T(8,128)(2,1)}) fusion(f32[4,640,2816]{2,1,0:T(8,128)} %fusion.144, f32[4,640,2816]{2,1,0:T(8,128)} %fusion.150, bf16[4,640,1024]{2,1,0:T(8,128)(2,1)} %all-to-all-done.4, bf16[1,1024,2816]{2,1,0:T(8,128)(2,1)} %all-gather.17.cloned.1.call-done), kind=kOutput, calls=%fused_computation.272 | convolution fusion | flops 14980218880 | bytes 111935488 | tf_op jit(solution)/shard_map/necd,edf->necf/dot_general | solution.py:299
  1168.9 59.4 %all-to-all-done.5 = bf16[4,640,1024]{2,1,0:T(8,128)(2,1)} async-done(((bf16[4,640,1024]{2,1,0:T(8,128)(2,1)}), bf16[4,640,1024]{2,1,0:T(8,128)(2,1)}, u32[]{:S(2)}, u32[]{:S(2)}) %all-to-all-start.5) | async-done | bytes 5242912 | tf_op jit(solution)/shard_map/all_to_all | solution.py:306
  1441.2 47.3 %all-to-all-done.8 = bf16[4,256,1024]{1,0,2:T(4,128)(2,1)S(1)} async-done(((bf16[4,256,1024]{1,0,2:T(4,128)(2,1)}), bf16[4,256,1024]{1,0,2:T(4,128)(2,1)S(1)}, u32[]{:S(2)}, u32[]{:S(2)}) %all-to-all-start.8) | async-done | bytes 2097184 | tf_op jit(solution)/shard_map/all_to_all | solution.py:398
  1497.0 1042.8 %while.30 = (s32[]{:T(128)}, f32[4,2048,2,64]{1,3,2,0:T(8,128)}, f32[4,2048,2,64]{1,3,2,0:T(8,128)}, f32[2,32]{1,0:T(2,128)S(1)}, bf16[4,4,512,2,64]{2,4,3,1,0:T...) while((s32[]{:T(128)}, f32[4,2048,2,64]{1,3,2,0:T(8,128)}, ...), condition=%wide.region_55.56_spmd.clone, body=%wide.region_20.55_spmd.clone.sunk | while | flops 11232626688 | bytes 458345472 | solution.py:174
  1588.5 34.5 %fusion.334 = f32[2,512,2048]{2,1,0:T(8,128)} fusion(f32[4,2,512,2048]{3,2,1,0:T(8,128)} %subtract_exponential_fusion.4, bf16[4,2048,2,64]{1,3,2,0:T(8,128)(2,1)} %get-tuple-element.1072, bf16[4,2048,2,64]{1,3,2,0:T(8,128)(2,1)} %get-tuple-element.1071, s32[]{:T(128)S(6)} %select_n.1244), kind=kOutput, calls=%fused_computation.405.clone.1 | convolution fusion | flops 2178947072 | bytes 80741376 | tf_op jit(solution)/shard_map/while/body/eval_jaxpr/sub | solution.py:160
  1847.7 34.5 %fusion.334 = f32[2,512,2048]{2,1,0:T(8,128)} fusion(f32[4,2,512,2048]{3,2,1,0:T(8,128)} %subtract_exponential_fusion.4, bf16[4,2048,2,64]{1,3,2,0:T(8,128)(2,1)} %get-tuple-element.1072, bf16[4,2048,2,64]{1,3,2,0:T(8,128)(2,1)} %get-tuple-element.1071, s32[]{:T(128)S(6)} %select_n.1244), kind=kOutput, calls=%fused_computation.405.clone.1 | convolution fusion | flops 2178947072 | bytes 80741376 | tf_op jit(solution)/shard_map/while/body/eval_jaxpr/sub | solution.py:160
  1950.0 34.0 %bitcast_add_fusion.5 = f32[4,2048,2,64]{1,3,2,0:T(8,128)} fusion(f32[4,2048,2,64]{1,3,2,0:T(8,128)} %get-tuple-element.1043, f32[4,2,512,2048]{3,2,1,0:T(8,128)} %subtract_exponential_fusion.4, bf16[4,2048,2,64]{1,3,2,0:T(8,128)(2,1)} %get-tuple-element.1072, pred[]{:T(512)S(6)} %compare.3, bf16[4,2048,2,64]{1,3,2,0:T(8,128)(2,1)} %get-tuple-element.1066, ...), kind=kOutput, calls=%fused_computation.143.clone.1 | convolution fusion | flops 3265271808 | bytes 81266688 | tf_op jit(solution)/shard_map/while/body/eval_jaxpr/ghqk,gqhd->gkhd/dot_general | solution.py:167
  2108.3 34.6 %fusion.334 = f32[2,512,2048]{2,1,0:T(8,128)} fusion(f32[4,2,512,2048]{3,2,1,0:T(8,128)} %subtract_exponential_fusion.4, bf16[4,2048,2,64]{1,3,2,0:T(8,128)(2,1)} %get-tuple-element.1072, bf16[4,2048,2,64]{1,3,2,0:T(8,128)(2,1)} %get-tuple-element.1071, s32[]{:T(128)S(6)} %select_n.1244), kind=kOutput, calls=%fused_computation.405.clone.1 | convolution fusion | flops 2178947072 | bytes 80741376 | tf_op jit(solution)/shard_map/while/body/eval_jaxpr/sub | solution.py:160
  2210.8 34.4 %bitcast_add_fusion.5 = f32[4,2048,2,64]{1,3,2,0:T(8,128)} fusion(f32[4,2048,2,64]{1,3,2,0:T(8,128)} %get-tuple-element.1043, f32[4,2,512,2048]{3,2,1,0:T(8,128)} %subtract_exponential_fusion.4, bf16[4,2048,2,64]{1,3,2,0:T(8,128)(2,1)} %get-tuple-element.1072, pred[]{:T(512)S(6)} %compare.3, bf16[4,2048,2,64]{1,3,2,0:T(8,128)(2,1)} %get-tuple-element.1066, ...), kind=kOutput, calls=%fused_computation.143.clone.1 | convolution fusion | flops 3265271808 | bytes 81266688 | tf_op jit(solution)/shard_map/while/body/eval_jaxpr/ghqk,gqhd->gkhd/dot_general | solution.py:167
  2369.6 34.6 %fusion.334 = f32[2,512,2048]{2,1,0:T(8,128)} fusion(f32[4,2,512,2048]{3,2,1,0:T(8,128)} %subtract_exponential_fusion.4, bf16[4,2048,2,64]{1,3,2,0:T(8,128)(2,1)} %get-tuple-element.1072, bf16[4,2048,2,64]{1,3,2,0:T(8,128)(2,1)} %get-tuple-element.1071, s32[]{:T(128)S(6)} %select_n.1244), kind=kOutput, calls=%fused_computation.405.clone.1 | convolution fusion | flops 2178947072 | bytes 80741376 | tf_op jit(solution)/shard_map/while/body/eval_jaxpr/sub | solution.py:160
  2472.0 34.3 %bitcast_add_fusion.5 = f32[4,2048,2,64]{1,3,2,0:T(8,128)} fusion(f32[4,2048,2,64]{1,3,2,0:T(8,128)} %get-tuple-element.1043, f32[4,2,512,2048]{3,2,1,0:T(8,128)} %subtract_exponential_fusion.4, bf16[4,2048,2,64]{1,3,2,0:T(8,128)(2,1)} %get-tuple-element.1072, pred[]{:T(512)S(6)} %compare.3, bf16[4,2048,2,64]{1,3,2,0:T(8,128)(2,1)} %get-tuple-element.1066, ...), kind=kOutput, calls=%fused_computation.143.clone.1 | convolution fusion | flops 3265271808 | bytes 81266688 | tf_op jit(solution)/shard_map/while/body/eval_jaxpr/ghqk,gqhd->gkhd/dot_general | solution.py:167
  2565.4 46.6 %all-to-all-done.9 = bf16[4,2048,128]{2,0,1:T(4,128)(2,1)} async-done(((bf16[4,2048,128]{2,0,1:T(4,128)(2,1)}), bf16[4,2048,128]{2,0,1:T(4,128)(2,1)}, u32[]{:S(2)}, u32[]{:S(2)}) %all-to-all-start.9) | async-done | bytes 2097184 | tf_op jit(solution)/shard_map/all_to_all | solution.py:411
  2629.1 60.3 %all_to_all.140 = bf16[4,2048,128]{2,0,1:T(4,128)(2,1)S(1)} all-to-all(bf16[4,2048,128]{2,0,1:T(4,128)(2,1)} %copy.248), channel_id=1, replica_groups=mesh['seq'=8,'exp'=4] {'seq'}, dimensions={1} | all-to-all | bytes 4194304 | tf_op jit(solution)/shard_map/all_to_all | solution.py:412
  2705.0 59.1 %all_to_all.141 = bf16[4,2048,128]{2,0,1:T(4,128)(2,1)S(1)} all-to-all(bf16[4,2048,128]{2,0,1:T(4,128)(2,1)} %copy.251), channel_id=1, replica_groups=mesh['seq'=8,'exp'=4] {'seq'}, dimensions={1} | all-to-all | bytes 4194304 | tf_op jit(solution)/shard_map/all_to_all | solution.py:413
  2785.4 40.2 %all-reduce.6 = (f32[1024]{0:T(1024)S(1)}, f32[512]{0:T(512)S(1)}, f32[1024]{0:T(1024)S(1)}) all-reduce(f32[1024]{0:T(1024)S(1)} %get-tuple-element.325, f32[512]{0:T(512)S(1)} %reshape.1893, f32[1024]{0:T(1024)S(1)} %copy-done.58), channel_id=2, replica_groups=mesh['seq'=8,'exp'=4] {'seq','exp'}, use_global_device_ids=true, to_apply=%region_58.59.clone | all-reduce | flops 2560 | bytes 20480
  2839.8 70.3 %reduce-scatter.13.cloned.1.call-done = f32[32,1024]{1,0:T(8,128)} async-done(((f32[1024,1024]{1,0:T(8,128)}), f32[32,1024]{1,0:T(8,128)}) %reduce-scatter.13.cloned.1.call-update) | async-done | bytes 131088 | tf_op jit(solution)/shard_map/reduce_scatter | solution.py:438
  2910.0 139.8 %reduce-scatter.15.cloned.1.call-done = f32[32,1024]{1,0:T(8,128)} async-done(((f32[1024,1024]{1,0:T(8,128)}), f32[32,1024]{1,0:T(8,128)}) %reduce-scatter.15.cloned.1.call-update) | async-done | bytes 131088 | tf_op jit(solution)/shard_map/reduce_scatter | solution.py:439
  (600 shorter events, 1881.8 us)
Async XLA Ops:
  7.2 63.4 %all-gather.9.cloned.1.call-start = ((), (), s32[]{:S(2)}) async-start(), calls=%async_computation.20 | async-start | bytes 2162688 | tf_op jit(solution)/shard_map/all_gather | solution.py:209
  8.9 145.6 %all-gather.11.cloned.1.call-start = ((), (), s32[]{:S(2)}) async-start(), calls=%async_computation.21 | async-start | bytes 2162688 | tf_op jit(solution)/shard_map/all_gather | solution.py:210
  10.6 225.8 %all-gather.13.cloned.1.call-start = ((), (), s32[]{:S(2)}) async-start(), calls=%async_computation.22 | async-start | bytes 2162688 | tf_op jit(solution)/shard_map/all_gather | solution.py:211
  12.2 906.4 %all-gather.15.cloned.1.call-start = ((), (), s32[]{:S(2)}) async-start(), calls=%async_computation.23 | async-start | bytes 2162688 | tf_op jit(solution)/shard_map/all_gather | solution.py:212
  77.8 86.9 %all-to-all-start = ((bf16[4,256,1024]{1,0,2:T(4,128)(2,1)}), bf16[4,256,1024]{1,0,2:T(4,128)(2,1)S(1)}, u32[]{:S(2)}, u32[]{:S(2)}) async-start(bf16[4,256,1024]{1,0,2:T(4,128)(2,1)} %copy.222), calls=%async_computation | async-start | bytes 4194304 | tf_op jit(solution)/shard_map/all_to_all | solution.py:245
  82.1 928.3 %all-gather.21.cloned.1.call-start = ((), (), s32[]{:S(2)}) async-start(), calls=%async_computation.26 | async-start | bytes 6488064 | tf_op jit(solution)/shard_map/all_gather | solution.py:220
  164.7 81.9 %all-to-all-start.1 = ((bf16[4,256,1024]{1,0,2:T(4,128)(2,1)}), bf16[4,256,1024]{1,0,2:T(4,128)(2,1)}, u32[]{:S(2)}, u32[]{:S(2)}) async-start(bf16[4,256,1024]{1,0,2:T(4,128)(2,1)} %copy.224), calls=%async_computation.1 | async-start | bytes 4194304 | tf_op jit(solution)/shard_map/all_to_all | solution.py:246
  246.6 56.8 %all-to-all-start.2 = ((bf16[4,256,1024]{1,0,2:T(4,128)(2,1)}), bf16[4,256,1024]{1,0,2:T(4,128)(2,1)}, u32[]{:S(2)}, u32[]{:S(2)}) async-start(bf16[4,256,1024]{1,0,2:T(4,128)(2,1)} %copy.226), calls=%async_computation.2 | async-start | bytes 4194304 | tf_op jit(solution)/shard_map/all_to_all | solution.py:247
  251.0 782.0 %all-gather.19.cloned.1.call-start = ((), (), s32[]{:S(2)}) async-start(), calls=%async_computation.25 | async-start | bytes 6488064 | tf_op jit(solution)/shard_map/all_gather | solution.py:219
  826.2 88.0 %all-to-all-start.3 = ((bf16[4,2048,128]{2,0,1:T(4,128)(2,1)}), bf16[4,2048,128]{2,0,1:T(4,128)(2,1)}, u32[]{:S(2)}, u32[]{:S(2)}) async-start(bf16[4,2048,128]{2,0,1:T(4,128)(2,1)} %reshape.1914), calls=%async_computation.3 | async-start | bytes 4194304 | tf_op jit(solution)/shard_map/all_to_all | solution.py:259
  940.5 64.6 %all-to-all-start.6 = ((bf16[4,640,1024]{2,1,0:T(8,128)(2,1)}), bf16[4,640,1024]{2,1,0:T(8,128)(2,1)}, u32[]{:S(2)}, u32[]{:S(2)}) async-start(bf16[4,640,1024]{2,1,0:T(8,128)(2,1)} %bitcast.591), calls=%async_computation.6 | async-start | bytes 10485760 | tf_op jit(solution)/shard_map/all_to_all | solution.py:338
  945.7 146.6 %all-gather.17.cloned.1.call-start = ((), (), s32[]{:S(2)}) async-start(), calls=%async_computation.24 | async-start | bytes 6488064 | tf_op jit(solution)/shard_map/all_gather | solution.py:218
  1005.1 64.7 %all-to-all-start.4 = ((bf16[4,640,1024]{2,1,0:T(8,128)(2,1)}), bf16[4,640,1024]{2,1,0:T(8,128)(2,1)}, u32[]{:S(2)}, u32[]{:S(2)}) async-start(bf16[4,640,1024]{2,1,0:T(8,128)(2,1)} %bitcast.590), calls=%async_computation.4 | async-start | bytes 10485760 | tf_op jit(solution)/shard_map/all_to_all | solution.py:295
  1163.7 64.6 %all-to-all-start.5 = ((bf16[4,640,1024]{2,1,0:T(8,128)(2,1)}), bf16[4,640,1024]{2,1,0:T(8,128)(2,1)}, u32[]{:S(2)}, u32[]{:S(2)}) async-start(bf16[4,640,1024]{2,1,0:T(8,128)(2,1)} %fusion.174), calls=%async_computation.5 | async-start | bytes 10485760 | tf_op jit(solution)/shard_map/all_to_all | solution.py:306
  1168.8 1602.7 %reduce-scatter.25.cloned.1.call-start = ((), (), s32[]{:S(2)}) async-start(), calls=%async_computation.34 | async-start | bytes 540672
  1250.6 1582.2 %reduce-scatter.19.cloned.1.call-start = ((), (), s32[]{:S(2)}) async-start(), calls=%async_computation.31 | async-start | bytes 6488064 | tf_op jit(solution)/shard_map/reduce_scatter | solution.py:372
  1273.4 1561.7 %reduce-scatter.21.cloned.1.call-start = ((), (), s32[]{:S(2)}) async-start(), calls=%async_computation.32 | async-start | bytes 6488064 | tf_op jit(solution)/shard_map/reduce_scatter | solution.py:375
  1340.7 66.0 %all-to-all-start.7 = ((bf16[4,640,1024]{2,1,0:T(8,128)(2,1)}), bf16[4,640,1024]{2,1,0:T(8,128)(2,1)}, u32[]{:S(2)}, u32[]{:S(2)}) async-start(bf16[4,640,1024]{2,1,0:T(8,128)(2,1)} %add_convert_fusion), calls=%async_computation.7 | async-start | bytes 10485760 | tf_op jit(solution)/shard_map/all_to_all | solution.py:359
  1345.7 1491.7 %reduce-scatter.23.cloned.1.call-start = ((), (), s32[]{:S(2)}) async-start(), calls=%async_computation.33 | async-start | bytes 6488064 | tf_op jit(solution)/shard_map/reduce_scatter | solution.py:378
  1428.3 60.1 %all-to-all-start.8 = ((bf16[4,256,1024]{1,0,2:T(4,128)(2,1)}), bf16[4,256,1024]{1,0,2:T(4,128)(2,1)S(1)}, u32[]{:S(2)}, u32[]{:S(2)}) async-start(bf16[4,256,1024]{1,0,2:T(4,128)(2,1)} %copy.242), calls=%async_computation.8 | async-start | bytes 4194304 | tf_op jit(solution)/shard_map/all_to_all | solution.py:398
  1433.8 1406.0 %reduce-scatter.17.cloned.1.call-start = ((), (), s32[]{:S(2)}) async-start(), calls=%async_computation.30 | async-start | bytes 4325376 | tf_op jit(solution)/shard_map/reduce_scatter | solution.py:440
  2563.5 276.2 %reduce-scatter.11.cloned.1.call-start = ((), (), s32[]{:S(2)}) async-start(), calls=%async_computation.27 | async-start | bytes 4325376 | tf_op jit(solution)/shard_map/reduce_scatter | solution.py:437
  2620.9 289.1 %reduce-scatter.13.cloned.1.call-start = ((), (), s32[]{:S(2)}) async-start(), calls=%async_computation.28 | async-start | bytes 4325376 | tf_op jit(solution)/shard_map/reduce_scatter | solution.py:438
  2696.8 353.1 %reduce-scatter.15.cloned.1.call-start = ((), (), s32[]{:S(2)}) async-start(), calls=%async_computation.29 | async-start | bytes 4325376 | tf_op jit(solution)/shard_map/reduce_scatter | solution.py:439
  (84 other events, 1342.6 us)
Sparse Core Ops, SparseCore 0:
  11.5 59.0 all-gather.8
  74.0 80.4 all-gather.10
  157.9 78.3 all-gather.12
  239.7 78.5 all-gather.14
  320.3 91.4 all-gather.20
  413.9 90.8 all-gather.18
  949.3 95.3 all-gather.16
  1250.7 136.2 reduce-scatter.24
  1391.1 135.4 reduce-scatter.18
  1530.5 109.7 reduce-scatter.20
  1644.3 109.7 reduce-scatter.22
  1757.0 140.6 reduce-scatter.16
  2621.1 148.5 reduce-scatter.10
  2772.4 137.5 reduce-scatter.12
  2912.8 137.0 reduce-scatter.14
where the time goes:
time: 3070 us; the launch traced here: 3060 us
  matrix products  1050 us (34%)
  other arithmetic  852 us (28%)
  waiting for transfers between devices  650 us (21%)
  blocking collectives  271 us (9%)
  local copies, waits for them, and re-layouts  146 us (5%)
  starting transfers between devices  60.2 us (2%)
    add x8, other arithmetic, bias_lookup(): total + jnp.where(bucket_ids[None] == bucket, table_rows[:, bucket][:, No...  270 us
    eq x8, other arithmetic, bias_lookup(): bucket_ids[None] == bucket  249 us
    reduce_sum x8, other arithmetic, bucket_totals(): jnp.sum(jnp.where(bucket_ids[None] == bucket, summed, 0.0), axis=(1, 2))  191 us
    dot_general x8, matrix products, scores_block(): jnp.einsum('gqhd,gkhd->ghqk', query_block, key_heads, preferred_element_t...  159 us
    reduce_scatter x1, waiting for transfers between devices, per_device(): lax.psum_scatter(value_sum, ('seq', 'exp'), scatter_dimension=0, tiled=True)  140 us
    sub x4, matrix products, one_block(): prob_grad - jnp.sum(probabilities * prob_grad, axis=-1, keepdims=True)  138 us
    dot_general x4, matrix products, one_block(): jnp.einsum('ghqk,gqhd->gkhd', raw_grad, query_block, preferred_element_ty...  136 us
    dot_general x4, matrix products, one_block(): jnp.einsum('ghqk,gkhd->gqhd', raw_grad, key_heads, preferred_element_type...  132 us
  transfers between devices with their start and end apart: 25, of which 12 were waited for; matrix products, arithmetic and copies ran while one was open for 63% of the time, Pallas kernels for 0%

commit v1 on v0

v1 whole, which is shorter than its diff:
```python
from functools import partial

import jax
import jax.numpy as jnp
import numpy as np
from jax import lax
from jax.experimental import pallas as pl
from jax.experimental.pallas import tpu as pltpu
from jax.sharding import PartitionSpec as P

HEAD_DIM = 64
BUCKETS = 32
THRESHOLDS = (12, 16, 23, 32, 46, 64, 91)
MASKED = -1e30
TILE = 256
LANES = 128
NT = (((1,), (1,)), ((), ()))


def bucket_of(d):
    a = np.abs(d)
    extra = sum((a >= t).astype(np.int64) for t in THRESHOLDS)
    return np.where(a < 8, a, 8 + extra) + 16 * (d > 0)


def bias_rows(table_rows, tile):
    u = np.arange(2 * tile)
    x = np.where(u < tile, u, u - 2 * tile)
    ids = np.stack([bucket_of(step * tile - x) for step in (-1, 0, 1)])
    hot = (ids.reshape(-1)[None, :] == np.arange(BUCKETS)[:, None]).astype(np.float32)
    rows = jnp.dot(table_rows.astype(jnp.bfloat16), jnp.asarray(hot, jnp.bfloat16), preferred_element_type=jnp.float32)
    return rows.reshape(table_rows.shape[0], 3, 2 * tile)


def tile_ranges(segments, tile):
    blocks = segments.reshape(-1, tile)
    first, last = blocks[:, 0], blocks[:, -1]
    low = jnp.sum((last[None, :] < first[:, None]).astype(jnp.int32), axis=1)
    high = jnp.sum((first[None, :] <= last[:, None]).astype(jnp.int32), axis=1)
    return jnp.stack([low, high])


def segment_columns(segments):
    lane = jnp.arange(LANES, dtype=jnp.int32)[None, :]
    seg = segments[:, None]
    same = seg == lane
    query_side = jnp.where(same & (lane < 4), MASKED, 0.0).astype(jnp.bfloat16)
    key_side = jnp.where(lane < 4, (~same).astype(jnp.float32), (lane < 9).astype(jnp.float32)).astype(jnp.bfloat16)
    return query_side, key_side


def toeplitz(row, tile):
    wide = jnp.broadcast_to(row, (tile, row.shape[1]))
    return pltpu.roll(wide, 0, 1, stride=1, stride_axis=0)[:, :tile]


def fwd_kernel(ranges, ends, q_ref, k_ref, v_ref, qs_ref, ks_ref, rows_ref, o_ref, lse_ref, bias_ref, vt_ref):
    group, qb = pl.program_id(0), pl.program_id(1)
    tile, span = q_ref.shape
    heads = span // HEAD_DIM

    @pl.when(qb == 0)
    def _():
        for h in range(heads):
            for step in range(3):
                bias_ref[h, step] = toeplitz(rows_ref[h, step : step + 1, :], tile)
        for start in range(0, v_ref.shape[0], tile):
            vt_ref[:, start : start + tile] = v_ref[start : start + tile, :].T

    low, high = ranges[0, qb], ranges[1, qb]
    lane = lax.broadcasted_iota(jnp.int32, (tile, LANES), 1)
    q = q_ref[...] * jnp.bfloat16(HEAD_DIM**-0.5)
    qs = qs_ref[...]
    halves = []
    for h in range(heads):
        part = q[:, h // 2 * LANES : (h // 2 + 1) * LANES]
        keep = (lane < HEAD_DIM) if h % 2 == 0 else (lane >= HEAD_DIM)
        halves.append(jnp.where(keep, part, jnp.zeros_like(part)))

    def side(h, which):
        if which == 1:
            extra = qs
        else:
            value = ends[heads * group + h, which // 2].astype(jnp.bfloat16)
            extra = jnp.where(lane == 7, value, qs)
        return jnp.concatenate([halves[h], extra], axis=1)

    def visit(which):
        queries = [side(h, which) for h in range(heads)]

        def step(kb, carry):
            keys = pl.ds(pl.multiple_of(kb * tile, tile), tile)
            ks = ks_ref[keys, :]
            scores = []
            for h in range(heads):
                kx = jnp.concatenate([k_ref[keys, h // 2 * LANES : (h // 2 + 1) * LANES], ks], axis=1)
                scores.append(lax.dot_general(kx, queries[h], NT, preferred_element_type=jnp.float32))
            out = []
            for h in range(heads):
                peak, total, acc = carry[h]
                s = scores[h]
                if which == 1:
                    s = s + bias_ref[h, kb - qb + 1]
                new = jnp.maximum(peak, jnp.max(s, axis=0, keepdims=True))
                p = jnp.exp(s - new)
                scale = jnp.exp(peak - new)
                total = total * scale + jnp.sum(p, axis=0, keepdims=True)
                vt = vt_ref[h * HEAD_DIM : (h + 1) * HEAD_DIM, keys]
                acc = acc * scale + jnp.dot(vt, p.astype(jnp.bfloat16), preferred_element_type=jnp.float32)
                out.append((new, total, acc))
            return tuple(out)

        return step

    start = tuple(
        (
            jnp.full((1, tile), -3e38, jnp.float32),
            jnp.zeros((1, tile), jnp.float32),
            jnp.zeros((HEAD_DIM, tile), jnp.float32),
        )
        for _ in range(heads)
    )
    near_low, near_high = jnp.maximum(low, qb - 1), jnp.minimum(high, qb + 2)
    state = lax.fori_loop(near_low, near_high, visit(1), start)
    state = lax.fori_loop(low, near_low, visit(0), state)
    state = lax.fori_loop(near_high, high, visit(2), state)
    outs = []
    for h in range(heads):
        peak, total, acc = state[h]
        outs.append(acc / total)
        lse_ref[h // 2, h % 2 : h % 2 + 1, :] = peak + jnp.log(total)
    o_ref[...] = jnp.concatenate(outs, axis=0).T.astype(o_ref.dtype)


FWD_PAIRS = 4


def attend_forward(qkv, qs, ks, ranges, rows, ends):
    length, width = qkv.shape[0], qkv.shape[1] // 3
    tile = min(TILE, length)
    pairs = width // LANES
    together = FWD_PAIRS if pairs % FWD_PAIRS == 0 else 1
    span = together * LANES
    tiles = length // tile
    spec = pltpu.PrefetchScalarGridSpec(
        num_scalar_prefetch=2,
        grid=(pairs // together, tiles),
        in_specs=[
            pl.BlockSpec((tile, span), lambda p, i, *_: (i, p)),
            pl.BlockSpec((length, span), lambda p, i, *_: (0, width // span + p)),
            pl.BlockSpec((length, span), lambda p, i, *_: (0, 2 * (width // span) + p)),
            pl.BlockSpec((tile, LANES), lambda p, i, *_: (i, 0)),
            pl.BlockSpec((length, LANES), lambda p, i, *_: (0, 0)),
            pl.BlockSpec((2 * together, 3, 2 * tile), lambda p, i, *_: (p, 0, 0)),
        ],
        out_specs=[
            pl.BlockSpec((tile, span), lambda p, i, *_: (i, p)),
            pl.BlockSpec((together, 2, tile), lambda p, i, *_: (p, 0, i)),
        ],
        scratch_shapes=[
            pltpu.VMEM((2 * together, 3, tile, tile), jnp.float32),
            pltpu.VMEM((span, length), jnp.bfloat16),
        ],
    )
    return pl.pallas_call(
        fwd_kernel,
        name="attend_forward",
        out_shape=(
            jax.ShapeDtypeStruct((length, width), jnp.bfloat16),
            jax.ShapeDtypeStruct((pairs, 2, length), jnp.float32),
        ),
        grid_spec=spec,
        compiler_params=pltpu.CompilerParams(
            dimension_semantics=("arbitrary", "arbitrary"), vmem_limit_bytes=48 << 20
        ),
        cost_estimate=pl.CostEstimate(flops=length * length * width * 4, bytes_accessed=length * width * 8, transcendentals=0),
    )(ranges, ends, qkv, qkv, qkv, qs, ks, rows)


def pieces(row):
    high = row.astype(jnp.bfloat16).astype(jnp.float32)
    mid = (row - high).astype(jnp.bfloat16).astype(jnp.float32)
    return high, mid, row - high - mid


def bwd_kernel(ranges, ends, q_ref, k_ref, v_ref, do_ref, o_ref, lse_ref, qs_ref, ks_ref, rows_ref,
               dq_ref, dk_ref, dv_ref, diag_ref, far_ref,
               qx_ref, dox_ref, kt_ref, bias_ref, dsum_ref, fsum_ref, dqt_ref, dka_ref, dva_ref):
    pair = pl.program_id(0)
    length = q_ref.shape[0]
    tile = bias_ref.shape[2]
    tiles = length // tile
    for h in range(2):
        for step in range(3):
            bias_ref[h, step] = toeplitz(rows_ref[h, step : step + 1, :], tile)
    dsum_ref[...] = jnp.zeros_like(dsum_ref)
    fsum_ref[...] = jnp.zeros_like(fsum_ref)
    dqt_ref[...] = jnp.zeros_like(dqt_ref)
    lane = lax.broadcasted_iota(jnp.int32, (tile, LANES), 1)
    sub = lax.broadcasted_iota(jnp.int32, (LANES, tile), 0)
    pick = (lax.broadcasted_iota(jnp.int32, (8, LANES), 1) // HEAD_DIM == lax.broadcasted_iota(jnp.int32, (8, LANES), 0)).astype(jnp.float32)

    @pl.loop(0, tiles)
    def _(i):
        at = pl.ds(pl.multiple_of(i * tile, tile), tile)
        q = q_ref[at, :] * jnp.bfloat16(HEAD_DIM**-0.5)
        do = do_ref[at, :]
        zero = jnp.zeros_like(q)
        product = do.astype(jnp.float32) * o_ref[at, :].astype(jnp.float32)
        delta = lax.dot_general(pick, product, NT, precision=lax.Precision.HIGHEST, preferred_element_type=jnp.float32)
        kt_ref[:, at] = k_ref[at, :].T
        for h in range(2):
            keep = (lane < HEAD_DIM) if h == 0 else (lane >= HEAD_DIM)
            a, b, c = pieces(-lse_ref[0, h : h + 1, at])
            extra = jnp.where(sub == 4, a, jnp.where(sub == 5, b, jnp.where(sub == 6, c, 0.0)))
            extra = extra.T.astype(jnp.bfloat16) + qs_ref[at, :]
            left, right = ends[2 * pair + h, 0].astype(jnp.bfloat16), ends[2 * pair + h, 1].astype(jnp.bfloat16)
            extra = jnp.where(lane == 7, left, jnp.where(lane == 8, right, extra))
            qx_ref[h, at, :] = jnp.concatenate([jnp.where(keep, q, zero), extra], axis=1)
            a, b, c = pieces(-delta[h : h + 1, :])
            extra = jnp.where(sub == 4, a, jnp.where(sub == 5, b, jnp.where(sub == 6, c, 0.0)))
            dox_ref[h, at, :] = jnp.concatenate([jnp.where(keep, do, zero), extra.T.astype(jnp.bfloat16)], axis=1)

    ones3 = ((lane >= 4) & (lane < 7)).astype(jnp.bfloat16)

    @pl.loop(0, tiles)
    def _(kb):
        low, high = ranges[0, kb], ranges[1, kb]
        keys = pl.ds(pl.multiple_of(kb * tile, tile), tile)
        k, ks = k_ref[keys, :], ks_ref[keys, :]
        vx = jnp.concatenate([v_ref[keys, :], ones3], axis=1)
        nil = jnp.zeros_like(ks)
        dka_ref[...] = jnp.zeros_like(dka_ref)
        dva_ref[...] = jnp.zeros_like(dva_ref)

        def visit(which):
            if which == 0:
                extra = jnp.where(lane == 8, nil, ks)
            elif which == 2:
                extra = jnp.where(lane == 7, nil, ks)
            else:
                extra = jnp.where((lane == 7) | (lane == 8), nil, ks)
            kx = jnp.concatenate([k, extra], axis=1)

            def step(qb, carry):
                at = pl.ds(pl.multiple_of(qb * tile, tile), tile)
                weights, grads = [], []
                for h in range(2):
                    qx, dox = qx_ref[h, at, :], dox_ref[h, at, :]
                    s = lax.dot_general(kx, qx, NT, preferred_element_type=jnp.float32)
                    if which == 1:
                        s = s + bias_ref[h, kb - qb + 1]
                    p = jnp.exp(s)
                    dp = lax.dot_general(vx, dox, NT, preferred_element_type=jnp.float32)
                    ds = p * dp
                    if which == 1:
                        dsum_ref[h, kb - qb + 1] += ds
                    else:
                        fsum_ref[h, which // 2] += jnp.sum(ds.reshape(tile // 8, 8, tile), axis=0)
                    weights.append(p.astype(jnp.bfloat16))
                    grads.append(ds.astype(jnp.bfloat16))
                    rows = slice(h * HEAD_DIM, (h + 1) * HEAD_DIM)
                    dqt_ref[rows, at] += jnp.dot(kt_ref[rows, keys], grads[h], preferred_element_type=jnp.float32)
                both_do = jnp.concatenate([dox_ref[0, at, :LANES], dox_ref[1, at, :LANES]], axis=0)
                both_q = jnp.concatenate([qx_ref[0, at, :LANES], qx_ref[1, at, :LANES]], axis=0)
                dva_ref[...] += jnp.dot(jnp.concatenate(weights, axis=1), both_do, preferred_element_type=jnp.float32)
                dka_ref[...] += jnp.dot(jnp.concatenate(grads, axis=1), both_q, preferred_element_type=jnp.float32)
                return carry

            return step

        near_low, near_high = jnp.maximum(low, kb - 1), jnp.minimum(high, kb + 2)
        lax.fori_loop(near_low, near_high, visit(1), 0)
        lax.fori_loop(near_high, high, visit(0), 0)
        lax.fori_loop(low, near_low, visit(2), 0)
        dk_ref[keys, :] = dka_ref[...].astype(dk_ref.dtype)
        dv_ref[keys, :] = dva_ref[...].astype(dv_ref.dtype)

    @pl.loop(0, tiles)
    def _(i):
        at = pl.ds(pl.multiple_of(i * tile, tile), tile)
        dq_ref[at, :] = (dqt_ref[:, at] * HEAD_DIM**-0.5).T.astype(dq_ref.dtype)

    for h in range(2):
        for step in range(3):
            diag_ref[h, step : step + 1, :] = diagonals(dsum_ref, h, step, tile)
        for step in range(2):
            total = jnp.sum(fsum_ref[h, step], axis=0, keepdims=True)
            far_ref[h, step : step + 1, :] = total


def diagonals(dsum_ref, h, step, tile):
    width = 2 * tile
    acc = jnp.zeros((8, width), jnp.float32)
    for group in range(tile // 8):
        part = dsum_ref[h, step, group * 8 : (group + 1) * 8, :]
        part = jnp.concatenate([part, jnp.zeros((8, tile), jnp.float32)], axis=1)
        acc = acc + (pltpu.roll(part, width - 8 * group, 1) if group else part)
    row = lax.broadcasted_iota(jnp.int32, (8, width), 0)
    for bit in (1, 2, 4):
        acc = jnp.where((row & bit) != 0, pltpu.roll(acc, width - bit, 1), acc)
    return jnp.sum(acc, axis=0, keepdims=True)


def attend_backward(qkv, do, o, lse, qs, ks, ranges, rows, ends):
    length, width = do.shape
    tile = min(TILE, length)
    pairs = width // LANES
    heads = width // HEAD_DIM
    column = pl.BlockSpec((length, LANES), lambda p, *_: (0, p))
    fixed = pl.BlockSpec((length, LANES), lambda p, *_: (0, 0))
    spec = pltpu.PrefetchScalarGridSpec(
        num_scalar_prefetch=2,
        grid=(pairs,),
        in_specs=[
            column,
            pl.BlockSpec((length, LANES), lambda p, *_: (0, pairs + p)),
            pl.BlockSpec((length, LANES), lambda p, *_: (0, 2 * pairs + p)),
            column,
            column,
            pl.BlockSpec((1, 2, length), lambda p, *_: (p, 0, 0)),
            fixed, fixed,
            pl.BlockSpec((2, 3, 2 * tile), lambda p, *_: (p, 0, 0)),
        ],
        out_specs=[
            column, column, column,
            pl.BlockSpec((2, 3, 2 * tile), lambda p, *_: (p, 0, 0)),
            pl.BlockSpec((2, 2, tile), lambda p, *_: (p, 0, 0)),
        ],
        scratch_shapes=[
            pltpu.VMEM((2, length, 2 * LANES), jnp.bfloat16),
            pltpu.VMEM((2, length, 2 * LANES), jnp.bfloat16),
            pltpu.VMEM((LANES, length), jnp.bfloat16),
            pltpu.VMEM((2, 3, tile, tile), jnp.float32),
            pltpu.VMEM((2, 3, tile, tile), jnp.float32),
            pltpu.VMEM((2, 2, 8, tile), jnp.float32),
            pltpu.VMEM((LANES, length), jnp.float32),
            pltpu.VMEM((tile, LANES), jnp.float32),
            pltpu.VMEM((tile, LANES), jnp.float32),
        ],
    )
    low = jax.ShapeDtypeStruct((length, width), jnp.bfloat16)
    return pl.pallas_call(
        bwd_kernel,
        name="attend_backward",
        out_shape=(
            low, low, low,
            jax.ShapeDtypeStruct((heads, 3, 2 * tile), jnp.float32),
            jax.ShapeDtypeStruct((heads, 2, tile), jnp.float32),
        ),
        grid_spec=spec,
        compiler_params=pltpu.CompilerParams(
            dimension_semantics=("arbitrary",), vmem_limit_bytes=40 << 20
        ),
        cost_estimate=pl.CostEstimate(flops=length * length * width * 10, bytes_accessed=length * width * 16, transcendentals=0),
    )(ranges, ends, qkv, qkv, qkv, do, o, lse, qs, ks, rows)


def bucket_sums(diag, far, tile):
    u = np.arange(2 * tile)
    x = np.where(u < tile, u, u - 2 * tile)
    ids = np.stack([bucket_of(step * tile - x) for step in (-1, 0, 1)])
    hot = (ids.reshape(-1)[:, None] == np.arange(BUCKETS)[None, :]).astype(np.float32)
    sums = jnp.dot(diag.reshape(diag.shape[0], -1), jnp.asarray(hot), precision=lax.Precision.HIGHEST)
    outer = jnp.sum(far, axis=2)
    ends = np.zeros((2, BUCKETS), np.float32)
    ends[0, 15] = 1
    ends[1, 31] = 1
    return sums + outer[:, 0:1] * ends[0] + outer[:, 1:2] * ends[1]


EPS = 1e-06
FULL_PRECISION = lax.Precision.HIGHEST


def gelu_tanh(value_entries):
    return (
        0.5
        * value_entries
        * (
            1.0
            + jnp.tanh(
                0.7978845608028654
                * (value_entries + 0.044715 * value_entries * value_entries * value_entries)
            )
        )
    )


def geglu_product(gate_part, up_part):
    return gelu_tanh(gate_part) * up_part


def rms_scale(value_entries, gain_row):
    return (
        value_entries
        * lax.rsqrt(jnp.mean(value_entries * value_entries, axis=-1, keepdims=True) + EPS)
        * gain_row
    )


def gate_values(routes, normed, router):
    logits = jnp.dot(normed, router, precision=FULL_PRECISION)
    row_peak = jnp.max(logits, axis=-1, keepdims=True)
    exponent = jnp.exp(logits - row_peak)
    probabilities = exponent / jnp.sum(exponent, axis=-1, keepdims=True)
    choose = (routes[..., None] == jnp.arange(router.shape[1], dtype=jnp.int32)).astype(
        probabilities.dtype
    )
    chosen = jnp.sum(probabilities[..., None, :] * choose, axis=-1)
    return chosen / jnp.sum(chosen, axis=-1, keepdims=True)


def dot32(a, b):
    return jnp.dot(a, b, preferred_element_type=jnp.float32)


ALL = ("z", "x", "exp")
SEQ = ("z", "x")


def per_device(
    block_in,
    cotangent,
    segment_ids,
    expert_routes,
    pair_priority,
    gain_attention,
    w_query,
    w_key,
    w_value,
    w_out,
    bias_table,
    gain_experts,
    w_router,
    w_gate,
    w_up,
    w_down,
):
    low_type = jnp.bfloat16
    groups, local_len, width = block_in.shape
    tokens = groups * local_len
    rows_own = w_query.shape[0]
    split = lax.axis_size("x")
    exp_count = lax.axis_size("exp")
    seq_count = groups * split
    length = local_len * seq_count
    x_at, z_at = lax.axis_index("x"), lax.axis_index("z")
    head_width = w_query.shape[1] // split
    experts_all = w_router.shape[1]
    bias_own = bias_table.shape[0]

    small = jnp.concatenate(
        [
            gain_attention[:, None],
            gain_experts[:, None],
            jnp.pad(bias_table, (0, rows_own - bias_own))[:, None],
            w_router,
        ],
        axis=1,
    )
    small = jnp.pad(small, ((0, 0), (0, LANES - small.shape[1])))
    packed = jnp.concatenate(
        [part.astype(low_type) for part in (w_query, w_key, w_value, w_out, small)], axis=1
    )
    packed = lax.all_gather(packed, ALL, axis=0, tiled=True)
    gate_w = lax.all_gather(w_gate[0].astype(low_type), SEQ, axis=0, tiled=True)
    up_w = lax.all_gather(w_up[0].astype(low_type), SEQ, axis=0, tiled=True)
    down_w = lax.all_gather(w_down[0].astype(low_type), SEQ, axis=0, tiled=True)

    outgoing = jnp.broadcast_to(block_in[:, None], (groups, split, local_len, width))
    sequence = lax.all_to_all(
        outgoing.reshape(seq_count, local_len, width), SEQ, split_axis=0, concat_axis=0, tiled=True
    ).reshape(length, width)

    hd = w_query.shape[1]
    out_w = packed[:, 3 * hd : 4 * hd]
    small_all = packed[:, 4 * hd :]
    gain_one = small_all[:, 0].astype(jnp.float32)
    gain_two = small_all[:, 1].astype(jnp.float32)
    table_all = small_all[:, 2].reshape(-1, rows_own)[:, :bias_own].reshape(-1, BUCKETS)
    router_w = small_all[:, 3 : 3 + experts_all]
    heads_here = head_width // HEAD_DIM
    qkv_w = [
        lax.dynamic_slice_in_dim(packed, part * hd + x_at * head_width, head_width, 1)
        for part in range(3)
    ]
    qkv_w = jnp.concatenate(qkv_w, axis=1)
    table_rows = lax.dynamic_slice_in_dim(table_all, x_at * heads_here, heads_here, 0)

    normed_one = rms_scale(sequence.astype(jnp.float32), gain_one).astype(low_type)
    qkv = dot32(normed_one, qkv_w).astype(low_type)
    segments = lax.dynamic_index_in_dim(segment_ids, z_at, 0, keepdims=False)
    tile = min(TILE, length)
    query_side, key_side = segment_columns(segments)
    ranges = tile_ranges(segments, tile)
    rows = bias_rows(table_rows, tile)
    ends = jnp.stack([table_rows[:, 15], table_rows[:, 31]], axis=1).astype(jnp.float32)
    contexts, log_totals = attend_forward(qkv, query_side, key_side, ranges, rows, ends)
    context_local = lax.all_to_all(
        contexts.reshape(seq_count, local_len, head_width), SEQ, split_axis=0, concat_axis=0, tiled=True
    )
    context_local = (
        context_local.reshape(groups, split, local_len, head_width)
        .transpose(0, 2, 1, 3)
        .reshape(tokens, hd)
    )
    inputs = block_in.astype(jnp.float32).reshape(tokens, width)
    mid = inputs + dot32(context_local, out_w)
    normed_two_full, norm_two_back = jax.vjp(rms_scale, mid, gain_two)
    normed_two = normed_two_full.astype(low_type)
    routes_local = expert_routes.reshape(tokens, -1)
    top_count = routes_local.shape[1]
    gates, gates_back = jax.vjp(
        partial(gate_values, routes_local),
        normed_two.astype(jnp.float32),
        router_w.astype(jnp.float32),
    )
    pair_experts = routes_local.reshape(-1)
    priority = pair_priority.reshape(-1)
    expert_table = (
        pair_experts[:, None] == jnp.arange(experts_all, dtype=jnp.int32)[None, :]
    ).astype(low_type)
    earlier = (priority[None, :] < priority[:, None]).astype(low_type)
    ahead_counts = dot32(earlier, expert_table)
    slots = jnp.sum(ahead_counts * expert_table, axis=1).astype(jnp.int32)
    capacity = (5 * top_count * tokens + 4 * experts_all - 1) // (4 * experts_all)
    slot_count = experts_all * capacity
    slot_index = jnp.where(slots < capacity, pair_experts * capacity + slots, slot_count)
    slot_table = (
        slot_index[:, None] == jnp.arange(slot_count, dtype=jnp.int32)[None, :]
    ).astype(low_type)
    slot_table = slot_table.reshape(tokens, top_count, slot_count)
    token_table = jnp.sum(slot_table, axis=1, dtype=jnp.float32).astype(low_type)
    buffer = jnp.einsum(
        "ts,td->sd", token_table, normed_two, preferred_element_type=jnp.float32
    ).astype(low_type)

    def swap_experts(rows_):
        return lax.all_to_all(
            rows_.reshape(exp_count, capacity, width), "exp", split_axis=0, concat_axis=0, tiled=True
        ).reshape(slot_count, width)

    arrived = swap_experts(buffer)
    gate_hidden = dot32(arrived, gate_w)
    up_hidden = dot32(arrived, up_w)
    hidden_pair, geglu_back = jax.vjp(geglu_product, gate_hidden, up_hidden)
    hidden = hidden_pair.astype(low_type)
    expert_out = dot32(hidden, down_w).astype(low_type)
    returned = swap_experts(expert_out)
    picked = jnp.einsum("tks,sd->tkd", slot_table, returned, preferred_element_type=jnp.float32)
    mixture = jnp.sum(picked * gates[..., None], axis=1)
    block_out = (mid + mixture).astype(low_type).reshape(groups, local_len, width)

    grad_out = cotangent.astype(jnp.float32).reshape(tokens, width)
    gate_grad_pairs = jnp.sum(picked * grad_out[:, None, :], axis=-1)
    pair_grad = (gates[..., None] * grad_out[:, None, :]).astype(low_type)
    slot_grad = jnp.einsum(
        "tks,tkd->sd", slot_table, pair_grad, preferred_element_type=jnp.float32
    ).astype(low_type)
    expert_grad_in = swap_experts(slot_grad)
    hidden_grad = jnp.einsum("sd,fd->sf", expert_grad_in, down_w, preferred_element_type=jnp.float32)
    gate_hidden_grad, up_hidden_grad = geglu_back(hidden_grad)
    gate_low = gate_hidden_grad.astype(low_type)
    up_low = up_hidden_grad.astype(low_type)
    arrived_grad = jnp.einsum("sf,df->sd", gate_low, gate_w, preferred_element_type=jnp.float32)
    arrived_grad = (
        arrived_grad
        + jnp.einsum("sf,df->sd", up_low, up_w, preferred_element_type=jnp.float32)
    ).astype(low_type)
    back_rows = swap_experts(arrived_grad)

    def summed(a, b):
        return jnp.einsum("sa,sb->ab", a, b, preferred_element_type=jnp.float32)

    def scatter_experts(total):
        return lax.psum_scatter(total.astype(low_type), SEQ, scatter_dimension=0, tiled=True).astype(
            jnp.float32
        )[None]

    down_owned = scatter_experts(summed(hidden, expert_grad_in))
    gate_owned = scatter_experts(summed(arrived, gate_low))
    up_owned = scatter_experts(summed(arrived, up_low))
    row_grad = jnp.einsum("ts,sd->td", token_table, back_rows, preferred_element_type=jnp.float32)
    normed_two_grad, router_sum = gates_back(gate_grad_pairs)
    mid_part, gain_two_sum = norm_two_back(normed_two_grad + row_grad)
    mid_grad = grad_out + mid_part
    attention_grad = mid_grad.astype(low_type)
    out_w_sum = summed(context_local, attention_grad)
    context_grad = jnp.einsum(
        "td,kd->tk", attention_grad, out_w, preferred_element_type=jnp.float32
    ).astype(low_type)
    context_grad = (
        context_grad.reshape(groups, local_len, split, head_width)
        .transpose(0, 2, 1, 3)
        .reshape(seq_count, local_len, head_width)
    )
    context_heads = lax.all_to_all(
        context_grad, SEQ, split_axis=0, concat_axis=0, tiled=True
    ).reshape(length, head_width)
    query_back, key_back, value_back, diag, far = attend_backward(
        qkv, context_heads, contexts, log_totals, query_side, key_side, ranges, rows, ends
    )
    table_local = bucket_sums(diag, far, tile)

    def through(grads, part):
        weight = qkv_w[:, part * head_width : (part + 1) * head_width]
        return jnp.einsum("tk,dk->td", grads, weight, preferred_element_type=jnp.float32)

    normed_part = (through(query_back, 0) + through(key_back, 1) + through(value_back, 2)).astype(low_type)
    normed_parts = lax.all_to_all(
        normed_part.reshape(seq_count, local_len, width), SEQ, split_axis=0, concat_axis=0, tiled=True
    ).reshape(groups, split, local_len, width)
    normed_one_grad = jnp.sum(normed_parts.astype(jnp.float32), axis=1).reshape(tokens, width)
    _, norm_one_back = jax.vjp(rms_scale, inputs, gain_one)
    input_part, gain_one_sum = norm_one_back(normed_one_grad)
    block_in_grad = (mid_grad + input_part).reshape(groups, local_len, width)

    def by_owner(total):
        columns = total.shape[1]
        shaped = total.reshape(groups, split, exp_count, rows_own, columns)
        return shaped.transpose(0, 2, 1, 3, 4).reshape(-1, columns)

    def scatter_rows(total):
        return lax.psum_scatter(
            by_owner(total).astype(low_type), ("z", "exp"), scatter_dimension=0, tiled=True
        ).reshape(split, rows_own, -1)

    out_part = lax.all_to_all(scatter_rows(out_w_sum), "x", split_axis=0, concat_axis=0, tiled=True)
    out_w_out = jnp.sum(out_part.astype(jnp.float32), axis=0)
    qkv_sum = jnp.concatenate(
        [summed(normed_one, grads) for grads in (query_back, key_back, value_back)], axis=1
    )
    qkv_part = lax.all_to_all(scatter_rows(qkv_sum), "x", split_axis=0, concat_axis=0, tiled=True)
    qkv_part = qkv_part.reshape(split, rows_own, 3, head_width).transpose(2, 1, 0, 3)
    qkv_part = qkv_part.reshape(3, rows_own, hd).astype(jnp.float32)

    table_sum = lax.dynamic_update_slice_in_dim(
        jnp.zeros(table_all.shape, jnp.float32), table_local, x_at * heads_here, 0
    ).reshape(-1, bias_own)
    table_sum = jnp.pad(table_sum, ((0, 0), (0, rows_own - bias_own)))[:, None, :]
    little = jnp.concatenate(
        [
            gain_one_sum.reshape(-1, 1, rows_own),
            gain_two_sum.reshape(-1, 1, rows_own),
            table_sum,
            router_sum.reshape(-1, rows_own, experts_all).transpose(0, 2, 1),
        ],
        axis=1,
    )
    little = jnp.sum(lax.all_to_all(little, ALL, split_axis=0, concat_axis=0, tiled=True), axis=0)
    return (
        block_out,
        block_in_grad,
        little[0],
        qkv_part[0],
        qkv_part[1],
        qkv_part[2],
        out_w_out,
        little[2, :bias_own],
        little[1],
        little[3:].T,
        gate_owned,
        up_owned,
        down_owned,
    )


def solution(mesh):
    def run(*args):
        groups = args[0].shape[0] // mesh.shape["exp"]
        seq_count, exp_count = mesh.shape["seq"], mesh.shape["exp"]
        grid = mesh.devices.reshape(groups, seq_count // groups, exp_count)
        fine = jax.sharding.Mesh(grid, ALL)
        placed = P("exp", SEQ, None)
        whole = P(ALL)
        matrix = P(ALL, None)
        return jax.shard_map(
            per_device,
            mesh=fine,
            in_specs=(
                placed, placed, P("exp", None), placed, placed,
                whole, matrix, matrix, matrix, matrix, whole, whole, matrix,
                placed, placed, placed,
            ),
            out_specs=(
                placed, placed, whole, matrix, matrix, matrix, matrix, whole, whole, matrix,
                placed, placed, placed,
            ),
            check_vma=False,
        )(*args)

    return run
```

time: 3070 us -> 1460 us (0.48)
  other arithmetic: 852 us -> 67.2 us
  matrix products: 1050 us -> 341 us
  blocking collectives: 271 us -> 0 us
  Pallas kernels: 0 us -> 170 us
  local copies, waits for them, and re-layouts: 146 us -> 62.5 us
  waiting for transfers between devices: 650 us -> 728 us
    dot_general x47 -> x23, matrix products: 878 us -> 304 us  [the longest x6 82.2 us: dot32(): return jnp.dot(a, b, preferred_element_type=jnp.float32)]
    eq x16 -> x0, other arithmetic: 275 us -> none  [the longest x8 249 us: bias_lookup(): bucket_ids[None] == bucket]
    add x21 -> x1, other arithmetic: 276 us -> 5.39 us  [per_device(): block_in_grad = (mid_grad + input_part).reshape(groups, local_len, width)]
    reduce_sum x12 -> x6, other arithmetic: 255 us -> 6.64 us  [the longest x1 3.87 us: per_device(): jnp.sum(normed_parts.astype(jnp.float32), axis=1).reshape(tokens, width)]
    reduce_scatter x7 -> x5, waiting for transfers between devices: 210 us -> 390 us  [the longest x3 378 us: scatter_experts(): lax.psum_scatter(total.astype(low_type), SEQ, scatter_dimension=0, tiled=...]
    pallas_call x0 -> x2, Pallas kernels: none -> 170 us  [the longest x1 113 us: attend_backward(): pl.pallas_call(bwd_kernel, name='attend_backward', out_shape=(low, low, l...]
    sub x4 -> x0, matrix products: 138 us -> none  [one_block(): prob_grad - jnp.sum(probabilities * prob_grad, axis=-1, keepdims=True)]
    all_gather x7 -> x4, waiting for transfers between devices: 145 us -> 13.1 us  [the longest x1 12.8 us: per_device(): down_w = lax.all_gather(w_down[0].astype(low_type), SEQ, axis=0, tiled=True)]
  transfers between devices with their start and end apart: 25 -> 20, of which waited for: 12 -> 14; matrix products, arithmetic and copies ran while one was open for 63% -> 23% of each run, Pallas kernels for 0% -> 12%
where the time goes in v1:
time: 1460 us; the launch traced here: 1450 us
  waiting for transfers between devices  728 us (50%)
  matrix products  341 us (23%)
  Pallas kernels  170 us (12%)
  other arithmetic  67.2 us (5%)
  local copies, waits for them, and re-layouts  62.5 us (4%)
  starting transfers between devices  60.4 us (4%)
  between operations  15.4 us (1%)
    reduce_scatter x3, waiting for transfers between devices, scatter_experts(): lax.psum_scatter(total.astype(low_type), SEQ, scatter_dimension=0, tiled=...  378 us
    all_to_all x1, waiting for transfers between devices, per_device(): lax.all_to_all(outgoing.reshape(seq_count, local_len, width), SEQ, split_...  127 us
    pallas_call x1, Pallas kernels, attend_backward(): pl.pallas_call(bwd_kernel, name='attend_backward', out_shape=(low, low, l...  113 us
    all_to_all x4, waiting for transfers between devices, swap_experts(): lax.all_to_all(rows_.reshape(exp_count, capacity, width), 'exp', split_ax...  91.6 us
    dot_general x6, matrix products, dot32(): return jnp.dot(a, b, preferred_element_type=jnp.float32)  82.2 us
    dot_general x7, matrix products, summed(): return jnp.einsum('sa,sb->ab', a, b, preferred_element_type=jnp.float32)  79.6 us
    pallas_call x1, Pallas kernels, attend_forward(): pl.pallas_call(fwd_kernel, name='attend_forward', out_shape=(jax.ShapeDty...  56.8 us
    all_to_all x1, waiting for transfers between devices, per_device(): lax.all_to_all(contexts.reshape(seq_count, local_len, head_width), SEQ, s...  54.9 us
  transfers between devices with their start and end apart: 20, of which 14 were waited for; matrix products, arithmetic and copies ran while one was open for 23% of the time, Pallas kernels for 12%

profile of v1, /device:TPU:0, one launch (start us, length us, event | category | flops | bytes accessed | tf_op | source)
XLA Modules:
  0.0 1445.3 jit_solution(17094284715270460673)
XLA Ops:
  31.6 126.6 %all-to-all-done = bf16[8,256,1024]{2,1,0:T(8,128)(2,1)} async-done(((bf16[8,256,1024]{2,1,0:T(8,128)(2,1)}), bf16[8,256,1024]{2,1,0:T(8,128)(2,1)}, u32[]{:S(2)}, u32[]{:S(2)}) %all-to-all-start) | async-done | bytes 4194336 | tf_op jit(solution)/shard_map/all_to_all | solution.py:472
  182.2 56.8 %attend_forward.1 = (bf16[2048,512]{1,0:T(8,128)(2,1)}, f32[4,2,2048]{2,1,0:T(2,128)S(1)}) custom-call(s32[2,8]{1,0:T(2,128)S(1)} %pad_add_fusion.ranges, f32[8,2]{1,0:T(8,128)S(1)} %maximum_convert_fusion.ends, bf16[2048,1536]{1,0:T(8,128)(2,1)} %convolution_convert_fusion.q_ref.k_ref.v_ref, bf16[2048,1536]{1,0:T(8,128)(2,1)} %convolution_convert_fusion.q_ref.k_ref.v_ref, ...), custom_call_target="tpu_custom_call" | custom-call | flops 8589934592 | bytes 8388608 | tf_op jit(solution)/shard_map/attend_forward/pallas_call | solution.py:165
  259.9 54.9 %all-to-all-done.1 = bf16[8,256,512]{2,1,0:T(8,128)(2,1)} async-done(((bf16[8,256,512]{2,1,0:T(8,128)(2,1)}), bf16[8,256,512]{2,1,0:T(8,128)(2,1)}, u32[]{:S(2)}, u32[]{:S(2)}) %all-to-all-start.1) | async-done | bytes 2097184 | tf_op jit(solution)/shard_map/all_to_all | solution.py:500
  362.5 14.9 %bitcast_convert_fusion = bf16[2560,1024]{1,0:T(8,128)(2,1)} fusion(s32[1024,2]{0,1:T(2,128)S(1)} %copy.127, f32[1024,1024]{0,1:T(8,128)} %copy.132, f32[1024,2]{0,1:T(2,128)S(1)} %broadcast_divide_fusion.1), kind=kOutput, calls=%fused_computation.22 | convolution fusion | flops 10749476864 | bytes 9453568 | tf_op jit(solution)/shard_map/tks,tkd->sd/dot_general | solution.py:558
  377.5 30.2 %all-to-all-done.2 = bf16[4,640,1024]{2,1,0:T(8,128)(2,1)} async-done(((bf16[4,640,1024]{2,1,0:T(8,128)(2,1)}), bf16[4,640,1024]{2,1,0:T(8,128)(2,1)}, u32[]{:S(2)}, u32[]{:S(2)}) %all-to-all-start.2) | async-done | bytes 5242912 | tf_op jit(solution)/shard_map/all_to_all | solution.py:540
  412.9 22.4 %fusion.25 = f32[2560,2816]{1,0:T(8,128)} fusion(bf16[2560,1024]{1,0:T(8,128)(2,1)} %bitcast.16, bf16[1,1024,2816]{2,1,0:T(8,128)(2,1)} %all-gather.12.cloned.1.call-done), kind=kOutput, calls=%fused_computation.45 | convolution fusion | flops 14763950080 | bytes 39845888 | tf_op jit(solution)/shard_map/dot_general | solution.py:415
  435.3 22.3 %fusion.29 = f32[2560,2816]{1,0:T(8,128)} fusion(bf16[2560,1024]{1,0:T(8,128)(2,1)} %bitcast.16, bf16[1,1024,2816]{2,1,0:T(8,128)(2,1)} %all-gather.10.cloned.1.call-done), kind=kOutput, calls=%fused_computation.49 | convolution fusion | flops 14763950080 | bytes 39845888 | tf_op jit(solution)/shard_map/dot_general | solution.py:415
  457.5 12.8 all-gather.14.cloned.1.call-done
  472.3 49.5 %multiply_convert_fusion = (bf16[2560,2816]{1,0:T(8,128)(2,1)}, bf16[2560,2816]{1,0:T(8,128)(2,1)}, bf16[2560,2816]{1,0:T(8,128)(2,1)}) fusion(f32[2560,2816]{1,0:T(8,128)} %fusion.29, f32[2560,2816]{1,0:T(8,128)} %fusion.25, bf16[2560,1024]{1,0:T(8,128)(2,1)} %bitcast.28, bf16[1,2816,1024]{2,1,0:T(8,128)(2,1)} %all-gather.14.cloned.1.call-done), kind=kOutput, calls=%fused_computation.10 | convolution fusion | flops 14980218880 | bytes 111935488 | tf_op jit(solution)/shard_map/sd,fd->sf/dot_general | solution.py:562
  521.8 20.8 %fusion.31 = bf16[2560,1024]{1,0:T(8,128)(2,1)} fusion(bf16[2560,2816]{1,0:T(8,128)(2,1)} %get-tuple-element.51, bf16[1,2816,1024]{2,1,0:T(8,128)(2,1)} %all-gather.14.cloned.1.call-done), kind=kOutput, calls=%fused_computation.51 | convolution fusion | flops 14766571520 | bytes 25427968 | tf_op jit(solution)/shard_map/dot_general | solution.py:415
  548.1 19.7 %fusion.27 = f32[2560,1024]{1,0:T(8,128)S(1)} fusion(bf16[2560,2816]{1,0:T(8,128)(2,1)} %get-tuple-element.50, bf16[1,1024,2816]{2,1,0:T(8,128)(2,1)} %all-gather.10.cloned.1.call-done), kind=kOutput, calls=%fused_computation.47 | convolution fusion | flops 14763950080 | bytes 30670848 | tf_op jit(solution)/shard_map/sf,df->sd/dot_general | solution.py:566
  567.8 20.9 %add_convert_fusion = bf16[2560,1024]{1,0:T(8,128)(2,1)} fusion(f32[2560,1024]{1,0:T(8,128)S(1)} %fusion.27, bf16[2560,2816]{1,0:T(8,128)(2,1)} %get-tuple-element.49, bf16[1,1024,2816]{2,1,0:T(8,128)(2,1)} %all-gather.12.cloned.1.call-done), kind=kOutput, calls=%fused_computation.23 | convolution fusion | flops 14769192960 | bytes 35913728 | tf_op jit(solution)/shard_map/sf,df->sd/dot_general | solution.py:569
  588.7 18.8 %all-to-all-done.3 = bf16[4,640,1024]{2,1,0:T(8,128)(2,1)} async-done(((bf16[4,640,1024]{2,1,0:T(8,128)(2,1)}), bf16[4,640,1024]{2,1,0:T(8,128)(2,1)}, u32[]{:S(2)}, u32[]{:S(2)}) %all-to-all-start.3) | async-done | bytes 5242912 | tf_op jit(solution)/shard_map/all_to_all | solution.py:540
  613.0 18.5 %multiply_reduce_fusion = (f32[1024,2]{0,1:T(2,128)S(1)}, f32[1024,1024]{0,1:T(8,128)}) fusion(f32[1024,1024]{0,1:T(8,128)} %copy.132, f32[1024,2]{0,1:T(2,128)S(1)} %copy-done.67, bf16[2560,1024,1]{1,0,2:T(8,128)(2,1)} %bitcast.69, s32[1024,2]{0,1:T(2,128)S(1)} %copy-done.59), kind=kOutput, calls=%fused_computation.32 | convolution fusion | flops 10749999104 | bytes 13656064 | tf_op jit(solution)/shard_map/tks,sd->tkd/dot_general | solution.py:551
  631.7 40.6 %all-to-all-done.5 = bf16[4,640,1024]{2,1,0:T(8,128)(2,1)} async-done(((bf16[4,640,1024]{2,1,0:T(8,128)(2,1)}), bf16[4,640,1024]{2,1,0:T(8,128)(2,1)}, u32[]{:S(2)}, u32[]{:S(2)}) %all-to-all-start.5) | async-done | bytes 5242912 | tf_op jit(solution)/shard_map/all_to_all | solution.py:540
  722.6 49.8 %all-to-all-done.6 = bf16[8,256,512]{2,1,0:T(8,128)(2,1)S(1)} async-done(((bf16[8,256,512]{2,1,0:T(8,128)(2,1)}), bf16[8,256,512]{2,1,0:T(8,128)(2,1)S(1)}, u32[]{:S(2)}, u32[]{:S(2)}) %all-to-all-start.6) | async-done | bytes 2097184 | tf_op jit(solution)/shard_map/all_to_all | solution.py:598
  775.3 113.5 %attend_backward.1 = (bf16[2048,512]{1,0:T(8,128)(2,1)S(1)}, bf16[2048,512]{1,0:T(8,128)(2,1)S(1)}, bf16[2048,512]{1,0:T(8,128)(2,1)S(1)}, f32[8,3,512]{2,1,0:T(4,128)S(1)}, f32[8,2,256]{2,1,0:T(2,128)S(1)}) custom-call(s32[2,8]{1,0:T(2,128)S(1)} %copy-done.11, f32[8,2]{1,0:T(8,128)S(1)} %copy-done.9, ...), custom_call_target="tpu_custom_call" | custom-call | flops 21474836480 | bytes 16777216 | tf_op jit(solution)/shard_map/attend_backward/pallas_call | solution.py:343
  906.6 22.0 %convolution_convert_fusion.1 = bf16[2816,1024]{1,0:T(8,128)(2,1)} fusion(bf16[2560,2816]{1,0:T(8,128)(2,1)} %get-tuple-element.51, bf16[2560,1024]{1,0:T(8,128)(2,1)} %bitcast.28), kind=kOutput, calls=%fused_computation.52 | convolution fusion | flops 14766833664 | bytes 25427968 | tf_op jit(solution)/shard_map/sa,sb->ab/dot_general | solution.py:574
  928.6 22.6 %convolution_convert_fusion.2 = bf16[1024,2816]{1,0:T(8,128)(2,1)} fusion(bf16[2560,1024]{1,0:T(8,128)(2,1)} %bitcast.16, bf16[2560,2816]{1,0:T(8,128)(2,1)} %get-tuple-element.49), kind=kOutput, calls=%fused_computation.53 | convolution fusion | flops 14766833664 | bytes 25427968 | tf_op jit(solution)/shard_map/sa,sb->ab/dot_general | solution.py:574
  951.3 22.8 %convolution_convert_fusion.3 = bf16[1024,2816]{1,0:T(8,128)(2,1)} fusion(bf16[2560,1024]{1,0:T(8,128)(2,1)} %bitcast.16, bf16[2560,2816]{1,0:T(8,128)(2,1)} %get-tuple-element.50), kind=kOutput, calls=%fused_computation.54 | convolution fusion | flops 14766833664 | bytes 25427968 | tf_op jit(solution)/shard_map/sa,sb->ab/dot_general | solution.py:574
  991.0 12.0 reduce-scatter.6.cloned.1.call-done
  1027.2 155.1 %reduce-scatter.14.cloned.1.call-done = bf16[352,1024]{1,0:T(8,128)(2,1)} async-done(((bf16[2816,1024]{1,0:T(8,128)(2,1)}), bf16[352,1024]{1,0:T(8,128)(2,1)}) %reduce-scatter.14.cloned.1.call-update) | async-done | bytes 720912 | tf_op jit(solution)/shard_map/reduce_scatter | solution.py:577
  1184.6 111.5 %reduce-scatter.12.cloned.1.call-done = bf16[128,2816]{1,0:T(8,128)(2,1)} async-done(((bf16[1024,2816]{1,0:T(8,128)(2,1)}), bf16[128,2816]{1,0:T(8,128)(2,1)}) %reduce-scatter.12.cloned.1.call-update) | async-done | bytes 720912 | tf_op jit(solution)/shard_map/reduce_scatter | solution.py:577
  1298.5 111.6 %reduce-scatter.10.cloned.1.call-done = bf16[128,2816]{1,0:T(8,128)(2,1)} async-done(((bf16[1024,2816]{1,0:T(8,128)(2,1)}), bf16[128,2816]{1,0:T(8,128)(2,1)}) %reduce-scatter.10.cloned.1.call-update) | async-done | bytes 720912 | tf_op jit(solution)/shard_map/reduce_scatter | solution.py:577
  (316 shorter events, 279.4 us)
Async XLA Ops:
  7.2 154.7 %all-gather.8.cloned.1.call-start = ((), (), s32[]{:S(2)}) async-start(), calls=%async_computation.16 | async-start | bytes 8921088 | tf_op jit(solution)/shard_map/all_gather | solution.py:466
  13.9 399.0 %all-gather.12.cloned.1.call-start = ((), (), s32[]{:S(2)}) async-start(), calls=%async_computation.23 | async-start | bytes 6488064 | tf_op jit(solution)/shard_map/all_gather | solution.py:468
  18.8 139.4 %all-to-all-start = ((bf16[8,256,1024]{2,1,0:T(8,128)(2,1)}), bf16[8,256,1024]{2,1,0:T(8,128)(2,1)}, u32[]{:S(2)}, u32[]{:S(2)}) async-start(bf16[8,256,1024]{2,1,0:T(8,128)(2,1)} %bitcast.196), calls=%async_computation | async-start | bytes 8388608 | tf_op jit(solution)/shard_map/all_to_all | solution.py:472
  26.1 409.1 %all-gather.10.cloned.1.call-start = ((), (), s32[]{:S(2)}) async-start(), calls=%async_computation.22 | async-start | bytes 6488064 | tf_op jit(solution)/shard_map/all_gather | solution.py:467
  30.9 151.2 %copy-start.10 = (s32[2,8]{1,0:T(2,128)}, s32[2,8]{1,0:T(2,128)S(1)}, u32[]{:S(2)}) copy-start(s32[2,8]{1,0:T(2,128)S(1)} %pad_add_fusion.ranges) | copy-start | bytes 196
  31.3 150.9 %copy-start.2 = (bf16[2048,128]{1,0:T(8,128)(2,1)}, bf16[2048,128]{1,0:T(8,128)(2,1)S(1)}, u32[]{:S(2)}) copy-start(bf16[2048,128]{1,0:T(8,128)(2,1)S(1)} %select_convert_fusion.1.qs_ref) | copy-start | bytes 1572868
  31.6 150.5 %copy-start.4 = (bf16[2048,128]{1,0:T(8,128)(2,1)}, bf16[2048,128]{1,0:T(8,128)(2,1)S(1)}, u32[]{:S(2)}) copy-start(bf16[2048,128]{1,0:T(8,128)(2,1)S(1)} %select_convert_fusion.ks_ref) | copy-start | bytes 1572868
  165.0 162.4 %copy-start.53 = (f32[1024]{0:T(1024)}, f32[1024]{0:T(1024)S(1)}, u32[]{:S(2)}) copy-start(f32[1024]{0:T(1024)S(1)} %get-tuple-element.27) | copy-start | bytes 12292
  239.0 75.9 %all-to-all-start.1 = ((bf16[8,256,512]{2,1,0:T(8,128)(2,1)}), bf16[8,256,512]{2,1,0:T(8,128)(2,1)}, u32[]{:S(2)}, u32[]{:S(2)}) async-start(bf16[8,256,512]{2,1,0:T(8,128)(2,1)} %bitcast.9), calls=%async_computation.1 | async-start | bytes 4194304 | tf_op jit(solution)/shard_map/all_to_all | solution.py:500
  243.5 226.8 %all-gather.14.cloned.1.call-start = ((), (), s32[]{:S(2)}) async-start(), calls=%async_computation.24 | async-start | bytes 6488064 | tf_op jit(solution)/shard_map/all_gather | solution.py:469
  336.7 70.9 %all-to-all-start.2 = ((bf16[4,640,1024]{2,1,0:T(8,128)(2,1)}), bf16[4,640,1024]{2,1,0:T(8,128)(2,1)}, u32[]{:S(2)}, u32[]{:S(2)}) async-start(bf16[4,640,1024]{2,1,0:T(8,128)(2,1)} %bitcast.208), calls=%async_computation.2 | async-start | bytes 10485760 | tf_op jit(solution)/shard_map/all_to_all | solution.py:540
  407.6 64.7 %all-to-all-start.4 = ((bf16[4,640,1024]{2,1,0:T(8,128)(2,1)}), bf16[4,640,1024]{2,1,0:T(8,128)(2,1)}, u32[]{:S(2)}, u32[]{:S(2)}) async-start(bf16[4,640,1024]{2,1,0:T(8,128)(2,1)} %bitcast.209), calls=%async_computation.4 | async-start | bytes 10485760 | tf_op jit(solution)/shard_map/all_to_all | solution.py:540
  542.6 64.9 %all-to-all-start.3 = ((bf16[4,640,1024]{2,1,0:T(8,128)(2,1)}), bf16[4,640,1024]{2,1,0:T(8,128)(2,1)}, u32[]{:S(2)}, u32[]{:S(2)}) async-start(bf16[4,640,1024]{2,1,0:T(8,128)(2,1)} %bitcast.210), calls=%async_computation.3 | async-start | bytes 10485760 | tf_op jit(solution)/shard_map/all_to_all | solution.py:540
  607.5 64.8 %all-to-all-start.5 = ((bf16[4,640,1024]{2,1,0:T(8,128)(2,1)}), bf16[4,640,1024]{2,1,0:T(8,128)(2,1)}, u32[]{:S(2)}, u32[]{:S(2)}) async-start(bf16[4,640,1024]{2,1,0:T(8,128)(2,1)} %bitcast.207), calls=%async_computation.5 | async-start | bytes 10485760 | tf_op jit(solution)/shard_map/all_to_all | solution.py:540
  712.1 60.3 %all-to-all-start.6 = ((bf16[8,256,512]{2,1,0:T(8,128)(2,1)}), bf16[8,256,512]{2,1,0:T(8,128)(2,1)S(1)}, u32[]{:S(2)}, u32[]{:S(2)}) async-start(bf16[8,256,512]{2,1,0:T(8,128)(2,1)} %bitcast.202), calls=%async_computation.6 | async-start | bytes 4194304 | tf_op jit(solution)/shard_map/all_to_all | solution.py:598
  715.7 258.4 %reduce-scatter.8.cloned.1.call-start = ((), (), s32[]{:S(2)}) async-start(), calls=%async_computation.18 | async-start | bytes 2228224 | tf_op jit(solution)/shard_map/reduce_scatter | solution.py:625
  722.5 280.5 %reduce-scatter.6.cloned.1.call-start = ((), (), s32[]{:S(2)}) async-start(), calls=%async_computation.17 | async-start | bytes 3342336 | tf_op jit(solution)/shard_map/reduce_scatter | solution.py:625
  906.5 275.8 %reduce-scatter.14.cloned.1.call-start = ((), (), s32[]{:S(2)}) async-start(), calls=%async_computation.21 | async-start | bytes 6488064 | tf_op jit(solution)/shard_map/reduce_scatter | solution.py:577
  928.6 367.6 %reduce-scatter.12.cloned.1.call-start = ((), (), s32[]{:S(2)}) async-start(), calls=%async_computation.20 | async-start | bytes 6488064 | tf_op jit(solution)/shard_map/reduce_scatter | solution.py:577
  951.2 458.8 %reduce-scatter.10.cloned.1.call-start = ((), (), s32[]{:S(2)}) async-start(), calls=%async_computation.19 | async-start | bytes 6488064 | tf_op jit(solution)/shard_map/reduce_scatter | solution.py:577
  974.1 16.9 %all-to-all-start.10 = ((bf16[2,32,1024]{2,1,0:T(8,128)(2,1)}), bf16[2,32,1024]{2,1,0:T(8,128)(2,1)S(1)}, u32[]{:S(2)}, u32[]{:S(2)}) async-start(bf16[2,32,1024]{2,1,0:T(8,128)(2,1)} %bitcast.222), calls=%async_computation.12 | async-start | bytes 262144 | tf_op jit(solution)/shard_map/all_to_all | solution.py:629
  1003.1 13.7 all-to-all-start.9
  1016.8 398.5 %all-to-all-start.7 = ((bf16[8,256,1024]{2,1,0:T(8,128)(2,1)}), bf16[8,256,1024]{2,1,0:T(8,128)(2,1)}, u32[]{:S(2)}, u32[]{:S(2)}) async-start(bf16[8,256,1024]{2,1,0:T(8,128)(2,1)} %bitcast.197), calls=%async_computation.7 | async-start | bytes 8388608 | tf_op jit(solution)/shard_map/all_to_all | solution.py:611
  1423.8 11.6 all-to-all-start.8
  (69 other events, 1230.9 us)
Sparse Core Ops, SparseCore 0:
  14.0 147.8 all-gather.7
  164.1 93.4 all-gather.11
  259.8 117.5 all-gather.9
  379.4 90.8 all-gather.13
  722.6 66.8 reduce-scatter.7
  906.6 96.3 reduce-scatter.5
  1007.1 175.0 reduce-scatter.13
  1186.4 109.7 reduce-scatter.11
  1300.2 109.7 reduce-scatter.9

commit v2 on v1

--- a/solution.py
+++ b/solution.py
@@ -54,7 +54,11 @@
     return pltpu.roll(wide, 0, 1, stride=1, stride_axis=0)[:, :tile]
 
 
-def fwd_kernel(ranges, ends, q_ref, k_ref, v_ref, qs_ref, ks_ref, rows_ref, o_ref, lse_ref, bias_ref, vt_ref):
+def block_at(index, own, tile):
+    return pl.ds(pl.multiple_of((index ^ own[0]) * tile, tile), tile)
+
+
+def fwd_kernel(ranges, ends, own, q_ref, k_ref, v_ref, qs_ref, ks_ref, rows_ref, o_ref, lse_ref, bias_ref, vt_ref):
     group, qb = pl.program_id(0), pl.program_id(1)
     tile, span = q_ref.shape
     heads = span // HEAD_DIM
@@ -89,7 +93,7 @@
         queries = [side(h, which) for h in range(heads)]
 
         def step(kb, carry):
-            keys = pl.ds(pl.multiple_of(kb * tile, tile), tile)
+            keys = block_at(kb, own, tile)
             ks = ks_ref[keys, :]
             scores = []
             for h in range(heads):
@@ -135,21 +139,20 @@
 FWD_PAIRS = 4
 
 
-def attend_forward(qkv, qs, ks, ranges, rows, ends):
+def attend_forward(qkv, qs, ks, ranges, rows, ends, own, tile):
     length, width = qkv.shape[0], qkv.shape[1] // 3
-    tile = min(TILE, length)
     pairs = width // LANES
     together = FWD_PAIRS if pairs % FWD_PAIRS == 0 else 1
     span = together * LANES
     tiles = length // tile
     spec = pltpu.PrefetchScalarGridSpec(
-        num_scalar_prefetch=2,
+        num_scalar_prefetch=3,
         grid=(pairs // together, tiles),
         in_specs=[
-            pl.BlockSpec((tile, span), lambda p, i, *_: (i, p)),
+            pl.BlockSpec((tile, span), lambda p, i, r, e, own: (i ^ own[0], p)),
             pl.BlockSpec((length, span), lambda p, i, *_: (0, width // span + p)),
             pl.BlockSpec((length, span), lambda p, i, *_: (0, 2 * (width // span) + p)),
-            pl.BlockSpec((tile, LANES), lambda p, i, *_: (i, 0)),
+            pl.BlockSpec((tile, LANES), lambda p, i, r, e, own: (i ^ own[0], 0)),
             pl.BlockSpec((length, LANES), lambda p, i, *_: (0, 0)),
             pl.BlockSpec((2 * together, 3, 2 * tile), lambda p, i, *_: (p, 0, 0)),
         ],
@@ -174,7 +177,7 @@
             dimension_semantics=("arbitrary", "arbitrary"), vmem_limit_bytes=48 << 20
         ),
         cost_estimate=pl.CostEstimate(flops=length * length * width * 4, bytes_accessed=length * width * 8, transcendentals=0),
-    )(ranges, ends, qkv, qkv, qkv, qs, ks, rows)
+    )(ranges, ends, own, qkv, qkv, qkv, qs, ks, rows)
 
 
 def pieces(row):
@@ -183,7 +186,7 @@
     return high, mid, row - high - mid
 
 
-def bwd_kernel(ranges, ends, q_ref, k_ref, v_ref, do_ref, o_ref, lse_ref, qs_ref, ks_ref, rows_ref,
+def bwd_kernel(ranges, ends, own, q_ref, k_ref, v_ref, do_ref, o_ref, lse_ref, qs_ref, ks_ref, rows_ref,
                dq_ref, dk_ref, dv_ref, diag_ref, far_ref,
                qx_ref, dox_ref, kt_ref, bias_ref, dsum_ref, fsum_ref, dqt_ref, dka_ref, dva_ref):
     pair = pl.program_id(0)
@@ -202,16 +205,17 @@
 
     @pl.loop(0, tiles)
     def _(i):
-        at = pl.ds(pl.multiple_of(i * tile, tile), tile)
+        line = pl.ds(pl.multiple_of(i * tile, tile), tile)
+        at = block_at(i, own, tile)
         q = q_ref[at, :] * jnp.bfloat16(HEAD_DIM**-0.5)
-        do = do_ref[at, :]
+        do = do_ref[line, :]
         zero = jnp.zeros_like(q)
-        product = do.astype(jnp.float32) * o_ref[at, :].astype(jnp.float32)
+        product = do.astype(jnp.float32) * o_ref[line, :].astype(jnp.float32)
         delta = lax.dot_general(pick, product, NT, precision=lax.Precision.HIGHEST, preferred_element_type=jnp.float32)
         kt_ref[:, at] = k_ref[at, :].T
         for h in range(2):
             keep = (lane < HEAD_DIM) if h == 0 else (lane >= HEAD_DIM)
-            a, b, c = pieces(-lse_ref[0, h : h + 1, at])
+            a, b, c = pieces(-lse_ref[0, h : h + 1, line])
             extra = jnp.where(sub == 4, a, jnp.where(sub == 5, b, jnp.where(sub == 6, c, 0.0)))
             extra = extra.T.astype(jnp.bfloat16) + qs_ref[at, :]
             left, right = ends[2 * pair + h, 0].astype(jnp.bfloat16), ends[2 * pair + h, 1].astype(jnp.bfloat16)
@@ -226,7 +230,7 @@
     @pl.loop(0, tiles)
     def _(kb):
         low, high = ranges[0, kb], ranges[1, kb]
-        keys = pl.ds(pl.multiple_of(kb * tile, tile), tile)
+        keys = block_at(kb, own, tile)
         k, ks = k_ref[keys, :], ks_ref[keys, :]
         vx = jnp.concatenate([v_ref[keys, :], ones3], axis=1)
         nil = jnp.zeros_like(ks)
@@ -243,7 +247,7 @@
             kx = jnp.concatenate([k, extra], axis=1)
 
             def step(qb, carry):
-                at = pl.ds(pl.multiple_of(qb * tile, tile), tile)
+                at = block_at(qb, own, tile)
                 weights, grads = [], []
                 for h in range(2):
                     qx, dox = qx_ref[h, at, :], dox_ref[h, at, :]
@@ -302,15 +306,14 @@
     return jnp.sum(acc, axis=0, keepdims=True)
 
 
-def attend_backward(qkv, do, o, lse, qs, ks, ranges, rows, ends):
+def attend_backward(qkv, do, o, lse, qs, ks, ranges, rows, ends, own, tile):
     length, width = do.shape
-    tile = min(TILE, length)
     pairs = width // LANES
     heads = width // HEAD_DIM
     column = pl.BlockSpec((length, LANES), lambda p, *_: (0, p))
     fixed = pl.BlockSpec((length, LANES), lambda p, *_: (0, 0))
     spec = pltpu.PrefetchScalarGridSpec(
-        num_scalar_prefetch=2,
+        num_scalar_prefetch=3,
         grid=(pairs,),
         in_specs=[
             column,
@@ -353,7 +356,7 @@
             dimension_semantics=("arbitrary",), vmem_limit_bytes=40 << 20
         ),
         cost_estimate=pl.CostEstimate(flops=length * length * width * 10, bytes_accessed=length * width * 16, transcendentals=0),
-    )(ranges, ends, qkv, qkv, qkv, do, o, lse, qs, ks, rows)
+    )(ranges, ends, own, qkv, qkv, qkv, do, o, lse, qs, ks, rows)
 
 
 def bucket_sums(diag, far, tile):
@@ -369,54 +372,202 @@
     return sums + outer[:, 0:1] * ends[0] + outer[:, 1:2] * ends[1]
 
 
+GELU_A, GELU_B = 0.7978845608028654, 0.044715
+FF_TILE = 256
+EXTRA = 16
+
+
+def expert_kernel(own_ref, x_ref, dy_ref, gate_ref, wg_ref, wu_ref, wd_ref, *refs):
+    h_ref, dg_ref, du_ref, dx_ref, part_ref, acc_ref = refs[-6:]
+    step = pl.program_id(0)
+    rows = gate_ref.shape[0]
+    chunk = rows // 2 if rows % 32 == 0 else rows
+
+    @pl.when(step == 0)
+    def _():
+        acc_ref[...] = jnp.zeros_like(acc_ref)
+        part_ref[...] = jnp.zeros_like(part_ref)
+
+    wg, wu, wd = wg_ref[...], wu_ref[...], wd_ref[...]
+    for start in range(0, rows, chunk):
+        at = slice(start, start + chunk)
+        x, dy = x_ref[at, :], dy_ref[at, :]
+        g = jnp.dot(x, wg, preferred_element_type=jnp.float32)
+        u = jnp.dot(x, wu, preferred_element_type=jnp.float32)
+        raw = lax.dot_general(dy, wd, NT, preferred_element_type=jnp.float32)
+        square = g * g
+        half = 0.5 + 0.5 * jnp.tanh(g * (GELU_A + (GELU_A * GELU_B) * square))
+        gelu = g * half
+        slope = half + 2.0 * gelu * (1.0 - half) * (GELU_A + (3.0 * GELU_A * GELU_B) * square)
+        h = gelu * u
+        product = raw * h
+        total = product[:, :LANES]
+        for column in range(LANES, product.shape[1], LANES):
+            total = total + product[:, column : column + LANES]
+        part_ref[at, :] += total
+        dh = raw * gate_ref[at, :]
+        du = (dh * gelu).astype(jnp.bfloat16)
+        dg = (dh * u * slope).astype(jnp.bfloat16)
+        h_ref[at, :] = h.astype(jnp.bfloat16)
+        dg_ref[at, :] = dg
+        du_ref[at, :] = du
+        acc_ref[at, :] += lax.dot_general(dg, wg, NT, preferred_element_type=jnp.float32) + lax.dot_general(
+            du, wu, NT, preferred_element_type=jnp.float32
+        )
+
+    @pl.when(step == pl.num_programs(0) - 1)
+    def _():
+        dx_ref[:rows, :] = acc_ref[...].astype(dx_ref.dtype)
+        sums = jnp.sum(part_ref[...].T, axis=0, keepdims=True)
+        high = sums.astype(jnp.bfloat16).astype(jnp.float32)
+        middle = (sums - high).astype(jnp.bfloat16).astype(jnp.float32)
+        line = lax.broadcasted_iota(jnp.int32, (EXTRA, rows), 0)
+        lines = jnp.where(line == 0, high, jnp.where(line == 1, middle, jnp.where(line == 2, sums - high - middle, 0.0)))
+        dx_ref[rows:, :] = jnp.zeros_like(dx_ref[rows:, :])
+        dx_ref[rows:, :rows] = lines.astype(dx_ref.dtype)
+
+
+def expert_block(at, count, x, dy, gate, wgu, wd, earlier):
+    rows, width = gate.shape[0], x.shape[1]
+    hidden = wd.shape[0]
+    tile = FF_TILE
+    whole = jax.ShapeDtypeStruct((count * rows, hidden), jnp.bfloat16)
+    fixed = lambda i, *_: (0, 0)
+    out_block = pl.BlockSpec((rows, tile), lambda i, *_: (at, i))
+    spec = pltpu.PrefetchScalarGridSpec(
+        num_scalar_prefetch=1,
+        grid=(hidden // tile,),
+        in_specs=[
+            pl.BlockSpec((rows, width), fixed),
+            pl.BlockSpec((rows, width), fixed),
+            pl.BlockSpec((rows, 1), fixed),
+            pl.BlockSpec((width, tile), lambda i, *_: (0, i)),
+            pl.BlockSpec((width, tile), lambda i, *_: (0, hidden // tile + i)),
+            pl.BlockSpec((tile, width), lambda i, *_: (i, 0)),
+        ]
+        + [pl.BlockSpec(memory_space=pl.ANY)] * len(earlier),
+        out_specs=[
+            out_block,
+            out_block,
+            out_block,
+            pl.BlockSpec((rows + EXTRA, width), fixed),
+        ],
+        scratch_shapes=[pltpu.VMEM((rows, LANES), jnp.float32), pltpu.VMEM((rows, width), jnp.float32)],
+    )
+    return pl.pallas_call(
+        expert_kernel,
+        name="expert_block",
+        out_shape=(
+            whole,
+            whole,
+            whole,
+            jax.ShapeDtypeStruct((rows + EXTRA, width), jnp.bfloat16),
+        ),
+        grid_spec=spec,
+        input_output_aliases={7 + i: i for i in range(len(earlier))},
+        compiler_params=pltpu.CompilerParams(dimension_semantics=("arbitrary",), vmem_limit_bytes=40 << 20),
+        cost_estimate=pl.CostEstimate(
+            flops=10 * rows * width * hidden, bytes_accessed=6 * width * hidden + 6 * rows * hidden, transcendentals=0
+        ),
+    )(jnp.zeros((1,), jnp.int32), x, dy, gate, wgu, wgu, wd, *earlier)
+
+
 EPS = 1e-06
 FULL_PRECISION = lax.Precision.HIGHEST
-
-
-def gelu_tanh(value_entries):
-    return (
-        0.5
-        * value_entries
-        * (
-            1.0
-            + jnp.tanh(
-                0.7978845608028654
-                * (value_entries + 0.044715 * value_entries * value_entries * value_entries)
-            )
-        )
-    )
-
-
-def geglu_product(gate_part, up_part):
-    return gelu_tanh(gate_part) * up_part
-
-
-def rms_scale(value_entries, gain_row):
-    return (
-        value_entries
-        * lax.rsqrt(jnp.mean(value_entries * value_entries, axis=-1, keepdims=True) + EPS)
-        * gain_row
-    )
-
-
-def gate_values(routes, normed, router):
-    logits = jnp.dot(normed, router, precision=FULL_PRECISION)
-    row_peak = jnp.max(logits, axis=-1, keepdims=True)
-    exponent = jnp.exp(logits - row_peak)
-    probabilities = exponent / jnp.sum(exponent, axis=-1, keepdims=True)
-    choose = (routes[..., None] == jnp.arange(router.shape[1], dtype=jnp.int32)).astype(
-        probabilities.dtype
-    )
-    chosen = jnp.sum(probabilities[..., None, :] * choose, axis=-1)
-    return chosen / jnp.sum(chosen, axis=-1, keepdims=True)
+ALL = ("z", "x", "exp")
+SEQ = ("z", "x")
+LOW = jnp.bfloat16
 
 
 def dot32(a, b):
     return jnp.dot(a, b, preferred_element_type=jnp.float32)
 
 
-ALL = ("z", "x", "exp")
-SEQ = ("z", "x")
+def dot_nt(a, b):
+    return lax.dot_general(a, b, NT, preferred_element_type=jnp.float32)
+
+
+def dot_tn(a, b):
+    return lax.dot_general(a, b, (((0,), (0,)), ((), ())), preferred_element_type=jnp.float32)
+
+
+def partner(value, axis, offset):
+    count = lax.axis_size(axis)
+    return lax.ppermute(value, axis, [(i, i ^ offset) for i in range(count)])
+
+
+def bits_of(count):
+    return [1 << b for b in reversed(range(count.bit_length() - 1))]
+
+
+def reorder(stacked, own):
+    count = stacked.shape[0]
+    return jnp.stack([lax.dynamic_index_in_dim(stacked, own ^ r, 0, keepdims=False) for r in range(count)])
+
+
+def gather_double(value, steps):
+    for axis, bit in steps:
+        other = partner(value, axis, bit)
+        high = (lax.axis_index(axis) & bit) != 0
+        value = jnp.stack([jnp.where(high, other, value), jnp.where(high, value, other)])
+    return value
+
+
+def scatter_halve(value, steps):
+    for axis, bit in steps:
+        high = (lax.axis_index(axis) & bit) != 0
+        keep = jnp.where(high, value[1], value[0])
+        give = jnp.where(high, value[0], value[1])
+        value = (keep.astype(jnp.float32) + partner(give, axis, bit).astype(jnp.float32)).astype(LOW)
+    return value
+
+
+def ring_of(groups, split):
+    order = []
+    for x in range(split):
+        line = range(groups) if x % 2 == 0 else reversed(range(groups))
+        order += [z * split + x for z in line]
+    place = [order.index(s) for s in range(len(order))]
+    ahead = [(order[i], order[(i + 1) % len(order)]) for i in range(len(order))]
+    return jnp.asarray(order, jnp.int32), jnp.asarray(place, jnp.int32), ahead
+
+
+def pick(values, index):
+    return lax.dynamic_index_in_dim(values, index, 0, keepdims=False)
+
+
+def ring_gather(piece, groups, split, own):
+    order, place, ahead = ring_of(groups, split)
+    count = groups * split
+    here = pick(place, own)
+    rows = piece.shape[0]
+    whole = jnp.zeros((count * rows, piece.shape[1]), piece.dtype)
+    whole = lax.dynamic_update_slice_in_dim(whole, piece, own * rows, 0)
+    forward = backward = piece
+    for k in range(1, count // 2 + 1):
+        forward = lax.ppermute(forward, SEQ, ahead)
+        if k < count - count // 2:
+            backward = lax.ppermute(backward, SEQ, [(b, a) for a, b in ahead])
+        whole = lax.dynamic_update_slice_in_dim(whole, forward, pick(order, (here - k + count) % count) * rows, 0)
+        if k < count - count // 2:
+            whole = lax.dynamic_update_slice_in_dim(whole, backward, pick(order, (here + k) % count) * rows, 0)
+    return whole
+
+
+def norm_scale(value):
+    return lax.rsqrt(jnp.mean(value * value, axis=-1, keepdims=True) + EPS)
+
+
+def norm_back(scale, normed, gain, grad):
+    scaled = grad * gain
+    return scale * (scaled - normed * jnp.mean(scaled * normed, axis=-1, keepdims=True))
+
+
+def split3(value):
+    high = value.astype(LOW)
+    rest = value - high.astype(jnp.float32)
+    middle = rest.astype(LOW)
+    return [high, middle, (rest - middle.astype(jnp.float32)).astype(LOW)]
 
 
 def per_device(
@@ -437,18 +588,37 @@
     w_up,
     w_down,
 ):
-    low_type = jnp.bfloat16
     groups, local_len, width = block_in.shape
     tokens = groups * local_len
-    rows_own = w_query.shape[0]
+    rows_own, hd = w_query.shape
     split = lax.axis_size("x")
     exp_count = lax.axis_size("exp")
     seq_count = groups * split
     length = local_len * seq_count
-    x_at, z_at = lax.axis_index("x"), lax.axis_index("z")
-    head_width = w_query.shape[1] // split
+    x_at, z_at, e_at = lax.axis_index("x"), lax.axis_index("z"), lax.axis_index("exp")
+    s_at = z_at * split + x_at
+    head_width = hd // split
+    heads_here = head_width // HEAD_DIM
     experts_all = w_router.shape[1]
     bias_own = bias_table.shape[0]
+    tile = min(TILE, local_len)
+    own = s_at.astype(jnp.int32).reshape(1)
+    z_bits, x_bits, e_bits = bits_of(groups), bits_of(split), bits_of(exp_count)
+
+    input_r = reorder(block_in, z_at)
+
+    arrived = [[None] * split for _ in range(groups)]
+    for rz in reversed(range(groups)):
+        arrived[rz][0] = partner(input_r[rz], "z", rz) if rz else input_r[0]
+    for rz in [0] + list(reversed(range(1, groups))):
+        for rx in range(1, split):
+            arrived[rz][rx] = partner(arrived[rz][0], "x", rx)
+    sequence = jnp.stack([block for line in arrived for block in line]).reshape(length, width)
+
+    gate_up_own = jnp.concatenate([w_gate[0].astype(LOW), w_up[0].astype(LOW)], axis=1)
+    sequence, gate_up_own, down_own = lax.optimization_barrier((sequence, gate_up_own, w_down[0].astype(LOW)))
+    gate_up_w = ring_gather(gate_up_own, groups, split, s_at)
+    down_w = lax.all_gather(down_own, SEQ, axis=0, tiled=True)
 
     small = jnp.concatenate(
         [
@@ -459,181 +629,208 @@
         ],
         axis=1,
     )
-    small = jnp.pad(small, ((0, 0), (0, LANES - small.shape[1])))
-    packed = jnp.concatenate(
-        [part.astype(low_type) for part in (w_query, w_key, w_value, w_out, small)], axis=1
-    )
-    packed = lax.all_gather(packed, ALL, axis=0, tiled=True)
-    gate_w = lax.all_gather(w_gate[0].astype(low_type), SEQ, axis=0, tiled=True)
-    up_w = lax.all_gather(w_up[0].astype(low_type), SEQ, axis=0, tiled=True)
-    down_w = lax.all_gather(w_down[0].astype(low_type), SEQ, axis=0, tiled=True)
-
-    outgoing = jnp.broadcast_to(block_in[:, None], (groups, split, local_len, width))
-    sequence = lax.all_to_all(
-        outgoing.reshape(seq_count, local_len, width), SEQ, split_axis=0, concat_axis=0, tiled=True
-    ).reshape(length, width)
-
-    hd = w_query.shape[1]
-    out_w = packed[:, 3 * hd : 4 * hd]
-    small_all = packed[:, 4 * hd :]
+    small = jnp.pad(small, ((0, 0), (0, LANES - small.shape[1]))).astype(LOW)
+    share = jnp.stack(
+        [part.astype(LOW).reshape(rows_own, split, head_width) for part in (w_query, w_key, w_value)], axis=2
+    )
+    share = share.reshape(rows_own, split, 3 * head_width).transpose(1, 0, 2)
+    share = jnp.concatenate([share, jnp.broadcast_to(small, (split,) + small.shape)], axis=2)
+    shares = [lax.dynamic_index_in_dim(share, x_at ^ r, 0, keepdims=False) for r in range(split)]
+    shares = [shares[0]] + [partner(shares[r], "x", r) for r in range(1, split)]
+    by_x = reorder(jnp.stack(shares), x_at)
+    steps = [("z", b) for b in z_bits] + [("exp", b) for b in e_bits]
+    packed = gather_double(by_x, steps)
+    ne, nz = len(e_bits), len(z_bits)
+    packed = packed.transpose(
+        tuple(ne + i for i in reversed(range(nz))) + (ne + nz,) + tuple(reversed(range(ne))) + (ne + nz + 1, ne + nz + 2)
+    ).reshape(width, 3 * head_width + LANES)
+    qkv_w, small_all = packed[:, : 3 * head_width], packed[:, 3 * head_width :]
+    out_steps = [("z", b) for b in z_bits] + [("x", b) for b in x_bits] + [("exp", b) for b in e_bits]
+    out_w = gather_double(w_out.astype(LOW), out_steps)
+    nx = len(x_bits)
+    out_w = out_w.transpose(
+        tuple(ne + nx + i for i in reversed(range(nz)))
+        + tuple(ne + i for i in reversed(range(nx)))
+        + tuple(reversed(range(ne)))
+        + (ne + nx + nz, ne + nx + nz + 1)
+    )
+    out_w = out_w.reshape(hd, width)
+
     gain_one = small_all[:, 0].astype(jnp.float32)
     gain_two = small_all[:, 1].astype(jnp.float32)
     table_all = small_all[:, 2].reshape(-1, rows_own)[:, :bias_own].reshape(-1, BUCKETS)
-    router_w = small_all[:, 3 : 3 + experts_all]
-    heads_here = head_width // HEAD_DIM
-    qkv_w = [
-        lax.dynamic_slice_in_dim(packed, part * hd + x_at * head_width, head_width, 1)
-        for part in range(3)
-    ]
-    qkv_w = jnp.concatenate(qkv_w, axis=1)
+    router_t = small_all[:, 3 : 3 + experts_all].T
     table_rows = lax.dynamic_slice_in_dim(table_all, x_at * heads_here, heads_here, 0)
 
-    normed_one = rms_scale(sequence.astype(jnp.float32), gain_one).astype(low_type)
-    qkv = dot32(normed_one, qkv_w).astype(low_type)
+    routes = expert_routes.reshape(tokens, -1)
+    top_count = routes.shape[1]
+    priority = pair_priority.reshape(-1)
+    pair_experts = routes.reshape(-1)
+    ahead = (pair_experts[None, :] == pair_experts[:, None]) & (priority[None, :] < priority[:, None])
+    slots = jnp.sum(ahead.astype(jnp.int32), axis=1)
+    capacity = (5 * top_count * tokens + 4 * experts_all - 1) // (4 * experts_all)
+    slot_count = experts_all * capacity
+    slot_index = jnp.where(slots < capacity, (pair_experts ^ e_at) * capacity + slots, slot_count)
+    slot_index = slot_index.reshape(tokens, top_count)
+    every_slot = jnp.arange(slot_count, dtype=jnp.int32)[None, :]
+    table = sum((slot_index[:, k : k + 1] == every_slot).astype(LOW) for k in range(top_count))
+    tables = [table[:, r * capacity : (r + 1) * capacity] for r in range(exp_count)]
+    grad_low = cotangent.reshape(tokens, width)
+    grad_slots = [dot_tn(part, grad_low).astype(LOW) for part in tables]
+
+    wide = sequence.astype(jnp.float32)
+    normed_one = (wide * norm_scale(wide) * gain_one).astype(LOW)
+    qkv = dot32(normed_one, qkv_w).astype(LOW)
+    qkv, grad_slots = lax.optimization_barrier((qkv, grad_slots))
+    grad_slots = [grad_slots[0]] + [partner(grad_slots[r], "exp", r) for r in range(1, exp_count)]
     segments = lax.dynamic_index_in_dim(segment_ids, z_at, 0, keepdims=False)
-    tile = min(TILE, length)
-    query_side, key_side = segment_columns(segments)
     ranges = tile_ranges(segments, tile)
+    seg_blocks = segments.reshape(seq_count, local_len)
+    query_side, key_side = segment_columns(reorder(seg_blocks, s_at).reshape(length))
     rows = bias_rows(table_rows, tile)
     ends = jnp.stack([table_rows[:, 15], table_rows[:, 31]], axis=1).astype(jnp.float32)
-    contexts, log_totals = attend_forward(qkv, query_side, key_side, ranges, rows, ends)
-    context_local = lax.all_to_all(
-        contexts.reshape(seq_count, local_len, head_width), SEQ, split_axis=0, concat_axis=0, tiled=True
-    )
+    contexts, log_totals = attend_forward(qkv, query_side, key_side, ranges, rows, ends, own, tile)
+
+    def exchange_positions(blocks):
+        return lax.all_to_all(blocks, SEQ, split_axis=0, concat_axis=0, tiled=True)
+
+    context_local = exchange_positions(contexts.reshape(seq_count, local_len, head_width))
     context_local = (
-        context_local.reshape(groups, split, local_len, head_width)
-        .transpose(0, 2, 1, 3)
-        .reshape(tokens, hd)
+        context_local.reshape(groups, split, local_len, head_width).transpose(0, 2, 1, 3).reshape(tokens, hd)
     )
     inputs = block_in.astype(jnp.float32).reshape(tokens, width)
     mid = inputs + dot32(context_local, out_w)
-    normed_two_full, norm_two_back = jax.vjp(rms_scale, mid, gain_two)
-    normed_two = normed_two_full.astype(low_type)
-    routes_local = expert_routes.reshape(tokens, -1)
-    top_count = routes_local.shape[1]
-    gates, gates_back = jax.vjp(
-        partial(gate_values, routes_local),
-        normed_two.astype(jnp.float32),
-        router_w.astype(jnp.float32),
-    )
-    pair_experts = routes_local.reshape(-1)
-    priority = pair_priority.reshape(-1)
-    expert_table = (
-        pair_experts[:, None] == jnp.arange(experts_all, dtype=jnp.int32)[None, :]
-    ).astype(low_type)
-    earlier = (priority[None, :] < priority[:, None]).astype(low_type)
-    ahead_counts = dot32(earlier, expert_table)
-    slots = jnp.sum(ahead_counts * expert_table, axis=1).astype(jnp.int32)
-    capacity = (5 * top_count * tokens + 4 * experts_all - 1) // (4 * experts_all)
-    slot_count = experts_all * capacity
-    slot_index = jnp.where(slots < capacity, pair_experts * capacity + slots, slot_count)
-    slot_table = (
-        slot_index[:, None] == jnp.arange(slot_count, dtype=jnp.int32)[None, :]
-    ).astype(low_type)
-    slot_table = slot_table.reshape(tokens, top_count, slot_count)
-    token_table = jnp.sum(slot_table, axis=1, dtype=jnp.float32).astype(low_type)
-    buffer = jnp.einsum(
-        "ts,td->sd", token_table, normed_two, preferred_element_type=jnp.float32
-    ).astype(low_type)
-
-    def swap_experts(rows_):
-        return lax.all_to_all(
-            rows_.reshape(exp_count, capacity, width), "exp", split_axis=0, concat_axis=0, tiled=True
-        ).reshape(slot_count, width)
-
-    arrived = swap_experts(buffer)
-    gate_hidden = dot32(arrived, gate_w)
-    up_hidden = dot32(arrived, up_w)
-    hidden_pair, geglu_back = jax.vjp(geglu_product, gate_hidden, up_hidden)
-    hidden = hidden_pair.astype(low_type)
-    expert_out = dot32(hidden, down_w).astype(low_type)
-    returned = swap_experts(expert_out)
-    picked = jnp.einsum("tks,sd->tkd", slot_table, returned, preferred_element_type=jnp.float32)
-    mixture = jnp.sum(picked * gates[..., None], axis=1)
-    block_out = (mid + mixture).astype(low_type).reshape(groups, local_len, width)
-
-    grad_out = cotangent.astype(jnp.float32).reshape(tokens, width)
-    gate_grad_pairs = jnp.sum(picked * grad_out[:, None, :], axis=-1)
-    pair_grad = (gates[..., None] * grad_out[:, None, :]).astype(low_type)
-    slot_grad = jnp.einsum(
-        "tks,tkd->sd", slot_table, pair_grad, preferred_element_type=jnp.float32
-    ).astype(low_type)
-    expert_grad_in = swap_experts(slot_grad)
-    hidden_grad = jnp.einsum("sd,fd->sf", expert_grad_in, down_w, preferred_element_type=jnp.float32)
-    gate_hidden_grad, up_hidden_grad = geglu_back(hidden_grad)
-    gate_low = gate_hidden_grad.astype(low_type)
-    up_low = up_hidden_grad.astype(low_type)
-    arrived_grad = jnp.einsum("sf,df->sd", gate_low, gate_w, preferred_element_type=jnp.float32)
-    arrived_grad = (
-        arrived_grad
-        + jnp.einsum("sf,df->sd", up_low, up_w, preferred_element_type=jnp.float32)
-    ).astype(low_type)
-    back_rows = swap_experts(arrived_grad)
-
-    def summed(a, b):
-        return jnp.einsum("sa,sb->ab", a, b, preferred_element_type=jnp.float32)
-
-    def scatter_experts(total):
-        return lax.psum_scatter(total.astype(low_type), SEQ, scatter_dimension=0, tiled=True).astype(
-            jnp.float32
-        )[None]
-
-    down_owned = scatter_experts(summed(hidden, expert_grad_in))
-    gate_owned = scatter_experts(summed(arrived, gate_low))
-    up_owned = scatter_experts(summed(arrived, up_low))
-    row_grad = jnp.einsum("ts,sd->td", token_table, back_rows, preferred_element_type=jnp.float32)
-    normed_two_grad, router_sum = gates_back(gate_grad_pairs)
-    mid_part, gain_two_sum = norm_two_back(normed_two_grad + row_grad)
-    mid_grad = grad_out + mid_part
-    attention_grad = mid_grad.astype(low_type)
-    out_w_sum = summed(context_local, attention_grad)
-    context_grad = jnp.einsum(
-        "td,kd->tk", attention_grad, out_w, preferred_element_type=jnp.float32
-    ).astype(low_type)
+    scale_two = norm_scale(mid)
+    normed_two = (mid * scale_two * gain_two).astype(LOW)
+
+    logits = dot_nt(router_t, normed_two)
+    exponent = jnp.exp(logits - jnp.max(logits, axis=0, keepdims=True))
+    probabilities = exponent / jnp.sum(exponent, axis=0, keepdims=True)
+    expert_ids = jnp.arange(experts_all, dtype=jnp.int32)[:, None]
+    chosen = sum((routes[:, k][None, :] == expert_ids).astype(jnp.float32) for k in range(top_count))
+    chosen_total = jnp.sum(probabilities * chosen, axis=0, keepdims=True)
+    gates = probabilities * chosen / chosen_total
+    gates_r = reorder(gates, e_at)
+
+    gate_slots = jnp.sum(
+        table.astype(jnp.float32).reshape(tokens, exp_count, capacity) * gates_r.T[:, :, None], axis=0
+    )
+    gate_lines = jnp.pad(jnp.stack(split3(gate_slots), axis=1), ((0, 0), (0, EXTRA - 3), (0, width - capacity)))
+
+    def values_below(rows_):
+        return jnp.sum(rows_[capacity : capacity + 3, :capacity].astype(jnp.float32), axis=0)
+
+    sent = [None] * exp_count
+    for r in reversed(range(exp_count)):
+        sent[r] = jnp.concatenate([dot_tn(tables[r], normed_two).astype(LOW), gate_lines[r]], axis=0)
+        if r:
+            sent[r] = partner(sent[r], "exp", r)
+    sent_gate = [values_below(rows_) for rows_ in sent]
+
+    earlier = ()
+    back = [None] * exp_count
+    for r in range(exp_count):
+        hidden, gate_low, up_low, dx = expert_block(
+            r, exp_count, sent[r], grad_slots[r], sent_gate[r][:, None], gate_up_w, down_w, earlier
+        )
+        earlier = (hidden, gate_low, up_low)
+        back[r] = partner(dx, "exp", r) if r else dx
+
+    slot_rows = jnp.concatenate([rows_[:capacity] for rows_ in sent], axis=0)
+    slot_gates = jnp.concatenate(sent_gate, axis=0)[:, None]
+    slot_grads = (slot_gates * jnp.concatenate(grad_slots, axis=0).astype(jnp.float32)).astype(LOW)
+    expert_out = (slot_gates * dot32(hidden, down_w)).astype(LOW)
+    down_sum = dot_tn(hidden, slot_grads).astype(LOW)
+    gate_sum = dot_tn(slot_rows, gate_low).astype(LOW)
+    up_sum = dot_tn(slot_rows, up_low).astype(LOW)
+
+    gate_grad = jnp.sum(
+        table.astype(jnp.float32).reshape(tokens, exp_count, capacity) * jnp.stack([values_below(rows_) for rows_ in back])[None], axis=2
+    )
+    gate_grad = reorder(gate_grad.T, e_at)
+    chosen_grad = chosen * (gate_grad - jnp.sum(gates * gate_grad, axis=0, keepdims=True)) / chosen_total
+    logit_grad = probabilities * (chosen_grad - jnp.sum(probabilities * chosen_grad, axis=0, keepdims=True))
+    logit_pieces = jnp.concatenate(split3(logit_grad), axis=0)
+    router_sum = jnp.sum(dot32(logit_pieces, normed_two).reshape(3, experts_all, width), axis=0)
+    normed_two_grad = dot_tn(logit_pieces, jnp.concatenate([router_t] * 3, axis=0))
+    for r in range(exp_count):
+        normed_two_grad = normed_two_grad + dot32(tables[r], back[r][:capacity])
+    unit_two = mid * scale_two
+    gain_two_sum = jnp.sum(normed_two_grad * unit_two, axis=0)
+    grad_out = grad_low.astype(jnp.float32)
+    mid_grad = grad_out + norm_back(scale_two, unit_two, gain_two, normed_two_grad)
+    attention_grad = mid_grad.astype(LOW)
+    context_grad = dot_nt(attention_grad, out_w).astype(LOW)
     context_grad = (
         context_grad.reshape(groups, local_len, split, head_width)
         .transpose(0, 2, 1, 3)
         .reshape(seq_count, local_len, head_width)
     )
-    context_heads = lax.all_to_all(
-        context_grad, SEQ, split_axis=0, concat_axis=0, tiled=True
-    ).reshape(length, head_width)
+    context_heads = exchange_positions(context_grad).reshape(length, head_width)
+
+    def scatter_experts(total):
+        return lax.psum_scatter(total, SEQ, scatter_dimension=0, tiled=True).astype(jnp.float32)[None]
+
+    down_owned = scatter_experts(down_sum)
+    gate_owned = scatter_experts(gate_sum)
+    up_owned = scatter_experts(up_sum)
+    context_heads, _, _, _, expert_out = lax.optimization_barrier(
+        (context_heads, down_sum[:8], gate_sum[:8], up_sum[:8], expert_out)
+    )
+
+    returned = [expert_out[:capacity]] + [
+        partner(expert_out[r * capacity : (r + 1) * capacity], "exp", r) for r in range(1, exp_count)
+    ]
+    block_out = (mid + dot32(table, jnp.concatenate(returned, axis=0))).astype(LOW)
+
+    block_out = block_out.reshape(groups, local_len, width)
+
+    def by_step(total, with_x):
+        columns = total.shape[1]
+        shaped = total.astype(LOW).reshape((2,) * (nz + nx + ne) + (rows_own, columns))
+        z_dims = tuple(reversed(range(nz)))
+        x_dims = tuple(nz + i for i in reversed(range(nx)))
+        e_dims = tuple(nz + nx + i for i in reversed(range(ne)))
+        rest = (nz + nx + ne, nz + nx + ne + 1)
+        if with_x:
+            return shaped.transpose(e_dims + z_dims + x_dims + rest)
+        return shaped.transpose(e_dims + z_dims + tuple(reversed(x_dims)) + rest)
+
+    halving = [("exp", b) for b in reversed(e_bits)] + [("z", b) for b in reversed(z_bits)]
+    x_halving = [("x", b) for b in reversed(x_bits)]
+    out_w_sum = dot_tn(context_local, attention_grad)
+    out_w_out = scatter_halve(by_step(out_w_sum, True), halving + x_halving).astype(jnp.float32)
+
     query_back, key_back, value_back, diag, far = attend_backward(
-        qkv, context_heads, contexts, log_totals, query_side, key_side, ranges, rows, ends
+        qkv, context_heads, contexts, log_totals, query_side, key_side, ranges, rows, ends, own, tile
     )
     table_local = bucket_sums(diag, far, tile)
 
     def through(grads, part):
-        weight = qkv_w[:, part * head_width : (part + 1) * head_width]
-        return jnp.einsum("tk,dk->td", grads, weight, preferred_element_type=jnp.float32)
-
-    normed_part = (through(query_back, 0) + through(key_back, 1) + through(value_back, 2)).astype(low_type)
-    normed_parts = lax.all_to_all(
-        normed_part.reshape(seq_count, local_len, width), SEQ, split_axis=0, concat_axis=0, tiled=True
-    ).reshape(groups, split, local_len, width)
-    normed_one_grad = jnp.sum(normed_parts.astype(jnp.float32), axis=1).reshape(tokens, width)
-    _, norm_one_back = jax.vjp(rms_scale, inputs, gain_one)
-    input_part, gain_one_sum = norm_one_back(normed_one_grad)
-    block_in_grad = (mid_grad + input_part).reshape(groups, local_len, width)
-
-    def by_owner(total):
-        columns = total.shape[1]
-        shaped = total.reshape(groups, split, exp_count, rows_own, columns)
-        return shaped.transpose(0, 2, 1, 3, 4).reshape(-1, columns)
-
-    def scatter_rows(total):
-        return lax.psum_scatter(
-            by_owner(total).astype(low_type), ("z", "exp"), scatter_dimension=0, tiled=True
-        ).reshape(split, rows_own, -1)
-
-    out_part = lax.all_to_all(scatter_rows(out_w_sum), "x", split_axis=0, concat_axis=0, tiled=True)
-    out_w_out = jnp.sum(out_part.astype(jnp.float32), axis=0)
+        return dot_nt(grads, qkv_w[:, part * head_width : (part + 1) * head_width])
+
+    normed_part = through(query_back, 0) + through(key_back, 1) + through(value_back, 2)
+    normed_part = normed_part.reshape(groups, split, local_len, width)
+    pieces_back = [None] * groups
+    for rz in list(reversed(range(1, groups))) + [0]:
+        total = normed_part[rz, 0]
+        for rx in range(1, split):
+            total = total + partner(normed_part[rz, rx].astype(LOW), "x", rx).astype(jnp.float32)
+        pieces_back[rz] = partner(total.astype(LOW), "z", rz).astype(jnp.float32) if rz else total
+    normed_one_grad = reorder(jnp.stack(pieces_back), z_at).reshape(tokens, width)
+    scale_one = norm_scale(inputs)
+    unit_one = inputs * scale_one
+    gain_one_sum = jnp.sum(normed_one_grad * unit_one, axis=0)
+    block_in_grad = (mid_grad + norm_back(scale_one, unit_one, gain_one, normed_one_grad)).reshape(groups, local_len, width)
+
     qkv_sum = jnp.concatenate(
-        [summed(normed_one, grads) for grads in (query_back, key_back, value_back)], axis=1
-    )
-    qkv_part = lax.all_to_all(scatter_rows(qkv_sum), "x", split_axis=0, concat_axis=0, tiled=True)
-    qkv_part = qkv_part.reshape(split, rows_own, 3, head_width).transpose(2, 1, 0, 3)
-    qkv_part = qkv_part.reshape(3, rows_own, hd).astype(jnp.float32)
+        [dot_tn(normed_one, grads).astype(LOW) for grads in (query_back, key_back, value_back)], axis=1
+    )
+    qkv_part = scatter_halve(by_step(qkv_sum, False), halving).reshape(split, rows_own, 3 * head_width)
+    qkv_own = [lax.dynamic_index_in_dim(qkv_part, x_at ^ r, 0, keepdims=False) for r in range(split)]
+    qkv_own = [qkv_own[0]] + [partner(qkv_own[r], "x", r) for r in range(1, split)]
+    qkv_own = reorder(jnp.stack(qkv_own), x_at).reshape(split, rows_own, 3, head_width)
+    qkv_own = qkv_own.transpose(2, 1, 0, 3).reshape(3, rows_own, hd).astype(jnp.float32)
 
     table_sum = lax.dynamic_update_slice_in_dim(
         jnp.zeros(table_all.shape, jnp.float32), table_local, x_at * heads_here, 0
@@ -644,7 +841,7 @@
             gain_one_sum.reshape(-1, 1, rows_own),
             gain_two_sum.reshape(-1, 1, rows_own),
             table_sum,
-            router_sum.reshape(-1, rows_own, experts_all).transpose(0, 2, 1),
+            router_sum.reshape(experts_all, -1, rows_own).transpose(1, 0, 2),
         ],
         axis=1,
     )
@@ -653,9 +850,9 @@
         block_out,
         block_in_grad,
         little[0],
-        qkv_part[0],
-        qkv_part[1],
-        qkv_part[2],
+        qkv_own[0],
+        qkv_own[1],
+        qkv_own[2],
         out_w_out,
         little[2, :bias_own],
         little[1],

time: 1460 us -> 1170 us (0.80)
  waiting for transfers between devices: 728 us -> 343 us
  matrix products: 341 us -> 185 us
  Pallas kernels: 170 us -> 292 us
  starting transfers between devices: 60.4 us -> 157 us
  local copies, waits for them, and re-layouts: 62.5 us -> 89.2 us
    reduce_scatter x5 -> x3, waiting for transfers between devices: 390 us -> 0.01 us  [scatter_experts(): lax.psum_scatter(total, SEQ, scatter_dimension=0, tiled=True)]
    ppermute x0 -> x53, waiting for transfers between devices: none -> 337 us  [the longest x46 268 us: partner(): return lax.ppermute(value, axis, [(i, i ^ offset) for i in range(count)])]
    all_to_all x10 -> x2, waiting for transfers between devices: 323 us -> 0.01 us  [exchange_positions(): return lax.all_to_all(blocks, SEQ, split_axis=0, concat_axis=0, tiled=True)]
    dot_general x21, matrix products: 258 us -> 121 us  [the longest x16 92 us: dot_tn(): lax.dot_general(a, b, (((0,), (0,)), ((), ())), preferred_element_type=jn...]
    ppermute x0 -> x53, starting transfers between devices: none -> 126 us  [the longest x46 106 us: partner(): return lax.ppermute(value, axis, [(i, i ^ offset) for i in range(count)])]
    pallas_call x0 -> x4, Pallas kernels: none -> 121 us  [expert_block(): pl.pallas_call(expert_kernel, name='expert_block', out_shape=(whole, whol...]
    all_to_all x10 -> x2, starting transfers between devices: 55.4 us -> 21.4 us  [exchange_positions(): return lax.all_to_all(blocks, SEQ, split_axis=0, concat_axis=0, tiled=True)]
    dot_general x6 -> x9, matrix products: 82.2 us -> 62.3 us  [dot32(): return jnp.dot(a, b, preferred_element_type=jnp.float32)]
  transfers between devices with their start and end apart: 20 -> 60, of which waited for: 14 -> 27; matrix products, arithmetic and copies ran while one was open for 23% -> 25% of each run, Pallas kernels for 12% -> 23%
where the time goes in v2:
time: 1170 us; the launch traced here: 1160 us
  waiting for transfers between devices  343 us (29%)
  Pallas kernels  292 us (25%)
  matrix products  185 us (16%)
  starting transfers between devices  157 us (13%)
  local copies, waits for them, and re-layouts  89.2 us (8%)
  other arithmetic  68.7 us (6%)
  between operations  25.5 us (2%)
    ppermute x46, waiting for transfers between devices, partner(): return lax.ppermute(value, axis, [(i, i ^ offset) for i in range(count)])  268 us
    pallas_call x4, Pallas kernels, expert_block(): pl.pallas_call(expert_kernel, name='expert_block', out_shape=(whole, whol...  121 us
    pallas_call x1, Pallas kernels, attend_backward(): pl.pallas_call(bwd_kernel, name='attend_backward', out_shape=(low, low, l...  114 us
    ppermute x46, starting transfers between devices, partner(): return lax.ppermute(value, axis, [(i, i ^ offset) for i in range(count)])  106 us
    dot_general x16, matrix products, dot_tn(): lax.dot_general(a, b, (((0,), (0,)), ((), ())), preferred_element_type=jn...  92 us
    ppermute x4, waiting for transfers between devices, ring_gather(): forward = lax.ppermute(forward, SEQ, ahead)  62.5 us
    dot_general x9, matrix products, dot32(): return jnp.dot(a, b, preferred_element_type=jnp.float32)  62.3 us
    pallas_call x1, Pallas kernels, attend_forward(): pl.pallas_call(fwd_kernel, name='attend_forward', out_shape=(jax.ShapeDty...  56.8 us
  transfers between devices with their start and end apart: 60, of which 27 were waited for; matrix products, arithmetic and copies ran while one was open for 25% of the time, Pallas kernels for 23%

profile of v2, /device:TPU:0, one launch (start us, length us, event | category | flops | bytes accessed | tf_op | source)
XLA Modules:
  0.0 1159.9 jit_solution(16244203012332867617)
XLA Ops:
  139.4 26.4 %collective-permute-done.17 = bf16[128,5632]{1,0:T(8,128)(2,1)} collective-permute-done((bf16[128,5632]{1,0:T(8,128)(2,1)}, bf16[128,5632]{1,0:T(8,128)(2,1)}, u32[]{:S(2)}, u32[]{:S(2)}) %collective-permute-start.17) | collective-permute-done | bytes 1441824 | tf_op jit(solution)/shard_map/ppermute | solution.py:548
  188.1 56.8 %attend_forward.1 = (bf16[2048,512]{1,0:T(8,128)(2,1)}, f32[4,2,2048]{2,1,0:T(2,128)S(1)}) custom-call(s32[2,8]{1,0:T(2,128)S(1)} %pad_add_fusion.ranges, f32[8,2]{1,0:T(8,128)S(1)} %maximum_convert_fusion.1.ends, s32[1]{0:T(128)} %bitcast.19.own, bf16[2048,1536]{1,0:T(8,128)(2,1)} %convolution_convert_fusion.q_ref.k_ref.v_ref, ...), custom_call_target="tpu_custom_call" | custom-call | flops 8589934592 | bytes 8388608 | tf_op jit(solution)/shard_map/attend_forward/pallas_call | solution.py:168
  244.9 16.9 %all-to-all-start = ((bf16[8,256,512]{2,1,0:T(8,128)(2,1)}), bf16[8,256,512]{2,1,0:T(8,128)(2,1)S(1)}, u32[]{:S(2)}, u32[]{:S(2)}) async-start(bf16[8,256,512]{2,1,0:T(8,128)(2,1)} %bitcast.38), calls=%async_computation | async-start | bytes 4194304 | tf_op jit(solution)/shard_map/all_to_all | solution.py:695
  274.5 36.1 %collective-permute-done.21 = bf16[128,5632]{1,0:T(8,128)(2,1)} collective-permute-done((bf16[128,5632]{1,0:T(8,128)(2,1)}, bf16[128,5632]{1,0:T(8,128)(2,1)}, u32[]{:S(2)}, u32[]{:S(2)}) %collective-permute-start.21) | collective-permute-done | bytes 1441824 | tf_op jit(solution)/shard_map/ppermute | solution.py:548
  310.5 16.0 %collective-permute-start.23 = (bf16[128,5632]{1,0:T(8,128)(2,1)}, bf16[128,5632]{1,0:T(8,128)(2,1)}, u32[]{:S(2)}, u32[]{:S(2)}) collective-permute-start(bf16[128,5632]{1,0:T(8,128)(2,1)} %collective-permute-done.21), channel_id=1, source_target_pairs={{0,8},{8,16},{16,24},{24,28},{28,20},{20,12},{12,4},{4,0},{1,9},{9... | collective-permute-start | bytes 4325384 | tf_op jit(solution)/shard_map/ppermute | solution.py:548
  355.9 16.2 %collective-permute-done.27.x_ref = bf16[656,1024]{1,0:T(8,128)(2,1)S(1)} collective-permute-done((bf16[656,1024]{1,0:T(8,128)(2,1)S(1)}, bf16[656,1024]{1,0:T(8,128)(2,1)S(1)}, u32[]{:S(2)}, u32[]{:S(2)}) %collective-permute-start.27) | collective-permute-done | bytes 1343520 | tf_op jit(solution)/shard_map/ppermute | solution.py:496
  372.3 24.9 %collective-permute-done.30.x_ref = bf16[656,1024]{1,0:T(8,128)(2,1)S(1)} collective-permute-done((bf16[656,1024]{1,0:T(8,128)(2,1)S(1)}, bf16[656,1024]{1,0:T(8,128)(2,1)S(1)}, u32[]{:S(2)}, u32[]{:S(2)}) %collective-permute-start.30) | collective-permute-done | bytes 1343520 | tf_op jit(solution)/shard_map/ppermute | solution.py:496
  404.8 29.9 %expert_block.4 = (bf16[2560,2816]{1,0:T(8,128)(2,1)}, bf16[2560,2816]{1,0:T(8,128)(2,1)}, bf16[2560,2816]{1,0:T(8,128)(2,1)}, bf16[656,1024]{1,0:T(8,128)(2,1)S(1)}) custom-call(s32[1]{0:T(128)} %constant.232.clone.1.own_ref, bf16[656,1024]{1,0:T(8,128)(2,1)S(1)} %copy-done.8, bf16[640,1024]{1,0:T(8,128)(2,1)S(1)} %copy-done.27, f32[640,1]{1,0:T(8,128)S(1)} %copy-done.16, ...), custom_call_target="tpu_custom_call" | custom-call | flops 18454937600 | bytes 28114944 | tf_op jit(solution)/shard_map/expert_block/pallas_call | solution.py:457
  435.8 30.5 %expert_block.5 = (bf16[2560,2816]{1,0:T(8,128)(2,1)}, bf16[2560,2816]{1,0:T(8,128)(2,1)}, bf16[2560,2816]{1,0:T(8,128)(2,1)}, bf16[656,1024]{1,0:T(8,128)(2,1)S(1)}) custom-call(s32[1]{0:T(128)} %constant.232.clone.1.own_ref, bf16[656,1024]{1,0:T(8,128)(2,1)S(1)} %collective-permute-done.24.x_ref, ...), custom_call_target="tpu_custom_call", output_to_operand_aliasing={{0}: (7, {}), {1}: (8, {}), {2}: (9, {})} | custom-call | flops 18454937600 | bytes 28114944 | tf_op jit(solution)/shard_map/expert_block/pallas_call | solution.py:457
  467.5 30.4 %expert_block.6 = (bf16[2560,2816]{1,0:T(8,128)(2,1)}, bf16[2560,2816]{1,0:T(8,128)(2,1)}, bf16[2560,2816]{1,0:T(8,128)(2,1)}, bf16[656,1024]{1,0:T(8,128)(2,1)S(1)}) custom-call(s32[1]{0:T(128)} %constant.232.clone.1.own_ref, bf16[656,1024]{1,0:T(8,128)(2,1)S(1)} %collective-permute-done.27.x_ref, ...), custom_call_target="tpu_custom_call", output_to_operand_aliasing={{0}: (7, {}), {1}: (8, {}), {2}: (9, {})} | custom-call | flops 18454937600 | bytes 28114944 | tf_op jit(solution)/shard_map/expert_block/pallas_call | solution.py:457
  498.9 30.5 %expert_block.7 = (bf16[2560,2816]{1,0:T(8,128)(2,1)}, bf16[2560,2816]{1,0:T(8,128)(2,1)}, bf16[2560,2816]{1,0:T(8,128)(2,1)}, bf16[656,1024]{1,0:T(8,128)(2,1)S(1)}) custom-call(s32[1]{0:T(128)} %constant.232.clone.1.own_ref, bf16[656,1024]{1,0:T(8,128)(2,1)S(1)} %copy-done.4, ...), custom_call_target="tpu_custom_call", output_to_operand_aliasing={{0}: (7, {}), {1}: (8, {}), {2}: (9, {})} | custom-call | flops 18454937600 | bytes 28114944 | tf_op jit(solution)/shard_map/expert_block/pallas_call | solution.py:457
  530.5 24.8 %convolution_convert_fusion.1 = bf16[2816,1024]{1,0:T(8,128)(2,1)} fusion(bf16[2560,2816]{1,0:T(8,128)(2,1)} %get-tuple-element.68, bf16[640,1024]{1,0:T(8,128)(2,1)} %collective-permute-done.31.dy_ref, bf16[640,1024]{1,0:T(8,128)(2,1)} %collective-permute-done.28.dy_ref, bf16[640,1024]{1,0:T(8,128)(2,1)} %collective-permute-done.25.dy_ref, ...), kind=kOutput, calls=%fused_computation.20 | convolution fusion | flops 14793048064 | bytes 25438208 | tf_op jit(solution)/shard_map/dot_general | solution.py:491
  558.6 21.0 %convolution_convert_fusion.2 = bf16[1024,2816]{1,0:T(8,128)(2,1)} fusion(bf16[2560,2816]{1,0:T(8,128)(2,1)} %get-tuple-element.78, bf16[640,1024]{1,0:T(8,128)(2,1)S(1)} %slice.416, bf16[640,1024]{1,0:T(8,128)(2,1)S(1)} %slice.415, bf16[640,1024]{1,0:T(8,128)(2,1)S(1)} %slice.414, bf16[640,1024]{1,0:T(8,128)(2,1)S(1)} %copy-done.58), kind=kOutput, calls=%fused_computation.21 | convolution fusion | flops 14787805184 | bytes 25427968 | tf_op jit(solution)/shard_map/dot_general | solution.py:491
  586.5 24.8 %collective-permute-done.32 = bf16[656,1024]{1,0:T(8,128)(2,1)} collective-permute-done((bf16[656,1024]{1,0:T(8,128)(2,1)}, bf16[656,1024]{1,0:T(8,128)(2,1)}, u32[]{:S(2)}, u32[]{:S(2)}) %collective-permute-start.32) | collective-permute-done | bytes 1343520 | tf_op jit(solution)/shard_map/ppermute | solution.py:496
  612.1 29.1 %collective-permute-done.29 = bf16[656,1024]{1,0:T(8,128)(2,1)} collective-permute-done((bf16[656,1024]{1,0:T(8,128)(2,1)}, bf16[656,1024]{1,0:T(8,128)(2,1)}, u32[]{:S(2)}, u32[]{:S(2)}) %collective-permute-start.29) | collective-permute-done | bytes 1343520 | tf_op jit(solution)/shard_map/ppermute | solution.py:496
  679.4 18.4 %convolution_convert_fusion.3 = bf16[1024,2816]{1,0:T(8,128)(2,1)} fusion(bf16[2560,2816]{1,0:T(8,128)(2,1)S(1)} %bitcast.349, bf16[640,1024]{1,0:T(8,128)(2,1)} %copy-done.64, bf16[640,1024]{1,0:T(8,128)(2,1)S(1)} %copy-done.63, bf16[640,1024]{1,0:T(8,128)(2,1)S(1)} %copy-done.61, bf16[640,1024]{1,0:T(8,128)(2,1)S(1)} %copy-done.59), kind=kOutput, calls=%fused_computation.22 | convolution fusion | flops 14787805184 | bytes 25427968 | tf_op jit(solution)/shard_map/dot_general | solution.py:491
  721.1 21.0 %multiply_convert_fusion.1 = bf16[2560,1024]{1,0:T(8,128)(2,1)} fusion(bf16[2560,2816]{1,0:T(8,128)(2,1)} %get-tuple-element.68, bf16[2816,1024]{1,0:T(8,128)(2,1)} %all-gather.2.cloned.1.call-done.wd_ref, f32[2560]{0:T(1024)S(1)} %pad_maximum_fusion.26), kind=kOutput, calls=%fused_computation.8 | convolution fusion | flops 14769192960 | bytes 25438208 | tf_op jit(solution)/shard_map/dot_general | solution.py:483
  742.1 42.1 %collective-permute-done.51 = bf16[2,32,1024]{2,1,0:T(8,128)(2,1)S(1)} collective-permute-done((bf16[2,32,1024]{2,1,0:T(8,128)(2,1)S(1)}, bf16[2,32,1024]{2,1,0:T(8,128)(2,1)S(1)}, u32[]{:S(2)}, u32[]{:S(2)}) %collective-permute-start.51) | collective-permute-done | bytes 131104 | tf_op jit(solution)/shard_map/ppermute | solution.py:496
  794.0 113.5 %attend_backward.1 = (bf16[2048,512]{1,0:T(8,128)(2,1)S(1)}, bf16[2048,512]{1,0:T(8,128)(2,1)S(1)}, bf16[2048,512]{1,0:T(8,128)(2,1)S(1)}, f32[8,3,512]{2,1,0:T(4,128)S(1)}, f32[8,2,256]{2,1,0:T(2,128)S(1)}) custom-call(s32[2,8]{1,0:T(2,128)S(1)} %copy-done.22, f32[8,2]{1,0:T(8,128)S(1)} %copy-done.20, s32[1]{0:T(128)} %bitcast.19.own, ...), custom_call_target="tpu_custom_call" | custom-call | flops 21474836480 | bytes 16777216 | tf_op jit(solution)/shard_map/attend_backward/pallas_call | solution.py:346
  958.0 11.2 collective-permute-done.37
  991.1 14.1 %collective-permute-start.42 = (bf16[256,1024]{1,0:T(8,128)(2,1)}, bf16[256,1024]{1,0:T(8,128)(2,1)}, u32[]{:S(2)}, u32[]{:S(2)}) collective-permute-start(bf16[256,1024]{1,0:T(8,128)(2,1)} %get-tuple-element.100), channel_id=1, source_target_pairs={{0,24},{8,16},{16,8},{24,0},{1,25},{9,17},{17,9},{25,1},{2,26},{10... | collective-permute-start | bytes 1572872 | tf_op jit(solution)/shard_map/ppermute | solution.py:496
  1009.2 20.6 %collective-permute-start.34 = (bf16[640,1024]{1,0:T(8,128)(2,1)}, bf16[640,1024]{1,0:T(8,128)(2,1)}, u32[]{:S(2)}, u32[]{:S(2)}) collective-permute-start(bf16[640,1024]{1,0:T(8,128)(2,1)} %get-tuple-element.105), channel_id=1, source_target_pairs={{0,2},{1,3},{2,0},{3,1},{4,6},{5,7},{6,4},{7,5},{8,10},{9,11},{10,... | collective-permute-start | bytes 3932168 | tf_op jit(solution)/shard_map/ppermute | solution.py:496
  1035.5 26.3 %collective-permute-start.35 = (bf16[640,1024]{1,0:T(8,128)(2,1)}, bf16[640,1024]{1,0:T(8,128)(2,1)}, u32[]{:S(2)}, u32[]{:S(2)}) collective-permute-start(bf16[640,1024]{1,0:T(8,128)(2,1)} %get-tuple-element.104), channel_id=1, source_target_pairs={{0,3},{1,2},{2,1},{3,0},{4,7},{5,6},{6,5},{7,4},{8,11},{9,10},{10,... | collective-permute-start | bytes 3932168 | tf_op jit(solution)/shard_map/ppermute | solution.py:496
  1093.6 15.0 %collective-permute-done.44 = bf16[2,2,2,32,1536]{4,3,2,0,1:T(8,128)(2,1)} collective-permute-done((bf16[2,2,2,32,1536]{4,3,2,0,1:T(8,128)(2,1)S(1)}, bf16[2,2,2,32,1536]{4,3,2,0,1:T(8,128)(2,1)}, u32[]{:S(2)}, u32[]{:S(2)}) %collective-permute-start.44) | collective-permute-done | bytes 786464 | tf_op jit(solution)/shard_map/ppermute | solution.py:496
  (562 shorter events, 437.8 us)
Async XLA Ops:
  7.2 391.3 %all-gather.2.cloned.1.call-start = ((), (), s32[]{:S(2)}) async-start(), calls=%async_computation.6 | async-start | bytes 6488064 | tf_op jit(solution)/shard_map/all_gather | solution.py:621
  8.2 50.8 %collective-permute-start.12 = (bf16[32,1024]{1,0:T(8,128)(2,1)S(1)}, bf16[32,1024]{1,0:T(8,128)(2,1)S(1)}, u32[]{:S(2)}, u32[]{:S(2)}) collective-permute-start(bf16[32,1024]{1,0:T(8,128)(2,1)S(1)} %convert_element_type.490), channel_id=1, source_target_pairs={{0,16},{8,24},{16,0},{24,8},{1,17},{9,25},{17,1},{25,9},{2,18},{10... | collective-permute-start | bytes 196616 | tf_op jit(solution)/shard_map/ppermute | solution.py:496
  15.4 72.5 %collective-permute-start.5 = (bf16[256,1024]{1,0:T(8,128)(2,1)}, bf16[256,1024]{1,0:T(8,128)(2,1)}, u32[]{:S(2)}, u32[]{:S(2)}) collective-permute-start(bf16[256,1024]{1,0:T(8,128)(2,1)} %get-tuple-element.123), channel_id=1, source_target_pairs={{0,4},{4,0},{1,5},{5,1},{2,6},{6,2},{3,7},{7,3},{8,12},{12,8},{9,1... | collective-permute-start | bytes 1572872 | tf_op jit(solution)/shard_map/ppermute | solution.py:496
  16.9 72.8 %collective-permute-start.6 = (bf16[256,1024]{1,0:T(8,128)(2,1)}, bf16[256,1024]{1,0:T(8,128)(2,1)}, u32[]{:S(2)}, u32[]{:S(2)}) collective-permute-start(bf16[256,1024]{1,0:T(8,128)(2,1)} %get-tuple-element.122), channel_id=1, source_target_pairs={{0,8},{8,0},{16,24},{24,16},{1,9},{9,1},{17,25},{25,17},{2,10},{10... | collective-permute-start | bytes 1572872 | tf_op jit(solution)/shard_map/ppermute | solution.py:496
  18.5 71.7 %collective-permute-start.8 = (bf16[256,1024]{1,0:T(8,128)(2,1)}, bf16[256,1024]{1,0:T(8,128)(2,1)}, u32[]{:S(2)}, u32[]{:S(2)}) collective-permute-start(bf16[256,1024]{1,0:T(8,128)(2,1)} %get-tuple-element.124), channel_id=1, source_target_pairs={{0,16},{8,24},{16,0},{24,8},{1,17},{9,25},{17,1},{25,9},{2,18},{10... | collective-permute-start | bytes 1572872 | tf_op jit(solution)/shard_map/ppermute | solution.py:496
  18.8 72.9 %collective-permute-start.10 = (bf16[256,1024]{1,0:T(8,128)(2,1)}, bf16[256,1024]{1,0:T(8,128)(2,1)}, u32[]{:S(2)}, u32[]{:S(2)}) collective-permute-start(bf16[256,1024]{1,0:T(8,128)(2,1)} %get-tuple-element.120), channel_id=1, source_target_pairs={{0,24},{8,16},{16,8},{24,0},{1,25},{9,17},{17,9},{25,1},{2,26},{10... | collective-permute-start | bytes 1572872 | tf_op jit(solution)/shard_map/ppermute | solution.py:496
  165.8 98.6 %collective-permute-start.19 = (bf16[128,5632]{1,0:T(8,128)(2,1)}, bf16[128,5632]{1,0:T(8,128)(2,1)}, u32[]{:S(2)}, u32[]{:S(2)}) collective-permute-start(bf16[128,5632]{1,0:T(8,128)(2,1)} %collective-permute-done.17), channel_id=1, source_target_pairs={{0,8},{8,16},{16,24},{24,28},{28,20},{20,12},{12,4},{4,0},{1,9},{9... | collective-permute-start | bytes 4325384 | tf_op jit(solution)/shard_map/ppermute | solution.py:548
  173.2 96.0 %collective-permute-start.20 = (bf16[128,5632]{1,0:T(8,128)(2,1)}, bf16[128,5632]{1,0:T(8,128)(2,1)}, u32[]{:S(2)}, u32[]{:S(2)}) collective-permute-start(bf16[128,5632]{1,0:T(8,128)(2,1)} %collective-permute-done.18), channel_id=1, source_target_pairs={{8,0},{16,8},{24,16},{28,24},{20,28},{12,20},{4,12},{0,4},{9,1},{1... | collective-permute-start | bytes 4325384 | tf_op jit(solution)/shard_map/ppermute | solution.py:550
  244.9 85.4 %all-to-all-start = ((bf16[8,256,512]{2,1,0:T(8,128)(2,1)}), bf16[8,256,512]{2,1,0:T(8,128)(2,1)S(1)}, u32[]{:S(2)}, u32[]{:S(2)}) async-start(bf16[8,256,512]{2,1,0:T(8,128)(2,1)} %bitcast.38), calls=%async_computation | async-start | bytes 4194304 | tf_op jit(solution)/shard_map/all_to_all | solution.py:695
  261.8 884.3 %reduce-scatter.8.cloned.1.call-start = ((), (), s32[]{:S(2)}) async-start(), calls=%async_computation.9 | async-start | bytes 6488064 | tf_op jit(solution)/shard_map/reduce_scatter | solution.py:772
  269.0 166.8 %collective-permute-start.25 = (bf16[640,1024]{1,0:T(8,128)(2,1)}, bf16[640,1024]{1,0:T(8,128)(2,1)}, u32[]{:S(2)}, u32[]{:S(2)}) collective-permute-start(bf16[640,1024]{1,0:T(8,128)(2,1)} %convolution_convert_fusion.12), channel_id=1, source_target_pairs={{0,1},{1,0},{2,3},{3,2},{4,5},{5,4},{6,7},{7,6},{8,9},{9,8},{10,11... | collective-permute-start | bytes 3932168 | tf_op jit(solution)/shard_map/ppermute | solution.py:496
  269.0 198.5 %collective-permute-start.28 = (bf16[640,1024]{1,0:T(8,128)(2,1)}, bf16[640,1024]{1,0:T(8,128)(2,1)}, u32[]{:S(2)}, u32[]{:S(2)}) collective-permute-start(bf16[640,1024]{1,0:T(8,128)(2,1)} %convolution_convert_fusion.11), channel_id=1, source_target_pairs={{0,2},{1,3},{2,0},{3,1},{4,6},{5,7},{6,4},{7,5},{8,10},{9,11},{10,... | collective-permute-start | bytes 3932168 | tf_op jit(solution)/shard_map/ppermute | solution.py:496
  269.2 59.9 %collective-permute-start.22 = (bf16[128,5632]{1,0:T(8,128)(2,1)}, bf16[128,5632]{1,0:T(8,128)(2,1)S(1)}, u32[]{:S(2)}, u32[]{:S(2)}) collective-permute-start(bf16[128,5632]{1,0:T(8,128)(2,1)} %collective-permute-done.20), channel_id=1, source_target_pairs={{8,0},{16,8},{24,16},{28,24},{20,28},{12,20},{4,12},{0,4},{9,1},{1... | collective-permute-start | bytes 4325384 | tf_op jit(solution)/shard_map/ppermute | solution.py:550
  355.0 143.9 %collective-permute-start.31 = (bf16[640,1024]{1,0:T(8,128)(2,1)}, bf16[640,1024]{1,0:T(8,128)(2,1)}, u32[]{:S(2)}, u32[]{:S(2)}) collective-permute-start(bf16[640,1024]{1,0:T(8,128)(2,1)} %convolution_convert_fusion.10), channel_id=1, source_target_pairs={{0,3},{1,2},{2,1},{3,0},{4,7},{5,6},{6,5},{7,4},{8,11},{9,10},{10,... | collective-permute-start | bytes 3932168 | tf_op jit(solution)/shard_map/ppermute | solution.py:496
  555.3 593.2 %reduce-scatter.6.cloned.1.call-start = ((), (), s32[]{:S(2)}) async-start(), calls=%async_computation.8 | async-start | bytes 6488064 | tf_op jit(solution)/shard_map/reduce_scatter | solution.py:772
  579.6 571.2 %reduce-scatter.4.cloned.1.call-start = ((), (), s32[]{:S(2)}) async-start(), calls=%async_computation.7 | async-start | bytes 6488064 | tf_op jit(solution)/shard_map/reduce_scatter | solution.py:772
  582.1 59.1 %collective-permute-start.29 = (bf16[656,1024]{1,0:T(8,128)(2,1)}, bf16[656,1024]{1,0:T(8,128)(2,1)}, u32[]{:S(2)}, u32[]{:S(2)}) collective-permute-start(bf16[656,1024]{1,0:T(8,128)(2,1)} %copy-done.25), channel_id=1, source_target_pairs={{0,2},{1,3},{2,0},{3,1},{4,6},{5,7},{6,4},{7,5},{8,10},{9,11},{10,... | collective-permute-start | bytes 4030472 | tf_op jit(solution)/shard_map/ppermute | solution.py:496
  585.3 56.7 %collective-permute-start.26 = (bf16[656,1024]{1,0:T(8,128)(2,1)S(1)}, bf16[656,1024]{1,0:T(8,128)(2,1)}, u32[]{:S(2)}, u32[]{:S(2)}) collective-permute-start(bf16[656,1024]{1,0:T(8,128)(2,1)S(1)} %copy-done.24), channel_id=1, source_target_pairs={{0,1},{1,0},{2,3},{3,2},{4,5},{5,4},{6,7},{7,6},{8,9},{9,8},{10,11... | collective-permute-start | bytes 4030472 | tf_op jit(solution)/shard_map/ppermute | solution.py:496
  712.7 78.3 %all-to-all-start.1 = ((bf16[8,256,512]{2,1,0:T(8,128)(2,1)}), bf16[8,256,512]{2,1,0:T(8,128)(2,1)S(1)}, u32[]{:S(2)}, u32[]{:S(2)}) async-start(bf16[8,256,512]{2,1,0:T(8,128)(2,1)} %bitcast.365), calls=%async_computation.1 | async-start | bytes 4194304 | tf_op jit(solution)/shard_map/all_to_all | solution.py:695
  721.1 63.2 %collective-permute-start.51 = (bf16[2,32,1024]{2,1,0:T(8,128)(2,1)S(1)}, bf16[2,32,1024]{2,1,0:T(8,128)(2,1)S(1)}, u32[]{:S(2)}, u32[]{:S(2)}) collective-permute-start(bf16[2,32,1024]{2,1,0:T(8,128)(2,1)S(1)} %select_bitcast_fusion.20), channel_id=1, source_target_pairs={{0,16},{8,24},{16,0},{24,8},{1,17},{9,25},{17,1},{25,9},{2,18},{10... | collective-permute-start | bytes 393224 | tf_op jit(solution)/shard_map/ppermute | solution.py:496
  948.5 128.9 %collective-permute-start.43 = (bf16[2,2,2,2,32,1536]{5,4,0,3,1,2:T(8,128)(2,1)}, bf16[2,2,2,2,32,1536]{5,4,0,3,1,2:T(8,128)(2,1)}, u32[]{:S(2)}, u32[]{:S(2)}) collective-permute-start(bf16[2,2,2,2,32,1536]{5,4,0,3,1,2:T(8,128)(2,1)} %select_bitcast_fusion.2), channel_id=1, source_target_pairs={{0,1},{1,0},{2,3},{3,2},{4,5},{5,4},{6,7},{7,6},{8,9},{9,8},{10,11... | collective-permute-start | bytes 4718600 | tf_op jit(solution)/shard_map/ppermute | solution.py:496
  1009.2 124.6 %collective-permute-start.33 = (bf16[640,1024]{1,0:T(8,128)(2,1)}, bf16[640,1024]{1,0:T(8,128)(2,1)}, u32[]{:S(2)}, u32[]{:S(2)}) collective-permute-start(bf16[640,1024]{1,0:T(8,128)(2,1)} %get-tuple-element.106), channel_id=1, source_target_pairs={{0,1},{1,0},{2,3},{3,2},{4,5},{5,4},{6,7},{7,6},{8,9},{9,8},{10,11... | collective-permute-start | bytes 3932168 | tf_op jit(solution)/shard_map/ppermute | solution.py:496
  1009.2 124.6 %collective-permute-start.34 = (bf16[640,1024]{1,0:T(8,128)(2,1)}, bf16[640,1024]{1,0:T(8,128)(2,1)}, u32[]{:S(2)}, u32[]{:S(2)}) collective-permute-start(bf16[640,1024]{1,0:T(8,128)(2,1)} %get-tuple-element.105), channel_id=1, source_target_pairs={{0,2},{1,3},{2,0},{3,1},{4,6},{5,7},{6,4},{7,5},{8,10},{9,11},{10,... | collective-permute-start | bytes 3932168 | tf_op jit(solution)/shard_map/ppermute | solution.py:496
  1035.5 98.4 %collective-permute-start.35 = (bf16[640,1024]{1,0:T(8,128)(2,1)}, bf16[640,1024]{1,0:T(8,128)(2,1)}, u32[]{:S(2)}, u32[]{:S(2)}) collective-permute-start(bf16[640,1024]{1,0:T(8,128)(2,1)} %get-tuple-element.104), channel_id=1, source_target_pairs={{0,3},{1,2},{2,1},{3,0},{4,7},{5,6},{6,5},{7,4},{8,11},{9,10},{10,... | collective-permute-start | bytes 3932168 | tf_op jit(solution)/shard_map/ppermute | solution.py:496
  (137 other events, 4407.8 us)
Sparse Core Ops, SparseCore 0:
  128.8 124.3 all-gather.1
  555.4 113.7 reduce-scatter.7
  672.8 146.0 reduce-scatter.5
  822.4 109.7 reduce-scatter.3

commit v3 on v2

--- a/solution.py
+++ b/solution.py
@@ -377,16 +377,19 @@
 EXTRA = 16
 
 
-def expert_kernel(own_ref, x_ref, dy_ref, gate_ref, wg_ref, wu_ref, wd_ref, *refs):
-    h_ref, dg_ref, du_ref, dx_ref, part_ref, acc_ref = refs[-6:]
+def expert_kernel(own_ref, x_ref, dy_ref, wg_ref, wu_ref, wd_ref, *refs):
+    h_ref, dg_ref, du_ref, dx_ref, part_ref, acc_ref, gate_ref = refs[-7:]
     step = pl.program_id(0)
-    rows = gate_ref.shape[0]
+    rows = dy_ref.shape[0]
     chunk = rows // 2 if rows % 32 == 0 else rows
 
     @pl.when(step == 0)
     def _():
         acc_ref[...] = jnp.zeros_like(acc_ref)
         part_ref[...] = jnp.zeros_like(part_ref)
+        lines = x_ref[rows:, :rows].astype(jnp.float32)
+        gate = jnp.sum(lines, axis=0, keepdims=True)
+        gate_ref[...] = jnp.broadcast_to(gate, (LANES, rows)).T
 
     wg, wu, wd = wg_ref[...], wu_ref[...], wd_ref[...]
     for start in range(0, rows, chunk):
@@ -405,7 +408,7 @@
         for column in range(LANES, product.shape[1], LANES):
             total = total + product[:, column : column + LANES]
         part_ref[at, :] += total
-        dh = raw * gate_ref[at, :]
+        dh = raw * gate_ref[at, :1]
         du = (dh * gelu).astype(jnp.bfloat16)
         dg = (dh * u * slope).astype(jnp.bfloat16)
         h_ref[at, :] = h.astype(jnp.bfloat16)
@@ -427,8 +430,8 @@
         dx_ref[rows:, :rows] = lines.astype(dx_ref.dtype)
 
 
-def expert_block(at, count, x, dy, gate, wgu, wd, earlier):
-    rows, width = gate.shape[0], x.shape[1]
+def expert_block(at, count, x, dy, wgu, wd, earlier):
+    rows, width = dy.shape
     hidden = wd.shape[0]
     tile = FF_TILE
     whole = jax.ShapeDtypeStruct((count * rows, hidden), jnp.bfloat16)
@@ -438,9 +441,8 @@
         num_scalar_prefetch=1,
         grid=(hidden // tile,),
         in_specs=[
+            pl.BlockSpec((rows + EXTRA, width), fixed),
             pl.BlockSpec((rows, width), fixed),
-            pl.BlockSpec((rows, width), fixed),
-            pl.BlockSpec((rows, 1), fixed),
             pl.BlockSpec((width, tile), lambda i, *_: (0, i)),
             pl.BlockSpec((width, tile), lambda i, *_: (0, hidden // tile + i)),
             pl.BlockSpec((tile, width), lambda i, *_: (i, 0)),
@@ -452,7 +454,11 @@
             out_block,
             pl.BlockSpec((rows + EXTRA, width), fixed),
         ],
-        scratch_shapes=[pltpu.VMEM((rows, LANES), jnp.float32), pltpu.VMEM((rows, width), jnp.float32)],
+        scratch_shapes=[
+            pltpu.VMEM((rows, LANES), jnp.float32),
+            pltpu.VMEM((rows, width), jnp.float32),
+            pltpu.VMEM((rows, LANES), jnp.float32),
+        ],
     )
     return pl.pallas_call(
         expert_kernel,
@@ -464,12 +470,12 @@
             jax.ShapeDtypeStruct((rows + EXTRA, width), jnp.bfloat16),
         ),
         grid_spec=spec,
-        input_output_aliases={7 + i: i for i in range(len(earlier))},
+        input_output_aliases={6 + i: i for i in range(len(earlier))},
         compiler_params=pltpu.CompilerParams(dimension_semantics=("arbitrary",), vmem_limit_bytes=40 << 20),
         cost_estimate=pl.CostEstimate(
             flops=10 * rows * width * hidden, bytes_accessed=6 * width * hidden + 6 * rows * hidden, transcendentals=0
         ),
-    )(jnp.zeros((1,), jnp.int32), x, dy, gate, wgu, wgu, wd, *earlier)
+    )(jnp.zeros((1,), jnp.int32), x, dy, wgu, wgu, wd, *earlier)
 
 
 EPS = 1e-06
@@ -536,22 +542,44 @@
     return lax.dynamic_index_in_dim(values, index, 0, keepdims=False)
 
 
-def ring_gather(piece, groups, split, own):
-    order, place, ahead = ring_of(groups, split)
-    count = groups * split
-    here = pick(place, own)
-    rows = piece.shape[0]
-    whole = jnp.zeros((count * rows, piece.shape[1]), piece.dtype)
-    whole = lax.dynamic_update_slice_in_dim(whole, piece, own * rows, 0)
-    forward = backward = piece
-    for k in range(1, count // 2 + 1):
-        forward = lax.ppermute(forward, SEQ, ahead)
-        if k < count - count // 2:
-            backward = lax.ppermute(backward, SEQ, [(b, a) for a, b in ahead])
-        whole = lax.dynamic_update_slice_in_dim(whole, forward, pick(order, (here - k + count) % count) * rows, 0)
-        if k < count - count // 2:
-            whole = lax.dynamic_update_slice_in_dim(whole, backward, pick(order, (here + k) % count) * rows, 0)
-    return whole
+class RingGather:
+    def __init__(self, piece, groups, split, own):
+        self.order, place, self.ahead = ring_of(groups, split)
+        self.count = groups * split
+        self.here = pick(place, own)
+        self.rows = piece.shape[0]
+        self.whole = jnp.zeros((self.count * self.rows, piece.shape[1]), piece.dtype)
+        self.whole = lax.dynamic_update_slice_in_dim(self.whole, piece, own * self.rows, 0)
+        self.forward = self.backward = piece
+        self.round = 0
+        self.waiting = []
+
+    def step(self):
+        self.settle()
+        self.round += 1
+        k = self.round
+        self.forward = lax.ppermute(self.forward, SEQ, self.ahead)
+        self.waiting.append((self.forward, -k))
+        if k < self.count - self.count // 2:
+            self.backward = lax.ppermute(self.backward, SEQ, [(b, a) for a, b in self.ahead])
+            self.waiting.append((self.backward, k))
+
+    def settle(self):
+        for piece, k in self.waiting:
+            at = pick(self.order, (self.here + k + self.count) % self.count) * self.rows
+            self.whole = lax.dynamic_update_slice_in_dim(self.whole, piece, at, 0)
+        self.waiting = []
+
+    def after(self, value):
+        value, self.forward, self.backward = lax.optimization_barrier((value, self.forward, self.backward))
+        self.waiting = [(self.forward if k < 0 else self.backward, k) for _, k in self.waiting]
+        return value
+
+    def finish(self):
+        while self.round < self.count // 2:
+            self.step()
+        self.settle()
+        return self.whole
 
 
 def norm_scale(value):
@@ -615,11 +643,6 @@
             arrived[rz][rx] = partner(arrived[rz][0], "x", rx)
     sequence = jnp.stack([block for line in arrived for block in line]).reshape(length, width)
 
-    gate_up_own = jnp.concatenate([w_gate[0].astype(LOW), w_up[0].astype(LOW)], axis=1)
-    sequence, gate_up_own, down_own = lax.optimization_barrier((sequence, gate_up_own, w_down[0].astype(LOW)))
-    gate_up_w = ring_gather(gate_up_own, groups, split, s_at)
-    down_w = lax.all_gather(down_own, SEQ, axis=0, tiled=True)
-
     small = jnp.concatenate(
         [
             gain_attention[:, None],
@@ -634,27 +657,25 @@
         [part.astype(LOW).reshape(rows_own, split, head_width) for part in (w_query, w_key, w_value)], axis=2
     )
     share = share.reshape(rows_own, split, 3 * head_width).transpose(1, 0, 2)
-    share = jnp.concatenate([share, jnp.broadcast_to(small, (split,) + small.shape)], axis=2)
+    common = jnp.concatenate([w_out.astype(LOW), small], axis=1)
+    share = jnp.concatenate([share, jnp.broadcast_to(common, (split,) + common.shape)], axis=2)
     shares = [lax.dynamic_index_in_dim(share, x_at ^ r, 0, keepdims=False) for r in range(split)]
     shares = [shares[0]] + [partner(shares[r], "x", r) for r in range(1, split)]
     by_x = reorder(jnp.stack(shares), x_at)
     steps = [("z", b) for b in z_bits] + [("exp", b) for b in e_bits]
     packed = gather_double(by_x, steps)
-    ne, nz = len(e_bits), len(z_bits)
+    ne, nz, nx = len(e_bits), len(z_bits), len(x_bits)
     packed = packed.transpose(
         tuple(ne + i for i in reversed(range(nz))) + (ne + nz,) + tuple(reversed(range(ne))) + (ne + nz + 1, ne + nz + 2)
-    ).reshape(width, 3 * head_width + LANES)
-    qkv_w, small_all = packed[:, : 3 * head_width], packed[:, 3 * head_width :]
-    out_steps = [("z", b) for b in z_bits] + [("x", b) for b in x_bits] + [("exp", b) for b in e_bits]
-    out_w = gather_double(w_out.astype(LOW), out_steps)
-    nx = len(x_bits)
-    out_w = out_w.transpose(
-        tuple(ne + nx + i for i in reversed(range(nz)))
-        + tuple(ne + i for i in reversed(range(nx)))
-        + tuple(reversed(range(ne)))
-        + (ne + nx + nz, ne + nx + nz + 1)
-    )
-    out_w = out_w.reshape(hd, width)
+    ).reshape(width, 3 * head_width + width + LANES)
+    sequence, packed = lax.optimization_barrier((sequence, packed))
+    qkv_w, small_all = packed[:, : 3 * head_width], packed[:, 3 * head_width + width :]
+    out_w = packed[:, 3 * head_width : 3 * head_width + width]
+    gate_up_own = jnp.concatenate([w_gate[0].astype(LOW), w_up[0].astype(LOW)], axis=1)
+    sequence, gate_up_own, down_own = lax.optimization_barrier((sequence, gate_up_own, w_down[0].astype(LOW)))
+    gate_up_ring = RingGather(gate_up_own, groups, split, s_at)
+    gate_up_ring.step()
+    down_w = lax.all_gather(down_own, SEQ, axis=0, tiled=True)
 
     gain_one = small_all[:, 0].astype(jnp.float32)
     gain_two = small_all[:, 1].astype(jnp.float32)
@@ -690,6 +711,9 @@
     rows = bias_rows(table_rows, tile)
     ends = jnp.stack([table_rows[:, 15], table_rows[:, 31]], axis=1).astype(jnp.float32)
     contexts, log_totals = attend_forward(qkv, query_side, key_side, ranges, rows, ends, own, tile)
+    contexts = gate_up_ring.after(contexts)
+    contexts, grad_slots = lax.optimization_barrier((contexts, grad_slots))
+    gate_up_w = gate_up_ring.finish()
 
     def exchange_positions(blocks):
         return lax.all_to_all(blocks, SEQ, split_axis=0, concat_axis=0, tiled=True)
@@ -725,24 +749,25 @@
         sent[r] = jnp.concatenate([dot_tn(tables[r], normed_two).astype(LOW), gate_lines[r]], axis=0)
         if r:
             sent[r] = partner(sent[r], "exp", r)
-    sent_gate = [values_below(rows_) for rows_ in sent]
 
     earlier = ()
     back = [None] * exp_count
-    for r in range(exp_count):
+    turns = [0] + list(range(2, exp_count)) + [1]
+    for turn, r in enumerate(turns):
+        if turn >= 3:
+            ready = turns[turn - 2]
+            sent[r], back[ready] = lax.optimization_barrier((sent[r], back[ready]))
         hidden, gate_low, up_low, dx = expert_block(
-            r, exp_count, sent[r], grad_slots[r], sent_gate[r][:, None], gate_up_w, down_w, earlier
+            r, exp_count, sent[r], grad_slots[r], gate_up_w, down_w, earlier
         )
         earlier = (hidden, gate_low, up_low)
         back[r] = partner(dx, "exp", r) if r else dx
 
+    sent, hidden = lax.optimization_barrier((sent, hidden))
     slot_rows = jnp.concatenate([rows_[:capacity] for rows_ in sent], axis=0)
-    slot_gates = jnp.concatenate(sent_gate, axis=0)[:, None]
+    slot_gates = jnp.concatenate([values_below(rows_) for rows_ in sent], axis=0)[:, None]
     slot_grads = (slot_gates * jnp.concatenate(grad_slots, axis=0).astype(jnp.float32)).astype(LOW)
-    expert_out = (slot_gates * dot32(hidden, down_w)).astype(LOW)
     down_sum = dot_tn(hidden, slot_grads).astype(LOW)
-    gate_sum = dot_tn(slot_rows, gate_low).astype(LOW)
-    up_sum = dot_tn(slot_rows, up_low).astype(LOW)
 
     gate_grad = jnp.sum(
         table.astype(jnp.float32).reshape(tokens, exp_count, capacity) * jnp.stack([values_below(rows_) for rows_ in back])[None], axis=2
@@ -761,6 +786,12 @@
     mid_grad = grad_out + norm_back(scale_two, unit_two, gain_two, normed_two_grad)
     attention_grad = mid_grad.astype(LOW)
     context_grad = dot_nt(attention_grad, out_w).astype(LOW)
+    context_grad, gate_low, up_low, hidden, down_sum = lax.optimization_barrier(
+        (context_grad, gate_low, up_low, hidden, down_sum)
+    )
+    gate_sum = dot_tn(slot_rows, gate_low).astype(LOW)
+    up_sum = dot_tn(slot_rows, up_low).astype(LOW)
+    expert_out = (slot_gates * dot32(hidden, down_w)).astype(LOW)
     context_grad = (
         context_grad.reshape(groups, local_len, split, head_width)
         .transpose(0, 2, 1, 3)
@@ -774,63 +805,65 @@
     down_owned = scatter_experts(down_sum)
     gate_owned = scatter_experts(gate_sum)
     up_owned = scatter_experts(up_sum)
-    context_heads, _, _, _, expert_out = lax.optimization_barrier(
-        (context_heads, down_sum[:8], gate_sum[:8], up_sum[:8], expert_out)
+    context_heads, _, _, expert_out = lax.optimization_barrier(
+        (context_heads, gate_sum[:8], up_sum[:8], expert_out)
     )
 
     returned = [expert_out[:capacity]] + [
         partner(expert_out[r * capacity : (r + 1) * capacity], "exp", r) for r in range(1, exp_count)
     ]
-    block_out = (mid + dot32(table, jnp.concatenate(returned, axis=0))).astype(LOW)
-
-    block_out = block_out.reshape(groups, local_len, width)
-
-    def by_step(total, with_x):
+    def by_step(total):
         columns = total.shape[1]
-        shaped = total.astype(LOW).reshape((2,) * (nz + nx + ne) + (rows_own, columns))
+        shaped = total.reshape((2,) * (nz + nx + ne) + (rows_own, columns))
         z_dims = tuple(reversed(range(nz)))
-        x_dims = tuple(nz + i for i in reversed(range(nx)))
+        x_dims = tuple(nz + i for i in range(nx))
         e_dims = tuple(nz + nx + i for i in reversed(range(ne)))
-        rest = (nz + nx + ne, nz + nx + ne + 1)
-        if with_x:
-            return shaped.transpose(e_dims + z_dims + x_dims + rest)
-        return shaped.transpose(e_dims + z_dims + tuple(reversed(x_dims)) + rest)
+        return shaped.transpose(e_dims + z_dims + x_dims + (nz + nx + ne, nz + nx + ne + 1))
 
     halving = [("exp", b) for b in reversed(e_bits)] + [("z", b) for b in reversed(z_bits)]
-    x_halving = [("x", b) for b in reversed(x_bits)]
-    out_w_sum = dot_tn(context_local, attention_grad)
-    out_w_out = scatter_halve(by_step(out_w_sum, True), halving + x_halving).astype(jnp.float32)
 
     query_back, key_back, value_back, diag, far = attend_backward(
         qkv, context_heads, contexts, log_totals, query_side, key_side, ranges, rows, ends, own, tile
     )
+    query_back, key_back, value_back, returned = lax.optimization_barrier(
+        (query_back, key_back, value_back, returned)
+    )
     table_local = bucket_sums(diag, far, tile)
 
     def through(grads, part):
         return dot_nt(grads, qkv_w[:, part * head_width : (part + 1) * head_width])
 
-    normed_part = through(query_back, 0) + through(key_back, 1) + through(value_back, 2)
-    normed_part = normed_part.reshape(groups, split, local_len, width)
-    pieces_back = [None] * groups
-    for rz in list(reversed(range(1, groups))) + [0]:
-        total = normed_part[rz, 0]
-        for rx in range(1, split):
-            total = total + partner(normed_part[rz, rx].astype(LOW), "x", rx).astype(jnp.float32)
-        pieces_back[rz] = partner(total.astype(LOW), "z", rz).astype(jnp.float32) if rz else total
-    normed_one_grad = reorder(jnp.stack(pieces_back), z_at).reshape(tokens, width)
+    normed_part = (through(query_back, 0) + through(key_back, 1) + through(value_back, 2)).astype(LOW)
+    normed_part = reorder(normed_part.reshape(seq_count, local_len, width), s_at)
+    normed_part, query_back, key_back, value_back = lax.optimization_barrier(
+        (normed_part, query_back, key_back, value_back)
+    )
+    normed_part = exchange_positions(normed_part)
+    weight_sum = jnp.concatenate(
+        [dot_tn(normed_one, grads).astype(LOW) for grads in (query_back, key_back, value_back)]
+        + [dot_tn(context_local, attention_grad).astype(LOW)],
+        axis=1,
+    )
+    weight_part = scatter_halve(by_step(weight_sum), halving).reshape(split, rows_own, 3 * head_width + width)
+    weight_own = [lax.dynamic_index_in_dim(weight_part, x_at ^ r, 0, keepdims=False) for r in range(split)]
+    weight_own = [weight_own[0]] + [partner(weight_own[r], "x", r) for r in range(1, split)]
+    out_w_out = sum(part[:, 3 * head_width :].astype(jnp.float32) for part in weight_own)
+    qkv_own = reorder(jnp.stack([part[:, : 3 * head_width] for part in weight_own]), x_at)
+    qkv_own = qkv_own.reshape(split, rows_own, 3, head_width)
+    qkv_own = qkv_own.transpose(2, 1, 0, 3).reshape(3, rows_own, hd).astype(jnp.float32)
+    block_out = (mid + dot32(table, jnp.concatenate(returned, axis=0))).astype(LOW)
+
+    block_out = block_out.reshape(groups, local_len, width)
+
+    normed_one_grad = jnp.sum(
+        normed_part.reshape(groups, split, local_len, width).astype(jnp.float32), axis=1
+    ).reshape(tokens, width)
     scale_one = norm_scale(inputs)
     unit_one = inputs * scale_one
     gain_one_sum = jnp.sum(normed_one_grad * unit_one, axis=0)
-    block_in_grad = (mid_grad + norm_back(scale_one, unit_one, gain_one, normed_one_grad)).reshape(groups, local_len, width)
-
-    qkv_sum = jnp.concatenate(
-        [dot_tn(normed_one, grads).astype(LOW) for grads in (query_back, key_back, value_back)], axis=1
-    )
-    qkv_part = scatter_halve(by_step(qkv_sum, False), halving).reshape(split, rows_own, 3 * head_width)
-    qkv_own = [lax.dynamic_index_in_dim(qkv_part, x_at ^ r, 0, keepdims=False) for r in range(split)]
-    qkv_own = [qkv_own[0]] + [partner(qkv_own[r], "x", r) for r in range(1, split)]
-    qkv_own = reorder(jnp.stack(qkv_own), x_at).reshape(split, rows_own, 3, head_width)
-    qkv_own = qkv_own.transpose(2, 1, 0, 3).reshape(3, rows_own, hd).astype(jnp.float32)
+    block_in_grad = (mid_grad + norm_back(scale_one, unit_one, gain_one, normed_one_grad)).reshape(
+        groups, local_len, width
+    )
 
     table_sum = lax.dynamic_update_slice_in_dim(
         jnp.zeros(table_all.shape, jnp.float32), table_local, x_at * heads_here, 0

time: 1170 us -> 1190 us (1.017)
  starting transfers between devices: 157 us -> 125 us
  waiting for transfers between devices: 343 us -> 364 us
  other arithmetic: 68.7 us -> 85.3 us
    ppermute x46 -> x29, starting transfers between devices: 106 us -> 69.5 us  [partner(): return lax.ppermute(value, axis, [(i, i ^ offset) for i in range(count)])]
    all_to_all x2 -> x3, waiting for transfers between devices: 0.01 us -> 33.8 us  [exchange_positions(): return lax.all_to_all(blocks, SEQ, split_axis=0, concat_axis=0, tiled=True)]
    ppermute x46 -> x29, waiting for transfers between devices: 268 us -> 243 us  [partner(): return lax.ppermute(value, axis, [(i, i ^ offset) for i in range(count)])]
    ppermute x7, starting transfers between devices: 20.3 us -> 38.5 us  [the longest x4 36.6 us: step(): self.forward = lax.ppermute(self.forward, SEQ, self.ahead)]
    ppermute x7, waiting for transfers between devices: 69.9 us -> 85.4 us  [the longest x4 85.4 us: step(): self.forward = lax.ppermute(self.forward, SEQ, self.ahead)]
    unnamed x220 -> x175, local copies, waits for them, and re-layouts: 33 us -> 30.2 us
  transfers between devices with their start and end apart: 60 -> 44, of which waited for: 27 -> 13; matrix products, arithmetic and copies ran while one was open for 25% -> 27% of each run, Pallas kernels for 23% -> 25%
where the time goes in v3:
time: 1190 us
  waiting for transfers between devices  364 us (31%)
  Pallas kernels  294 us (25%)
  matrix products  196 us (16%)
  starting transfers between devices  125 us (11%)
  local copies, waits for them, and re-layouts  98.4 us (8%)
  other arithmetic  85.3 us (7%)
  between operations  25 us (2%)
    ppermute x29, waiting for transfers between devices, partner(): return lax.ppermute(value, axis, [(i, i ^ offset) for i in range(count)])  243 us
    pallas_call x4, Pallas kernels, expert_block(): pl.pallas_call(expert_kernel, name='expert_block', out_shape=(whole, whol...  123 us
    pallas_call x1, Pallas kernels, attend_backward(): pl.pallas_call(bwd_kernel, name='attend_backward', out_shape=(low, low, l...  114 us
    dot_general x16, matrix products, dot_tn(): lax.dot_general(a, b, (((0,), (0,)), ((), ())), preferred_element_type=jn...  101 us
    ppermute x4, waiting for transfers between devices, step(): self.forward = lax.ppermute(self.forward, SEQ, self.ahead)  85.4 us
    ppermute x29, starting transfers between devices, partner(): return lax.ppermute(value, axis, [(i, i ^ offset) for i in range(count)])  69.5 us
    dot_general x9, matrix products, dot32(): return jnp.dot(a, b, preferred_element_type=jnp.float32)  64.6 us
    pallas_call x1, Pallas kernels, attend_forward(): pl.pallas_call(fwd_kernel, name='attend_forward', out_shape=(jax.ShapeDty...  56.8 us
  transfers between devices with their start and end apart: 44, of which 13 were waited for; matrix products, arithmetic and copies ran while one was open for 27% of the time, Pallas kernels for 25%

profile of v3, /device:TPU:0, one launch (start us, length us, event | category | flops | bytes accessed | tf_op | source)
XLA Modules:
  0.0 1188.3 jit_solution(16080587658773774559)
XLA Ops:
  44.7 39.6 %collective-permute-done.8 = bf16[2,32,2688]{2,1,0:T(8,128)(2,1)S(1)} collective-permute-done((bf16[2,32,2688]{2,1,0:T(8,128)(2,1)S(1)}, bf16[2,32,2688]{2,1,0:T(8,128)(2,1)S(1)}, u32[]{:S(2)}, u32[]{:S(2)}) %collective-permute-start.8) | collective-permute-done | bytes 344096 | tf_op jit(solution)/shard_map/ppermute | solution.py:502
  86.6 14.3 %collective-permute-done.9 = bf16[2,2,32,2688]{3,2,1,0:T(8,128)(2,1)S(1)} collective-permute-done((bf16[2,2,32,2688]{3,2,1,0:T(8,128)(2,1)}, bf16[2,2,32,2688]{3,2,1,0:T(8,128)(2,1)S(1)}, u32[]{:S(2)}, u32[]{:S(2)}) %collective-permute-start.9) | collective-permute-done | bytes 688160 | tf_op jit(solution)/shard_map/ppermute | solution.py:502
  104.3 26.3 %collective-permute-done.10 = bf16[2,2,2,32,2688]{4,3,2,1,0:T(8,128)(2,1)S(1)} collective-permute-done((bf16[2,2,2,32,2688]{4,3,2,1,0:T(8,128)(2,1)S(1)}, bf16[2,2,2,32,2688]{4,3,2,1,0:T(8,128)(2,1)S(1)}, u32[]{:S(2)}, u32[]{:S(2)}) %collective-permute-start.10) | collective-permute-done | bytes 1376288 | tf_op jit(solution)/shard_map/ppermute | solution.py:502
  196.3 56.8 %attend_forward.1 = (bf16[2048,512]{1,0:T(8,128)(2,1)}, f32[4,2,2048]{2,1,0:T(2,128)S(1)}) custom-call(s32[2,8]{1,0:T(2,128)S(1)} %pad_add_fusion.ranges, f32[8,2]{1,0:T(8,128)S(1)} %maximum_convert_fusion.1.ends, s32[1]{0:T(128)} %bitcast.31.own, bf16[2048,1536]{1,0:T(8,128)(2,1)} %convolution_convert_fusion.q_ref.k_ref.v_ref, ...), custom_call_target="tpu_custom_call" | custom-call | flops 8589934592 | bytes 8388608 | tf_op jit(solution)/shard_map/attend_forward/pallas_call | solution.py:168
  253.2 13.5 %collective-permute-start.17 = (bf16[128,5632]{1,0:T(8,128)(2,1)}, bf16[128,5632]{1,0:T(8,128)(2,1)}, u32[]{:S(2)}, u32[]{:S(2)}) collective-permute-start(bf16[128,5632]{1,0:T(8,128)(2,1)} %collective-permute-done.12), channel_id=1, source_target_pairs={{0,8},{8,16},{16,24},{24,28},{28,20},{20,12},{12,4},{4,0},{1,9},{9... | collective-permute-start | bytes 4325384 | tf_op jit(solution)/shard_map/ppermute | solution.py:561
  282.9 35.9 %collective-permute-done.17 = bf16[128,5632]{1,0:T(8,128)(2,1)} collective-permute-done((bf16[128,5632]{1,0:T(8,128)(2,1)}, bf16[128,5632]{1,0:T(8,128)(2,1)}, u32[]{:S(2)}, u32[]{:S(2)}) %collective-permute-start.17) | collective-permute-done | bytes 1441824 | tf_op jit(solution)/shard_map/ppermute | solution.py:561
  337.5 49.5 %collective-permute-done.19 = bf16[128,5632]{1,0:T(8,128)(2,1)} collective-permute-done((bf16[128,5632]{1,0:T(8,128)(2,1)}, bf16[128,5632]{1,0:T(8,128)(2,1)}, u32[]{:S(2)}, u32[]{:S(2)}) %collective-permute-start.19) | collective-permute-done | bytes 1441824 | tf_op jit(solution)/shard_map/ppermute | solution.py:561
  387.0 11.5 collective-permute-start.21
  438.5 30.6 %expert_block.4 = (bf16[2560,2816]{1,0:T(8,128)(2,1)}, bf16[2560,2816]{1,0:T(8,128)(2,1)}, bf16[2560,2816]{1,0:T(8,128)(2,1)}, bf16[656,1024]{1,0:T(8,128)(2,1)S(1)}) custom-call(s32[1]{0:T(128)} %constant.245.clone.1.own_ref, bf16[656,1024]{1,0:T(8,128)(2,1)S(1)} %copy-done.3, bf16[640,1024]{1,0:T(8,128)(2,1)S(1)} %copy-done.18, ...), custom_call_target="tpu_custom_call" | custom-call | flops 18454937600 | bytes 28114944 | tf_op jit(solution)/shard_map/expert_block/pallas_call | solution.py:463
  469.1 30.8 %expert_block.5 = (bf16[2560,2816]{1,0:T(8,128)(2,1)}, bf16[2560,2816]{1,0:T(8,128)(2,1)}, bf16[2560,2816]{1,0:T(8,128)(2,1)}, bf16[656,1024]{1,0:T(8,128)(2,1)S(1)}) custom-call(s32[1]{0:T(128)} %constant.245.clone.1.own_ref, bf16[656,1024]{1,0:T(8,128)(2,1)S(1)} %collective-permute-done.23.x_ref, ...), custom_call_target="tpu_custom_call", output_to_operand_aliasing={{0}: (6, {}), {1}: (7, {}), {2}: (8, {})} | custom-call | flops 18454937600 | bytes 28114944 | tf_op jit(solution)/shard_map/expert_block/pallas_call | solution.py:463
  500.2 31.3 %expert_block.6 = (bf16[2560,2816]{1,0:T(8,128)(2,1)}, bf16[2560,2816]{1,0:T(8,128)(2,1)}, bf16[2560,2816]{1,0:T(8,128)(2,1)}, bf16[656,1024]{1,0:T(8,128)(2,1)S(1)}) custom-call(s32[1]{0:T(128)} %constant.245.clone.1.own_ref, bf16[656,1024]{1,0:T(8,128)(2,1)} %collective-permute-done.25.x_ref, ...), custom_call_target="tpu_custom_call", output_to_operand_aliasing={{0}: (6, {}), {1}: (7, {}), {2}: (8, {})} | custom-call | flops 18454937600 | bytes 28114944 | tf_op jit(solution)/shard_map/expert_block/pallas_call | solution.py:463
  532.6 30.7 %expert_block.7 = (bf16[2560,2816]{1,0:T(8,128)(2,1)}, bf16[2560,2816]{1,0:T(8,128)(2,1)}, bf16[2560,2816]{1,0:T(8,128)(2,1)}, bf16[656,1024]{1,0:T(8,128)(2,1)}) custom-call(s32[1]{0:T(128)} %constant.245.clone.1.own_ref, bf16[656,1024]{1,0:T(8,128)(2,1)S(1)} %collective-permute-done.22.x_ref, ...), custom_call_target="tpu_custom_call", output_to_operand_aliasing={{0}: (6, {}), {1}: (7, {}), {2}: (8, {})} | custom-call | flops 18454937600 | bytes 28114944 | tf_op jit(solution)/shard_map/expert_block/pallas_call | solution.py:463
  573.5 21.5 %convolution_convert_fusion.3 = bf16[2816,1024]{1,0:T(8,128)(2,1)} fusion(bf16[2560,2816]{1,0:T(8,128)(2,1)} %get-tuple-element.122, bf16[640,1024]{1,0:T(8,128)(2,1)} %collective-permute-done.16.dy_ref, bf16[640,1024]{1,0:T(8,128)(2,1)S(1)} %copy-done.7, bf16[640,1024]{1,0:T(8,128)(2,1)S(1)} %copy-done.5, bf16[640,1024]{1,0:T(8,128)(2,1)S(1)} %copy-done.19, ...), kind=kOutput, calls=%fused_computation.23 | convolution fusion | flops 14793048064 | bytes 25438208 | tf_op jit(solution)/shard_map/dot_general | solution.py:497
  638.4 22.8 %convolution_convert_fusion.1 = bf16[1024,2816]{1,0:T(8,128)(2,1)} fusion(bf16[2560,2816]{1,0:T(8,128)(2,1)} %get-tuple-element.143, bf16[640,1024]{1,0:T(8,128)(2,1)} %slice.288, bf16[640,1024]{1,0:T(8,128)(2,1)} %slice.287, bf16[640,1024]{1,0:T(8,128)(2,1)} %slice.286, bf16[640,1024]{1,0:T(8,128)(2,1)} %slice.285), kind=kOutput, calls=%fused_computation.21 | convolution fusion | flops 14787805184 | bytes 25427968 | tf_op jit(solution)/shard_map/dot_general | solution.py:497
  667.9 21.1 %multiply_convert_fusion = bf16[2560,1024]{1,0:T(8,128)(2,1)} fusion(bf16[2560,2816]{1,0:T(8,128)(2,1)} %get-tuple-element.122, bf16[2816,1024]{1,0:T(8,128)(2,1)} %all-gather.2.cloned.1.call-done.wd_ref, f32[2560]{0:T(1024)S(1)} %pad_maximum_fusion.19), kind=kOutput, calls=%fused_computation.7 | convolution fusion | flops 14769192960 | bytes 25438208 | tf_op jit(solution)/shard_map/dot_general | solution.py:489
  689.0 33.8 %all-to-all-done.1 = bf16[8,256,512]{2,1,0:T(8,128)(2,1)S(1)} async-done(((bf16[8,256,512]{2,1,0:T(8,128)(2,1)}), bf16[8,256,512]{2,1,0:T(8,128)(2,1)S(1)}, u32[]{:S(2)}, u32[]{:S(2)}) %all-to-all-start.1) | async-done | bytes 2097184 | tf_op jit(solution)/shard_map/all_to_all | solution.py:719
  729.1 113.6 %attend_backward.1 = (bf16[2048,512]{1,0:T(8,128)(2,1)S(1)}, bf16[2048,512]{1,0:T(8,128)(2,1)S(1)}, bf16[2048,512]{1,0:T(8,128)(2,1)S(1)}, f32[8,3,512]{2,1,0:T(4,128)S(1)}, f32[8,2,256]{2,1,0:T(2,128)S(1)}) custom-call(s32[2,8]{1,0:T(2,128)S(1)} %copy-done.17, f32[8,2]{1,0:T(8,128)S(1)} %copy-done.15, s32[1]{0:T(128)} %bitcast.31.own, ...), custom_call_target="tpu_custom_call" | custom-call | flops 21474836480 | bytes 16777216 | tf_op jit(solution)/shard_map/attend_backward/pallas_call | solution.py:346
  877.9 13.1 %pad_maximum_fusion = bf16[1024,2560]{0,1:T(8,128)(2,1)} fusion(bf16[1024,1024]{0,1:T(8,128)(2,1)S(1)} %copy-done.35, bf16[1024,512]{0,1:T(8,128)(2,1)S(1)} %convolution_convert_fusion.14, bf16[1024,512]{0,1:T(8,128)(2,1)S(1)} %convolution_convert_fusion.15, bf16[1024,512]{0,1:T(8,128)(2,1)S(1)} %convolution_convert_fusion.16), kind=kLoop, calls=%fused_computation.42 | loop fusion | flops 20971520 | bytes 10485760 | tf_op jit(solution)/shard_map/concatenate | solution.py:842
  901.9 32.9 %collective-permute-start.31 = (bf16[2,2,2,2,32,2560]{5,4,0,3,1,2:T(8,128)(2,1)S(1)}, bf16[2,2,2,2,32,2560]{5,4,0,3,1,2:T(8,128)(2,1)}, u32[]{:S(2)}, u32[]{:S(2)}) collective-permute-start(bf16[2,2,2,2,32,2560]{5,4,0,3,1,2:T(8,128)(2,1)S(1)} %select_bitcast_fusion.2), channel_id=1, source_target_pairs={{0,1},{1,0},{2,3},{3,2},{4,5},{5,4},{6,7},{7,6},{8,9},{9,8},{10,11... | collective-permute-start | bytes 7864328 | tf_op jit(solution)/shard_map/ppermute | solution.py:502
  934.8 21.1 %convolution_convert_fusion.2 = bf16[1024,2816]{1,0:T(8,128)(2,1)} fusion(bf16[2560,2816]{1,0:T(8,128)(2,1)} %get-tuple-element.142, bf16[640,1024]{1,0:T(8,128)(2,1)S(1)} %copy-done.44, bf16[640,1024]{1,0:T(8,128)(2,1)S(1)} %copy-done.43, bf16[640,1024]{1,0:T(8,128)(2,1)S(1)} %copy-done.42, bf16[640,1024]{1,0:T(8,128)(2,1)S(1)} %copy-done.41), kind=kOutput, calls=%fused_computation.22 | convolution fusion | flops 14787805184 | bytes 25427968 | tf_op jit(solution)/shard_map/dot_general | solution.py:497
  963.7 28.6 %collective-permute-done.32 = bf16[2,2,2,32,2560]{4,3,2,0,1:T(8,128)(2,1)S(1)} collective-permute-done((bf16[2,2,2,32,2560]{4,3,2,0,1:T(8,128)(2,1)S(1)}, bf16[2,2,2,32,2560]{4,3,2,0,1:T(8,128)(2,1)S(1)}, u32[]{:S(2)}, u32[]{:S(2)}) %collective-permute-start.32) | collective-permute-done | bytes 1310752 | tf_op jit(solution)/shard_map/ppermute | solution.py:502
  1004.0 21.5 %collective-permute-done.33 = bf16[2,2,32,2560]{3,2,1,0:T(8,128)(2,1)} collective-permute-done((bf16[2,2,32,2560]{3,2,1,0:T(8,128)(2,1)}, bf16[2,2,32,2560]{3,2,1,0:T(8,128)(2,1)}, u32[]{:S(2)}, u32[]{:S(2)}) %collective-permute-start.33) | collective-permute-done | bytes 655392 | tf_op jit(solution)/shard_map/ppermute | solution.py:502
  1026.9 11.8 collective-permute-start.34
  1048.2 95.4 %collective-permute-done.34 = bf16[2,32,2560]{2,1,0:T(8,128)(2,1)S(1)} collective-permute-done((bf16[2,32,2560]{2,1,0:T(8,128)(2,1)S(1)}, bf16[2,32,2560]{2,1,0:T(8,128)(2,1)S(1)}, u32[]{:S(2)}, u32[]{:S(2)}) %collective-permute-start.34) | collective-permute-done | bytes 327712 | tf_op jit(solution)/shard_map/ppermute | solution.py:502
  (457 shorter events, 355.2 us)
Async XLA Ops:
  7.2 426.0 %all-gather.2.cloned.1.call-start = ((), (), s32[]{:S(2)}) async-start(), calls=%async_computation.7 | async-start | bytes 6488064 | tf_op jit(solution)/shard_map/all_gather | solution.py:678
  19.7 131.4 %collective-permute-start = (bf16[256,1024]{1,0:T(8,128)(2,1)}, bf16[256,1024]{1,0:T(8,128)(2,1)}, u32[]{:S(2)}, u32[]{:S(2)}) collective-permute-start(bf16[256,1024]{1,0:T(8,128)(2,1)} %get-tuple-element.176), channel_id=1, source_target_pairs={{0,4},{4,0},{1,5},{5,1},{2,6},{6,2},{3,7},{7,3},{8,12},{12,8},{9,1... | collective-permute-start | bytes 1572872 | tf_op jit(solution)/shard_map/ppermute | solution.py:502
  19.7 118.8 %collective-permute-start.1 = (bf16[256,1024]{1,0:T(8,128)(2,1)}, bf16[256,1024]{1,0:T(8,128)(2,1)}, u32[]{:S(2)}, u32[]{:S(2)}) collective-permute-start(bf16[256,1024]{1,0:T(8,128)(2,1)} %get-tuple-element.175), channel_id=1, source_target_pairs={{0,8},{8,0},{16,24},{24,16},{1,9},{9,1},{17,25},{25,17},{2,10},{10... | collective-permute-start | bytes 1572872 | tf_op jit(solution)/shard_map/ppermute | solution.py:502
  21.8 128.7 %collective-permute-start.3 = (bf16[256,1024]{1,0:T(8,128)(2,1)}, bf16[256,1024]{1,0:T(8,128)(2,1)}, u32[]{:S(2)}, u32[]{:S(2)}) collective-permute-start(bf16[256,1024]{1,0:T(8,128)(2,1)} %get-tuple-element.177), channel_id=1, source_target_pairs={{0,16},{8,24},{16,0},{24,8},{1,17},{9,25},{17,1},{25,9},{2,18},{10... | collective-permute-start | bytes 1572872 | tf_op jit(solution)/shard_map/ppermute | solution.py:502
  24.4 130.4 %collective-permute-start.5 = (bf16[256,1024]{1,0:T(8,128)(2,1)}, bf16[256,1024]{1,0:T(8,128)(2,1)}, u32[]{:S(2)}, u32[]{:S(2)}) collective-permute-start(bf16[256,1024]{1,0:T(8,128)(2,1)} %get-tuple-element.173), channel_id=1, source_target_pairs={{0,24},{8,16},{16,8},{24,0},{1,25},{9,17},{17,9},{25,1},{2,26},{10... | collective-permute-start | bytes 1572872 | tf_op jit(solution)/shard_map/ppermute | solution.py:502
  181.1 72.0 %collective-permute-start.12 = (bf16[128,5632]{1,0:T(8,128)(2,1)}, bf16[128,5632]{1,0:T(8,128)(2,1)}, u32[]{:S(2)}, u32[]{:S(2)}) collective-permute-start(bf16[128,5632]{1,0:T(8,128)(2,1)} %pad_maximum_fusion.3), channel_id=1, source_target_pairs={{0,8},{8,16},{16,24},{24,28},{28,20},{20,12},{12,4},{4,0},{1,9},{9... | collective-permute-start | bytes 4325384 | tf_op jit(solution)/shard_map/ppermute | solution.py:561
  181.7 71.4 %collective-permute-start.13 = (bf16[128,5632]{1,0:T(8,128)(2,1)}, bf16[128,5632]{1,0:T(8,128)(2,1)}, u32[]{:S(2)}, u32[]{:S(2)}) collective-permute-start(bf16[128,5632]{1,0:T(8,128)(2,1)} %pad_maximum_fusion.3), channel_id=1, source_target_pairs={{8,0},{16,8},{24,16},{28,24},{20,28},{12,20},{4,12},{0,4},{9,1},{1... | collective-permute-start | bytes 4325384 | tf_op jit(solution)/shard_map/ppermute | solution.py:564
  193.2 82.6 %collective-permute-start.14 = (bf16[640,1024]{1,0:T(8,128)(2,1)}, bf16[640,1024]{1,0:T(8,128)(2,1)S(1)}, u32[]{:S(2)}, u32[]{:S(2)}) collective-permute-start(bf16[640,1024]{1,0:T(8,128)(2,1)} %convolution_convert_fusion.12), channel_id=1, source_target_pairs={{0,1},{1,0},{2,3},{3,2},{4,5},{5,4},{6,7},{7,6},{8,9},{9,8},{10,11... | collective-permute-start | bytes 3932168 | tf_op jit(solution)/shard_map/ppermute | solution.py:502
  193.3 82.6 %collective-permute-start.15 = (bf16[640,1024]{1,0:T(8,128)(2,1)}, bf16[640,1024]{1,0:T(8,128)(2,1)S(1)}, u32[]{:S(2)}, u32[]{:S(2)}) collective-permute-start(bf16[640,1024]{1,0:T(8,128)(2,1)} %convolution_convert_fusion.11), channel_id=1, source_target_pairs={{0,2},{1,3},{2,0},{3,1},{4,6},{5,7},{6,4},{7,5},{8,10},{9,11},{10,... | collective-permute-start | bytes 3932168 | tf_op jit(solution)/shard_map/ppermute | solution.py:502
  194.8 81.1 %collective-permute-start.16 = (bf16[640,1024]{1,0:T(8,128)(2,1)}, bf16[640,1024]{1,0:T(8,128)(2,1)}, u32[]{:S(2)}, u32[]{:S(2)}) collective-permute-start(bf16[640,1024]{1,0:T(8,128)(2,1)} %convolution_convert_fusion.10), channel_id=1, source_target_pairs={{0,3},{1,2},{2,1},{3,0},{4,7},{5,6},{6,5},{7,4},{8,11},{9,10},{10,... | collective-permute-start | bytes 3932168 | tf_op jit(solution)/shard_map/ppermute | solution.py:502
  275.9 126.5 %all-to-all-start = ((bf16[8,256,512]{2,1,0:T(8,128)(2,1)}), bf16[8,256,512]{2,1,0:T(8,128)(2,1)}, u32[]{:S(2)}, u32[]{:S(2)}) async-start(bf16[8,256,512]{2,1,0:T(8,128)(2,1)} %bitcast.38), calls=%async_computation | async-start | bytes 4194304 | tf_op jit(solution)/shard_map/all_to_all | solution.py:719
  280.2 873.1 %reduce-scatter.8.cloned.1.call-start = ((), (), s32[]{:S(2)}) async-start(), calls=%async_computation.10 | async-start | bytes 6488064 | tf_op jit(solution)/shard_map/reduce_scatter | solution.py:803
  318.8 68.2 %collective-permute-start.19 = (bf16[128,5632]{1,0:T(8,128)(2,1)}, bf16[128,5632]{1,0:T(8,128)(2,1)}, u32[]{:S(2)}, u32[]{:S(2)}) collective-permute-start(bf16[128,5632]{1,0:T(8,128)(2,1)} %collective-permute-done.17), channel_id=1, source_target_pairs={{0,8},{8,16},{16,24},{24,28},{28,20},{20,12},{12,4},{4,0},{1,9},{9... | collective-permute-start | bytes 4325384 | tf_op jit(solution)/shard_map/ppermute | solution.py:561
  332.3 68.8 %collective-permute-start.20 = (bf16[128,5632]{1,0:T(8,128)(2,1)}, bf16[128,5632]{1,0:T(8,128)(2,1)S(1)}, u32[]{:S(2)}, u32[]{:S(2)}) collective-permute-start(bf16[128,5632]{1,0:T(8,128)(2,1)} %collective-permute-done.18), channel_id=1, source_target_pairs={{8,0},{16,8},{24,16},{28,24},{20,28},{12,20},{4,12},{0,4},{9,1},{1... | collective-permute-start | bytes 4325384 | tf_op jit(solution)/shard_map/ppermute | solution.py:564
  423.0 109.5 %collective-permute-start.22 = (bf16[656,1024]{1,0:T(8,128)(2,1)}, bf16[656,1024]{1,0:T(8,128)(2,1)S(1)}, u32[]{:S(2)}, u32[]{:S(2)}) collective-permute-start(bf16[656,1024]{1,0:T(8,128)(2,1)} %pad_maximum_fusion.6), channel_id=1, source_target_pairs={{0,1},{1,0},{2,3},{3,2},{4,5},{5,4},{6,7},{7,6},{8,9},{9,8},{10,11... | collective-permute-start | bytes 4030472 | tf_op jit(solution)/shard_map/ppermute | solution.py:502
  426.6 73.6 %collective-permute-start.25 = (bf16[656,1024]{1,0:T(8,128)(2,1)}, bf16[656,1024]{1,0:T(8,128)(2,1)}, u32[]{:S(2)}, u32[]{:S(2)}) collective-permute-start(bf16[656,1024]{1,0:T(8,128)(2,1)} %pad_maximum_fusion.8), channel_id=1, source_target_pairs={{0,3},{1,2},{2,1},{3,0},{4,7},{5,6},{6,5},{7,4},{8,11},{9,10},{10,... | collective-permute-start | bytes 4030472 | tf_op jit(solution)/shard_map/ppermute | solution.py:502
  633.2 89.6 %all-to-all-start.1 = ((bf16[8,256,512]{2,1,0:T(8,128)(2,1)}), bf16[8,256,512]{2,1,0:T(8,128)(2,1)S(1)}, u32[]{:S(2)}, u32[]{:S(2)}) async-start(bf16[8,256,512]{2,1,0:T(8,128)(2,1)} %bitcast.273), calls=%async_computation.1 | async-start | bytes 4194304 | tf_op jit(solution)/shard_map/all_to_all | solution.py:719
  638.4 517.3 %reduce-scatter.6.cloned.1.call-start = ((), (), s32[]{:S(2)}) async-start(), calls=%async_computation.9 | async-start | bytes 6488064 | tf_op jit(solution)/shard_map/reduce_scatter | solution.py:803
  667.9 490.1 %reduce-scatter.4.cloned.1.call-start = ((), (), s32[]{:S(2)}) async-start(), calls=%async_computation.8 | async-start | bytes 6488064 | tf_op jit(solution)/shard_map/reduce_scatter | solution.py:803
  727.2 115.5 %collective-permute-start.28 = (bf16[640,1024]{1,0:T(8,128)(2,1)S(1)}, bf16[640,1024]{1,0:T(8,128)(2,1)S(1)}, u32[]{:S(2)}, u32[]{:S(2)}) collective-permute-start(bf16[640,1024]{1,0:T(8,128)(2,1)S(1)} %get-tuple-element.169), channel_id=1, source_target_pairs={{0,1},{1,0},{2,3},{3,2},{4,5},{5,4},{6,7},{7,6},{8,9},{9,8},{10,11... | collective-permute-start | bytes 3932168 | tf_op jit(solution)/shard_map/ppermute | solution.py:502
  727.3 115.4 %collective-permute-start.29 = (bf16[640,1024]{1,0:T(8,128)(2,1)S(1)}, bf16[640,1024]{1,0:T(8,128)(2,1)}, u32[]{:S(2)}, u32[]{:S(2)}) collective-permute-start(bf16[640,1024]{1,0:T(8,128)(2,1)S(1)} %get-tuple-element.168), channel_id=1, source_target_pairs={{0,2},{1,3},{2,0},{3,1},{4,6},{5,7},{6,4},{7,5},{8,10},{9,11},{10,... | collective-permute-start | bytes 3932168 | tf_op jit(solution)/shard_map/ppermute | solution.py:502
  728.7 114.0 %collective-permute-start.30 = (bf16[640,1024]{1,0:T(8,128)(2,1)S(1)}, bf16[640,1024]{1,0:T(8,128)(2,1)}, u32[]{:S(2)}, u32[]{:S(2)}) collective-permute-start(bf16[640,1024]{1,0:T(8,128)(2,1)S(1)} %get-tuple-element.167), channel_id=1, source_target_pairs={{0,3},{1,2},{2,1},{3,0},{4,7},{5,6},{6,5},{7,4},{8,11},{9,10},{10,... | collective-permute-start | bytes 3932168 | tf_op jit(solution)/shard_map/ppermute | solution.py:502
  999.2 161.1 %all-to-all-start.2 = ((bf16[8,256,1024]{2,1,0:T(8,128)(2,1)}), bf16[8,256,1024]{2,1,0:T(8,128)(2,1)}, u32[]{:S(2)}, u32[]{:S(2)}) async-start(bf16[8,256,1024]{2,1,0:T(8,128)(2,1)} %dynamic-slice_dynamic-update-slice_fusion), calls=%async_computation.2 | async-start | bytes 8388608 | tf_op jit(solution)/shard_map/all_to_all | solution.py:719
  1026.9 116.7 %collective-permute-start.34 = (bf16[2,32,2560]{2,1,0:T(8,128)(2,1)S(1)}, bf16[2,32,2560]{2,1,0:T(8,128)(2,1)S(1)}, u32[]{:S(2)}, u32[]{:S(2)}) collective-permute-start(bf16[2,32,2560]{2,1,0:T(8,128)(2,1)S(1)} %select_bitcast_fusion.10), channel_id=1, source_target_pairs={{0,16},{8,24},{16,0},{24,8},{1,17},{9,25},{17,1},{25,9},{2,18},{10... | collective-permute-start | bytes 983048 | tf_op jit(solution)/shard_map/ppermute | solution.py:502
  (95 other events, 3418.1 us)
Sparse Core Ops, SparseCore 0:
  195.3 128.5 all-gather.1
  620.9 150.5 reduce-scatter.7
  775.2 109.6 reduce-scatter.5
  956.1 181.6 reduce-scatter.3

commit v4 on v3

--- a/solution.py
+++ b/solution.py
@@ -520,10 +520,15 @@
 
 
 def scatter_halve(value, steps):
-    for axis, bit in steps:
+    gone = []
+    for axis, bit, dim in steps:
+        at = dim - sum(1 for d in gone if d < dim)
+        gone.append(dim)
         high = (lax.axis_index(axis) & bit) != 0
-        keep = jnp.where(high, value[1], value[0])
-        give = jnp.where(high, value[0], value[1])
+        low_half = lax.index_in_dim(value, 0, at, keepdims=False)
+        high_half = lax.index_in_dim(value, 1, at, keepdims=False)
+        keep = jnp.where(high, high_half, low_half)
+        give = jnp.where(high, low_half, high_half)
         value = (keep.astype(jnp.float32) + partner(give, axis, bit).astype(jnp.float32)).astype(LOW)
     return value
 
@@ -638,11 +643,6 @@
     arrived = [[None] * split for _ in range(groups)]
     for rz in reversed(range(groups)):
         arrived[rz][0] = partner(input_r[rz], "z", rz) if rz else input_r[0]
-    for rz in [0] + list(reversed(range(1, groups))):
-        for rx in range(1, split):
-            arrived[rz][rx] = partner(arrived[rz][0], "x", rx)
-    sequence = jnp.stack([block for line in arrived for block in line]).reshape(length, width)
-
     small = jnp.concatenate(
         [
             gain_attention[:, None],
@@ -662,8 +662,19 @@
     shares = [lax.dynamic_index_in_dim(share, x_at ^ r, 0, keepdims=False) for r in range(split)]
     shares = [shares[0]] + [partner(shares[r], "x", r) for r in range(1, split)]
     by_x = reorder(jnp.stack(shares), x_at)
-    steps = [("z", b) for b in z_bits] + [("exp", b) for b in e_bits]
-    packed = gather_double(by_x, steps)
+    for rx in range(1, split):
+        arrived[0][rx] = partner(arrived[0][0], "x", rx)
+    packed = gather_double(by_x, [("z", b) for b in z_bits])
+    near = [arrived[rz][0] for rz in range(1, groups)]
+    packed, near = lax.optimization_barrier((packed, near))
+    for rz in range(1, groups):
+        arrived[rz][0] = near[rz - 1]
+        for rx in range(1, split):
+            arrived[rz][rx] = partner(arrived[rz][0], "x", rx)
+    packed = gather_double(packed, [("exp", b) for b in e_bits[:-1]])
+    packed, arrived = lax.optimization_barrier((packed, arrived))
+    sequence = jnp.stack([block for line in arrived for block in line]).reshape(length, width)
+    packed = gather_double(packed, [("exp", b) for b in e_bits[-1:]])
     ne, nz, nx = len(e_bits), len(z_bits), len(x_bits)
     packed = packed.transpose(
         tuple(ne + i for i in reversed(range(nz))) + (ne + nz,) + tuple(reversed(range(ne))) + (ne + nz + 1, ne + nz + 2)
@@ -672,10 +683,10 @@
     qkv_w, small_all = packed[:, : 3 * head_width], packed[:, 3 * head_width + width :]
     out_w = packed[:, 3 * head_width : 3 * head_width + width]
     gate_up_own = jnp.concatenate([w_gate[0].astype(LOW), w_up[0].astype(LOW)], axis=1)
-    sequence, gate_up_own, down_own = lax.optimization_barrier((sequence, gate_up_own, w_down[0].astype(LOW)))
+    sequence, gate_up_own = lax.optimization_barrier((sequence, gate_up_own))
     gate_up_ring = RingGather(gate_up_own, groups, split, s_at)
     gate_up_ring.step()
-    down_w = lax.all_gather(down_own, SEQ, axis=0, tiled=True)
+    down_w = lax.all_gather(w_down[0].astype(LOW), SEQ, axis=0, tiled=True)
 
     gain_one = small_all[:, 0].astype(jnp.float32)
     gain_two = small_all[:, 1].astype(jnp.float32)
@@ -767,7 +778,7 @@
     slot_rows = jnp.concatenate([rows_[:capacity] for rows_ in sent], axis=0)
     slot_gates = jnp.concatenate([values_below(rows_) for rows_ in sent], axis=0)[:, None]
     slot_grads = (slot_gates * jnp.concatenate(grad_slots, axis=0).astype(jnp.float32)).astype(LOW)
-    down_sum = dot_tn(hidden, slot_grads).astype(LOW)
+    gate_sum = dot_tn(slot_rows, gate_low).astype(LOW)
 
     gate_grad = jnp.sum(
         table.astype(jnp.float32).reshape(tokens, exp_count, capacity) * jnp.stack([values_below(rows_) for rows_ in back])[None], axis=2
@@ -786,12 +797,9 @@
     mid_grad = grad_out + norm_back(scale_two, unit_two, gain_two, normed_two_grad)
     attention_grad = mid_grad.astype(LOW)
     context_grad = dot_nt(attention_grad, out_w).astype(LOW)
-    context_grad, gate_low, up_low, hidden, down_sum = lax.optimization_barrier(
-        (context_grad, gate_low, up_low, hidden, down_sum)
-    )
-    gate_sum = dot_tn(slot_rows, gate_low).astype(LOW)
+    context_grad, up_low, hidden, gate_sum = lax.optimization_barrier((context_grad, up_low, hidden, gate_sum))
+    down_sum = dot_tn(hidden, slot_grads).astype(LOW)
     up_sum = dot_tn(slot_rows, up_low).astype(LOW)
-    expert_out = (slot_gates * dot32(hidden, down_w)).astype(LOW)
     context_grad = (
         context_grad.reshape(groups, local_len, split, head_width)
         .transpose(0, 2, 1, 3)
@@ -800,64 +808,65 @@
     context_heads = exchange_positions(context_grad).reshape(length, head_width)
 
     def scatter_experts(total):
-        return lax.psum_scatter(total, SEQ, scatter_dimension=0, tiled=True).astype(jnp.float32)[None]
+        return lax.psum_scatter(total, SEQ, scatter_dimension=0, tiled=True)
 
     down_owned = scatter_experts(down_sum)
     gate_owned = scatter_experts(gate_sum)
     up_owned = scatter_experts(up_sum)
-    context_heads, _, _, expert_out = lax.optimization_barrier(
-        (context_heads, gate_sum[:8], up_sum[:8], expert_out)
-    )
-
+    context_heads, down_sum, up_sum = lax.optimization_barrier((context_heads, down_sum, up_sum))
+
+    halving = [("exp", b, 1 + nz + nx + ne - 1 - i) for i, b in enumerate(reversed(e_bits))]
+    halving += [("z", b, 1 + nz - 1 - i) for i, b in enumerate(reversed(z_bits))]
+    out_sum = dot_tn(context_local, attention_grad).astype(LOW)
+
+    query_back, key_back, value_back, diag, far = attend_backward(
+        qkv, context_heads, contexts, log_totals, query_side, key_side, ranges, rows, ends, own, tile
+    )
+    table_local = bucket_sums(diag, far, tile)
+
+    def through(grads, part):
+        return dot_nt(grads, qkv_w[:, part * head_width : (part + 1) * head_width])
+
+    out_parts = width // head_width
+    weight_sum = jnp.stack(
+        [dot_tn(normed_one, grads).astype(LOW) for grads in (query_back, key_back, value_back)]
+        + [out_sum[:, i * head_width : (i + 1) * head_width] for i in range(out_parts)]
+    )
+    weight_sum, query_back, key_back, value_back = lax.optimization_barrier(
+        (weight_sum, query_back, key_back, value_back)
+    )
+    normed_part = (through(query_back, 0) + through(key_back, 1) + through(value_back, 2)).astype(LOW)
+    normed_part = reorder(normed_part.reshape(seq_count, local_len, width), s_at)
+    half = width // 2
+    normed_first = exchange_positions(normed_part[:, :, :half])
+    normed_first, hidden, normed_second = lax.optimization_barrier(
+        (normed_first, hidden, normed_part[:, :, half:])
+    )
+    normed_second = exchange_positions(normed_second)
+    weight_part = scatter_halve(
+        weight_sum.reshape((3 + out_parts,) + (2,) * (nz + nx + ne) + (rows_own, head_width)), halving
+    ).reshape(3 + out_parts, split, rows_own, head_width)
+    weight_own = [lax.dynamic_index_in_dim(weight_part, x_at ^ r, 1, keepdims=False) for r in range(split)]
+    weight_own = [weight_own[0]] + [partner(weight_own[r], "x", r) for r in range(1, split)]
+    out_w_out = sum(part[3:].astype(jnp.float32) for part in weight_own)
+    out_w_out = out_w_out.transpose(1, 0, 2).reshape(rows_own, width)
+    qkv_own = reorder(jnp.stack([part[:3] for part in weight_own]), x_at)
+    qkv_own = qkv_own.transpose(1, 2, 0, 3).reshape(3, rows_own, hd).astype(jnp.float32)
+    expert_out = (slot_gates * dot32(hidden, down_w)).astype(LOW)
     returned = [expert_out[:capacity]] + [
         partner(expert_out[r * capacity : (r + 1) * capacity], "exp", r) for r in range(1, exp_count)
     ]
-    def by_step(total):
-        columns = total.shape[1]
-        shaped = total.reshape((2,) * (nz + nx + ne) + (rows_own, columns))
-        z_dims = tuple(reversed(range(nz)))
-        x_dims = tuple(nz + i for i in range(nx))
-        e_dims = tuple(nz + nx + i for i in reversed(range(ne)))
-        return shaped.transpose(e_dims + z_dims + x_dims + (nz + nx + ne, nz + nx + ne + 1))
-
-    halving = [("exp", b) for b in reversed(e_bits)] + [("z", b) for b in reversed(z_bits)]
-
-    query_back, key_back, value_back, diag, far = attend_backward(
-        qkv, context_heads, contexts, log_totals, query_side, key_side, ranges, rows, ends, own, tile
-    )
-    query_back, key_back, value_back, returned = lax.optimization_barrier(
-        (query_back, key_back, value_back, returned)
-    )
-    table_local = bucket_sums(diag, far, tile)
-
-    def through(grads, part):
-        return dot_nt(grads, qkv_w[:, part * head_width : (part + 1) * head_width])
-
-    normed_part = (through(query_back, 0) + through(key_back, 1) + through(value_back, 2)).astype(LOW)
-    normed_part = reorder(normed_part.reshape(seq_count, local_len, width), s_at)
-    normed_part, query_back, key_back, value_back = lax.optimization_barrier(
-        (normed_part, query_back, key_back, value_back)
-    )
-    normed_part = exchange_positions(normed_part)
-    weight_sum = jnp.concatenate(
-        [dot_tn(normed_one, grads).astype(LOW) for grads in (query_back, key_back, value_back)]
-        + [dot_tn(context_local, attention_grad).astype(LOW)],
+    block_out = (mid + dot32(table, jnp.concatenate(returned, axis=0))).astype(LOW)
+
+    block_out = block_out.reshape(groups, local_len, width)
+
+    normed_one_grad = jnp.concatenate(
+        [
+            jnp.sum(part.reshape(groups, split, local_len, half).astype(jnp.float32), axis=1).reshape(tokens, half)
+            for part in (normed_first, normed_second)
+        ],
         axis=1,
     )
-    weight_part = scatter_halve(by_step(weight_sum), halving).reshape(split, rows_own, 3 * head_width + width)
-    weight_own = [lax.dynamic_index_in_dim(weight_part, x_at ^ r, 0, keepdims=False) for r in range(split)]
-    weight_own = [weight_own[0]] + [partner(weight_own[r], "x", r) for r in range(1, split)]
-    out_w_out = sum(part[:, 3 * head_width :].astype(jnp.float32) for part in weight_own)
-    qkv_own = reorder(jnp.stack([part[:, : 3 * head_width] for part in weight_own]), x_at)
-    qkv_own = qkv_own.reshape(split, rows_own, 3, head_width)
-    qkv_own = qkv_own.transpose(2, 1, 0, 3).reshape(3, rows_own, hd).astype(jnp.float32)
-    block_out = (mid + dot32(table, jnp.concatenate(returned, axis=0))).astype(LOW)
-
-    block_out = block_out.reshape(groups, local_len, width)
-
-    normed_one_grad = jnp.sum(
-        normed_part.reshape(groups, split, local_len, width).astype(jnp.float32), axis=1
-    ).reshape(tokens, width)
     scale_one = norm_scale(inputs)
     unit_one = inputs * scale_one
     gain_one_sum = jnp.sum(normed_one_grad * unit_one, axis=0)
@@ -890,9 +899,9 @@
         little[2, :bias_own],
         little[1],
         little[3:].T,
-        gate_owned,
-        up_owned,
-        down_owned,
+        gate_owned.astype(jnp.float32)[None],
+        up_owned.astype(jnp.float32)[None],
+        down_owned.astype(jnp.float32)[None],
     )
 
 

time: 1190 us -> 1180 us (level)
  local copies, waits for them, and re-layouts: 98.4 us -> 68.1 us
  waiting for transfers between devices: 364 us -> 390 us
  matrix products: 196 us -> 184 us
    all_to_all x3 -> x4, waiting for transfers between devices: 33.8 us -> 114 us  [exchange_positions(): return lax.all_to_all(blocks, SEQ, split_axis=0, concat_axis=0, tiled=True)]
    ppermute x29, waiting for transfers between devices: 243 us -> 202 us  [partner(): return lax.ppermute(value, axis, [(i, i ^ offset) for i in range(count)])]
    all_to_all x3 -> x4, starting transfers between devices: 14.3 us -> 39.2 us  [exchange_positions(): return lax.all_to_all(blocks, SEQ, split_axis=0, concat_axis=0, tiled=True)]
    ppermute x4, waiting for transfers between devices: 85.4 us -> 60.7 us  [step(): self.forward = lax.ppermute(self.forward, SEQ, self.ahead)]
    ppermute x4, starting transfers between devices: 36.6 us -> 20 us  [step(): self.forward = lax.ppermute(self.forward, SEQ, self.ahead)]
    ppermute x29, starting transfers between devices: 69.5 us -> 53.7 us  [partner(): return lax.ppermute(value, axis, [(i, i ^ offset) for i in range(count)])]
    concatenate x1 -> x0, other arithmetic: 13.1 us -> none  [per_device(): jnp.concatenate([dot_tn(normed_one, grads).astype(LOW) for grads in (quer...]
    unnamed x175 -> x199, local copies, waits for them, and re-layouts: 30.2 us -> 17.2 us
  transfers between devices with their start and end apart: 44 -> 45, of which waited for: 13 -> 12; matrix products, arithmetic and copies ran while one was open for 27% -> 23% of each run, Pallas kernels for 25% -> 26%
where the time goes in v4:
time: 1180 us; the launch traced here: 1170 us
  waiting for transfers between devices  390 us (33%)
  Pallas kernels  301 us (26%)
  matrix products  184 us (16%)
  starting transfers between devices  118 us (10%)
  other arithmetic  84.8 us (7%)
  local copies, waits for them, and re-layouts  68.1 us (6%)
  between operations  25.3 us (2%)
    ppermute x29, waiting for transfers between devices, partner(): return lax.ppermute(value, axis, [(i, i ^ offset) for i in range(count)])  202 us
    pallas_call x4, Pallas kernels, expert_block(): pl.pallas_call(expert_kernel, name='expert_block', out_shape=(whole, whol...  122 us
    pallas_call x1, Pallas kernels, attend_backward(): pl.pallas_call(bwd_kernel, name='attend_backward', out_shape=(low, low, l...  121 us
    all_to_all x4, waiting for transfers between devices, exchange_positions(): return lax.all_to_all(blocks, SEQ, split_axis=0, concat_axis=0, tiled=True)  114 us
    dot_general x16, matrix products, dot_tn(): lax.dot_general(a, b, (((0,), (0,)), ((), ())), preferred_element_type=jn...  93.8 us
    dot_general x9, matrix products, dot32(): return jnp.dot(a, b, preferred_element_type=jnp.float32)  66.2 us
    ppermute x4, waiting for transfers between devices, step(): self.forward = lax.ppermute(self.forward, SEQ, self.ahead)  60.7 us
    pallas_call x1, Pallas kernels, attend_forward(): pl.pallas_call(fwd_kernel, name='attend_forward', out_shape=(jax.ShapeDty...  59.1 us
  transfers between devices with their start and end apart: 45, of which 12 were waited for; matrix products, arithmetic and copies ran while one was open for 23% of the time, Pallas kernels for 26%

profile of v4, /device:TPU:0, one launch (start us, length us, event | category | flops | bytes accessed | tf_op | source)
XLA Modules:
  0.0 1171.9 jit_solution(16776360049531304303)
XLA Ops:
  47.0 59.3 %collective-permute-done.1 = bf16[2,32,2688]{2,1,0:T(8,128)(2,1)S(1)} collective-permute-done((bf16[2,32,2688]{2,1,0:T(8,128)(2,1)S(1)}, bf16[2,32,2688]{2,1,0:T(8,128)(2,1)S(1)}, u32[]{:S(2)}, u32[]{:S(2)}) %collective-permute-start.1) | collective-permute-done | bytes 344096 | tf_op jit(solution)/shard_map/ppermute | solution.py:502
  112.6 48.3 %collective-permute-done.2 = bf16[2,2,32,2688]{3,2,1,0:T(8,128)(2,1)S(1)} collective-permute-done((bf16[2,2,32,2688]{3,2,1,0:T(8,128)(2,1)S(1)}, bf16[2,2,32,2688]{3,2,1,0:T(8,128)(2,1)S(1)}, u32[]{:S(2)}, u32[]{:S(2)}) %collective-permute-start.2) | collective-permute-done | bytes 688160 | tf_op jit(solution)/shard_map/ppermute | solution.py:502
  169.3 22.0 %collective-permute-done.6 = bf16[2,2,2,32,2688]{4,3,2,1,0:T(8,128)(2,1)} collective-permute-done((bf16[2,2,2,32,2688]{4,3,2,1,0:T(8,128)(2,1)S(1)}, bf16[2,2,2,32,2688]{4,3,2,1,0:T(8,128)(2,1)}, u32[]{:S(2)}, u32[]{:S(2)}) %collective-permute-start.6) | collective-permute-done | bytes 1376288 | tf_op jit(solution)/shard_map/ppermute | solution.py:502
  240.8 59.1 %attend_forward.1 = (bf16[2048,512]{1,0:T(8,128)(2,1)}, f32[4,2,2048]{2,1,0:T(2,128)S(1)}) custom-call(s32[2,8]{1,0:T(2,128)S(1)} %pad_add_fusion.ranges, f32[8,2]{1,0:T(8,128)S(1)} %maximum_convert_fusion.ends, s32[1]{0:T(128)} %bitcast.32.own, bf16[2048,1536]{1,0:T(8,128)(2,1)} %convolution_convert_fusion.q_ref.k_ref.v_ref, ...), custom_call_target="tpu_custom_call" | custom-call | flops 8589934592 | bytes 8388608 | tf_op jit(solution)/shard_map/attend_forward/pallas_call | solution.py:168
  324.4 16.5 %collective-permute-done.19 = bf16[128,5632]{1,0:T(8,128)(2,1)} collective-permute-done((bf16[128,5632]{1,0:T(8,128)(2,1)}, bf16[128,5632]{1,0:T(8,128)(2,1)}, u32[]{:S(2)}, u32[]{:S(2)}) %collective-permute-start.19) | collective-permute-done | bytes 1441824 | tf_op jit(solution)/shard_map/ppermute | solution.py:566
  345.9 10.6 collective-permute-done.20
  361.7 44.3 %collective-permute-done.21 = bf16[128,5632]{1,0:T(8,128)(2,1)} collective-permute-done((bf16[128,5632]{1,0:T(8,128)(2,1)}, bf16[128,5632]{1,0:T(8,128)(2,1)}, u32[]{:S(2)}, u32[]{:S(2)}) %collective-permute-start.21) | collective-permute-done | bytes 1441824 | tf_op jit(solution)/shard_map/ppermute | solution.py:566
  455.7 30.0 %expert_block.4 = (bf16[2560,2816]{1,0:T(8,128)(2,1)}, bf16[2560,2816]{1,0:T(8,128)(2,1)}, bf16[2560,2816]{1,0:T(8,128)(2,1)}, bf16[656,1024]{1,0:T(8,128)(2,1)S(1)}) custom-call(s32[1]{0:T(128)} %constant.245.clone.1.own_ref, bf16[656,1024]{1,0:T(8,128)(2,1)S(1)} %copy-done.3, bf16[640,1024]{1,0:T(8,128)(2,1)S(1)} %copy-done.21, ...), custom_call_target="tpu_custom_call" | custom-call | flops 18454937600 | bytes 28114944 | tf_op jit(solution)/shard_map/expert_block/pallas_call | solution.py:463
  486.8 29.9 %expert_block.5 = (bf16[2560,2816]{1,0:T(8,128)(2,1)}, bf16[2560,2816]{1,0:T(8,128)(2,1)}, bf16[2560,2816]{1,0:T(8,128)(2,1)}, bf16[656,1024]{1,0:T(8,128)(2,1)S(1)}) custom-call(s32[1]{0:T(128)} %constant.245.clone.1.own_ref, bf16[656,1024]{1,0:T(8,128)(2,1)S(1)} %collective-permute-done.18.x_ref, ...), custom_call_target="tpu_custom_call", output_to_operand_aliasing={{0}: (6, {}), {1}: (7, {}), {2}: (8, {})} | custom-call | flops 18454937600 | bytes 28114944 | tf_op jit(solution)/shard_map/expert_block/pallas_call | solution.py:463
  517.1 31.1 %expert_block.6 = (bf16[2560,2816]{1,0:T(8,128)(2,1)}, bf16[2560,2816]{1,0:T(8,128)(2,1)}, bf16[2560,2816]{1,0:T(8,128)(2,1)}, bf16[656,1024]{1,0:T(8,128)(2,1)S(1)}) custom-call(s32[1]{0:T(128)} %constant.245.clone.1.own_ref, bf16[656,1024]{1,0:T(8,128)(2,1)} %collective-permute-done.25.x_ref, ...), custom_call_target="tpu_custom_call", output_to_operand_aliasing={{0}: (6, {}), {1}: (7, {}), {2}: (8, {})} | custom-call | flops 18454937600 | bytes 28114944 | tf_op jit(solution)/shard_map/expert_block/pallas_call | solution.py:463
  549.6 30.9 %expert_block.7 = (bf16[2560,2816]{1,0:T(8,128)(2,1)}, bf16[2560,2816]{1,0:T(8,128)(2,1)}, bf16[2560,2816]{1,0:T(8,128)(2,1)}, bf16[656,1024]{1,0:T(8,128)(2,1)}) custom-call(s32[1]{0:T(128)} %constant.245.clone.1.own_ref, bf16[656,1024]{1,0:T(8,128)(2,1)S(1)} %collective-permute-done.17.x_ref, ...), custom_call_target="tpu_custom_call", output_to_operand_aliasing={{0}: (6, {}), {1}: (7, {}), {2}: (8, {})} | custom-call | flops 18454937600 | bytes 28114944 | tf_op jit(solution)/shard_map/expert_block/pallas_call | solution.py:463
  598.1 17.1 %convolution_convert_fusion.3 = bf16[1024,2816]{1,0:T(8,128)(2,1)} fusion(bf16[2560,2816]{1,0:T(8,128)(2,1)S(1)} %bitcast.333, bf16[640,1024]{1,0:T(8,128)(2,1)S(1)} %slice.264, bf16[640,1024]{1,0:T(8,128)(2,1)S(1)} %slice.263, bf16[640,1024]{1,0:T(8,128)(2,1)S(1)} %slice.262, bf16[640,1024]{1,0:T(8,128)(2,1)S(1)} %slice.261), kind=kOutput, calls=%fused_computation.22 | convolution fusion | flops 14787805184 | bytes 25427968 | tf_op jit(solution)/shard_map/dot_general | solution.py:497
  644.1 21.1 %convolution_convert_fusion.2 = bf16[2816,1024]{1,0:T(8,128)(2,1)} fusion(bf16[2560,2816]{1,0:T(8,128)(2,1)S(1)} %bitcast.331, bf16[640,1024]{1,0:T(8,128)(2,1)} %collective-permute-done.16.dy_ref, bf16[640,1024]{1,0:T(8,128)(2,1)S(1)} %copy-done.10, bf16[640,1024]{1,0:T(8,128)(2,1)S(1)} %copy-done.7, bf16[640,1024]{1,0:T(8,128)(2,1)S(1)} %copy-done.22, ...), kind=kOutput, calls=%fused_computation.21 | convolution fusion | flops 14793048064 | bytes 25438208 | tf_op jit(solution)/shard_map/dot_general | solution.py:497
  670.4 10.6 all-to-all-start.1
  681.0 22.6 %convolution_convert_fusion.1 = bf16[1024,2816]{1,0:T(8,128)(2,1)} fusion(bf16[2560,2816]{1,0:T(8,128)(2,1)} %get-tuple-element.141, bf16[640,1024]{1,0:T(8,128)(2,1)} %copy-done.49, bf16[640,1024]{1,0:T(8,128)(2,1)} %copy-done.48, bf16[640,1024]{1,0:T(8,128)(2,1)} %copy-done.47, bf16[640,1024]{1,0:T(8,128)(2,1)} %copy-done.46), kind=kOutput, calls=%fused_computation.20 | convolution fusion | flops 14787805184 | bytes 25427968 | tf_op jit(solution)/shard_map/dot_general | solution.py:497
  710.3 61.6 %all-to-all-done.1 = bf16[8,256,512]{2,1,0:T(8,128)(2,1)S(1)} async-done(((bf16[8,256,512]{2,1,0:T(8,128)(2,1)}), bf16[8,256,512]{2,1,0:T(8,128)(2,1)S(1)}, u32[]{:S(2)}, u32[]{:S(2)}) %all-to-all-start.1) | async-done | bytes 2097184 | tf_op jit(solution)/shard_map/all_to_all | solution.py:730
  772.0 120.5 %attend_backward.1 = (bf16[2048,512]{1,0:T(8,128)(2,1)S(1)}, bf16[2048,512]{1,0:T(8,128)(2,1)S(1)}, bf16[2048,512]{1,0:T(8,128)(2,1)S(1)}, f32[8,3,512]{2,1,0:T(4,128)S(1)}, f32[8,2,256]{2,1,0:T(2,128)S(1)}) custom-call(s32[2,8]{1,0:T(2,128)S(1)} %copy-done.20, f32[8,2]{1,0:T(8,128)S(1)} %copy-done.18, s32[1]{0:T(128)} %bitcast.32.own, ...), custom_call_target="tpu_custom_call" | custom-call | flops 21474836480 | bytes 16777216 | tf_op jit(solution)/shard_map/attend_backward/pallas_call | solution.py:346
  902.1 19.7 %collective-permute-start.31 = (bf16[5,2,2,2,2,32,512]{6,5,4,3,2,1,0:T(8,128)(2,1)}, bf16[5,2,2,2,2,32,512]{6,5,4,3,2,1,0:T(8,128)(2,1)}, u32[]{:S(2)}, u32[]{:S(2)}) collective-permute-start(bf16[5,2,2,2,2,32,512]{6,5,4,3,2,1,0:T(8,128)(2,1)} %fusion.36), channel_id=1, source_target_pairs={{0,1},{1,0},{2,3},{3,2},{4,5},{5,4},{6,7},{7,6},{8,9},{9,8},{10,11... | collective-permute-start | bytes 7864328 | tf_op jit(solution)/shard_map/ppermute | solution.py:502
  938.5 10.3 all-to-all-start.2
  964.3 52.9 %all-to-all-done.2 = bf16[8,256,512]{2,1,0:T(8,128)(2,1)} async-done(((bf16[8,256,512]{2,1,0:T(8,128)(2,1)}), bf16[8,256,512]{2,1,0:T(8,128)(2,1)}, u32[]{:S(2)}, u32[]{:S(2)}) %all-to-all-start.2) | async-done | bytes 2097184 | tf_op jit(solution)/shard_map/all_to_all | solution.py:730
  1017.2 14.0 %all-to-all-start.3 = ((bf16[8,256,512]{2,1,0:T(8,128)(2,1)}), bf16[8,256,512]{2,1,0:T(8,128)(2,1)}, u32[]{:S(2)}, u32[]{:S(2)}) async-start(bf16[8,256,512]{2,1,0:T(8,128)(2,1)} %get-tuple-element.152), calls=%async_computation.3 | async-start | bytes 4194304 | tf_op jit(solution)/shard_map/all_to_all | solution.py:730
  1036.1 19.4 %multiply_convert_fusion = bf16[2560,1024]{1,0:T(8,128)(2,1)S(1)} fusion(bf16[2560,2816]{1,0:T(8,128)(2,1)} %get-tuple-element.150, f32[2560]{0:T(1024)S(1)} %pad_maximum_fusion.19, bf16[1,2816,1024]{2,1,0:T(8,128)(2,1)} %all-gather.3.cloned.1.call-done), kind=kOutput, calls=%fused_computation.7 | convolution fusion | flops 14769192960 | bytes 25438208 | tf_op jit(solution)/shard_map/dot_general | solution.py:489
  1058.9 34.8 %collective-permute-done.33 = bf16[5,2,2,32,512]{4,3,2,1,0:T(8,128)(2,1)S(1)} collective-permute-done((bf16[5,2,2,32,512]{4,3,2,1,0:T(8,128)(2,1)S(1)}, bf16[5,2,2,32,512]{4,3,2,1,0:T(8,128)(2,1)S(1)}, u32[]{:S(2)}, u32[]{:S(2)}) %collective-permute-start.33) | collective-permute-done | bytes 655392 | tf_op jit(solution)/shard_map/ppermute | solution.py:502
  1097.9 30.7 %collective-permute-done.34 = bf16[5,2,32,512]{3,2,1,0:T(8,128)(2,1)S(1)} collective-permute-done((bf16[5,2,32,512]{3,2,1,0:T(8,128)(2,1)S(1)}, bf16[5,2,32,512]{3,2,1,0:T(8,128)(2,1)S(1)}, u32[]{:S(2)}, u32[]{:S(2)}) %collective-permute-start.34) | collective-permute-done | bytes 327712 | tf_op jit(solution)/shard_map/ppermute | solution.py:502
  (485 shorter events, 329.5 us)
Async XLA Ops:
  7.2 443.2 %all-gather.3.cloned.1.call-start = ((), (), s32[]{:S(2)}) async-start(), calls=%async_computation.11 | async-start | bytes 6488064 | tf_op jit(solution)/shard_map/all_gather | solution.py:689
  18.7 142.5 %collective-permute-start.3 = (bf16[256,1024]{1,0:T(8,128)(2,1)}, bf16[256,1024]{1,0:T(8,128)(2,1)}, u32[]{:S(2)}, u32[]{:S(2)}) collective-permute-start(bf16[256,1024]{1,0:T(8,128)(2,1)} %get-tuple-element.189), channel_id=1, source_target_pairs={{0,8},{8,0},{16,24},{24,16},{1,9},{9,1},{17,25},{25,17},{2,10},{10... | collective-permute-start | bytes 1572872 | tf_op jit(solution)/shard_map/ppermute | solution.py:502
  20.3 141.0 %collective-permute-start.4 = (bf16[256,1024]{1,0:T(8,128)(2,1)}, bf16[256,1024]{1,0:T(8,128)(2,1)}, u32[]{:S(2)}, u32[]{:S(2)}) collective-permute-start(bf16[256,1024]{1,0:T(8,128)(2,1)} %get-tuple-element.188), channel_id=1, source_target_pairs={{0,16},{8,24},{16,0},{24,8},{1,17},{9,25},{17,1},{25,9},{2,18},{10... | collective-permute-start | bytes 1572872 | tf_op jit(solution)/shard_map/ppermute | solution.py:502
  22.8 138.4 %collective-permute-start.5 = (bf16[256,1024]{1,0:T(8,128)(2,1)}, bf16[256,1024]{1,0:T(8,128)(2,1)}, u32[]{:S(2)}, u32[]{:S(2)}) collective-permute-start(bf16[256,1024]{1,0:T(8,128)(2,1)} %get-tuple-element.190), channel_id=1, source_target_pairs={{0,24},{8,16},{16,8},{24,0},{1,25},{9,17},{17,9},{25,1},{2,26},{10... | collective-permute-start | bytes 1572872 | tf_op jit(solution)/shard_map/ppermute | solution.py:502
  23.1 171.7 %collective-permute-start.7 = (bf16[256,1024]{1,0:T(8,128)(2,1)S(1)}, bf16[256,1024]{1,0:T(8,128)(2,1)}, u32[]{:S(2)}, u32[]{:S(2)}) collective-permute-start(bf16[256,1024]{1,0:T(8,128)(2,1)S(1)} %get-tuple-element.89), channel_id=1, source_target_pairs={{0,4},{4,0},{1,5},{5,1},{2,6},{6,2},{3,7},{7,3},{8,12},{12,8},{9,1... | collective-permute-start | bytes 1572872 | tf_op jit(solution)/shard_map/ppermute | solution.py:502
  41.1 65.3 %collective-permute-start.1 = (bf16[2,32,2688]{2,1,0:T(8,128)(2,1)S(1)}, bf16[2,32,2688]{2,1,0:T(8,128)(2,1)S(1)}, u32[]{:S(2)}, u32[]{:S(2)}) collective-permute-start(bf16[2,32,2688]{2,1,0:T(8,128)(2,1)S(1)} %pad_maximum_fusion.12), channel_id=1, source_target_pairs={{0,16},{8,24},{16,0},{24,8},{1,17},{9,25},{17,1},{25,9},{2,18},{10... | collective-permute-start | bytes 1032200 | tf_op jit(solution)/shard_map/ppermute | solution.py:502
  225.1 74.8 %collective-permute-start.12 = (bf16[128,5632]{1,0:T(8,128)(2,1)}, bf16[128,5632]{1,0:T(8,128)(2,1)}, u32[]{:S(2)}, u32[]{:S(2)}) collective-permute-start(bf16[128,5632]{1,0:T(8,128)(2,1)} %pad_maximum_fusion.3), channel_id=1, source_target_pairs={{0,8},{8,16},{16,24},{24,28},{28,20},{20,12},{12,4},{4,0},{1,9},{9... | collective-permute-start | bytes 4325384 | tf_op jit(solution)/shard_map/ppermute | solution.py:566
  225.1 74.8 %collective-permute-start.13 = (bf16[128,5632]{1,0:T(8,128)(2,1)}, bf16[128,5632]{1,0:T(8,128)(2,1)}, u32[]{:S(2)}, u32[]{:S(2)}) collective-permute-start(bf16[128,5632]{1,0:T(8,128)(2,1)} %pad_maximum_fusion.3), channel_id=1, source_target_pairs={{8,0},{16,8},{24,16},{28,24},{20,28},{12,20},{4,12},{0,4},{9,1},{1... | collective-permute-start | bytes 4325384 | tf_op jit(solution)/shard_map/ppermute | solution.py:569
  237.6 79.7 %collective-permute-start.14 = (bf16[640,1024]{1,0:T(8,128)(2,1)}, bf16[640,1024]{1,0:T(8,128)(2,1)S(1)}, u32[]{:S(2)}, u32[]{:S(2)}) collective-permute-start(bf16[640,1024]{1,0:T(8,128)(2,1)} %convolution_convert_fusion.12), channel_id=1, source_target_pairs={{0,1},{1,0},{2,3},{3,2},{4,5},{5,4},{6,7},{7,6},{8,9},{9,8},{10,11... | collective-permute-start | bytes 3932168 | tf_op jit(solution)/shard_map/ppermute | solution.py:502
  237.7 79.7 %collective-permute-start.15 = (bf16[640,1024]{1,0:T(8,128)(2,1)}, bf16[640,1024]{1,0:T(8,128)(2,1)S(1)}, u32[]{:S(2)}, u32[]{:S(2)}) collective-permute-start(bf16[640,1024]{1,0:T(8,128)(2,1)} %convolution_convert_fusion.11), channel_id=1, source_target_pairs={{0,2},{1,3},{2,0},{3,1},{4,6},{5,7},{6,4},{7,5},{8,10},{9,11},{10,... | collective-permute-start | bytes 3932168 | tf_op jit(solution)/shard_map/ppermute | solution.py:502
  238.1 79.3 %collective-permute-start.16 = (bf16[640,1024]{1,0:T(8,128)(2,1)}, bf16[640,1024]{1,0:T(8,128)(2,1)}, u32[]{:S(2)}, u32[]{:S(2)}) collective-permute-start(bf16[640,1024]{1,0:T(8,128)(2,1)} %convolution_convert_fusion.10), channel_id=1, source_target_pairs={{0,3},{1,2},{2,1},{3,0},{4,7},{5,6},{6,5},{7,4},{8,11},{9,10},{10,... | collective-permute-start | bytes 3932168 | tf_op jit(solution)/shard_map/ppermute | solution.py:502
  317.4 101.2 %all-to-all-start = ((bf16[8,256,512]{2,1,0:T(8,128)(2,1)}), bf16[8,256,512]{2,1,0:T(8,128)(2,1)}, u32[]{:S(2)}, u32[]{:S(2)}) async-start(bf16[8,256,512]{2,1,0:T(8,128)(2,1)} %bitcast.38), calls=%async_computation | async-start | bytes 4194304 | tf_op jit(solution)/shard_map/all_to_all | solution.py:730
  321.8 836.4 %reduce-scatter.8.cloned.1.call-start = ((), (), s32[]{:S(2)}) async-start(), calls=%async_computation.10 | async-start | bytes 6488064 | tf_op jit(solution)/shard_map/reduce_scatter | solution.py:811
  439.2 110.5 %collective-permute-start.17 = (bf16[656,1024]{1,0:T(8,128)(2,1)}, bf16[656,1024]{1,0:T(8,128)(2,1)S(1)}, u32[]{:S(2)}, u32[]{:S(2)}) collective-permute-start(bf16[656,1024]{1,0:T(8,128)(2,1)} %pad_maximum_fusion.6), channel_id=1, source_target_pairs={{0,1},{1,0},{2,3},{3,2},{4,5},{5,4},{6,7},{7,6},{8,9},{9,8},{10,11... | collective-permute-start | bytes 4030472 | tf_op jit(solution)/shard_map/ppermute | solution.py:502
  443.8 73.3 %collective-permute-start.25 = (bf16[656,1024]{1,0:T(8,128)(2,1)}, bf16[656,1024]{1,0:T(8,128)(2,1)}, u32[]{:S(2)}, u32[]{:S(2)}) collective-permute-start(bf16[656,1024]{1,0:T(8,128)(2,1)} %pad_maximum_fusion.8), channel_id=1, source_target_pairs={{0,3},{1,2},{2,1},{3,0},{4,7},{5,6},{6,5},{7,4},{8,11},{9,10},{10,... | collective-permute-start | bytes 4030472 | tf_op jit(solution)/shard_map/ppermute | solution.py:502
  670.4 101.5 %all-to-all-start.1 = ((bf16[8,256,512]{2,1,0:T(8,128)(2,1)}), bf16[8,256,512]{2,1,0:T(8,128)(2,1)S(1)}, u32[]{:S(2)}, u32[]{:S(2)}) async-start(bf16[8,256,512]{2,1,0:T(8,128)(2,1)} %bitcast.358), calls=%async_computation.1 | async-start | bytes 4194304 | tf_op jit(solution)/shard_map/all_to_all | solution.py:730
  681.0 479.6 %reduce-scatter.6.cloned.1.call-start = ((), (), s32[]{:S(2)}) async-start(), calls=%async_computation.9 | async-start | bytes 6488064 | tf_op jit(solution)/shard_map/reduce_scatter | solution.py:811
  938.5 78.7 %all-to-all-start.2 = ((bf16[8,256,512]{2,1,0:T(8,128)(2,1)}), bf16[8,256,512]{2,1,0:T(8,128)(2,1)}, u32[]{:S(2)}, u32[]{:S(2)}) async-start(bf16[8,256,512]{2,1,0:T(8,128)(2,1)} %get-tuple-element.184), calls=%async_computation.2 | async-start | bytes 4194304 | tf_op jit(solution)/shard_map/all_to_all | solution.py:730
  948.8 214.1 %reduce-scatter.4.cloned.1.call-start = ((), (), s32[]{:S(2)}) async-start(), calls=%async_computation.8 | async-start | bytes 6488064 | tf_op jit(solution)/shard_map/reduce_scatter | solution.py:811
  958.6 72.6 %collective-permute-start.32 = (bf16[5,2,2,2,32,512]{5,4,3,2,1,0:T(8,128)(2,1)}, bf16[5,2,2,2,32,512]{5,4,3,2,1,0:T(8,128)(2,1)}, u32[]{:S(2)}, u32[]{:S(2)}) collective-permute-start(bf16[5,2,2,2,32,512]{5,4,3,2,1,0:T(8,128)(2,1)} %fusion.49), channel_id=1, source_target_pairs={{0,2},{1,3},{2,0},{3,1},{4,6},{5,7},{6,4},{7,5},{8,10},{9,11},{10,... | collective-permute-start | bytes 3932168 | tf_op jit(solution)/shard_map/ppermute | solution.py:502
  1017.2 122.6 %all-to-all-start.3 = ((bf16[8,256,512]{2,1,0:T(8,128)(2,1)}), bf16[8,256,512]{2,1,0:T(8,128)(2,1)}, u32[]{:S(2)}, u32[]{:S(2)}) async-start(bf16[8,256,512]{2,1,0:T(8,128)(2,1)} %get-tuple-element.152), calls=%async_computation.3 | async-start | bytes 4194304 | tf_op jit(solution)/shard_map/all_to_all | solution.py:730
  1056.1 73.3 %collective-permute-start.28 = (bf16[640,1024]{1,0:T(8,128)(2,1)S(1)}, bf16[640,1024]{1,0:T(8,128)(2,1)S(1)}, u32[]{:S(2)}, u32[]{:S(2)}) collective-permute-start(bf16[640,1024]{1,0:T(8,128)(2,1)S(1)} %get-tuple-element.182), channel_id=1, source_target_pairs={{0,1},{1,0},{2,3},{3,2},{4,5},{5,4},{6,7},{7,6},{8,9},{9,8},{10,11... | collective-permute-start | bytes 3932168 | tf_op jit(solution)/shard_map/ppermute | solution.py:502
  1056.9 72.5 %collective-permute-start.29 = (bf16[640,1024]{1,0:T(8,128)(2,1)S(1)}, bf16[640,1024]{1,0:T(8,128)(2,1)S(1)}, u32[]{:S(2)}, u32[]{:S(2)}) collective-permute-start(bf16[640,1024]{1,0:T(8,128)(2,1)S(1)} %get-tuple-element.181), channel_id=1, source_target_pairs={{0,2},{1,3},{2,0},{3,1},{4,6},{5,7},{6,4},{7,5},{8,10},{9,11},{10,... | collective-permute-start | bytes 3932168 | tf_op jit(solution)/shard_map/ppermute | solution.py:502
  1058.9 70.5 %collective-permute-start.30 = (bf16[640,1024]{1,0:T(8,128)(2,1)S(1)}, bf16[640,1024]{1,0:T(8,128)(2,1)S(1)}, u32[]{:S(2)}, u32[]{:S(2)}) collective-permute-start(bf16[640,1024]{1,0:T(8,128)(2,1)S(1)} %get-tuple-element.180), channel_id=1, source_target_pairs={{0,3},{1,2},{2,1},{3,0},{4,7},{5,6},{6,5},{7,4},{8,11},{9,10},{10,... | collective-permute-start | bytes 3932168 | tf_op jit(solution)/shard_map/ppermute | solution.py:502
  (107 other events, 3710.1 us)
Sparse Core Ops, SparseCore 0:
  24.5 143.1 all-gather.2
  665.3 159.2 reduce-scatter.7
  828.3 109.7 reduce-scatter.5
  963.5 172.6 reduce-scatter.3

commit v5 on v4

--- a/solution.py
+++ b/solution.py
@@ -186,10 +186,10 @@
     return high, mid, row - high - mid
 
 
-def bwd_kernel(ranges, ends, own, q_ref, k_ref, v_ref, do_ref, o_ref, lse_ref, qs_ref, ks_ref, rows_ref,
-               dq_ref, dk_ref, dv_ref, diag_ref, far_ref,
-               qx_ref, dox_ref, kt_ref, bias_ref, dsum_ref, fsum_ref, dqt_ref, dka_ref, dva_ref):
-    pair = pl.program_id(0)
+def bwd_kernel(ranges, ends, own, q_ref, k_ref, v_ref, do_ref, o_ref, lse_ref, qs_ref, ks_ref, rows_ref, *refs):
+    (dq_ref, dk_ref, dv_ref, diag_ref, far_ref,
+     qx_ref, dox_ref, kt_ref, bias_ref, dsum_ref, fsum_ref, dqt_ref, dka_ref, dva_ref) = refs[-14:]
+    pair = own[1]
     length = q_ref.shape[0]
     tile = bias_ref.shape[2]
     tiles = length // tile
@@ -306,25 +306,26 @@
     return jnp.sum(acc, axis=0, keepdims=True)
 
 
-def attend_backward(qkv, do, o, lse, qs, ks, ranges, rows, ends, own, tile):
+def attend_backward(pair, qkv, do, o, lse, qs, ks, ranges, rows, ends, own, tile, earlier):
     length, width = do.shape
     pairs = width // LANES
-    heads = width // HEAD_DIM
-    column = pl.BlockSpec((length, LANES), lambda p, *_: (0, p))
+    own = jnp.concatenate([own, jnp.full((1,), pair, jnp.int32)])
+    column = pl.BlockSpec((length, LANES), lambda p, r, e, own: (0, own[1]))
     fixed = pl.BlockSpec((length, LANES), lambda p, *_: (0, 0))
     spec = pltpu.PrefetchScalarGridSpec(
         num_scalar_prefetch=3,
-        grid=(pairs,),
+        grid=(1,),
         in_specs=[
             column,
-            pl.BlockSpec((length, LANES), lambda p, *_: (0, pairs + p)),
-            pl.BlockSpec((length, LANES), lambda p, *_: (0, 2 * pairs + p)),
+            pl.BlockSpec((length, LANES), lambda p, r, e, own: (0, pairs + own[1])),
+            pl.BlockSpec((length, LANES), lambda p, r, e, own: (0, 2 * pairs + own[1])),
             column,
             column,
-            pl.BlockSpec((1, 2, length), lambda p, *_: (p, 0, 0)),
+            pl.BlockSpec((1, 2, length), lambda p, r, e, own: (own[1], 0, 0)),
             fixed, fixed,
-            pl.BlockSpec((2, 3, 2 * tile), lambda p, *_: (p, 0, 0)),
-        ],
+            pl.BlockSpec((2, 3, 2 * tile), lambda p, r, e, own: (own[1], 0, 0)),
+        ]
+        + [pl.BlockSpec(memory_space=pl.ANY)] * len(earlier),
         out_specs=[
             column, column, column,
             pl.BlockSpec((2, 3, 2 * tile), lambda p, *_: (p, 0, 0)),
@@ -348,15 +349,16 @@
         name="attend_backward",
         out_shape=(
             low, low, low,
-            jax.ShapeDtypeStruct((heads, 3, 2 * tile), jnp.float32),
-            jax.ShapeDtypeStruct((heads, 2, tile), jnp.float32),
+            jax.ShapeDtypeStruct((2, 3, 2 * tile), jnp.float32),
+            jax.ShapeDtypeStruct((2, 2, tile), jnp.float32),
         ),
         grid_spec=spec,
+        input_output_aliases={12 + i: i for i in range(len(earlier))},
         compiler_params=pltpu.CompilerParams(
             dimension_semantics=("arbitrary",), vmem_limit_bytes=40 << 20
         ),
-        cost_estimate=pl.CostEstimate(flops=length * length * width * 10, bytes_accessed=length * width * 16, transcendentals=0),
-    )(ranges, ends, own, qkv, qkv, qkv, do, o, lse, qs, ks, rows)
+        cost_estimate=pl.CostEstimate(flops=length * length * LANES * 10, bytes_accessed=length * LANES * 16, transcendentals=0),
+    )(ranges, ends, own, qkv, qkv, qkv, do, o, lse, qs, ks, rows, *earlier)
 
 
 def bucket_sums(diag, far, tile):
@@ -585,6 +587,50 @@
             self.step()
         self.settle()
         return self.whole
+
+
+class RingScatter:
+    def __init__(self, totals, groups, split, own):
+        self.order, place, self.ahead = ring_of(groups, split)
+        self.count = groups * split
+        self.here = pick(place, own)
+        self.rows = totals[0].shape[0] // self.count
+        self.totals = totals
+        self.round = 0
+        self.forward = self.backward = None
+
+    def block(self, total, offset):
+        at = pick(self.order, (self.here + offset + self.count) % self.count) * self.rows
+        return lax.dynamic_slice_in_dim(total, at, self.rows, 0)
+
+    def load(self, coming, offset):
+        own = [self.block(total, offset) for total in self.totals]
+        if coming is None:
+            return own
+        return [(a.astype(jnp.float32) + b.astype(jnp.float32)).astype(LOW) for a, b in zip(own, coming)]
+
+    def step(self):
+        self.round += 1
+        k, far = self.round, self.count // 2
+        near = self.count - 1 - far
+        if k <= far:
+            parts = self.load(self.forward, far - k + 1)
+            self.forward = [lax.ppermute(part, SEQ, self.ahead) for part in parts]
+        if k <= near:
+            parts = self.load(self.backward, k - near - 1)
+            self.backward = [lax.ppermute(part, SEQ, [(b, a) for a, b in self.ahead]) for part in parts]
+
+    def after(self, value):
+        value, self.forward, self.backward = lax.optimization_barrier((value, self.forward, self.backward))
+        return value
+
+    def finish(self):
+        while self.round < self.count // 2:
+            self.step()
+        own = [self.block(total, 0).astype(jnp.float32) for total in self.totals]
+        return [
+            a + b.astype(jnp.float32) + c.astype(jnp.float32) for a, b, c in zip(own, self.forward, self.backward)
+        ]
 
 
 def norm_scale(value):
@@ -674,20 +720,19 @@
     packed = gather_double(packed, [("exp", b) for b in e_bits[:-1]])
     packed, arrived = lax.optimization_barrier((packed, arrived))
     sequence = jnp.stack([block for line in arrived for block in line]).reshape(length, width)
+
+    gate_up_own = jnp.concatenate([w_gate[0].astype(LOW), w_up[0].astype(LOW)], axis=1)
+    sequence, gate_up_own, down_own = lax.optimization_barrier((sequence, gate_up_own, w_down[0].astype(LOW)))
+    down_w = lax.all_gather(down_own, SEQ, axis=0, tiled=True)
+    gate_up_ring = RingGather(gate_up_own, groups, split, s_at)
+    gate_up_ring.step()
     packed = gather_double(packed, [("exp", b) for b in e_bits[-1:]])
     ne, nz, nx = len(e_bits), len(z_bits), len(x_bits)
     packed = packed.transpose(
         tuple(ne + i for i in reversed(range(nz))) + (ne + nz,) + tuple(reversed(range(ne))) + (ne + nz + 1, ne + nz + 2)
     ).reshape(width, 3 * head_width + width + LANES)
-    sequence, packed = lax.optimization_barrier((sequence, packed))
     qkv_w, small_all = packed[:, : 3 * head_width], packed[:, 3 * head_width + width :]
     out_w = packed[:, 3 * head_width : 3 * head_width + width]
-    gate_up_own = jnp.concatenate([w_gate[0].astype(LOW), w_up[0].astype(LOW)], axis=1)
-    sequence, gate_up_own = lax.optimization_barrier((sequence, gate_up_own))
-    gate_up_ring = RingGather(gate_up_own, groups, split, s_at)
-    gate_up_ring.step()
-    down_w = lax.all_gather(w_down[0].astype(LOW), SEQ, axis=0, tiled=True)
-
     gain_one = small_all[:, 0].astype(jnp.float32)
     gain_two = small_all[:, 1].astype(jnp.float32)
     table_all = small_all[:, 2].reshape(-1, rows_own)[:, :bias_own].reshape(-1, BUCKETS)
@@ -714,6 +759,8 @@
     normed_one = (wide * norm_scale(wide) * gain_one).astype(LOW)
     qkv = dot32(normed_one, qkv_w).astype(LOW)
     qkv, grad_slots = lax.optimization_barrier((qkv, grad_slots))
+    qkv = gate_up_ring.after(qkv)
+    gate_up_ring.step()
     grad_slots = [grad_slots[0]] + [partner(grad_slots[r], "exp", r) for r in range(1, exp_count)]
     segments = lax.dynamic_index_in_dim(segment_ids, z_at, 0, keepdims=False)
     ranges = tile_ranges(segments, tile)
@@ -778,7 +825,7 @@
     slot_rows = jnp.concatenate([rows_[:capacity] for rows_ in sent], axis=0)
     slot_gates = jnp.concatenate([values_below(rows_) for rows_ in sent], axis=0)[:, None]
     slot_grads = (slot_gates * jnp.concatenate(grad_slots, axis=0).astype(jnp.float32)).astype(LOW)
-    gate_sum = dot_tn(slot_rows, gate_low).astype(LOW)
+    down_sum = dot_tn(hidden, slot_grads).astype(LOW)
 
     gate_grad = jnp.sum(
         table.astype(jnp.float32).reshape(tokens, exp_count, capacity) * jnp.stack([values_below(rows_) for rows_ in back])[None], axis=2
@@ -797,8 +844,10 @@
     mid_grad = grad_out + norm_back(scale_two, unit_two, gain_two, normed_two_grad)
     attention_grad = mid_grad.astype(LOW)
     context_grad = dot_nt(attention_grad, out_w).astype(LOW)
-    context_grad, up_low, hidden, gate_sum = lax.optimization_barrier((context_grad, up_low, hidden, gate_sum))
-    down_sum = dot_tn(hidden, slot_grads).astype(LOW)
+    context_grad, up_low, gate_low, hidden, down_sum = lax.optimization_barrier(
+        (context_grad, up_low, gate_low, hidden, down_sum)
+    )
+    gate_sum = dot_tn(slot_rows, gate_low).astype(LOW)
     up_sum = dot_tn(slot_rows, up_low).astype(LOW)
     context_grad = (
         context_grad.reshape(groups, local_len, split, head_width)
@@ -811,17 +860,26 @@
         return lax.psum_scatter(total, SEQ, scatter_dimension=0, tiled=True)
 
     down_owned = scatter_experts(down_sum)
-    gate_owned = scatter_experts(gate_sum)
-    up_owned = scatter_experts(up_sum)
-    context_heads, down_sum, up_sum = lax.optimization_barrier((context_heads, down_sum, up_sum))
+    context_heads, gate_sum, up_sum = lax.optimization_barrier((context_heads, gate_sum, up_sum))
 
     halving = [("exp", b, 1 + nz + nx + ne - 1 - i) for i, b in enumerate(reversed(e_bits))]
     halving += [("z", b, 1 + nz - 1 - i) for i, b in enumerate(reversed(z_bits))]
     out_sum = dot_tn(context_local, attention_grad).astype(LOW)
 
-    query_back, key_back, value_back, diag, far = attend_backward(
-        qkv, context_heads, contexts, log_totals, query_side, key_side, ranges, rows, ends, own, tile
-    )
+    ring = RingScatter([gate_sum, up_sum], groups, split, s_at)
+    grads, diag, far = (), [], []
+    pairs = head_width // LANES
+    for pair in range(pairs):
+        ring.step()
+        *grads, pair_diag, pair_far = attend_backward(
+            pair, qkv, context_heads, contexts, log_totals, query_side, key_side, ranges, rows, ends, own, tile, tuple(grads)
+        )
+        grads = ring.after(grads)
+        diag.append(pair_diag)
+        far.append(pair_far)
+    diag, far = jnp.concatenate(diag), jnp.concatenate(far)
+    query_back, key_back, value_back, down_owned = lax.optimization_barrier((*grads, down_owned))
+    gate_owned, up_owned = ring.finish()
     table_local = bucket_sums(diag, far, tile)
 
     def through(grads, part):

time: 1180 us -> 1140 us (0.966)
  waiting for transfers between devices: 390 us -> 298 us
  Pallas kernels: 301 us -> 345 us
  starting transfers between devices: 118 us -> 92.4 us
  local copies, waits for them, and re-layouts: 68.1 us -> 93.2 us
    ppermute x29, waiting for transfers between devices: 202 us -> 113 us  [partner(): return lax.ppermute(value, axis, [(i, i ^ offset) for i in range(count)])]
    all_to_all x4, waiting for transfers between devices: 114 us -> 69.3 us  [exchange_positions(): return lax.all_to_all(blocks, SEQ, split_axis=0, concat_axis=0, tiled=True)]
    pallas_call x1 -> x4, Pallas kernels: 121 us -> 153 us  [attend_backward(): pl.pallas_call(bwd_kernel, name='attend_backward', out_shape=(low, low, l...]
    ppermute x3, waiting for transfers between devices: 10.6 us -> 39.9 us  [step(): lax.ppermute(self.backward, SEQ, [(b, a) for a, b in self.ahead])]
    ppermute x0 -> x14, starting transfers between devices: none -> 26.9 us  [the longest x8 15 us: step(): self.forward = [lax.ppermute(part, SEQ, self.ahead) for part in parts]]
    ppermute x29, starting transfers between devices: 53.7 us -> 28.3 us  [partner(): return lax.ppermute(value, axis, [(i, i ^ offset) for i in range(count)])]
    unnamed x199 -> x217, local copies, waits for them, and re-layouts: 17.2 us -> 36.3 us
    ppermute x4, starting transfers between devices: 20 us -> 2.63 us  [step(): self.forward = lax.ppermute(self.forward, SEQ, self.ahead)]
  transfers between devices with their start and end apart: 45 -> 57, of which waited for: 12 -> 19; matrix products, arithmetic and copies ran while one was open for 23% -> 25% of each run, Pallas kernels for 26% -> 30%
where the time goes in v5:
time: 1140 us
  Pallas kernels  345 us (30%)
  waiting for transfers between devices  298 us (26%)
  matrix products  195 us (17%)
  local copies, waits for them, and re-layouts  93.2 us (8%)
  starting transfers between devices  92.4 us (8%)
  other arithmetic  85.3 us (7%)
  between operations  28.4 us (2%)
    pallas_call x4, Pallas kernels, attend_backward(): pl.pallas_call(bwd_kernel, name='attend_backward', out_shape=(low, low, l...  153 us
    pallas_call x4, Pallas kernels, expert_block(): pl.pallas_call(expert_kernel, name='expert_block', out_shape=(whole, whol...  122 us
    ppermute x29, waiting for transfers between devices, partner(): return lax.ppermute(value, axis, [(i, i ^ offset) for i in range(count)])  113 us
    dot_general x16, matrix products, dot_tn(): lax.dot_general(a, b, (((0,), (0,)), ((), ())), preferred_element_type=jn...  101 us
    pallas_call x1, Pallas kernels, attend_forward(): pl.pallas_call(fwd_kernel, name='attend_forward', out_shape=(jax.ShapeDty...  69.7 us
    all_to_all x4, waiting for transfers between devices, exchange_positions(): return lax.all_to_all(blocks, SEQ, split_axis=0, concat_axis=0, tiled=True)  69.3 us
    dot_general x9, matrix products, dot32(): return jnp.dot(a, b, preferred_element_type=jnp.float32)  66.3 us
    ppermute x4, waiting for transfers between devices, step(): self.forward = lax.ppermute(self.forward, SEQ, self.ahead)  64.1 us
  transfers between devices with their start and end apart: 57, of which 19 were waited for; matrix products, arithmetic and copies ran while one was open for 25% of the time, Pallas kernels for 30%

profile of v5, /device:TPU:0, one launch (start us, length us, event | category | flops | bytes accessed | tf_op | source)
XLA Modules:
  0.0 1136.7 jit_solution(328863355910208401)
XLA Ops:
  60.1 23.8 %collective-permute-done.1 = bf16[2,32,2688]{2,1,0:T(8,128)(2,1)} collective-permute-done((bf16[2,32,2688]{2,1,0:T(8,128)(2,1)S(1)}, bf16[2,32,2688]{2,1,0:T(8,128)(2,1)}, u32[]{:S(2)}, u32[]{:S(2)}) %collective-permute-start.1) | collective-permute-done | bytes 344096 | tf_op jit(solution)/shard_map/ppermute | solution.py:504
  109.9 24.1 %collective-permute-done.6 = bf16[2,2,2,32,2688]{4,3,2,1,0:T(8,128)(2,1)S(1)} collective-permute-done((bf16[2,2,2,32,2688]{4,3,2,1,0:T(8,128)(2,1)S(1)}, bf16[2,2,2,32,2688]{4,3,2,1,0:T(8,128)(2,1)S(1)}, u32[]{:S(2)}, u32[]{:S(2)}) %collective-permute-start.6) | collective-permute-done | bytes 1376288 | tf_op jit(solution)/shard_map/ppermute | solution.py:504
  183.8 24.3 %collective-permute-done.12 = bf16[128,5632]{1,0:T(8,128)(2,1)} collective-permute-done((bf16[128,5632]{1,0:T(8,128)(2,1)}, bf16[128,5632]{1,0:T(8,128)(2,1)}, u32[]{:S(2)}, u32[]{:S(2)}) %collective-permute-start.12) | collective-permute-done | bytes 1441824 | tf_op jit(solution)/shard_map/ppermute | solution.py:568
  215.5 69.7 %attend_forward.1 = (bf16[2048,512]{1,0:T(8,128)(2,1)}, f32[4,2,2048]{2,1,0:T(2,128)S(1)}) custom-call(s32[2,8]{1,0:T(2,128)S(1)} %pad_add_fusion.ranges, f32[8,2]{1,0:T(8,128)S(1)} %maximum_convert_fusion.ends, s32[1]{0:T(128)} %bitcast.23.own, bf16[2048,1536]{1,0:T(8,128)(2,1)} %convolution_convert_fusion.q_ref.k_ref.v_ref, ...), custom_call_target="tpu_custom_call" | custom-call | flops 8589934592 | bytes 8388608 | tf_op jit(solution)/shard_map/attend_forward/pallas_call | solution.py:168
  308.7 21.5 %collective-permute-done.21 = bf16[128,5632]{1,0:T(8,128)(2,1)} collective-permute-done((bf16[128,5632]{1,0:T(8,128)(2,1)}, bf16[128,5632]{1,0:T(8,128)(2,1)}, u32[]{:S(2)}, u32[]{:S(2)}) %collective-permute-start.21) | collective-permute-done | bytes 1441824 | tf_op jit(solution)/shard_map/ppermute | solution.py:568
  335.8 32.8 %collective-permute-done.22 = bf16[128,5632]{1,0:T(8,128)(2,1)S(1)} collective-permute-done((bf16[128,5632]{1,0:T(8,128)(2,1)}, bf16[128,5632]{1,0:T(8,128)(2,1)S(1)}, u32[]{:S(2)}, u32[]{:S(2)}) %collective-permute-start.22) | collective-permute-done | bytes 1441824 | tf_op jit(solution)/shard_map/ppermute | solution.py:571
  369.9 18.3 %collective-permute-done.23 = bf16[128,5632]{1,0:T(8,128)(2,1)S(1)} collective-permute-done((bf16[128,5632]{1,0:T(8,128)(2,1)}, bf16[128,5632]{1,0:T(8,128)(2,1)S(1)}, u32[]{:S(2)}, u32[]{:S(2)}) %collective-permute-start.23) | collective-permute-done | bytes 1441824 | tf_op jit(solution)/shard_map/ppermute | solution.py:568
  422.7 30.0 %expert_block.4 = (bf16[2560,2816]{1,0:T(8,128)(2,1)}, bf16[2560,2816]{1,0:T(8,128)(2,1)}, bf16[2560,2816]{1,0:T(8,128)(2,1)}, bf16[656,1024]{1,0:T(8,128)(2,1)S(1)}) custom-call(s32[1]{0:T(128)} %constant.353.clone.1.own_ref, bf16[656,1024]{1,0:T(8,128)(2,1)S(1)} %copy-done.13, bf16[640,1024]{1,0:T(8,128)(2,1)S(1)} %copy-done.29, ...), custom_call_target="tpu_custom_call" | custom-call | flops 18454937600 | bytes 28114944 | tf_op jit(solution)/shard_map/expert_block/pallas_call | solution.py:465
  452.7 30.4 %expert_block.5 = (bf16[2560,2816]{1,0:T(8,128)(2,1)}, bf16[2560,2816]{1,0:T(8,128)(2,1)}, bf16[2560,2816]{1,0:T(8,128)(2,1)}, bf16[656,1024]{1,0:T(8,128)(2,1)S(1)}) custom-call(s32[1]{0:T(128)} %constant.353.clone.1.own_ref, bf16[656,1024]{1,0:T(8,128)(2,1)S(1)} %collective-permute-done.20.x_ref, ...), custom_call_target="tpu_custom_call", output_to_operand_aliasing={{0}: (6, {}), {1}: (7, {}), {2}: (8, {})} | custom-call | flops 18454937600 | bytes 28114944 | tf_op jit(solution)/shard_map/expert_block/pallas_call | solution.py:465
  484.9 30.7 %expert_block.6 = (bf16[2560,2816]{1,0:T(8,128)(2,1)}, bf16[2560,2816]{1,0:T(8,128)(2,1)}, bf16[2560,2816]{1,0:T(8,128)(2,1)}, bf16[656,1024]{1,0:T(8,128)(2,1)S(1)}) custom-call(s32[1]{0:T(128)} %constant.353.clone.1.own_ref, bf16[656,1024]{1,0:T(8,128)(2,1)} %collective-permute-done.25.x_ref, ...), custom_call_target="tpu_custom_call", output_to_operand_aliasing={{0}: (6, {}), {1}: (7, {}), {2}: (8, {})} | custom-call | flops 18454937600 | bytes 28114944 | tf_op jit(solution)/shard_map/expert_block/pallas_call | solution.py:465
  516.7 30.5 %expert_block.7 = (bf16[2560,2816]{1,0:T(8,128)(2,1)}, bf16[2560,2816]{1,0:T(8,128)(2,1)}, bf16[2560,2816]{1,0:T(8,128)(2,1)}, bf16[656,1024]{1,0:T(8,128)(2,1)}) custom-call(s32[1]{0:T(128)} %constant.353.clone.1.own_ref, bf16[656,1024]{1,0:T(8,128)(2,1)S(1)} %collective-permute-done.19.x_ref, ...), custom_call_target="tpu_custom_call", output_to_operand_aliasing={{0}: (6, {}), {1}: (7, {}), {2}: (8, {})} | custom-call | flops 18454937600 | bytes 28114944 | tf_op jit(solution)/shard_map/expert_block/pallas_call | solution.py:465
  564.3 21.0 %convolution_convert_fusion.3 = bf16[2816,1024]{1,0:T(8,128)(2,1)} fusion(bf16[2560,2816]{1,0:T(8,128)(2,1)} %get-tuple-element.244, bf16[640,1024]{1,0:T(8,128)(2,1)S(1)} %copy-done.22, bf16[640,1024]{1,0:T(8,128)(2,1)S(1)} %copy-done.20, bf16[640,1024]{1,0:T(8,128)(2,1)S(1)} %copy-done.18, bf16[640,1024]{1,0:T(8,128)(2,1)S(1)} %copy-done.30, ...), kind=kOutput, calls=%fused_computation.22 | convolution fusion | flops 14793048064 | bytes 25438208 | tf_op jit(solution)/shard_map/dot_general | solution.py:499
  614.8 13.1 %all-to-all-start.1 = ((bf16[8,256,512]{2,1,0:T(8,128)(2,1)}), bf16[8,256,512]{2,1,0:T(8,128)(2,1)S(1)}, u32[]{:S(2)}, u32[]{:S(2)}) async-start(bf16[8,256,512]{2,1,0:T(8,128)(2,1)} %bitcast.355), calls=%async_computation.1 | async-start | bytes 4194304 | tf_op jit(solution)/shard_map/all_to_all | solution.py:777
  628.7 22.9 %convolution_convert_fusion.1 = bf16[1024,2816]{1,0:T(8,128)(2,1)} fusion(bf16[2560,2816]{1,0:T(8,128)(2,1)} %get-tuple-element.195, bf16[640,1024]{1,0:T(8,128)(2,1)} %slice.264, bf16[640,1024]{1,0:T(8,128)(2,1)} %slice.263, bf16[640,1024]{1,0:T(8,128)(2,1)} %slice.262, bf16[640,1024]{1,0:T(8,128)(2,1)} %slice.261), kind=kOutput, calls=%fused_computation.20 | convolution fusion | flops 14787805184 | bytes 25427968 | tf_op jit(solution)/shard_map/dot_general | solution.py:499
  651.6 20.9 %convolution_convert_fusion.2 = bf16[1024,2816]{1,0:T(8,128)(2,1)} fusion(bf16[2560,2816]{1,0:T(8,128)(2,1)} %get-tuple-element.194, bf16[640,1024]{1,0:T(8,128)(2,1)S(1)} %copy-done.61, bf16[640,1024]{1,0:T(8,128)(2,1)S(1)} %copy-done.60, bf16[640,1024]{1,0:T(8,128)(2,1)S(1)} %copy-done.59, bf16[640,1024]{1,0:T(8,128)(2,1)S(1)} %copy-done.58), kind=kOutput, calls=%fused_computation.21 | convolution fusion | flops 14787805184 | bytes 25427968 | tf_op jit(solution)/shard_map/dot_general | solution.py:499
  672.5 39.9 %all-to-all-done.1 = bf16[8,256,512]{2,1,0:T(8,128)(2,1)S(1)} async-done(((bf16[8,256,512]{2,1,0:T(8,128)(2,1)}), bf16[8,256,512]{2,1,0:T(8,128)(2,1)S(1)}, u32[]{:S(2)}, u32[]{:S(2)}) %all-to-all-start.1) | async-done | bytes 2097184 | tf_op jit(solution)/shard_map/all_to_all | solution.py:777
  723.6 38.7 %attend_backward.4 = (bf16[2048,512]{1,0:T(8,128)(2,1)S(1)}, bf16[2048,512]{1,0:T(8,128)(2,1)S(1)}, bf16[2048,512]{1,0:T(8,128)(2,1)S(1)}, f32[2,3,512]{2,1,0:T(4,128)S(1)}, f32[2,2,256]{2,1,0:T(2,128)S(1)}) custom-call(s32[2,8]{1,0:T(2,128)S(1)} %copy-done.28, f32[8,2]{1,0:T(8,128)S(1)} %copy-done.26, s32[2]{0:T(128)S(1)} %get-tuple-element.371.own, ...), custom_call_target="tpu_custom_call" | custom-call | flops 5368709120 | bytes 4194304 | tf_op jit(solution)/shard_map/attend_backward/pallas_call | solution.py:347
  769.9 38.0 %attend_backward.5 = (bf16[2048,512]{1,0:T(8,128)(2,1)S(1)}, bf16[2048,512]{1,0:T(8,128)(2,1)S(1)}, bf16[2048,512]{1,0:T(8,128)(2,1)S(1)}, f32[2,3,512]{2,1,0:T(4,128)S(1)}, f32[2,2,256]{2,1,0:T(2,128)S(1)}) custom-call(s32[2,8]{1,0:T(2,128)S(1)} %copy-done.28, f32[8,2]{1,0:T(8,128)S(1)} %copy-done.26, ...), custom_call_target="tpu_custom_call", output_to_operand_aliasing={{0}: (12, {}), {1}: (13, {}), {2}: (14, {})} | custom-call | flops 5368709120 | bytes 4194304 | tf_op jit(solution)/shard_map/attend_backward/pallas_call | solution.py:347
  829.4 38.5 %attend_backward.6 = (bf16[2048,512]{1,0:T(8,128)(2,1)S(1)}, bf16[2048,512]{1,0:T(8,128)(2,1)S(1)}, bf16[2048,512]{1,0:T(8,128)(2,1)S(1)}, f32[2,3,512]{2,1,0:T(4,128)S(1)}, f32[2,2,256]{2,1,0:T(2,128)S(1)}) custom-call(s32[2,8]{1,0:T(2,128)S(1)} %copy-done.28, f32[8,2]{1,0:T(8,128)S(1)} %copy-done.26, ...), custom_call_target="tpu_custom_call", output_to_operand_aliasing={{0}: (12, {}), {1}: (13, {}), {2}: (14, {})} | custom-call | flops 5368709120 | bytes 4194304 | tf_op jit(solution)/shard_map/attend_backward/pallas_call | solution.py:347
  877.6 38.2 %attend_backward.7 = (bf16[2048,512]{1,0:T(8,128)(2,1)S(1)}, bf16[2048,512]{1,0:T(8,128)(2,1)S(1)}, bf16[2048,512]{1,0:T(8,128)(2,1)S(1)}, f32[2,3,512]{2,1,0:T(4,128)S(1)}, f32[2,2,256]{2,1,0:T(2,128)S(1)}) custom-call(s32[2,8]{1,0:T(2,128)S(1)} %copy-done.28, f32[8,2]{1,0:T(8,128)S(1)} %copy-done.26, ...), custom_call_target="tpu_custom_call", output_to_operand_aliasing={{0}: (12, {}), {1}: (13, {}), {2}: (14, {})} | custom-call | flops 5368709120 | bytes 4194304 | tf_op jit(solution)/shard_map/attend_backward/pallas_call | solution.py:347
  983.3 29.4 %all-to-all-done.2 = bf16[8,256,512]{2,1,0:T(8,128)(2,1)} async-done(((bf16[8,256,512]{2,1,0:T(8,128)(2,1)}), bf16[8,256,512]{2,1,0:T(8,128)(2,1)}, u32[]{:S(2)}, u32[]{:S(2)}) %all-to-all-start.2) | async-done | bytes 2097184 | tf_op jit(solution)/shard_map/all_to_all | solution.py:777
  1021.9 19.3 %multiply_convert_fusion = bf16[2560,1024]{1,0:T(8,128)(2,1)S(1)} fusion(bf16[2560,2816]{1,0:T(8,128)(2,1)} %get-tuple-element.244, bf16[2816,1024]{1,0:T(8,128)(2,1)} %all-gather.2.cloned.1.call-done.wd_ref, f32[2560]{0:T(1024)S(1)} %copy-done.78), kind=kOutput, calls=%fused_computation.7 | convolution fusion | flops 14769192960 | bytes 25438208 | tf_op jit(solution)/shard_map/dot_general | solution.py:491
  1043.8 22.7 %collective-permute-done.47 = bf16[5,2,2,32,512]{4,3,2,1,0:T(8,128)(2,1)S(1)} collective-permute-done((bf16[5,2,2,32,512]{4,3,2,1,0:T(8,128)(2,1)S(1)}, bf16[5,2,2,32,512]{4,3,2,1,0:T(8,128)(2,1)S(1)}, u32[]{:S(2)}, u32[]{:S(2)}) %collective-permute-start.47) | collective-permute-done | bytes 655392 | tf_op jit(solution)/shard_map/ppermute | solution.py:504
  1084.3 16.4 %collective-permute-done.44 = bf16[640,1024]{1,0:T(8,128)(2,1)S(1)} collective-permute-done((bf16[640,1024]{1,0:T(8,128)(2,1)S(1)}, bf16[640,1024]{1,0:T(8,128)(2,1)S(1)}, u32[]{:S(2)}, u32[]{:S(2)}) %collective-permute-start.44) | collective-permute-done | bytes 1310752 | tf_op jit(solution)/shard_map/ppermute | solution.py:504
  (539 shorter events, 413.2 us)
Async XLA Ops:
  7.2 410.1 %all-gather.2.cloned.1.call-start = ((), (), s32[]{:S(2)}) async-start(), calls=%async_computation.6 | async-start | bytes 6488064 | tf_op jit(solution)/shard_map/all_gather | solution.py:726
  19.5 84.8 %collective-permute-start.3 = (bf16[256,1024]{1,0:T(8,128)(2,1)}, bf16[256,1024]{1,0:T(8,128)(2,1)}, u32[]{:S(2)}, u32[]{:S(2)}) collective-permute-start(bf16[256,1024]{1,0:T(8,128)(2,1)} %get-tuple-element.305), channel_id=1, source_target_pairs={{0,8},{8,0},{16,24},{24,16},{1,9},{9,1},{17,25},{25,17},{2,10},{10... | collective-permute-start | bytes 1572872 | tf_op jit(solution)/shard_map/ppermute | solution.py:504
  21.1 83.2 %collective-permute-start.4 = (bf16[256,1024]{1,0:T(8,128)(2,1)}, bf16[256,1024]{1,0:T(8,128)(2,1)}, u32[]{:S(2)}, u32[]{:S(2)}) collective-permute-start(bf16[256,1024]{1,0:T(8,128)(2,1)} %get-tuple-element.304), channel_id=1, source_target_pairs={{0,16},{8,24},{16,0},{24,8},{1,17},{9,25},{17,1},{25,9},{2,18},{10... | collective-permute-start | bytes 1572872 | tf_op jit(solution)/shard_map/ppermute | solution.py:504
  23.7 80.6 %collective-permute-start.5 = (bf16[256,1024]{1,0:T(8,128)(2,1)}, bf16[256,1024]{1,0:T(8,128)(2,1)}, u32[]{:S(2)}, u32[]{:S(2)}) collective-permute-start(bf16[256,1024]{1,0:T(8,128)(2,1)} %get-tuple-element.306), channel_id=1, source_target_pairs={{0,24},{8,16},{16,8},{24,0},{1,25},{9,17},{17,9},{25,1},{2,26},{10... | collective-permute-start | bytes 1572872 | tf_op jit(solution)/shard_map/ppermute | solution.py:504
  23.9 112.2 %collective-permute-start.7 = (bf16[256,1024]{1,0:T(8,128)(2,1)}, bf16[256,1024]{1,0:T(8,128)(2,1)}, u32[]{:S(2)}, u32[]{:S(2)}) collective-permute-start(bf16[256,1024]{1,0:T(8,128)(2,1)} %get-tuple-element.142), channel_id=1, source_target_pairs={{0,4},{4,0},{1,5},{5,1},{2,6},{6,2},{3,7},{7,3},{8,12},{12,8},{9,1... | collective-permute-start | bytes 1572872 | tf_op jit(solution)/shard_map/ppermute | solution.py:504
  152.8 55.2 %collective-permute-start.12 = (bf16[128,5632]{1,0:T(8,128)(2,1)}, bf16[128,5632]{1,0:T(8,128)(2,1)}, u32[]{:S(2)}, u32[]{:S(2)}) collective-permute-start(bf16[128,5632]{1,0:T(8,128)(2,1)} %pad_maximum_fusion.3), channel_id=1, source_target_pairs={{0,8},{8,16},{16,24},{24,28},{28,20},{20,12},{12,4},{4,0},{1,9},{9... | collective-permute-start | bytes 4325384 | tf_op jit(solution)/shard_map/ppermute | solution.py:568
  153.4 57.4 %collective-permute-start.13 = (bf16[128,5632]{1,0:T(8,128)(2,1)}, bf16[128,5632]{1,0:T(8,128)(2,1)}, u32[]{:S(2)}, u32[]{:S(2)}) collective-permute-start(bf16[128,5632]{1,0:T(8,128)(2,1)} %pad_maximum_fusion.3), channel_id=1, source_target_pairs={{8,0},{16,8},{24,16},{28,24},{20,28},{12,20},{4,12},{0,4},{9,1},{1... | collective-permute-start | bytes 4325384 | tf_op jit(solution)/shard_map/ppermute | solution.py:571
  211.2 76.6 %collective-permute-start.14 = (bf16[128,5632]{1,0:T(8,128)(2,1)}, bf16[128,5632]{1,0:T(8,128)(2,1)}, u32[]{:S(2)}, u32[]{:S(2)}) collective-permute-start(bf16[128,5632]{1,0:T(8,128)(2,1)} %collective-permute-done.12), channel_id=1, source_target_pairs={{0,8},{8,16},{16,24},{24,28},{28,20},{20,12},{12,4},{4,0},{1,9},{9... | collective-permute-start | bytes 4325384 | tf_op jit(solution)/shard_map/ppermute | solution.py:568
  212.8 79.3 %collective-permute-start.15 = (bf16[128,5632]{1,0:T(8,128)(2,1)}, bf16[128,5632]{1,0:T(8,128)(2,1)S(1)}, u32[]{:S(2)}, u32[]{:S(2)}) collective-permute-start(bf16[128,5632]{1,0:T(8,128)(2,1)} %collective-permute-done.13), channel_id=1, source_target_pairs={{8,0},{16,8},{24,16},{28,24},{20,28},{12,20},{4,12},{0,4},{9,1},{1... | collective-permute-start | bytes 4325384 | tf_op jit(solution)/shard_map/ppermute | solution.py:571
  213.5 81.7 %collective-permute-start.16 = (bf16[640,1024]{1,0:T(8,128)(2,1)}, bf16[640,1024]{1,0:T(8,128)(2,1)S(1)}, u32[]{:S(2)}, u32[]{:S(2)}) collective-permute-start(bf16[640,1024]{1,0:T(8,128)(2,1)} %convolution_convert_fusion.12), channel_id=1, source_target_pairs={{0,1},{1,0},{2,3},{3,2},{4,5},{5,4},{6,7},{7,6},{8,9},{9,8},{10,11... | collective-permute-start | bytes 3932168 | tf_op jit(solution)/shard_map/ppermute | solution.py:504
  213.5 82.8 %collective-permute-start.17 = (bf16[640,1024]{1,0:T(8,128)(2,1)}, bf16[640,1024]{1,0:T(8,128)(2,1)S(1)}, u32[]{:S(2)}, u32[]{:S(2)}) collective-permute-start(bf16[640,1024]{1,0:T(8,128)(2,1)} %convolution_convert_fusion.11), channel_id=1, source_target_pairs={{0,2},{1,3},{2,0},{3,1},{4,6},{5,7},{6,4},{7,5},{8,10},{9,11},{10,... | collective-permute-start | bytes 3932168 | tf_op jit(solution)/shard_map/ppermute | solution.py:504
  214.1 83.4 %collective-permute-start.18 = (bf16[640,1024]{1,0:T(8,128)(2,1)}, bf16[640,1024]{1,0:T(8,128)(2,1)S(1)}, u32[]{:S(2)}, u32[]{:S(2)}) collective-permute-start(bf16[640,1024]{1,0:T(8,128)(2,1)} %convolution_convert_fusion.10), channel_id=1, source_target_pairs={{0,3},{1,2},{2,1},{3,0},{4,7},{5,6},{6,5},{7,4},{8,11},{9,10},{10,... | collective-permute-start | bytes 3932168 | tf_op jit(solution)/shard_map/ppermute | solution.py:504
  298.6 90.8 %all-to-all-start = ((bf16[8,256,512]{2,1,0:T(8,128)(2,1)}), bf16[8,256,512]{2,1,0:T(8,128)(2,1)}, u32[]{:S(2)}, u32[]{:S(2)}) async-start(bf16[8,256,512]{2,1,0:T(8,128)(2,1)} %bitcast.39), calls=%async_computation | async-start | bytes 4194304 | tf_op jit(solution)/shard_map/all_to_all | solution.py:777
  304.2 64.4 %collective-permute-start.22 = (bf16[128,5632]{1,0:T(8,128)(2,1)}, bf16[128,5632]{1,0:T(8,128)(2,1)S(1)}, u32[]{:S(2)}, u32[]{:S(2)}) collective-permute-start(bf16[128,5632]{1,0:T(8,128)(2,1)} %copy-done.57), channel_id=1, source_target_pairs={{8,0},{16,8},{24,16},{28,24},{20,28},{12,20},{4,12},{0,4},{9,1},{1... | collective-permute-start | bytes 4325384 | tf_op jit(solution)/shard_map/ppermute | solution.py:571
  330.2 58.0 %collective-permute-start.23 = (bf16[128,5632]{1,0:T(8,128)(2,1)}, bf16[128,5632]{1,0:T(8,128)(2,1)S(1)}, u32[]{:S(2)}, u32[]{:S(2)}) collective-permute-start(bf16[128,5632]{1,0:T(8,128)(2,1)} %collective-permute-done.21), channel_id=1, source_target_pairs={{0,8},{8,16},{16,24},{24,28},{28,20},{20,12},{12,4},{4,0},{1,9},{9... | collective-permute-start | bytes 4325384 | tf_op jit(solution)/shard_map/ppermute | solution.py:568
  411.5 104.1 %collective-permute-start.19 = (bf16[656,1024]{1,0:T(8,128)(2,1)}, bf16[656,1024]{1,0:T(8,128)(2,1)S(1)}, u32[]{:S(2)}, u32[]{:S(2)}) collective-permute-start(bf16[656,1024]{1,0:T(8,128)(2,1)} %pad_maximum_fusion.6), channel_id=1, source_target_pairs={{0,1},{1,0},{2,3},{3,2},{4,5},{5,4},{6,7},{7,6},{8,9},{9,8},{10,11... | collective-permute-start | bytes 4030472 | tf_op jit(solution)/shard_map/ppermute | solution.py:504
  414.2 70.6 %collective-permute-start.25 = (bf16[656,1024]{1,0:T(8,128)(2,1)}, bf16[656,1024]{1,0:T(8,128)(2,1)}, u32[]{:S(2)}, u32[]{:S(2)}) collective-permute-start(bf16[656,1024]{1,0:T(8,128)(2,1)} %pad_maximum_fusion.8), channel_id=1, source_target_pairs={{0,3},{1,2},{2,1},{3,0},{4,7},{5,6},{6,5},{7,4},{8,11},{9,10},{10,... | collective-permute-start | bytes 4030472 | tf_op jit(solution)/shard_map/ppermute | solution.py:504
  614.8 97.6 %all-to-all-start.1 = ((bf16[8,256,512]{2,1,0:T(8,128)(2,1)}), bf16[8,256,512]{2,1,0:T(8,128)(2,1)S(1)}, u32[]{:S(2)}, u32[]{:S(2)}) async-start(bf16[8,256,512]{2,1,0:T(8,128)(2,1)} %bitcast.355), calls=%async_computation.1 | async-start | bytes 4194304 | tf_op jit(solution)/shard_map/all_to_all | solution.py:777
  627.9 292.7 %reduce-scatter.2.cloned.1.call-start = ((), (), s32[]{:S(2)}) async-start(), calls=%async_computation.7 | async-start | bytes 6488064 | tf_op jit(solution)/shard_map/reduce_scatter | solution.py:860
  817.2 50.8 %collective-permute-start.37 = (bf16[128,2816]{1,0:T(8,128)(2,1)S(1)}, bf16[128,2816]{1,0:T(8,128)(2,1)}, u32[]{:S(2)}, u32[]{:S(2)}) collective-permute-start(bf16[128,2816]{1,0:T(8,128)(2,1)S(1)} %get-tuple-element.282), channel_id=1, source_target_pairs={{0,8},{8,16},{16,24},{24,28},{28,20},{20,12},{12,4},{4,0},{1,9},{9... | collective-permute-start | bytes 2162696 | tf_op jit(solution)/shard_map/ppermute | solution.py:618
  869.6 50.1 %collective-permute-start.41 = (bf16[128,2816]{1,0:T(8,128)(2,1)S(1)}, bf16[128,2816]{1,0:T(8,128)(2,1)}, u32[]{:S(2)}, u32[]{:S(2)}) collective-permute-start(bf16[128,2816]{1,0:T(8,128)(2,1)S(1)} %add_convert_fusion.2), channel_id=1, source_target_pairs={{0,8},{8,16},{16,24},{24,28},{28,20},{20,12},{12,4},{4,0},{1,9},{9... | collective-permute-start | bytes 2162696 | tf_op jit(solution)/shard_map/ppermute | solution.py:618
  962.1 50.6 %all-to-all-start.2 = ((bf16[8,256,512]{2,1,0:T(8,128)(2,1)}), bf16[8,256,512]{2,1,0:T(8,128)(2,1)}, u32[]{:S(2)}, u32[]{:S(2)}) async-start(bf16[8,256,512]{2,1,0:T(8,128)(2,1)} %get-tuple-element.300), calls=%async_computation.3 | async-start | bytes 4194304 | tf_op jit(solution)/shard_map/all_to_all | solution.py:777
  1012.7 98.3 %all-to-all-start.3 = ((bf16[8,256,512]{2,1,0:T(8,128)(2,1)}), bf16[8,256,512]{2,1,0:T(8,128)(2,1)}, u32[]{:S(2)}, u32[]{:S(2)}) async-start(bf16[8,256,512]{2,1,0:T(8,128)(2,1)} %get-tuple-element.246), calls=%async_computation.4 | async-start | bytes 4194304 | tf_op jit(solution)/shard_map/all_to_all | solution.py:777
  1042.1 58.6 %collective-permute-start.44 = (bf16[640,1024]{1,0:T(8,128)(2,1)S(1)}, bf16[640,1024]{1,0:T(8,128)(2,1)S(1)}, u32[]{:S(2)}, u32[]{:S(2)}) collective-permute-start(bf16[640,1024]{1,0:T(8,128)(2,1)S(1)} %get-tuple-element.296), channel_id=1, source_target_pairs={{0,3},{1,2},{2,1},{3,0},{4,7},{5,6},{6,5},{7,4},{8,11},{9,10},{10,... | collective-permute-start | bytes 3932168 | tf_op jit(solution)/shard_map/ppermute | solution.py:504
  (128 other events, 4394.1 us)
Sparse Core Ops, SparseCore 0:
  155.2 137.1 all-gather.1
  632.4 178.3 reduce-scatter.1

commit v6 on v5

--- a/solution.py
+++ b/solution.py
@@ -686,9 +686,6 @@
 
     input_r = reorder(block_in, z_at)
 
-    arrived = [[None] * split for _ in range(groups)]
-    for rz in reversed(range(groups)):
-        arrived[rz][0] = partner(input_r[rz], "z", rz) if rz else input_r[0]
     small = jnp.concatenate(
         [
             gain_attention[:, None],
@@ -708,17 +705,21 @@
     shares = [lax.dynamic_index_in_dim(share, x_at ^ r, 0, keepdims=False) for r in range(split)]
     shares = [shares[0]] + [partner(shares[r], "x", r) for r in range(1, split)]
     by_x = reorder(jnp.stack(shares), x_at)
+    packed = gather_double(by_x, [("z", b) for b in z_bits[:1]])
+
+    packed, input_r = lax.optimization_barrier((packed, input_r))
+    arrived = [[input_r[rz]] + [None] * (split - 1) for rz in range(groups)]
+    for rz in reversed(range(1, groups)):
+        arrived[rz][0] = partner(input_r[rz], "z", rz)
     for rx in range(1, split):
         arrived[0][rx] = partner(arrived[0][0], "x", rx)
-    packed = gather_double(by_x, [("z", b) for b in z_bits])
+    packed = gather_double(packed, [("z", b) for b in z_bits[1:]] + [("exp", b) for b in e_bits[:-1]])
     near = [arrived[rz][0] for rz in range(1, groups)]
     packed, near = lax.optimization_barrier((packed, near))
     for rz in range(1, groups):
         arrived[rz][0] = near[rz - 1]
         for rx in range(1, split):
             arrived[rz][rx] = partner(arrived[rz][0], "x", rx)
-    packed = gather_double(packed, [("exp", b) for b in e_bits[:-1]])
-    packed, arrived = lax.optimization_barrier((packed, arrived))
     sequence = jnp.stack([block for line in arrived for block in line]).reshape(length, width)
 
     gate_up_own = jnp.concatenate([w_gate[0].astype(LOW), w_up[0].astype(LOW)], axis=1)
@@ -825,7 +826,6 @@
     slot_rows = jnp.concatenate([rows_[:capacity] for rows_ in sent], axis=0)
     slot_gates = jnp.concatenate([values_below(rows_) for rows_ in sent], axis=0)[:, None]
     slot_grads = (slot_gates * jnp.concatenate(grad_slots, axis=0).astype(jnp.float32)).astype(LOW)
-    down_sum = dot_tn(hidden, slot_grads).astype(LOW)
 
     gate_grad = jnp.sum(
         table.astype(jnp.float32).reshape(tokens, exp_count, capacity) * jnp.stack([values_below(rows_) for rows_ in back])[None], axis=2
@@ -844,9 +844,8 @@
     mid_grad = grad_out + norm_back(scale_two, unit_two, gain_two, normed_two_grad)
     attention_grad = mid_grad.astype(LOW)
     context_grad = dot_nt(attention_grad, out_w).astype(LOW)
-    context_grad, up_low, gate_low, hidden, down_sum = lax.optimization_barrier(
-        (context_grad, up_low, gate_low, hidden, down_sum)
-    )
+    context_grad, up_low, gate_low, hidden = lax.optimization_barrier((context_grad, up_low, gate_low, hidden))
+    down_sum = dot_tn(hidden, slot_grads).astype(LOW)
     gate_sum = dot_tn(slot_rows, gate_low).astype(LOW)
     up_sum = dot_tn(slot_rows, up_low).astype(LOW)
     context_grad = (
@@ -859,8 +858,10 @@
     def scatter_experts(total):
         return lax.psum_scatter(total, SEQ, scatter_dimension=0, tiled=True)
 
+    context_heads, gate_sum, up_sum, down_sum = lax.optimization_barrier(
+        (context_heads, gate_sum, up_sum, down_sum)
+    )
     down_owned = scatter_experts(down_sum)
-    context_heads, gate_sum, up_sum = lax.optimization_barrier((context_heads, gate_sum, up_sum))
 
     halving = [("exp", b, 1 + nz + nx + ne - 1 - i) for i, b in enumerate(reversed(e_bits))]
     halving += [("z", b, 1 + nz - 1 - i) for i, b in enumerate(reversed(z_bits))]
@@ -893,38 +894,43 @@
     weight_sum, query_back, key_back, value_back = lax.optimization_barrier(
         (weight_sum, query_back, key_back, value_back)
     )
-    normed_part = (through(query_back, 0) + through(key_back, 1) + through(value_back, 2)).astype(LOW)
-    normed_part = reorder(normed_part.reshape(seq_count, local_len, width), s_at)
+    normed_part = through(query_back, 0) + through(key_back, 1) + through(value_back, 2)
     half = width // 2
-    normed_first = exchange_positions(normed_part[:, :, :half])
-    normed_first, hidden, normed_second = lax.optimization_barrier(
-        (normed_first, hidden, normed_part[:, :, half:])
-    )
-    normed_second = exchange_positions(normed_second)
+    normed_part = normed_part.reshape(groups, split, local_len, width)
+
+    sides = [normed_part[:, rx].astype(LOW) for rx in range(1, split)]
+    first = [partner(side[:, :, :half], "x", rx) for rx, side in enumerate(sides, 1)]
+    first, hidden, rest = lax.optimization_barrier((first, hidden, [side[:, :, half:] for side in sides]))
+
+    def send_back(own_part, coming):
+        total = own_part + sum(part.astype(jnp.float32) for part in coming)
+        total = reorder(total.astype(LOW), z_at)
+        return lax.all_to_all(total, "z", split_axis=0, concat_axis=0, tiled=True)
+
+    normed_first = send_back(normed_part[:, 0, :, :half], first)
+    rest = [partner(side, "x", rx) for rx, side in enumerate(rest, 1)]
+    normed_second = send_back(normed_part[:, 0, :, half:], rest)
+    expert_out = (slot_gates * dot32(hidden, down_w)).astype(LOW)
     weight_part = scatter_halve(
-        weight_sum.reshape((3 + out_parts,) + (2,) * (nz + nx + ne) + (rows_own, head_width)), halving
-    ).reshape(3 + out_parts, split, rows_own, head_width)
+        weight_sum.reshape((3 + out_parts,) + (2,) * (nz + nx + ne) + (rows_own, head_width)), halving[:ne]
+    )
+    weight_part, expert_out = lax.optimization_barrier((weight_part, expert_out))
+    weight_part = scatter_halve(weight_part, halving[ne:]).reshape(3 + out_parts, split, rows_own, head_width)
     weight_own = [lax.dynamic_index_in_dim(weight_part, x_at ^ r, 1, keepdims=False) for r in range(split)]
     weight_own = [weight_own[0]] + [partner(weight_own[r], "x", r) for r in range(1, split)]
+    returned = [expert_out[:capacity]] + [
+        partner(expert_out[r * capacity : (r + 1) * capacity], "exp", r) for r in range(1, exp_count)
+    ]
+    normed_second, returned, weight_own = lax.optimization_barrier((normed_second, returned, weight_own))
+    block_out = (mid + dot32(table, jnp.concatenate(returned, axis=0))).astype(LOW)
+
+    block_out = block_out.reshape(groups, local_len, width)
     out_w_out = sum(part[3:].astype(jnp.float32) for part in weight_own)
     out_w_out = out_w_out.transpose(1, 0, 2).reshape(rows_own, width)
     qkv_own = reorder(jnp.stack([part[:3] for part in weight_own]), x_at)
     qkv_own = qkv_own.transpose(1, 2, 0, 3).reshape(3, rows_own, hd).astype(jnp.float32)
-    expert_out = (slot_gates * dot32(hidden, down_w)).astype(LOW)
-    returned = [expert_out[:capacity]] + [
-        partner(expert_out[r * capacity : (r + 1) * capacity], "exp", r) for r in range(1, exp_count)
-    ]
-    block_out = (mid + dot32(table, jnp.concatenate(returned, axis=0))).astype(LOW)
-
-    block_out = block_out.reshape(groups, local_len, width)
-
-    normed_one_grad = jnp.concatenate(
-        [
-            jnp.sum(part.reshape(groups, split, local_len, half).astype(jnp.float32), axis=1).reshape(tokens, half)
-            for part in (normed_first, normed_second)
-        ],
-        axis=1,
-    )
+
+    normed_one_grad = jnp.concatenate([normed_first, normed_second], axis=2).astype(jnp.float32).reshape(tokens, width)
     scale_one = norm_scale(inputs)
     unit_one = inputs * scale_one
     gain_one_sum = jnp.sum(normed_one_grad * unit_one, axis=0)

time: 1140 us -> 1140 us (level)
  Pallas kernels: 345 us -> 306 us
  starting transfers between devices: 92.4 us -> 116 us
    all_to_all x4 -> x2, waiting for transfers between devices: 69.3 us -> 0.01 us  [exchange_positions(): return lax.all_to_all(blocks, SEQ, split_axis=0, concat_axis=0, tiled=True)]
    ppermute x29 -> x31, waiting for transfers between devices: 113 us -> 143 us  [partner(): return lax.ppermute(value, axis, [(i, i ^ offset) for i in range(count)])]
    pallas_call x4, Pallas kernels: 153 us -> 126 us  [attend_backward(): pl.pallas_call(bwd_kernel, name='attend_backward', out_shape=(low, low, l...]
    ppermute x6, waiting for transfers between devices: 2.27 us -> 23.6 us  [step(): lax.ppermute(part, SEQ, [(b, a) for a, b in self.ahead])]
    ppermute x29 -> x31, starting transfers between devices: 28.3 us -> 49.3 us  [partner(): return lax.ppermute(value, axis, [(i, i ^ offset) for i in range(count)])]
    ppermute x8, waiting for transfers between devices: 6.81 us -> 25 us  [step(): self.forward = [lax.ppermute(part, SEQ, self.ahead) for part in parts]]
    ppermute x4, starting transfers between devices: 2.63 us -> 19.9 us  [step(): self.forward = lax.ppermute(self.forward, SEQ, self.ahead)]
    all_to_all x4 -> x2, starting transfers between devices: 26.5 us -> 14 us  [exchange_positions(): return lax.all_to_all(blocks, SEQ, split_axis=0, concat_axis=0, tiled=True)]
  transfers between devices with their start and end apart: 57 -> 59, of which waited for: 19 -> 24; matrix products, arithmetic and copies ran while one was open for 25% -> 25% of each run, Pallas kernels for 30% -> 27%
where the time goes in v6:
time: 1140 us; the launch traced here: 1130 us
  Pallas kernels  306 us (27%)
  waiting for transfers between devices  298 us (26%)
  matrix products  188 us (16%)
  starting transfers between devices  116 us (10%)
  local copies, waits for them, and re-layouts  101 us (9%)
  other arithmetic  93.4 us (8%)
  between operations  28.5 us (2%)
    ppermute x31, waiting for transfers between devices, partner(): return lax.ppermute(value, axis, [(i, i ^ offset) for i in range(count)])  143 us
    pallas_call x4, Pallas kernels, attend_backward(): pl.pallas_call(bwd_kernel, name='attend_backward', out_shape=(low, low, l...  126 us
    pallas_call x4, Pallas kernels, expert_block(): pl.pallas_call(expert_kernel, name='expert_block', out_shape=(whole, whol...  121 us
    dot_general x16, matrix products, dot_tn(): lax.dot_general(a, b, (((0,), (0,)), ((), ())), preferred_element_type=jn...  96.4 us
    ppermute x4, waiting for transfers between devices, step(): self.forward = lax.ppermute(self.forward, SEQ, self.ahead)  61.1 us
    pallas_call x1, Pallas kernels, attend_forward(): pl.pallas_call(fwd_kernel, name='attend_forward', out_shape=(jax.ShapeDty...  59.1 us
    dot_general x9, matrix products, dot32(): return jnp.dot(a, b, preferred_element_type=jnp.float32)  59 us
    ppermute x31, starting transfers between devices, partner(): return lax.ppermute(value, axis, [(i, i ^ offset) for i in range(count)])  49.3 us
  transfers between devices with their start and end apart: 59, of which 24 were waited for; matrix products, arithmetic and copies ran while one was open for 25% of the time, Pallas kernels for 27%

profile of v6, /device:TPU:0, one launch (start us, length us, event | category | flops | bytes accessed | tf_op | source)
XLA Modules:
  0.0 1131.7 jit_solution(6099089660858071829)
XLA Ops:
  91.2 16.0 %collective-permute-done.3 = bf16[2,2,2,32,2688]{4,3,2,1,0:T(8,128)(2,1)S(1)} collective-permute-done((bf16[2,2,2,32,2688]{4,3,2,1,0:T(8,128)(2,1)S(1)}, bf16[2,2,2,32,2688]{4,3,2,1,0:T(8,128)(2,1)S(1)}, u32[]{:S(2)}, u32[]{:S(2)}) %collective-permute-start.3) | collective-permute-done | bytes 1376288 | tf_op jit(solution)/shard_map/ppermute | solution.py:504
  109.4 17.1 %collective-permute-done.5 = bf16[256,1024]{1,0:T(8,128)(2,1)S(1)} collective-permute-done((bf16[256,1024]{1,0:T(8,128)(2,1)S(1)}, bf16[256,1024]{1,0:T(8,128)(2,1)S(1)}, u32[]{:S(2)}, u32[]{:S(2)}) %collective-permute-start.5) | collective-permute-done | bytes 524320 | tf_op jit(solution)/shard_map/ppermute | solution.py:504
  201.5 24.6 %collective-permute-done.12 = bf16[128,5632]{1,0:T(8,128)(2,1)} collective-permute-done((bf16[128,5632]{1,0:T(8,128)(2,1)}, bf16[128,5632]{1,0:T(8,128)(2,1)}, u32[]{:S(2)}, u32[]{:S(2)}) %collective-permute-start.12) | collective-permute-done | bytes 1441824 | tf_op jit(solution)/shard_map/ppermute | solution.py:568
  234.5 59.1 %attend_forward.1 = (bf16[2048,512]{1,0:T(8,128)(2,1)}, f32[4,2,2048]{2,1,0:T(2,128)S(1)}) custom-call(s32[2,8]{1,0:T(2,128)S(1)} %pad_add_fusion.ranges, f32[8,2]{1,0:T(8,128)S(1)} %maximum_convert_fusion.ends, s32[1]{0:T(128)} %bitcast.22.own, bf16[2048,1536]{1,0:T(8,128)(2,1)} %convolution_convert_fusion.q_ref.k_ref.v_ref, ...), custom_call_target="tpu_custom_call" | custom-call | flops 8589934592 | bytes 8388608 | tf_op jit(solution)/shard_map/attend_forward/pallas_call | solution.py:168
  322.8 20.8 %collective-permute-done.19 = bf16[128,5632]{1,0:T(8,128)(2,1)} collective-permute-done((bf16[128,5632]{1,0:T(8,128)(2,1)}, bf16[128,5632]{1,0:T(8,128)(2,1)}, u32[]{:S(2)}, u32[]{:S(2)}) %collective-permute-start.19) | collective-permute-done | bytes 1441824 | tf_op jit(solution)/shard_map/ppermute | solution.py:568
  352.0 32.6 %collective-permute-done.20 = bf16[128,5632]{1,0:T(8,128)(2,1)S(1)} collective-permute-done((bf16[128,5632]{1,0:T(8,128)(2,1)}, bf16[128,5632]{1,0:T(8,128)(2,1)S(1)}, u32[]{:S(2)}, u32[]{:S(2)}) %collective-permute-start.20) | collective-permute-done | bytes 1441824 | tf_op jit(solution)/shard_map/ppermute | solution.py:571
  385.8 15.7 %collective-permute-done.21 = bf16[128,5632]{1,0:T(8,128)(2,1)S(1)} collective-permute-done((bf16[128,5632]{1,0:T(8,128)(2,1)}, bf16[128,5632]{1,0:T(8,128)(2,1)S(1)}, u32[]{:S(2)}, u32[]{:S(2)}) %collective-permute-start.21) | collective-permute-done | bytes 1441824 | tf_op jit(solution)/shard_map/ppermute | solution.py:568
  441.9 30.1 %expert_block.4 = (bf16[2560,2816]{1,0:T(8,128)(2,1)}, bf16[2560,2816]{1,0:T(8,128)(2,1)}, bf16[2560,2816]{1,0:T(8,128)(2,1)}, bf16[656,1024]{1,0:T(8,128)(2,1)S(1)}) custom-call(s32[1]{0:T(128)} %constant.354.clone.1.own_ref, bf16[656,1024]{1,0:T(8,128)(2,1)S(1)} %copy-done.20, bf16[640,1024]{1,0:T(8,128)(2,1)S(1)} %copy-done.36, ...), custom_call_target="tpu_custom_call" | custom-call | flops 18454937600 | bytes 28114944 | tf_op jit(solution)/shard_map/expert_block/pallas_call | solution.py:465
  472.0 30.0 %expert_block.5 = (bf16[2560,2816]{1,0:T(8,128)(2,1)}, bf16[2560,2816]{1,0:T(8,128)(2,1)}, bf16[2560,2816]{1,0:T(8,128)(2,1)}, bf16[656,1024]{1,0:T(8,128)(2,1)S(1)}) custom-call(s32[1]{0:T(128)} %constant.354.clone.1.own_ref, bf16[656,1024]{1,0:T(8,128)(2,1)S(1)} %collective-permute-done.23.x_ref, ...), custom_call_target="tpu_custom_call", output_to_operand_aliasing={{0}: (6, {}), {1}: (7, {}), {2}: (8, {})} | custom-call | flops 18454937600 | bytes 28114944 | tf_op jit(solution)/shard_map/expert_block/pallas_call | solution.py:465
  504.0 30.9 %expert_block.6 = (bf16[2560,2816]{1,0:T(8,128)(2,1)}, bf16[2560,2816]{1,0:T(8,128)(2,1)}, bf16[2560,2816]{1,0:T(8,128)(2,1)}, bf16[656,1024]{1,0:T(8,128)(2,1)S(1)}) custom-call(s32[1]{0:T(128)} %constant.354.clone.1.own_ref, bf16[656,1024]{1,0:T(8,128)(2,1)} %collective-permute-done.25.x_ref, ...), custom_call_target="tpu_custom_call", output_to_operand_aliasing={{0}: (6, {}), {1}: (7, {}), {2}: (8, {})} | custom-call | flops 18454937600 | bytes 28114944 | tf_op jit(solution)/shard_map/expert_block/pallas_call | solution.py:465
  535.0 30.1 %expert_block.7 = (bf16[2560,2816]{1,0:T(8,128)(2,1)}, bf16[2560,2816]{1,0:T(8,128)(2,1)}, bf16[2560,2816]{1,0:T(8,128)(2,1)}, bf16[656,1024]{1,0:T(8,128)(2,1)S(1)}) custom-call(s32[1]{0:T(128)} %constant.354.clone.1.own_ref, bf16[656,1024]{1,0:T(8,128)(2,1)S(1)} %collective-permute-done.22.x_ref, ...), custom_call_target="tpu_custom_call", output_to_operand_aliasing={{0}: (6, {}), {1}: (7, {}), {2}: (8, {})} | custom-call | flops 18454937600 | bytes 28114944 | tf_op jit(solution)/shard_map/expert_block/pallas_call | solution.py:465
  620.2 22.8 %convolution_convert_fusion.2 = bf16[1024,2816]{1,0:T(8,128)(2,1)} fusion(bf16[2560,2816]{1,0:T(8,128)(2,1)} %get-tuple-element.190, bf16[640,1024]{1,0:T(8,128)(2,1)} %slice.284, bf16[640,1024]{1,0:T(8,128)(2,1)} %slice.283, bf16[640,1024]{1,0:T(8,128)(2,1)} %slice.282, bf16[640,1024]{1,0:T(8,128)(2,1)} %slice.281), kind=kOutput, calls=%fused_computation.21 | convolution fusion | flops 14787805184 | bytes 25427968 | tf_op jit(solution)/shard_map/dot_general | solution.py:499
  643.1 22.6 %convolution_convert_fusion.3 = bf16[1024,2816]{1,0:T(8,128)(2,1)} fusion(bf16[2560,2816]{1,0:T(8,128)(2,1)} %get-tuple-element.189, bf16[640,1024]{1,0:T(8,128)(2,1)} %slice.284, bf16[640,1024]{1,0:T(8,128)(2,1)} %slice.283, bf16[640,1024]{1,0:T(8,128)(2,1)} %slice.282, bf16[640,1024]{1,0:T(8,128)(2,1)S(1)} %copy-done.69), kind=kOutput, calls=%fused_computation.22 | convolution fusion | flops 14787805184 | bytes 25427968 | tf_op jit(solution)/shard_map/dot_general | solution.py:499
  665.7 17.7 %convolution_convert_fusion.1 = bf16[2816,1024]{1,0:T(8,128)(2,1)} fusion(bf16[2560,2816]{1,0:T(8,128)(2,1)S(1)} %bitcast.275, bf16[640,1024]{1,0:T(8,128)(2,1)S(1)} %copy-done.31, bf16[640,1024]{1,0:T(8,128)(2,1)S(1)} %copy-done.28, bf16[640,1024]{1,0:T(8,128)(2,1)S(1)} %copy-done.25, bf16[640,1024]{1,0:T(8,128)(2,1)S(1)} %copy-done.37, ...), kind=kOutput, calls=%fused_computation.20 | convolution fusion | flops 14793048064 | bytes 25438208 | tf_op jit(solution)/shard_map/dot_general | solution.py:499
  694.9 31.7 %attend_backward.4 = (bf16[2048,512]{1,0:T(8,128)(2,1)S(1)}, bf16[2048,512]{1,0:T(8,128)(2,1)S(1)}, bf16[2048,512]{1,0:T(8,128)(2,1)S(1)}, f32[2,3,512]{2,1,0:T(4,128)S(1)}, f32[2,2,256]{2,1,0:T(2,128)S(1)}) custom-call(s32[2,8]{1,0:T(2,128)S(1)} %copy-done.35, f32[8,2]{1,0:T(8,128)S(1)} %copy-done.33, s32[2]{0:T(128)S(1)} %get-tuple-element.392.own, ...), custom_call_target="tpu_custom_call" | custom-call | flops 5368709120 | bytes 4194304 | tf_op jit(solution)/shard_map/attend_backward/pallas_call | solution.py:347
  733.7 18.3 %collective-permute-done.28 = bf16[128,2816]{1,0:T(8,128)(2,1)S(1)} collective-permute-done((bf16[128,2816]{1,0:T(8,128)(2,1)S(1)}, bf16[128,2816]{1,0:T(8,128)(2,1)S(1)}, u32[]{:S(2)}, u32[]{:S(2)}) %collective-permute-start.28) | collective-permute-done | bytes 720928 | tf_op jit(solution)/shard_map/ppermute | solution.py:618
  752.0 14.6 %collective-permute-done.30 = bf16[128,2816]{1,0:T(8,128)(2,1)S(1)} collective-permute-done((bf16[128,2816]{1,0:T(8,128)(2,1)S(1)}, bf16[128,2816]{1,0:T(8,128)(2,1)S(1)}, u32[]{:S(2)}, u32[]{:S(2)}) %collective-permute-start.30) | collective-permute-done | bytes 720928 | tf_op jit(solution)/shard_map/ppermute | solution.py:621
  778.7 31.4 %attend_backward.5 = (bf16[2048,512]{1,0:T(8,128)(2,1)S(1)}, bf16[2048,512]{1,0:T(8,128)(2,1)S(1)}, bf16[2048,512]{1,0:T(8,128)(2,1)S(1)}, f32[2,3,512]{2,1,0:T(4,128)S(1)}, f32[2,2,256]{2,1,0:T(2,128)S(1)}) custom-call(s32[2,8]{1,0:T(2,128)S(1)} %copy-done.35, f32[8,2]{1,0:T(8,128)S(1)} %copy-done.33, ...), custom_call_target="tpu_custom_call", output_to_operand_aliasing={{0}: (12, {}), {1}: (13, {}), {2}: (14, {})} | custom-call | flops 5368709120 | bytes 4194304 | tf_op jit(solution)/shard_map/attend_backward/pallas_call | solution.py:347
  831.3 31.4 %attend_backward.6 = (bf16[2048,512]{1,0:T(8,128)(2,1)S(1)}, bf16[2048,512]{1,0:T(8,128)(2,1)S(1)}, bf16[2048,512]{1,0:T(8,128)(2,1)S(1)}, f32[2,3,512]{2,1,0:T(4,128)S(1)}, f32[2,2,256]{2,1,0:T(2,128)S(1)}) custom-call(s32[2,8]{1,0:T(2,128)S(1)} %copy-done.35, f32[8,2]{1,0:T(8,128)S(1)} %copy-done.33, ...), custom_call_target="tpu_custom_call", output_to_operand_aliasing={{0}: (12, {}), {1}: (13, {}), {2}: (14, {})} | custom-call | flops 5368709120 | bytes 4194304 | tf_op jit(solution)/shard_map/attend_backward/pallas_call | solution.py:347
  872.3 31.6 %attend_backward.7 = (bf16[2048,512]{1,0:T(8,128)(2,1)S(1)}, bf16[2048,512]{1,0:T(8,128)(2,1)S(1)}, bf16[2048,512]{1,0:T(8,128)(2,1)S(1)}, f32[2,3,512]{2,1,0:T(4,128)S(1)}, f32[2,2,256]{2,1,0:T(2,128)S(1)}) custom-call(s32[2,8]{1,0:T(2,128)S(1)} %copy-done.35, f32[8,2]{1,0:T(8,128)S(1)} %copy-done.33, ...), custom_call_target="tpu_custom_call", output_to_operand_aliasing={{0}: (12, {}), {1}: (13, {}), {2}: (14, {})} | custom-call | flops 5368709120 | bytes 4194304 | tf_op jit(solution)/shard_map/attend_backward/pallas_call | solution.py:347
  957.8 18.4 %collective-permute-done.42 = bf16[4,256,512]{2,1,0:T(8,128)(2,1)} collective-permute-done((bf16[4,256,512]{2,1,0:T(8,128)(2,1)S(1)}, bf16[4,256,512]{2,1,0:T(8,128)(2,1)}, u32[]{:S(2)}, u32[]{:S(2)}) %collective-permute-start.42) | collective-permute-done | bytes 1048608 | tf_op jit(solution)/shard_map/ppermute | solution.py:504
  993.9 16.9 %multiply_convert_fusion = bf16[2560,1024]{1,0:T(8,128)(2,1)} fusion(bf16[2560,2816]{1,0:T(8,128)(2,1)S(1)} %bitcast.277, bf16[2816,1024]{1,0:T(8,128)(2,1)S(1)} %bitcast.273, f32[2560]{0:T(1024)S(1)} %pad_maximum_fusion.22), kind=kOutput, calls=%fused_computation.7 | convolution fusion | flops 14769192960 | bytes 25438208 | tf_op jit(solution)/shard_map/dot_general | solution.py:491
  1034.5 15.2 %collective-permute-done.49 = bf16[5,2,2,32,512]{4,3,0,2,1:T(8,128)(2,1)S(1)} collective-permute-done((bf16[5,2,2,32,512]{4,3,0,2,1:T(8,128)(2,1)S(1)}, bf16[5,2,2,32,512]{4,3,0,2,1:T(8,128)(2,1)S(1)}, u32[]{:S(2)}, u32[]{:S(2)}) %collective-permute-start.49) | collective-permute-done | bytes 655392 | tf_op jit(solution)/shard_map/ppermute | solution.py:504
  1059.0 16.3 %collective-permute-done.50 = bf16[5,2,32,512]{3,2,0,1:T(8,128)(2,1)S(1)} collective-permute-done((bf16[5,2,32,512]{3,2,0,1:T(8,128)(2,1)S(1)}, bf16[5,2,32,512]{3,2,0,1:T(8,128)(2,1)S(1)}, u32[]{:S(2)}, u32[]{:S(2)}) %collective-permute-start.50) | collective-permute-done | bytes 327712 | tf_op jit(solution)/shard_map/ppermute | solution.py:504
  (584 shorter events, 507.2 us)
Async XLA Ops:
  7.2 429.4 %all-gather.2.cloned.1.call-start = ((), (), s32[]{:S(2)}) async-start(), calls=%async_computation.6 | async-start | bytes 6488064 | tf_op jit(solution)/shard_map/all_gather | solution.py:727
  85.6 54.4 %collective-permute-start.8 = (bf16[256,1024]{1,0:T(8,128)(2,1)}, bf16[256,1024]{1,0:T(8,128)(2,1)}, u32[]{:S(2)}, u32[]{:S(2)}) collective-permute-start(bf16[256,1024]{1,0:T(8,128)(2,1)} %get-tuple-element.311), channel_id=1, source_target_pairs={{0,4},{4,0},{1,5},{5,1},{2,6},{6,2},{3,7},{7,3},{8,12},{12,8},{9,1... | collective-permute-start | bytes 1572872 | tf_op jit(solution)/shard_map/ppermute | solution.py:504
  163.4 62.6 %collective-permute-start.12 = (bf16[128,5632]{1,0:T(8,128)(2,1)}, bf16[128,5632]{1,0:T(8,128)(2,1)}, u32[]{:S(2)}, u32[]{:S(2)}) collective-permute-start(bf16[128,5632]{1,0:T(8,128)(2,1)} %pad_maximum_fusion.4), channel_id=1, source_target_pairs={{0,8},{8,16},{16,24},{24,28},{28,20},{20,12},{12,4},{4,0},{1,9},{9... | collective-permute-start | bytes 4325384 | tf_op jit(solution)/shard_map/ppermute | solution.py:568
  174.9 54.3 %collective-permute-start.13 = (bf16[128,5632]{1,0:T(8,128)(2,1)}, bf16[128,5632]{1,0:T(8,128)(2,1)}, u32[]{:S(2)}, u32[]{:S(2)}) collective-permute-start(bf16[128,5632]{1,0:T(8,128)(2,1)} %pad_maximum_fusion.4), channel_id=1, source_target_pairs={{8,0},{16,8},{24,16},{28,24},{20,28},{12,20},{4,12},{0,4},{9,1},{1... | collective-permute-start | bytes 4325384 | tf_op jit(solution)/shard_map/ppermute | solution.py:571
  229.6 66.6 %collective-permute-start.14 = (bf16[128,5632]{1,0:T(8,128)(2,1)}, bf16[128,5632]{1,0:T(8,128)(2,1)}, u32[]{:S(2)}, u32[]{:S(2)}) collective-permute-start(bf16[128,5632]{1,0:T(8,128)(2,1)} %collective-permute-done.12), channel_id=1, source_target_pairs={{0,8},{8,16},{16,24},{24,28},{28,20},{20,12},{12,4},{4,0},{1,9},{9... | collective-permute-start | bytes 4325384 | tf_op jit(solution)/shard_map/ppermute | solution.py:568
  232.2 73.4 %collective-permute-start.15 = (bf16[128,5632]{1,0:T(8,128)(2,1)}, bf16[128,5632]{1,0:T(8,128)(2,1)S(1)}, u32[]{:S(2)}, u32[]{:S(2)}) collective-permute-start(bf16[128,5632]{1,0:T(8,128)(2,1)} %collective-permute-done.13), channel_id=1, source_target_pairs={{8,0},{16,8},{24,16},{28,24},{20,28},{12,20},{4,12},{0,4},{9,1},{1... | collective-permute-start | bytes 4325384 | tf_op jit(solution)/shard_map/ppermute | solution.py:571
  232.5 77.0 %collective-permute-start.16 = (bf16[640,1024]{1,0:T(8,128)(2,1)}, bf16[640,1024]{1,0:T(8,128)(2,1)S(1)}, u32[]{:S(2)}, u32[]{:S(2)}) collective-permute-start(bf16[640,1024]{1,0:T(8,128)(2,1)} %convolution_convert_fusion.12), channel_id=1, source_target_pairs={{0,1},{1,0},{2,3},{3,2},{4,5},{5,4},{6,7},{7,6},{8,9},{9,8},{10,11... | collective-permute-start | bytes 3932168 | tf_op jit(solution)/shard_map/ppermute | solution.py:504
  232.6 78.0 %collective-permute-start.17 = (bf16[640,1024]{1,0:T(8,128)(2,1)}, bf16[640,1024]{1,0:T(8,128)(2,1)S(1)}, u32[]{:S(2)}, u32[]{:S(2)}) collective-permute-start(bf16[640,1024]{1,0:T(8,128)(2,1)} %convolution_convert_fusion.11), channel_id=1, source_target_pairs={{0,2},{1,3},{2,0},{3,1},{4,6},{5,7},{6,4},{7,5},{8,10},{9,11},{10,... | collective-permute-start | bytes 3932168 | tf_op jit(solution)/shard_map/ppermute | solution.py:504
  232.8 78.9 %collective-permute-start.18 = (bf16[640,1024]{1,0:T(8,128)(2,1)}, bf16[640,1024]{1,0:T(8,128)(2,1)S(1)}, u32[]{:S(2)}, u32[]{:S(2)}) collective-permute-start(bf16[640,1024]{1,0:T(8,128)(2,1)} %convolution_convert_fusion.10), channel_id=1, source_target_pairs={{0,3},{1,2},{2,1},{3,0},{4,7},{5,6},{6,5},{7,4},{8,11},{9,10},{10,... | collective-permute-start | bytes 3932168 | tf_op jit(solution)/shard_map/ppermute | solution.py:504
  312.7 90.0 %all-to-all-start = ((bf16[8,256,512]{2,1,0:T(8,128)(2,1)}), bf16[8,256,512]{2,1,0:T(8,128)(2,1)}, u32[]{:S(2)}, u32[]{:S(2)}) async-start(bf16[8,256,512]{2,1,0:T(8,128)(2,1)} %bitcast.38), calls=%async_computation | async-start | bytes 4194304 | tf_op jit(solution)/shard_map/all_to_all | solution.py:778
  318.3 66.3 %collective-permute-start.20 = (bf16[128,5632]{1,0:T(8,128)(2,1)}, bf16[128,5632]{1,0:T(8,128)(2,1)S(1)}, u32[]{:S(2)}, u32[]{:S(2)}) collective-permute-start(bf16[128,5632]{1,0:T(8,128)(2,1)} %copy-done.66), channel_id=1, source_target_pairs={{8,0},{16,8},{24,16},{28,24},{20,28},{12,20},{4,12},{0,4},{9,1},{1... | collective-permute-start | bytes 4325384 | tf_op jit(solution)/shard_map/ppermute | solution.py:571
  343.6 57.9 %collective-permute-start.21 = (bf16[128,5632]{1,0:T(8,128)(2,1)}, bf16[128,5632]{1,0:T(8,128)(2,1)S(1)}, u32[]{:S(2)}, u32[]{:S(2)}) collective-permute-start(bf16[128,5632]{1,0:T(8,128)(2,1)} %collective-permute-done.19), channel_id=1, source_target_pairs={{0,8},{8,16},{16,24},{24,28},{28,20},{20,12},{12,4},{4,0},{1,9},{9... | collective-permute-start | bytes 4325384 | tf_op jit(solution)/shard_map/ppermute | solution.py:568
  421.9 50.1 %collective-permute-start.23 = (bf16[656,1024]{1,0:T(8,128)(2,1)}, bf16[656,1024]{1,0:T(8,128)(2,1)S(1)}, u32[]{:S(2)}, u32[]{:S(2)}) collective-permute-start(bf16[656,1024]{1,0:T(8,128)(2,1)} %pad_maximum_fusion.8), channel_id=1, source_target_pairs={{0,2},{1,3},{2,0},{3,1},{4,6},{5,7},{6,4},{7,5},{8,10},{9,11},{10,... | collective-permute-start | bytes 4030472 | tf_op jit(solution)/shard_map/ppermute | solution.py:504
  431.0 103.9 %collective-permute-start.22 = (bf16[656,1024]{1,0:T(8,128)(2,1)}, bf16[656,1024]{1,0:T(8,128)(2,1)S(1)}, u32[]{:S(2)}, u32[]{:S(2)}) collective-permute-start(bf16[656,1024]{1,0:T(8,128)(2,1)} %pad_maximum_fusion.7), channel_id=1, source_target_pairs={{0,1},{1,0},{2,3},{3,2},{4,5},{5,4},{6,7},{7,6},{8,9},{9,8},{10,11... | collective-permute-start | bytes 4030472 | tf_op jit(solution)/shard_map/ppermute | solution.py:504
  433.7 70.3 %collective-permute-start.25 = (bf16[656,1024]{1,0:T(8,128)(2,1)}, bf16[656,1024]{1,0:T(8,128)(2,1)}, u32[]{:S(2)}, u32[]{:S(2)}) collective-permute-start(bf16[656,1024]{1,0:T(8,128)(2,1)} %pad_maximum_fusion.9), channel_id=1, source_target_pairs={{0,3},{1,2},{2,1},{3,0},{4,7},{5,6},{6,5},{7,4},{8,11},{9,10},{10,... | collective-permute-start | bytes 4030472 | tf_op jit(solution)/shard_map/ppermute | solution.py:504
  610.5 72.9 %all-to-all-start.1 = ((bf16[8,256,512]{2,1,0:T(8,128)(2,1)}), bf16[8,256,512]{2,1,0:T(8,128)(2,1)S(1)}, u32[]{:S(2)}, u32[]{:S(2)}) async-start(bf16[8,256,512]{2,1,0:T(8,128)(2,1)} %bitcast.291), calls=%async_computation.1 | async-start | bytes 4194304 | tf_op jit(solution)/shard_map/all_to_all | solution.py:778
  620.1 288.7 %reduce-scatter.2.cloned.1.call-start = ((), (), s32[]{:S(2)}) async-start(), calls=%async_computation.7 | async-start | bytes 6488064 | tf_op jit(solution)/shard_map/reduce_scatter | solution.py:859
  692.4 59.6 %collective-permute-start.28 = (bf16[128,2816]{1,0:T(8,128)(2,1)S(1)}, bf16[128,2816]{1,0:T(8,128)(2,1)S(1)}, u32[]{:S(2)}, u32[]{:S(2)}) collective-permute-start(bf16[128,2816]{1,0:T(8,128)(2,1)S(1)} %get-tuple-element.298), channel_id=1, source_target_pairs={{0,8},{8,16},{16,24},{24,28},{28,20},{20,12},{12,4},{4,0},{1,9},{9... | collective-permute-start | bytes 2162696 | tf_op jit(solution)/shard_map/ppermute | solution.py:618
  694.4 72.2 %collective-permute-start.30 = (bf16[128,2816]{1,0:T(8,128)(2,1)S(1)}, bf16[128,2816]{1,0:T(8,128)(2,1)S(1)}, u32[]{:S(2)}, u32[]{:S(2)}) collective-permute-start(bf16[128,2816]{1,0:T(8,128)(2,1)S(1)} %get-tuple-element.297), channel_id=1, source_target_pairs={{8,0},{16,8},{24,16},{28,24},{20,28},{12,20},{4,12},{0,4},{9,1},{1... | collective-permute-start | bytes 2162696 | tf_op jit(solution)/shard_map/ppermute | solution.py:621
  773.0 43.9 %collective-permute-start.32 = (bf16[128,2816]{1,0:T(8,128)(2,1)}, bf16[128,2816]{1,0:T(8,128)(2,1)S(1)}, u32[]{:S(2)}, u32[]{:S(2)}) collective-permute-start(bf16[128,2816]{1,0:T(8,128)(2,1)} %get-tuple-element.294), channel_id=1, source_target_pairs={{0,8},{8,16},{16,24},{24,28},{28,20},{20,12},{12,4},{4,0},{1,9},{9... | collective-permute-start | bytes 2162696 | tf_op jit(solution)/shard_map/ppermute | solution.py:618
  773.0 43.9 %collective-permute-start.34 = (bf16[128,2816]{1,0:T(8,128)(2,1)}, bf16[128,2816]{1,0:T(8,128)(2,1)S(1)}, u32[]{:S(2)}, u32[]{:S(2)}) collective-permute-start(bf16[128,2816]{1,0:T(8,128)(2,1)} %get-tuple-element.293), channel_id=1, source_target_pairs={{8,0},{16,8},{24,16},{28,24},{20,28},{12,20},{4,12},{0,4},{9,1},{1... | collective-permute-start | bytes 2162696 | tf_op jit(solution)/shard_map/ppermute | solution.py:621
  1032.6 48.2 %collective-permute-start.46 = (bf16[640,1024]{1,0:T(8,128)(2,1)}, bf16[640,1024]{1,0:T(8,128)(2,1)}, u32[]{:S(2)}, u32[]{:S(2)}) collective-permute-start(bf16[640,1024]{1,0:T(8,128)(2,1)} %get-tuple-element.303), channel_id=1, source_target_pairs={{0,1},{1,0},{2,3},{3,2},{4,5},{5,4},{6,7},{7,6},{8,9},{9,8},{10,11... | collective-permute-start | bytes 3932168 | tf_op jit(solution)/shard_map/ppermute | solution.py:504
  1032.6 48.2 %collective-permute-start.47 = (bf16[640,1024]{1,0:T(8,128)(2,1)}, bf16[640,1024]{1,0:T(8,128)(2,1)}, u32[]{:S(2)}, u32[]{:S(2)}) collective-permute-start(bf16[640,1024]{1,0:T(8,128)(2,1)} %get-tuple-element.302), channel_id=1, source_target_pairs={{0,2},{1,3},{2,0},{3,1},{4,6},{5,7},{6,4},{7,5},{8,10},{9,11},{10,... | collective-permute-start | bytes 3932168 | tf_op jit(solution)/shard_map/ppermute | solution.py:504
  1034.4 57.3 %collective-permute-start.48 = (bf16[640,1024]{1,0:T(8,128)(2,1)}, bf16[640,1024]{1,0:T(8,128)(2,1)}, u32[]{:S(2)}, u32[]{:S(2)}) collective-permute-start(bf16[640,1024]{1,0:T(8,128)(2,1)} %get-tuple-element.301), channel_id=1, source_target_pairs={{0,3},{1,2},{2,1},{3,0},{4,7},{5,6},{6,5},{7,4},{8,11},{9,10},{10,... | collective-permute-start | bytes 3932168 | tf_op jit(solution)/shard_map/ppermute | solution.py:504
  (149 other events, 4592.6 us)
Sparse Core Ops, SparseCore 0:
  175.3 130.3 all-gather.1
  683.6 164.0 reduce-scatter.1

commit v7 on v6

--- a/solution.py
+++ b/solution.py
@@ -686,6 +686,9 @@
 
     input_r = reorder(block_in, z_at)
 
+    arrived = [[None] * split for _ in range(groups)]
+    for rz in reversed(range(groups)):
+        arrived[rz][0] = partner(input_r[rz], "z", rz) if rz else input_r[0]
     small = jnp.concatenate(
         [
             gain_attention[:, None],
@@ -705,21 +708,17 @@
     shares = [lax.dynamic_index_in_dim(share, x_at ^ r, 0, keepdims=False) for r in range(split)]
     shares = [shares[0]] + [partner(shares[r], "x", r) for r in range(1, split)]
     by_x = reorder(jnp.stack(shares), x_at)
-    packed = gather_double(by_x, [("z", b) for b in z_bits[:1]])
-
-    packed, input_r = lax.optimization_barrier((packed, input_r))
-    arrived = [[input_r[rz]] + [None] * (split - 1) for rz in range(groups)]
-    for rz in reversed(range(1, groups)):
-        arrived[rz][0] = partner(input_r[rz], "z", rz)
     for rx in range(1, split):
         arrived[0][rx] = partner(arrived[0][0], "x", rx)
-    packed = gather_double(packed, [("z", b) for b in z_bits[1:]] + [("exp", b) for b in e_bits[:-1]])
+    packed = gather_double(by_x, [("z", b) for b in z_bits])
     near = [arrived[rz][0] for rz in range(1, groups)]
     packed, near = lax.optimization_barrier((packed, near))
     for rz in range(1, groups):
         arrived[rz][0] = near[rz - 1]
         for rx in range(1, split):
             arrived[rz][rx] = partner(arrived[rz][0], "x", rx)
+    packed = gather_double(packed, [("exp", b) for b in e_bits[:-1]])
+    packed, arrived = lax.optimization_barrier((packed, arrived))
     sequence = jnp.stack([block for line in arrived for block in line]).reshape(length, width)
 
     gate_up_own = jnp.concatenate([w_gate[0].astype(LOW), w_up[0].astype(LOW)], axis=1)
@@ -876,6 +875,15 @@
             pair, qkv, context_heads, contexts, log_totals, query_side, key_side, ranges, rows, ends, own, tile, tuple(grads)
         )
         grads = ring.after(grads)
+        if pair == 0:
+            grads, hidden = lax.optimization_barrier((grads, hidden))
+            expert_out = (slot_gates * dot32(hidden, down_w)).astype(LOW)
+            expert_out = reorder(expert_out.reshape(exp_count, capacity, width), e_at)
+            returned = lax.all_to_all(expert_out, "exp", split_axis=0, concat_axis=0, tiled=True)
+        if pair == min(1, pairs - 1):
+            grads, expert_out = lax.optimization_barrier((grads, expert_out))
+        if pair == pairs - 1:
+            grads, returned = lax.optimization_barrier((grads, returned))
         diag.append(pair_diag)
         far.append(pair_far)
     diag, far = jnp.concatenate(diag), jnp.concatenate(far)
@@ -900,7 +908,7 @@
 
     sides = [normed_part[:, rx].astype(LOW) for rx in range(1, split)]
     first = [partner(side[:, :, :half], "x", rx) for rx, side in enumerate(sides, 1)]
-    first, hidden, rest = lax.optimization_barrier((first, hidden, [side[:, :, half:] for side in sides]))
+    first, rest = lax.optimization_barrier((first, [side[:, :, half:] for side in sides]))
 
     def send_back(own_part, coming):
         total = own_part + sum(part.astype(jnp.float32) for part in coming)
@@ -910,19 +918,14 @@
     normed_first = send_back(normed_part[:, 0, :, :half], first)
     rest = [partner(side, "x", rx) for rx, side in enumerate(rest, 1)]
     normed_second = send_back(normed_part[:, 0, :, half:], rest)
-    expert_out = (slot_gates * dot32(hidden, down_w)).astype(LOW)
     weight_part = scatter_halve(
         weight_sum.reshape((3 + out_parts,) + (2,) * (nz + nx + ne) + (rows_own, head_width)), halving[:ne]
     )
-    weight_part, expert_out = lax.optimization_barrier((weight_part, expert_out))
     weight_part = scatter_halve(weight_part, halving[ne:]).reshape(3 + out_parts, split, rows_own, head_width)
     weight_own = [lax.dynamic_index_in_dim(weight_part, x_at ^ r, 1, keepdims=False) for r in range(split)]
     weight_own = [weight_own[0]] + [partner(weight_own[r], "x", r) for r in range(1, split)]
-    returned = [expert_out[:capacity]] + [
-        partner(expert_out[r * capacity : (r + 1) * capacity], "exp", r) for r in range(1, exp_count)
-    ]
-    normed_second, returned, weight_own = lax.optimization_barrier((normed_second, returned, weight_own))
-    block_out = (mid + dot32(table, jnp.concatenate(returned, axis=0))).astype(LOW)
+    normed_second, weight_own = lax.optimization_barrier((normed_second, weight_own))
+    block_out = (mid + dot32(table, reorder(returned, e_at).reshape(slot_count, width))).astype(LOW)
 
     block_out = block_out.reshape(groups, local_len, width)
     out_w_out = sum(part[3:].astype(jnp.float32) for part in weight_own)

time: 1140 us -> 1120 us (0.982)
  waiting for transfers between devices: 298 us -> 276 us
    ppermute x8, waiting for transfers between devices: 25 us -> 3.22 us  [step(): self.forward = [lax.ppermute(part, SEQ, self.ahead) for part in parts]]
    ppermute x8, starting transfers between devices: 7.03 us -> 24.6 us  [step(): self.forward = [lax.ppermute(part, SEQ, self.ahead) for part in parts]]
    ppermute x4, starting transfers between devices: 19.9 us -> 2.82 us  [step(): self.forward = lax.ppermute(self.forward, SEQ, self.ahead)]
    ppermute x31 -> x28, starting transfers between devices: 49.3 us -> 35.8 us  [partner(): return lax.ppermute(value, axis, [(i, i ^ offset) for i in range(count)])]
    ppermute x31 -> x28, waiting for transfers between devices: 143 us -> 134 us  [partner(): return lax.ppermute(value, axis, [(i, i ^ offset) for i in range(count)])]
    unnamed x247 -> x242, local copies, waits for them, and re-layouts: 37.9 us -> 43.7 us
  transfers between devices with their start and end apart: 59 -> 57, of which waited for: 24 -> 19; matrix products, arithmetic and copies ran while one was open for 25% -> 28% of each run, Pallas kernels for 27% -> 27%
where the time goes in v7:
time: 1120 us; the launch traced here: 1110 us
  Pallas kernels  298 us (27%)
  waiting for transfers between devices  276 us (25%)
  matrix products  195 us (17%)
  starting transfers between devices  107 us (10%)
  local copies, waits for them, and re-layouts  106 us (9%)
  other arithmetic  101 us (9%)
  between operations  28.1 us (3%)
    ppermute x28, waiting for transfers between devices, partner(): return lax.ppermute(value, axis, [(i, i ^ offset) for i in range(count)])  134 us
    pallas_call x4, Pallas kernels, expert_block(): pl.pallas_call(expert_kernel, name='expert_block', out_shape=(whole, whol...  121 us
    pallas_call x4, Pallas kernels, attend_backward(): pl.pallas_call(bwd_kernel, name='attend_backward', out_shape=(low, low, l...  120 us
    dot_general x16, matrix products, dot_tn(): lax.dot_general(a, b, (((0,), (0,)), ((), ())), preferred_element_type=jn...  101 us
    ppermute x4, waiting for transfers between devices, step(): self.forward = lax.ppermute(self.forward, SEQ, self.ahead)  64.3 us
    dot_general x9, matrix products, dot32(): return jnp.dot(a, b, preferred_element_type=jnp.float32)  63.9 us
    pallas_call x1, Pallas kernels, attend_forward(): pl.pallas_call(fwd_kernel, name='attend_forward', out_shape=(jax.ShapeDty...  56.8 us
    ppermute x3, waiting for transfers between devices, step(): lax.ppermute(self.backward, SEQ, [(b, a) for a, b in self.ahead])  54 us
  transfers between devices with their start and end apart: 57, of which 19 were waited for; matrix products, arithmetic and copies ran while one was open for 28% of the time, Pallas kernels for 27%

profile of v7, /device:TPU:0, one launch (start us, length us, event | category | flops | bytes accessed | tf_op | source)
XLA Modules:
  0.0 1109.8 jit_solution(6556611265158112926)
XLA Ops:
  61.4 22.5 %collective-permute-done.1 = bf16[2,32,2688]{2,1,0:T(8,128)(2,1)} collective-permute-done((bf16[2,32,2688]{2,1,0:T(8,128)(2,1)S(1)}, bf16[2,32,2688]{2,1,0:T(8,128)(2,1)}, u32[]{:S(2)}, u32[]{:S(2)}) %collective-permute-start.1) | collective-permute-done | bytes 344096 | tf_op jit(solution)/shard_map/ppermute | solution.py:504
  109.8 24.1 %collective-permute-done.6 = bf16[2,2,2,32,2688]{4,3,2,1,0:T(8,128)(2,1)S(1)} collective-permute-done((bf16[2,2,2,32,2688]{4,3,2,1,0:T(8,128)(2,1)S(1)}, bf16[2,2,2,32,2688]{4,3,2,1,0:T(8,128)(2,1)S(1)}, u32[]{:S(2)}, u32[]{:S(2)}) %collective-permute-start.6) | collective-permute-done | bytes 1376288 | tf_op jit(solution)/shard_map/ppermute | solution.py:504
  183.8 24.6 %collective-permute-done.12 = bf16[128,5632]{1,0:T(8,128)(2,1)} collective-permute-done((bf16[128,5632]{1,0:T(8,128)(2,1)}, bf16[128,5632]{1,0:T(8,128)(2,1)}, u32[]{:S(2)}, u32[]{:S(2)}) %collective-permute-start.12) | collective-permute-done | bytes 1441824 | tf_op jit(solution)/shard_map/ppermute | solution.py:568
  215.5 56.8 %attend_forward.1 = (bf16[2048,512]{1,0:T(8,128)(2,1)}, f32[4,2,2048]{2,1,0:T(2,128)S(1)}) custom-call(s32[2,8]{1,0:T(2,128)S(1)} %pad_add_fusion.ranges, f32[8,2]{1,0:T(8,128)S(1)} %maximum_convert_fusion.ends, s32[1]{0:T(128)} %bitcast.23.own, bf16[2048,1536]{1,0:T(8,128)(2,1)} %convolution_convert_fusion.q_ref.k_ref.v_ref, ...), custom_call_target="tpu_custom_call" | custom-call | flops 8589934592 | bytes 8388608 | tf_op jit(solution)/shard_map/attend_forward/pallas_call | solution.py:168
  274.9 17.3 %collective-permute-done.15 = bf16[128,5632]{1,0:T(8,128)(2,1)S(1)} collective-permute-done((bf16[128,5632]{1,0:T(8,128)(2,1)}, bf16[128,5632]{1,0:T(8,128)(2,1)S(1)}, u32[]{:S(2)}, u32[]{:S(2)}) %collective-permute-start.15) | collective-permute-done | bytes 1441824 | tf_op jit(solution)/shard_map/ppermute | solution.py:571
  308.6 21.3 %collective-permute-done.19 = bf16[128,5632]{1,0:T(8,128)(2,1)} collective-permute-done((bf16[128,5632]{1,0:T(8,128)(2,1)}, bf16[128,5632]{1,0:T(8,128)(2,1)}, u32[]{:S(2)}, u32[]{:S(2)}) %collective-permute-start.19) | collective-permute-done | bytes 1441824 | tf_op jit(solution)/shard_map/ppermute | solution.py:568
  334.1 34.4 %collective-permute-done.20 = bf16[128,5632]{1,0:T(8,128)(2,1)S(1)} collective-permute-done((bf16[128,5632]{1,0:T(8,128)(2,1)}, bf16[128,5632]{1,0:T(8,128)(2,1)S(1)}, u32[]{:S(2)}, u32[]{:S(2)}) %collective-permute-start.20) | collective-permute-done | bytes 1441824 | tf_op jit(solution)/shard_map/ppermute | solution.py:571
  369.7 18.4 %collective-permute-done.21 = bf16[128,5632]{1,0:T(8,128)(2,1)S(1)} collective-permute-done((bf16[128,5632]{1,0:T(8,128)(2,1)}, bf16[128,5632]{1,0:T(8,128)(2,1)S(1)}, u32[]{:S(2)}, u32[]{:S(2)}) %collective-permute-start.21) | collective-permute-done | bytes 1441824 | tf_op jit(solution)/shard_map/ppermute | solution.py:568
  424.1 30.0 %expert_block.4 = (bf16[2560,2816]{1,0:T(8,128)(2,1)}, bf16[2560,2816]{1,0:T(8,128)(2,1)}, bf16[2560,2816]{1,0:T(8,128)(2,1)}, bf16[656,1024]{1,0:T(8,128)(2,1)S(1)}) custom-call(s32[1]{0:T(128)} %constant.372.clone.1.own_ref, bf16[656,1024]{1,0:T(8,128)(2,1)S(1)} %copy-done.25, bf16[640,1024]{1,0:T(8,128)(2,1)S(1)} %copy-done.42, ...), custom_call_target="tpu_custom_call" | custom-call | flops 18454937600 | bytes 28114944 | tf_op jit(solution)/shard_map/expert_block/pallas_call | solution.py:465
  454.1 30.0 %expert_block.5 = (bf16[2560,2816]{1,0:T(8,128)(2,1)}, bf16[2560,2816]{1,0:T(8,128)(2,1)}, bf16[2560,2816]{1,0:T(8,128)(2,1)}, bf16[656,1024]{1,0:T(8,128)(2,1)S(1)}) custom-call(s32[1]{0:T(128)} %constant.372.clone.1.own_ref, bf16[656,1024]{1,0:T(8,128)(2,1)S(1)} %collective-permute-done.23.x_ref, ...), custom_call_target="tpu_custom_call", output_to_operand_aliasing={{0}: (6, {}), {1}: (7, {}), {2}: (8, {})} | custom-call | flops 18454937600 | bytes 28114944 | tf_op jit(solution)/shard_map/expert_block/pallas_call | solution.py:465
  485.5 30.9 %expert_block.6 = (bf16[2560,2816]{1,0:T(8,128)(2,1)}, bf16[2560,2816]{1,0:T(8,128)(2,1)}, bf16[2560,2816]{1,0:T(8,128)(2,1)}, bf16[656,1024]{1,0:T(8,128)(2,1)S(1)}) custom-call(s32[1]{0:T(128)} %constant.372.clone.1.own_ref, bf16[656,1024]{1,0:T(8,128)(2,1)} %collective-permute-done.25.x_ref, ...), custom_call_target="tpu_custom_call", output_to_operand_aliasing={{0}: (6, {}), {1}: (7, {}), {2}: (8, {})} | custom-call | flops 18454937600 | bytes 28114944 | tf_op jit(solution)/shard_map/expert_block/pallas_call | solution.py:465
  517.5 30.1 %expert_block.7 = (bf16[2560,2816]{1,0:T(8,128)(2,1)}, bf16[2560,2816]{1,0:T(8,128)(2,1)}, bf16[2560,2816]{1,0:T(8,128)(2,1)}, bf16[656,1024]{1,0:T(8,128)(2,1)S(1)}) custom-call(s32[1]{0:T(128)} %constant.372.clone.1.own_ref, bf16[656,1024]{1,0:T(8,128)(2,1)S(1)} %collective-permute-done.22.x_ref, ...), custom_call_target="tpu_custom_call", output_to_operand_aliasing={{0}: (6, {}), {1}: (7, {}), {2}: (8, {})} | custom-call | flops 18454937600 | bytes 28114944 | tf_op jit(solution)/shard_map/expert_block/pallas_call | solution.py:465
  605.9 22.6 %convolution_convert_fusion.2 = bf16[1024,2816]{1,0:T(8,128)(2,1)} fusion(bf16[2560,2816]{1,0:T(8,128)(2,1)} %get-tuple-element.208, bf16[640,1024]{1,0:T(8,128)(2,1)} %slice.256, bf16[640,1024]{1,0:T(8,128)(2,1)} %slice.255, bf16[640,1024]{1,0:T(8,128)(2,1)} %slice.254, bf16[640,1024]{1,0:T(8,128)(2,1)S(1)} %copy-done.67), kind=kOutput, calls=%fused_computation.21 | convolution fusion | flops 14787805184 | bytes 25427968 | tf_op jit(solution)/shard_map/dot_general | solution.py:499
  628.5 22.5 %convolution_convert_fusion.3 = bf16[1024,2816]{1,0:T(8,128)(2,1)} fusion(bf16[2560,2816]{1,0:T(8,128)(2,1)} %get-tuple-element.207, bf16[640,1024]{1,0:T(8,128)(2,1)} %slice.256, bf16[640,1024]{1,0:T(8,128)(2,1)} %slice.255, bf16[640,1024]{1,0:T(8,128)(2,1)S(1)} %copy-done.68, bf16[640,1024]{1,0:T(8,128)(2,1)S(1)} %copy-done.67), kind=kOutput, calls=%fused_computation.22 | convolution fusion | flops 14787805184 | bytes 25427968 | tf_op jit(solution)/shard_map/dot_general | solution.py:499
  651.1 17.7 %convolution_convert_fusion.1 = bf16[2816,1024]{1,0:T(8,128)(2,1)} fusion(bf16[2560,2816]{1,0:T(8,128)(2,1)S(1)} %bitcast.278, bf16[640,1024]{1,0:T(8,128)(2,1)S(1)} %copy-done.37, bf16[640,1024]{1,0:T(8,128)(2,1)S(1)} %copy-done.34, bf16[640,1024]{1,0:T(8,128)(2,1)S(1)} %copy-done.31, bf16[640,1024]{1,0:T(8,128)(2,1)S(1)} %copy-done.43, ...), kind=kOutput, calls=%fused_computation.20 | convolution fusion | flops 14793048064 | bytes 25438208 | tf_op jit(solution)/shard_map/dot_general | solution.py:499
  685.0 30.1 %attend_backward.4 = (bf16[2048,512]{1,0:T(8,128)(2,1)S(1)}, bf16[2048,512]{1,0:T(8,128)(2,1)S(1)}, bf16[2048,512]{1,0:T(8,128)(2,1)S(1)}, f32[2,3,512]{2,1,0:T(4,128)S(1)}, f32[2,2,256]{2,1,0:T(2,128)S(1)}) custom-call(s32[2,8]{1,0:T(2,128)S(1)} %copy-done.41, f32[8,2]{1,0:T(8,128)S(1)} %copy-done.39, s32[2]{0:T(128)S(1)} %get-tuple-element.413.own, ...), custom_call_target="tpu_custom_call" | custom-call | flops 5368709120 | bytes 4194304 | tf_op jit(solution)/shard_map/attend_backward/pallas_call | solution.py:347
  718.4 17.0 %collective-permute-done.30 = bf16[128,2816]{1,0:T(8,128)(2,1)} collective-permute-done((bf16[128,2816]{1,0:T(8,128)(2,1)}, bf16[128,2816]{1,0:T(8,128)(2,1)}, u32[]{:S(2)}, u32[]{:S(2)}) %collective-permute-start.30) | collective-permute-done | bytes 720928 | tf_op jit(solution)/shard_map/ppermute | solution.py:621
  746.1 17.2 %multiply_convert_fusion = bf16[2560,1024]{1,0:T(8,128)(2,1)S(1)} fusion(bf16[2560,2816]{1,0:T(8,128)(2,1)S(1)} %bitcast.280, bf16[2816,1024]{1,0:T(8,128)(2,1)} %all-gather.2.cloned.1.call-done.wd_ref, f32[2560]{0:T(1024)S(1)} %pad_maximum_fusion.23), kind=kOutput, calls=%fused_computation.7 | convolution fusion | flops 14769192960 | bytes 25438208 | tf_op jit(solution)/shard_map/dot_general | solution.py:491
  777.0 29.8 %attend_backward.5 = (bf16[2048,512]{1,0:T(8,128)(2,1)S(1)}, bf16[2048,512]{1,0:T(8,128)(2,1)S(1)}, bf16[2048,512]{1,0:T(8,128)(2,1)S(1)}, f32[2,3,512]{2,1,0:T(4,128)S(1)}, f32[2,2,256]{2,1,0:T(2,128)S(1)}) custom-call(s32[2,8]{1,0:T(2,128)S(1)} %copy-done.41, f32[8,2]{1,0:T(8,128)S(1)} %copy-done.39, ...), custom_call_target="tpu_custom_call", output_to_operand_aliasing={{0}: (12, {}), {1}: (13, {}), {2}: (14, {})} | custom-call | flops 5368709120 | bytes 4194304 | tf_op jit(solution)/shard_map/attend_backward/pallas_call | solution.py:347
  831.1 29.8 %attend_backward.6 = (bf16[2048,512]{1,0:T(8,128)(2,1)S(1)}, bf16[2048,512]{1,0:T(8,128)(2,1)S(1)}, bf16[2048,512]{1,0:T(8,128)(2,1)S(1)}, f32[2,3,512]{2,1,0:T(4,128)S(1)}, f32[2,2,256]{2,1,0:T(2,128)S(1)}) custom-call(s32[2,8]{1,0:T(2,128)S(1)} %copy-done.41, f32[8,2]{1,0:T(8,128)S(1)} %copy-done.39, ...), custom_call_target="tpu_custom_call", output_to_operand_aliasing={{0}: (12, {}), {1}: (13, {}), {2}: (14, {})} | custom-call | flops 5368709120 | bytes 4194304 | tf_op jit(solution)/shard_map/attend_backward/pallas_call | solution.py:347
  875.9 30.0 %attend_backward.7 = (bf16[2048,512]{1,0:T(8,128)(2,1)S(1)}, bf16[2048,512]{1,0:T(8,128)(2,1)S(1)}, bf16[2048,512]{1,0:T(8,128)(2,1)S(1)}, f32[2,3,512]{2,1,0:T(4,128)S(1)}, f32[2,2,256]{2,1,0:T(2,128)S(1)}) custom-call(s32[2,8]{1,0:T(2,128)S(1)} %copy-done.41, f32[8,2]{1,0:T(8,128)S(1)} %copy-done.39, ...), custom_call_target="tpu_custom_call", output_to_operand_aliasing={{0}: (12, {}), {1}: (13, {}), {2}: (14, {})} | custom-call | flops 5368709120 | bytes 4194304 | tf_op jit(solution)/shard_map/attend_backward/pallas_call | solution.py:347
  968.1 14.5 %collective-permute-done.42 = bf16[4,256,512]{2,1,0:T(8,128)(2,1)S(1)} collective-permute-done((bf16[4,256,512]{2,1,0:T(8,128)(2,1)S(1)}, bf16[4,256,512]{2,1,0:T(8,128)(2,1)S(1)}, u32[]{:S(2)}, u32[]{:S(2)}) %collective-permute-start.42) | collective-permute-done | bytes 1048608 | tf_op jit(solution)/shard_map/ppermute | solution.py:504
  1031.8 13.5 %collective-permute-done.46 = bf16[5,2,2,32,512]{4,3,0,2,1:T(8,128)(2,1)S(1)} collective-permute-done((bf16[5,2,2,32,512]{4,3,0,2,1:T(8,128)(2,1)S(1)}, bf16[5,2,2,32,512]{4,3,0,2,1:T(8,128)(2,1)S(1)}, u32[]{:S(2)}, u32[]{:S(2)}) %collective-permute-start.46) | collective-permute-done | bytes 655392 | tf_op jit(solution)/shard_map/ppermute | solution.py:504
  1052.9 19.9 %collective-permute-done.47 = bf16[5,2,32,512]{3,2,0,1:T(8,128)(2,1)S(1)} collective-permute-done((bf16[5,2,32,512]{3,2,0,1:T(8,128)(2,1)S(1)}, bf16[5,2,32,512]{3,2,0,1:T(8,128)(2,1)S(1)}, u32[]{:S(2)}, u32[]{:S(2)}) %collective-permute-start.47) | collective-permute-done | bytes 327712 | tf_op jit(solution)/shard_map/ppermute | solution.py:504
  (574 shorter events, 476.7 us)
Async XLA Ops:
  7.2 411.6 %all-gather.2.cloned.1.call-start = ((), (), s32[]{:S(2)}) async-start(), calls=%async_computation.7 | async-start | bytes 6488064 | tf_op jit(solution)/shard_map/all_gather | solution.py:726
  19.5 84.8 %collective-permute-start.3 = (bf16[256,1024]{1,0:T(8,128)(2,1)}, bf16[256,1024]{1,0:T(8,128)(2,1)}, u32[]{:S(2)}, u32[]{:S(2)}) collective-permute-start(bf16[256,1024]{1,0:T(8,128)(2,1)} %get-tuple-element.339), channel_id=1, source_target_pairs={{0,8},{8,0},{16,24},{24,16},{1,9},{9,1},{17,25},{25,17},{2,10},{10... | collective-permute-start | bytes 1572872 | tf_op jit(solution)/shard_map/ppermute | solution.py:504
  21.1 83.2 %collective-permute-start.4 = (bf16[256,1024]{1,0:T(8,128)(2,1)}, bf16[256,1024]{1,0:T(8,128)(2,1)}, u32[]{:S(2)}, u32[]{:S(2)}) collective-permute-start(bf16[256,1024]{1,0:T(8,128)(2,1)} %get-tuple-element.338), channel_id=1, source_target_pairs={{0,16},{8,24},{16,0},{24,8},{1,17},{9,25},{17,1},{25,9},{2,18},{10... | collective-permute-start | bytes 1572872 | tf_op jit(solution)/shard_map/ppermute | solution.py:504
  23.7 80.6 %collective-permute-start.5 = (bf16[256,1024]{1,0:T(8,128)(2,1)}, bf16[256,1024]{1,0:T(8,128)(2,1)}, u32[]{:S(2)}, u32[]{:S(2)}) collective-permute-start(bf16[256,1024]{1,0:T(8,128)(2,1)} %get-tuple-element.340), channel_id=1, source_target_pairs={{0,24},{8,16},{16,8},{24,0},{1,25},{9,17},{17,9},{25,1},{2,26},{10... | collective-permute-start | bytes 1572872 | tf_op jit(solution)/shard_map/ppermute | solution.py:504
  23.9 112.1 %collective-permute-start.7 = (bf16[256,1024]{1,0:T(8,128)(2,1)}, bf16[256,1024]{1,0:T(8,128)(2,1)}, u32[]{:S(2)}, u32[]{:S(2)}) collective-permute-start(bf16[256,1024]{1,0:T(8,128)(2,1)} %get-tuple-element.155), channel_id=1, source_target_pairs={{0,4},{4,0},{1,5},{5,1},{2,6},{6,2},{3,7},{7,3},{8,12},{12,8},{9,1... | collective-permute-start | bytes 1572872 | tf_op jit(solution)/shard_map/ppermute | solution.py:504
  153.5 57.2 %collective-permute-start.13 = (bf16[128,5632]{1,0:T(8,128)(2,1)}, bf16[128,5632]{1,0:T(8,128)(2,1)}, u32[]{:S(2)}, u32[]{:S(2)}) collective-permute-start(bf16[128,5632]{1,0:T(8,128)(2,1)} %pad_maximum_fusion.5), channel_id=1, source_target_pairs={{8,0},{16,8},{24,16},{28,24},{20,28},{12,20},{4,12},{0,4},{9,1},{1... | collective-permute-start | bytes 4325384 | tf_op jit(solution)/shard_map/ppermute | solution.py:571
  211.2 63.7 %collective-permute-start.14 = (bf16[128,5632]{1,0:T(8,128)(2,1)}, bf16[128,5632]{1,0:T(8,128)(2,1)}, u32[]{:S(2)}, u32[]{:S(2)}) collective-permute-start(bf16[128,5632]{1,0:T(8,128)(2,1)} %collective-permute-done.12), channel_id=1, source_target_pairs={{0,8},{8,16},{16,24},{24,28},{28,20},{20,12},{12,4},{4,0},{1,9},{9... | collective-permute-start | bytes 4325384 | tf_op jit(solution)/shard_map/ppermute | solution.py:568
  212.8 79.3 %collective-permute-start.15 = (bf16[128,5632]{1,0:T(8,128)(2,1)}, bf16[128,5632]{1,0:T(8,128)(2,1)S(1)}, u32[]{:S(2)}, u32[]{:S(2)}) collective-permute-start(bf16[128,5632]{1,0:T(8,128)(2,1)} %collective-permute-done.13), channel_id=1, source_target_pairs={{8,0},{16,8},{24,16},{28,24},{20,28},{12,20},{4,12},{0,4},{9,1},{1... | collective-permute-start | bytes 4325384 | tf_op jit(solution)/shard_map/ppermute | solution.py:571
  213.5 81.7 %collective-permute-start.16 = (bf16[640,1024]{1,0:T(8,128)(2,1)}, bf16[640,1024]{1,0:T(8,128)(2,1)S(1)}, u32[]{:S(2)}, u32[]{:S(2)}) collective-permute-start(bf16[640,1024]{1,0:T(8,128)(2,1)} %convolution_convert_fusion.12), channel_id=1, source_target_pairs={{0,1},{1,0},{2,3},{3,2},{4,5},{5,4},{6,7},{7,6},{8,9},{9,8},{10,11... | collective-permute-start | bytes 3932168 | tf_op jit(solution)/shard_map/ppermute | solution.py:504
  213.5 82.8 %collective-permute-start.17 = (bf16[640,1024]{1,0:T(8,128)(2,1)}, bf16[640,1024]{1,0:T(8,128)(2,1)S(1)}, u32[]{:S(2)}, u32[]{:S(2)}) collective-permute-start(bf16[640,1024]{1,0:T(8,128)(2,1)} %convolution_convert_fusion.11), channel_id=1, source_target_pairs={{0,2},{1,3},{2,0},{3,1},{4,6},{5,7},{6,4},{7,5},{8,10},{9,11},{10,... | collective-permute-start | bytes 3932168 | tf_op jit(solution)/shard_map/ppermute | solution.py:504
  214.0 83.4 %collective-permute-start.18 = (bf16[640,1024]{1,0:T(8,128)(2,1)}, bf16[640,1024]{1,0:T(8,128)(2,1)S(1)}, u32[]{:S(2)}, u32[]{:S(2)}) collective-permute-start(bf16[640,1024]{1,0:T(8,128)(2,1)} %convolution_convert_fusion.10), channel_id=1, source_target_pairs={{0,3},{1,2},{2,1},{3,0},{4,7},{5,6},{6,5},{7,4},{8,11},{9,10},{10,... | collective-permute-start | bytes 3932168 | tf_op jit(solution)/shard_map/ppermute | solution.py:504
  298.5 90.8 %all-to-all-start = ((bf16[8,256,512]{2,1,0:T(8,128)(2,1)}), bf16[8,256,512]{2,1,0:T(8,128)(2,1)}, u32[]{:S(2)}, u32[]{:S(2)}) async-start(bf16[8,256,512]{2,1,0:T(8,128)(2,1)} %bitcast.39), calls=%async_computation | async-start | bytes 4194304 | tf_op jit(solution)/shard_map/all_to_all | solution.py:777
  304.1 64.4 %collective-permute-start.20 = (bf16[128,5632]{1,0:T(8,128)(2,1)}, bf16[128,5632]{1,0:T(8,128)(2,1)S(1)}, u32[]{:S(2)}, u32[]{:S(2)}) collective-permute-start(bf16[128,5632]{1,0:T(8,128)(2,1)} %copy-done.65), channel_id=1, source_target_pairs={{8,0},{16,8},{24,16},{28,24},{20,28},{12,20},{4,12},{0,4},{9,1},{1... | collective-permute-start | bytes 4325384 | tf_op jit(solution)/shard_map/ppermute | solution.py:571
  329.9 58.3 %collective-permute-start.21 = (bf16[128,5632]{1,0:T(8,128)(2,1)}, bf16[128,5632]{1,0:T(8,128)(2,1)S(1)}, u32[]{:S(2)}, u32[]{:S(2)}) collective-permute-start(bf16[128,5632]{1,0:T(8,128)(2,1)} %collective-permute-done.19), channel_id=1, source_target_pairs={{0,8},{8,16},{16,24},{24,28},{28,20},{20,12},{12,4},{4,0},{1,9},{9... | collective-permute-start | bytes 4325384 | tf_op jit(solution)/shard_map/ppermute | solution.py:568
  412.5 103.9 %collective-permute-start.22 = (bf16[656,1024]{1,0:T(8,128)(2,1)}, bf16[656,1024]{1,0:T(8,128)(2,1)S(1)}, u32[]{:S(2)}, u32[]{:S(2)}) collective-permute-start(bf16[656,1024]{1,0:T(8,128)(2,1)} %pad_maximum_fusion.8), channel_id=1, source_target_pairs={{0,1},{1,0},{2,3},{3,2},{4,5},{5,4},{6,7},{7,6},{8,9},{9,8},{10,11... | collective-permute-start | bytes 4030472 | tf_op jit(solution)/shard_map/ppermute | solution.py:504
  415.3 70.2 %collective-permute-start.25 = (bf16[656,1024]{1,0:T(8,128)(2,1)}, bf16[656,1024]{1,0:T(8,128)(2,1)}, u32[]{:S(2)}, u32[]{:S(2)}) collective-permute-start(bf16[656,1024]{1,0:T(8,128)(2,1)} %pad_maximum_fusion.10), channel_id=1, source_target_pairs={{0,3},{1,2},{2,1},{3,0},{4,7},{5,6},{6,5},{7,4},{8,11},{9,10},{10,... | collective-permute-start | bytes 4030472 | tf_op jit(solution)/shard_map/ppermute | solution.py:504
  592.3 76.5 %all-to-all-start.1 = ((bf16[8,256,512]{2,1,0:T(8,128)(2,1)}), bf16[8,256,512]{2,1,0:T(8,128)(2,1)S(1)}, u32[]{:S(2)}, u32[]{:S(2)}) async-start(bf16[8,256,512]{2,1,0:T(8,128)(2,1)} %bitcast.296), calls=%async_computation.1 | async-start | bytes 4194304 | tf_op jit(solution)/shard_map/all_to_all | solution.py:777
  605.8 305.1 %reduce-scatter.2.cloned.1.call-start = ((), (), s32[]{:S(2)}) async-start(), calls=%async_computation.8 | async-start | bytes 6488064 | tf_op jit(solution)/shard_map/reduce_scatter | solution.py:858
  678.0 57.4 %collective-permute-start.30 = (bf16[128,2816]{1,0:T(8,128)(2,1)}, bf16[128,2816]{1,0:T(8,128)(2,1)}, u32[]{:S(2)}, u32[]{:S(2)}) collective-permute-start(bf16[128,2816]{1,0:T(8,128)(2,1)} %get-tuple-element.319), channel_id=1, source_target_pairs={{8,0},{16,8},{24,16},{28,24},{20,28},{12,20},{4,12},{0,4},{9,1},{1... | collective-permute-start | bytes 2162696 | tf_op jit(solution)/shard_map/ppermute | solution.py:621
  738.8 68.1 %collective-permute-start.33 = (bf16[128,2816]{1,0:T(8,128)(2,1)}, bf16[128,2816]{1,0:T(8,128)(2,1)}, u32[]{:S(2)}, u32[]{:S(2)}) collective-permute-start(bf16[128,2816]{1,0:T(8,128)(2,1)} %get-tuple-element.314), channel_id=1, source_target_pairs={{0,8},{8,16},{16,24},{24,28},{28,20},{20,12},{12,4},{4,0},{1,9},{9... | collective-permute-start | bytes 2162696 | tf_op jit(solution)/shard_map/ppermute | solution.py:618
  738.8 68.1 %collective-permute-start.35 = (bf16[128,2816]{1,0:T(8,128)(2,1)}, bf16[128,2816]{1,0:T(8,128)(2,1)}, u32[]{:S(2)}, u32[]{:S(2)}) collective-permute-start(bf16[128,2816]{1,0:T(8,128)(2,1)} %get-tuple-element.313), channel_id=1, source_target_pairs={{8,0},{16,8},{24,16},{28,24},{20,28},{12,20},{4,12},{0,4},{9,1},{1... | collective-permute-start | bytes 2162696 | tf_op jit(solution)/shard_map/ppermute | solution.py:621
  744.0 62.8 %collective-permute-start.32 = (bf16[128,2816]{1,0:T(8,128)(2,1)}, bf16[128,2816]{1,0:T(8,128)(2,1)}, u32[]{:S(2)}, u32[]{:S(2)}) collective-permute-start(bf16[128,2816]{1,0:T(8,128)(2,1)} %get-tuple-element.316), channel_id=1, source_target_pairs={{0,8},{8,16},{16,24},{24,28},{28,20},{20,12},{12,4},{4,0},{1,9},{9... | collective-permute-start | bytes 2162696 | tf_op jit(solution)/shard_map/ppermute | solution.py:618
  744.1 62.8 %collective-permute-start.34 = (bf16[128,2816]{1,0:T(8,128)(2,1)}, bf16[128,2816]{1,0:T(8,128)(2,1)}, u32[]{:S(2)}, u32[]{:S(2)}) collective-permute-start(bf16[128,2816]{1,0:T(8,128)(2,1)} %get-tuple-element.315), channel_id=1, source_target_pairs={{8,0},{16,8},{24,16},{28,24},{20,28},{12,20},{4,12},{0,4},{9,1},{1... | collective-permute-start | bytes 2162696 | tf_op jit(solution)/shard_map/ppermute | solution.py:621
  766.9 144.1 %all-to-all-start.2 = ((bf16[4,640,1024]{2,1,0:T(8,128)(2,1)}), bf16[4,640,1024]{2,1,0:T(8,128)(2,1)}, u32[]{:S(2)}, u32[]{:S(2)}) async-start(bf16[4,640,1024]{2,1,0:T(8,128)(2,1)} %pad_maximum_fusion.1), calls=%async_computation.2 | async-start | bytes 10485760 | tf_op jit(solution)/shard_map/all_to_all | solution.py:882
  (144 other events, 4326.7 us)
Sparse Core Ops, SparseCore 0:
  155.2 137.1 all-gather.1
  684.0 139.2 reduce-scatter.1

commit v8 on v7

--- a/solution.py
+++ b/solution.py
@@ -394,6 +394,7 @@
         gate_ref[...] = jnp.broadcast_to(gate, (LANES, rows)).T
 
     wg, wu, wd = wg_ref[...], wu_ref[...], wd_ref[...]
+    kept = []
     for start in range(0, rows, chunk):
         at = slice(start, start + chunk)
         x, dy = x_ref[at, :], dy_ref[at, :]
@@ -416,6 +417,8 @@
         h_ref[at, :] = h.astype(jnp.bfloat16)
         dg_ref[at, :] = dg
         du_ref[at, :] = du
+        kept.append((at, dg, du))
+    for at, dg, du in kept:
         acc_ref[at, :] += lax.dot_general(dg, wg, NT, preferred_element_type=jnp.float32) + lax.dot_general(
             du, wu, NT, preferred_element_type=jnp.float32
         )
@@ -549,13 +552,22 @@
     return lax.dynamic_index_in_dim(values, index, 0, keepdims=False)
 
 
+def unwritten(shape, dtype):
+    return pl.pallas_call(
+        lambda out_ref: None,
+        name="unwritten",
+        out_shape=jax.ShapeDtypeStruct(shape, dtype),
+        out_specs=pl.BlockSpec(memory_space=pl.ANY),
+    )()
+
+
 class RingGather:
     def __init__(self, piece, groups, split, own):
         self.order, place, self.ahead = ring_of(groups, split)
         self.count = groups * split
         self.here = pick(place, own)
         self.rows = piece.shape[0]
-        self.whole = jnp.zeros((self.count * self.rows, piece.shape[1]), piece.dtype)
+        self.whole = unwritten((self.count * self.rows, piece.shape[1]), piece.dtype)
         self.whole = lax.dynamic_update_slice_in_dim(self.whole, piece, own * self.rows, 0)
         self.forward = self.backward = piece
         self.round = 0
@@ -843,8 +855,7 @@
     mid_grad = grad_out + norm_back(scale_two, unit_two, gain_two, normed_two_grad)
     attention_grad = mid_grad.astype(LOW)
     context_grad = dot_nt(attention_grad, out_w).astype(LOW)
-    context_grad, up_low, gate_low, hidden = lax.optimization_barrier((context_grad, up_low, gate_low, hidden))
-    down_sum = dot_tn(hidden, slot_grads).astype(LOW)
+    context_grad, up_low, gate_low = lax.optimization_barrier((context_grad, up_low, gate_low))
     gate_sum = dot_tn(slot_rows, gate_low).astype(LOW)
     up_sum = dot_tn(slot_rows, up_low).astype(LOW)
     context_grad = (
@@ -857,10 +868,7 @@
     def scatter_experts(total):
         return lax.psum_scatter(total, SEQ, scatter_dimension=0, tiled=True)
 
-    context_heads, gate_sum, up_sum, down_sum = lax.optimization_barrier(
-        (context_heads, gate_sum, up_sum, down_sum)
-    )
-    down_owned = scatter_experts(down_sum)
+    context_heads, gate_sum, up_sum = lax.optimization_barrier((context_heads, gate_sum, up_sum))
 
     halving = [("exp", b, 1 + nz + nx + ne - 1 - i) for i, b in enumerate(reversed(e_bits))]
     halving += [("z", b, 1 + nz - 1 - i) for i, b in enumerate(reversed(z_bits))]
@@ -877,10 +885,14 @@
         grads = ring.after(grads)
         if pair == 0:
             grads, hidden = lax.optimization_barrier((grads, hidden))
+            down_sum = dot_tn(hidden, slot_grads).astype(LOW)
+            down_owned = scatter_experts(down_sum)
+        if pair == min(1, pairs - 1):
+            grads, hidden, down_sum = lax.optimization_barrier((grads, hidden, down_sum))
             expert_out = (slot_gates * dot32(hidden, down_w)).astype(LOW)
             expert_out = reorder(expert_out.reshape(exp_count, capacity, width), e_at)
             returned = lax.all_to_all(expert_out, "exp", split_axis=0, concat_axis=0, tiled=True)
-        if pair == min(1, pairs - 1):
+        if pair == min(2, pairs - 1):
             grads, expert_out = lax.optimization_barrier((grads, expert_out))
         if pair == pairs - 1:
             grads, returned = lax.optimization_barrier((grads, returned))

time: 1120 us -> 1120 us (level)
  Pallas kernels: 298 us -> 324 us
  starting transfers between devices: 107 us -> 87.4 us
  waiting for transfers between devices: 276 us -> 290 us
    pallas_call x4, Pallas kernels: 120 us -> 147 us  [attend_backward(): pl.pallas_call(bwd_kernel, name='attend_backward', out_shape=(low, low, l...]
    ppermute x8, starting transfers between devices: 24.6 us -> 10.5 us  [step(): self.forward = [lax.ppermute(part, SEQ, self.ahead) for part in parts]]
    pallas_call x4, Pallas kernels: 121 us -> 109 us  [expert_block(): pl.pallas_call(expert_kernel, name='expert_block', out_shape=(whole, whol...]
    unnamed x242 -> x240, local copies, waits for them, and re-layouts: 43.7 us -> 42.5 us
  transfers between devices with their start and end apart: 57 -> 57, of which waited for: 19 -> 21; matrix products, arithmetic and copies ran while one was open for 28% -> 25% of each run, Pallas kernels for 27% -> 29%
where the time goes in v8:
time: 1120 us
  Pallas kernels  324 us (29%)
  waiting for transfers between devices  290 us (26%)
  matrix products  193 us (17%)
  local copies, waits for them, and re-layouts  97.3 us (9%)
  other arithmetic  96.9 us (9%)
  starting transfers between devices  87.4 us (8%)
  between operations  28.3 us (3%)
    pallas_call x4, Pallas kernels, attend_backward(): pl.pallas_call(bwd_kernel, name='attend_backward', out_shape=(low, low, l...  147 us
    ppermute x28, waiting for transfers between devices, partner(): return lax.ppermute(value, axis, [(i, i ^ offset) for i in range(count)])  137 us
    pallas_call x4, Pallas kernels, expert_block(): pl.pallas_call(expert_kernel, name='expert_block', out_shape=(whole, whol...  109 us
    dot_general x16, matrix products, dot_tn(): lax.dot_general(a, b, (((0,), (0,)), ((), ())), preferred_element_type=jn...  101 us
    ppermute x4, waiting for transfers between devices, step(): self.forward = lax.ppermute(self.forward, SEQ, self.ahead)  69.2 us
    pallas_call x1, Pallas kernels, attend_forward(): pl.pallas_call(fwd_kernel, name='attend_forward', out_shape=(jax.ShapeDty...  67.4 us
    dot_general x9, matrix products, dot32(): return jnp.dot(a, b, preferred_element_type=jnp.float32)  63 us
    ppermute x3, waiting for transfers between devices, step(): lax.ppermute(self.backward, SEQ, [(b, a) for a, b in self.ahead])  43.3 us
  transfers between devices with their start and end apart: 57, of which 21 were waited for; matrix products, arithmetic and copies ran while one was open for 25% of the time, Pallas kernels for 29%

profile of v8, /device:TPU:0, one launch (start us, length us, event | category | flops | bytes accessed | tf_op | source)
XLA Modules:
  0.0 1117.2 jit_solution(14630059572916947806)
XLA Ops:
  62.0 21.9 %collective-permute-done.1 = bf16[2,32,2688]{2,1,0:T(8,128)(2,1)} collective-permute-done((bf16[2,32,2688]{2,1,0:T(8,128)(2,1)S(1)}, bf16[2,32,2688]{2,1,0:T(8,128)(2,1)}, u32[]{:S(2)}, u32[]{:S(2)}) %collective-permute-start.1) | collective-permute-done | bytes 344096 | tf_op jit(solution)/shard_map/ppermute | solution.py:507
  109.8 24.1 %collective-permute-done.6 = bf16[2,2,2,32,2688]{4,3,2,1,0:T(8,128)(2,1)S(1)} collective-permute-done((bf16[2,2,2,32,2688]{4,3,2,1,0:T(8,128)(2,1)S(1)}, bf16[2,2,2,32,2688]{4,3,2,1,0:T(8,128)(2,1)S(1)}, u32[]{:S(2)}, u32[]{:S(2)}) %collective-permute-start.6) | collective-permute-done | bytes 1376288 | tf_op jit(solution)/shard_map/ppermute | solution.py:507
  178.9 29.5 %collective-permute-done.12 = bf16[128,5632]{1,0:T(8,128)(2,1)} collective-permute-done((bf16[128,5632]{1,0:T(8,128)(2,1)}, bf16[128,5632]{1,0:T(8,128)(2,1)}, u32[]{:S(2)}, u32[]{:S(2)}) %collective-permute-start.12) | collective-permute-done | bytes 1441824 | tf_op jit(solution)/shard_map/ppermute | solution.py:580
  215.5 67.4 %attend_forward.1 = (bf16[2048,512]{1,0:T(8,128)(2,1)}, f32[4,2,2048]{2,1,0:T(2,128)S(1)}) custom-call(s32[2,8]{1,0:T(2,128)S(1)} %pad_add_fusion.ranges, f32[8,2]{1,0:T(8,128)S(1)} %maximum_convert_fusion.ends, s32[1]{0:T(128)} %bitcast.23.own, bf16[2048,1536]{1,0:T(8,128)(2,1)} %convolution_convert_fusion.q_ref.k_ref.v_ref, ...), custom_call_target="tpu_custom_call" | custom-call | flops 8589934592 | bytes 8388608 | tf_op jit(solution)/shard_map/attend_forward/pallas_call | solution.py:168
  308.7 21.2 %collective-permute-done.19 = bf16[128,5632]{1,0:T(8,128)(2,1)} collective-permute-done((bf16[128,5632]{1,0:T(8,128)(2,1)}, bf16[128,5632]{1,0:T(8,128)(2,1)}, u32[]{:S(2)}, u32[]{:S(2)}) %collective-permute-start.19) | collective-permute-done | bytes 1441824 | tf_op jit(solution)/shard_map/ppermute | solution.py:580
  334.2 34.4 %collective-permute-done.20 = bf16[128,5632]{1,0:T(8,128)(2,1)S(1)} collective-permute-done((bf16[128,5632]{1,0:T(8,128)(2,1)}, bf16[128,5632]{1,0:T(8,128)(2,1)S(1)}, u32[]{:S(2)}, u32[]{:S(2)}) %collective-permute-start.20) | collective-permute-done | bytes 1441824 | tf_op jit(solution)/shard_map/ppermute | solution.py:583
  369.8 18.4 %collective-permute-done.21 = bf16[128,5632]{1,0:T(8,128)(2,1)S(1)} collective-permute-done((bf16[128,5632]{1,0:T(8,128)(2,1)}, bf16[128,5632]{1,0:T(8,128)(2,1)S(1)}, u32[]{:S(2)}, u32[]{:S(2)}) %collective-permute-start.21) | collective-permute-done | bytes 1441824 | tf_op jit(solution)/shard_map/ppermute | solution.py:580
  424.1 26.9 %expert_block.4 = (bf16[2560,2816]{1,0:T(8,128)(2,1)}, bf16[2560,2816]{1,0:T(8,128)(2,1)}, bf16[2560,2816]{1,0:T(8,128)(2,1)}, bf16[656,1024]{1,0:T(8,128)(2,1)S(1)}) custom-call(s32[1]{0:T(128)} %constant.371.clone.1.own_ref, bf16[656,1024]{1,0:T(8,128)(2,1)S(1)} %copy-done.26, bf16[640,1024]{1,0:T(8,128)(2,1)S(1)} %copy-done.42, ...), custom_call_target="tpu_custom_call" | custom-call | flops 18454937600 | bytes 28114944 | tf_op jit(solution)/shard_map/expert_block/pallas_call | solution.py:468
  451.0 27.0 %expert_block.5 = (bf16[2560,2816]{1,0:T(8,128)(2,1)}, bf16[2560,2816]{1,0:T(8,128)(2,1)}, bf16[2560,2816]{1,0:T(8,128)(2,1)}, bf16[656,1024]{1,0:T(8,128)(2,1)S(1)}) custom-call(s32[1]{0:T(128)} %constant.371.clone.1.own_ref, bf16[656,1024]{1,0:T(8,128)(2,1)S(1)} %collective-permute-done.23.x_ref, ...), custom_call_target="tpu_custom_call", output_to_operand_aliasing={{0}: (6, {}), {1}: (7, {}), {2}: (8, {})} | custom-call | flops 18454937600 | bytes 28114944 | tf_op jit(solution)/shard_map/expert_block/pallas_call | solution.py:468
  479.8 28.0 %expert_block.6 = (bf16[2560,2816]{1,0:T(8,128)(2,1)}, bf16[2560,2816]{1,0:T(8,128)(2,1)}, bf16[2560,2816]{1,0:T(8,128)(2,1)}, bf16[656,1024]{1,0:T(8,128)(2,1)S(1)}) custom-call(s32[1]{0:T(128)} %constant.371.clone.1.own_ref, bf16[656,1024]{1,0:T(8,128)(2,1)} %collective-permute-done.25.x_ref, ...), custom_call_target="tpu_custom_call", output_to_operand_aliasing={{0}: (6, {}), {1}: (7, {}), {2}: (8, {})} | custom-call | flops 18454937600 | bytes 28114944 | tf_op jit(solution)/shard_map/expert_block/pallas_call | solution.py:468
  509.5 27.4 %expert_block.7 = (bf16[2560,2816]{1,0:T(8,128)(2,1)}, bf16[2560,2816]{1,0:T(8,128)(2,1)}, bf16[2560,2816]{1,0:T(8,128)(2,1)}, bf16[656,1024]{1,0:T(8,128)(2,1)S(1)}) custom-call(s32[1]{0:T(128)} %constant.371.clone.1.own_ref, bf16[656,1024]{1,0:T(8,128)(2,1)S(1)} %collective-permute-done.22.x_ref, ...), custom_call_target="tpu_custom_call", output_to_operand_aliasing={{0}: (6, {}), {1}: (7, {}), {2}: (8, {})} | custom-call | flops 18454937600 | bytes 28114944 | tf_op jit(solution)/shard_map/expert_block/pallas_call | solution.py:468
  578.8 13.2 %all-to-all-start.1 = ((bf16[8,256,512]{2,1,0:T(8,128)(2,1)}), bf16[8,256,512]{2,1,0:T(8,128)(2,1)S(1)}, u32[]{:S(2)}, u32[]{:S(2)}) async-start(bf16[8,256,512]{2,1,0:T(8,128)(2,1)} %bitcast.294), calls=%async_computation.1 | async-start | bytes 4194304 | tf_op jit(solution)/shard_map/all_to_all | solution.py:789
  592.1 22.6 %convolution_convert_fusion.2 = bf16[1024,2816]{1,0:T(8,128)(2,1)} fusion(bf16[2560,2816]{1,0:T(8,128)(2,1)} %get-tuple-element.209, bf16[640,1024]{1,0:T(8,128)(2,1)} %slice.256, bf16[640,1024]{1,0:T(8,128)(2,1)} %slice.255, bf16[640,1024]{1,0:T(8,128)(2,1)} %slice.254, bf16[640,1024]{1,0:T(8,128)(2,1)S(1)} %copy-done.68), kind=kOutput, calls=%fused_computation.21 | convolution fusion | flops 14787805184 | bytes 25427968 | tf_op jit(solution)/shard_map/dot_general | solution.py:502
  614.7 20.8 %convolution_convert_fusion.3 = bf16[1024,2816]{1,0:T(8,128)(2,1)} fusion(bf16[2560,2816]{1,0:T(8,128)(2,1)} %get-tuple-element.208, bf16[640,1024]{1,0:T(8,128)(2,1)S(1)} %copy-done.71, bf16[640,1024]{1,0:T(8,128)(2,1)S(1)} %copy-done.70, bf16[640,1024]{1,0:T(8,128)(2,1)S(1)} %copy-done.69, bf16[640,1024]{1,0:T(8,128)(2,1)S(1)} %copy-done.68), kind=kOutput, calls=%fused_computation.22 | convolution fusion | flops 14787805184 | bytes 25427968 | tf_op jit(solution)/shard_map/dot_general | solution.py:502
  648.9 37.1 %attend_backward.4 = (bf16[2048,512]{1,0:T(8,128)(2,1)S(1)}, bf16[2048,512]{1,0:T(8,128)(2,1)S(1)}, bf16[2048,512]{1,0:T(8,128)(2,1)S(1)}, f32[2,3,512]{2,1,0:T(4,128)S(1)}, f32[2,2,256]{2,1,0:T(2,128)S(1)}) custom-call(s32[2,8]{1,0:T(2,128)S(1)} %copy-done.41, f32[8,2]{1,0:T(8,128)S(1)} %copy-done.39, s32[2]{0:T(128)S(1)} %get-tuple-element.417.own, ...), custom_call_target="tpu_custom_call" | custom-call | flops 5368709120 | bytes 4194304 | tf_op jit(solution)/shard_map/attend_backward/pallas_call | solution.py:347
  690.1 20.9 %convolution_convert_fusion.1 = bf16[2816,1024]{1,0:T(8,128)(2,1)} fusion(bf16[2560,2816]{1,0:T(8,128)(2,1)} %get-tuple-element.248, bf16[640,1024]{1,0:T(8,128)(2,1)S(1)} %copy-done.37, bf16[640,1024]{1,0:T(8,128)(2,1)S(1)} %copy-done.34, bf16[640,1024]{1,0:T(8,128)(2,1)S(1)} %copy-done.31, bf16[640,1024]{1,0:T(8,128)(2,1)S(1)} %copy-done.43, ...), kind=kOutput, calls=%fused_computation.20 | convolution fusion | flops 14793048064 | bytes 25438208 | tf_op jit(solution)/shard_map/dot_general | solution.py:502
  723.4 36.7 %attend_backward.5 = (bf16[2048,512]{1,0:T(8,128)(2,1)S(1)}, bf16[2048,512]{1,0:T(8,128)(2,1)S(1)}, bf16[2048,512]{1,0:T(8,128)(2,1)S(1)}, f32[2,3,512]{2,1,0:T(4,128)S(1)}, f32[2,2,256]{2,1,0:T(2,128)S(1)}) custom-call(s32[2,8]{1,0:T(2,128)S(1)} %copy-done.41, f32[8,2]{1,0:T(8,128)S(1)} %copy-done.39, ...), custom_call_target="tpu_custom_call", output_to_operand_aliasing={{0}: (12, {}), {1}: (13, {}), {2}: (14, {})} | custom-call | flops 5368709120 | bytes 4194304 | tf_op jit(solution)/shard_map/attend_backward/pallas_call | solution.py:347
  765.4 26.6 %collective-permute-done.34 = bf16[128,2816]{1,0:T(8,128)(2,1)S(1)} collective-permute-done((bf16[128,2816]{1,0:T(8,128)(2,1)S(1)}, bf16[128,2816]{1,0:T(8,128)(2,1)S(1)}, u32[]{:S(2)}, u32[]{:S(2)}) %collective-permute-start.34) | collective-permute-done | bytes 720928 | tf_op jit(solution)/shard_map/ppermute | solution.py:633
  797.1 17.6 %multiply_convert_fusion = bf16[2560,1024]{1,0:T(8,128)(2,1)S(1)} fusion(bf16[2560,2816]{1,0:T(8,128)(2,1)} %get-tuple-element.248, bf16[2816,1024]{1,0:T(8,128)(2,1)S(1)} %bitcast.278, f32[2560]{0:T(1024)S(1)} %pad_maximum_fusion.23), kind=kOutput, calls=%fused_computation.7 | convolution fusion | flops 14769192960 | bytes 25438208 | tf_op jit(solution)/shard_map/dot_general | solution.py:494
  834.9 36.4 %attend_backward.6 = (bf16[2048,512]{1,0:T(8,128)(2,1)S(1)}, bf16[2048,512]{1,0:T(8,128)(2,1)S(1)}, bf16[2048,512]{1,0:T(8,128)(2,1)S(1)}, f32[2,3,512]{2,1,0:T(4,128)S(1)}, f32[2,2,256]{2,1,0:T(2,128)S(1)}) custom-call(s32[2,8]{1,0:T(2,128)S(1)} %copy-done.41, f32[8,2]{1,0:T(8,128)S(1)} %copy-done.39, ...), custom_call_target="tpu_custom_call", output_to_operand_aliasing={{0}: (12, {}), {1}: (13, {}), {2}: (14, {})} | custom-call | flops 5368709120 | bytes 4194304 | tf_op jit(solution)/shard_map/attend_backward/pallas_call | solution.py:347
  881.5 36.8 %attend_backward.7 = (bf16[2048,512]{1,0:T(8,128)(2,1)S(1)}, bf16[2048,512]{1,0:T(8,128)(2,1)S(1)}, bf16[2048,512]{1,0:T(8,128)(2,1)S(1)}, f32[2,3,512]{2,1,0:T(4,128)S(1)}, f32[2,2,256]{2,1,0:T(2,128)S(1)}) custom-call(s32[2,8]{1,0:T(2,128)S(1)} %copy-done.41, f32[8,2]{1,0:T(8,128)S(1)} %copy-done.39, ...), custom_call_target="tpu_custom_call", output_to_operand_aliasing={{0}: (12, {}), {1}: (13, {}), {2}: (14, {})} | custom-call | flops 5368709120 | bytes 4194304 | tf_op jit(solution)/shard_map/attend_backward/pallas_call | solution.py:347
  970.8 16.7 %collective-permute-done.42 = bf16[4,256,512]{2,1,0:T(8,128)(2,1)S(1)} collective-permute-done((bf16[4,256,512]{2,1,0:T(8,128)(2,1)S(1)}, bf16[4,256,512]{2,1,0:T(8,128)(2,1)S(1)}, u32[]{:S(2)}, u32[]{:S(2)}) %collective-permute-start.42) | collective-permute-done | bytes 1048608 | tf_op jit(solution)/shard_map/ppermute | solution.py:507
  1036.5 14.5 %collective-permute-done.46 = bf16[5,2,2,32,512]{4,3,0,2,1:T(8,128)(2,1)S(1)} collective-permute-done((bf16[5,2,2,32,512]{4,3,0,2,1:T(8,128)(2,1)S(1)}, bf16[5,2,2,32,512]{4,3,0,2,1:T(8,128)(2,1)S(1)}, u32[]{:S(2)}, u32[]{:S(2)}) %collective-permute-start.46) | collective-permute-done | bytes 655392 | tf_op jit(solution)/shard_map/ppermute | solution.py:507
  1059.0 20.0 %collective-permute-done.47 = bf16[5,2,32,512]{3,2,0,1:T(8,128)(2,1)S(1)} collective-permute-done((bf16[5,2,32,512]{3,2,0,1:T(8,128)(2,1)S(1)}, bf16[5,2,32,512]{3,2,0,1:T(8,128)(2,1)S(1)}, u32[]{:S(2)}, u32[]{:S(2)}) %collective-permute-start.47) | collective-permute-done | bytes 327712 | tf_op jit(solution)/shard_map/ppermute | solution.py:507
  (571 shorter events, 442.8 us)
Async XLA Ops:
  7.2 411.6 %all-gather.2.cloned.1.call-start = ((), (), s32[]{:S(2)}) async-start(), calls=%async_computation.7 | async-start | bytes 6488064 | tf_op jit(solution)/shard_map/all_gather | solution.py:738
  19.5 84.7 %collective-permute-start.3 = (bf16[256,1024]{1,0:T(8,128)(2,1)}, bf16[256,1024]{1,0:T(8,128)(2,1)}, u32[]{:S(2)}, u32[]{:S(2)}) collective-permute-start(bf16[256,1024]{1,0:T(8,128)(2,1)} %get-tuple-element.343), channel_id=1, source_target_pairs={{0,8},{8,0},{16,24},{24,16},{1,9},{9,1},{17,25},{25,17},{2,10},{10... | collective-permute-start | bytes 1572872 | tf_op jit(solution)/shard_map/ppermute | solution.py:507
  21.1 83.2 %collective-permute-start.4 = (bf16[256,1024]{1,0:T(8,128)(2,1)}, bf16[256,1024]{1,0:T(8,128)(2,1)}, u32[]{:S(2)}, u32[]{:S(2)}) collective-permute-start(bf16[256,1024]{1,0:T(8,128)(2,1)} %get-tuple-element.342), channel_id=1, source_target_pairs={{0,16},{8,24},{16,0},{24,8},{1,17},{9,25},{17,1},{25,9},{2,18},{10... | collective-permute-start | bytes 1572872 | tf_op jit(solution)/shard_map/ppermute | solution.py:507
  23.7 80.6 %collective-permute-start.5 = (bf16[256,1024]{1,0:T(8,128)(2,1)}, bf16[256,1024]{1,0:T(8,128)(2,1)}, u32[]{:S(2)}, u32[]{:S(2)}) collective-permute-start(bf16[256,1024]{1,0:T(8,128)(2,1)} %get-tuple-element.344), channel_id=1, source_target_pairs={{0,24},{8,16},{16,8},{24,0},{1,25},{9,17},{17,9},{25,1},{2,26},{10... | collective-permute-start | bytes 1572872 | tf_op jit(solution)/shard_map/ppermute | solution.py:507
  23.9 112.1 %collective-permute-start.7 = (bf16[256,1024]{1,0:T(8,128)(2,1)}, bf16[256,1024]{1,0:T(8,128)(2,1)}, u32[]{:S(2)}, u32[]{:S(2)}) collective-permute-start(bf16[256,1024]{1,0:T(8,128)(2,1)} %get-tuple-element.157), channel_id=1, source_target_pairs={{0,4},{4,0},{1,5},{5,1},{2,6},{6,2},{3,7},{7,3},{8,12},{12,8},{9,1... | collective-permute-start | bytes 1572872 | tf_op jit(solution)/shard_map/ppermute | solution.py:507
  152.8 55.6 %collective-permute-start.12 = (bf16[128,5632]{1,0:T(8,128)(2,1)}, bf16[128,5632]{1,0:T(8,128)(2,1)}, u32[]{:S(2)}, u32[]{:S(2)}) collective-permute-start(bf16[128,5632]{1,0:T(8,128)(2,1)} %pad_maximum_fusion.5), channel_id=1, source_target_pairs={{0,8},{8,16},{16,24},{24,28},{28,20},{20,12},{12,4},{4,0},{1,9},{9... | collective-permute-start | bytes 4325384 | tf_op jit(solution)/shard_map/ppermute | solution.py:580
  153.6 57.2 %collective-permute-start.13 = (bf16[128,5632]{1,0:T(8,128)(2,1)}, bf16[128,5632]{1,0:T(8,128)(2,1)}, u32[]{:S(2)}, u32[]{:S(2)}) collective-permute-start(bf16[128,5632]{1,0:T(8,128)(2,1)} %pad_maximum_fusion.5), channel_id=1, source_target_pairs={{8,0},{16,8},{24,16},{28,24},{20,28},{12,20},{4,12},{0,4},{9,1},{1... | collective-permute-start | bytes 4325384 | tf_op jit(solution)/shard_map/ppermute | solution.py:583
  211.2 74.3 %collective-permute-start.14 = (bf16[128,5632]{1,0:T(8,128)(2,1)}, bf16[128,5632]{1,0:T(8,128)(2,1)}, u32[]{:S(2)}, u32[]{:S(2)}) collective-permute-start(bf16[128,5632]{1,0:T(8,128)(2,1)} %collective-permute-done.12), channel_id=1, source_target_pairs={{0,8},{8,16},{16,24},{24,28},{28,20},{20,12},{12,4},{4,0},{1,9},{9... | collective-permute-start | bytes 4325384 | tf_op jit(solution)/shard_map/ppermute | solution.py:580
  212.8 79.3 %collective-permute-start.15 = (bf16[128,5632]{1,0:T(8,128)(2,1)}, bf16[128,5632]{1,0:T(8,128)(2,1)S(1)}, u32[]{:S(2)}, u32[]{:S(2)}) collective-permute-start(bf16[128,5632]{1,0:T(8,128)(2,1)} %collective-permute-done.13), channel_id=1, source_target_pairs={{8,0},{16,8},{24,16},{28,24},{20,28},{12,20},{4,12},{0,4},{9,1},{1... | collective-permute-start | bytes 4325384 | tf_op jit(solution)/shard_map/ppermute | solution.py:583
  213.5 81.7 %collective-permute-start.16 = (bf16[640,1024]{1,0:T(8,128)(2,1)}, bf16[640,1024]{1,0:T(8,128)(2,1)S(1)}, u32[]{:S(2)}, u32[]{:S(2)}) collective-permute-start(bf16[640,1024]{1,0:T(8,128)(2,1)} %convolution_convert_fusion.12), channel_id=1, source_target_pairs={{0,1},{1,0},{2,3},{3,2},{4,5},{5,4},{6,7},{7,6},{8,9},{9,8},{10,11... | collective-permute-start | bytes 3932168 | tf_op jit(solution)/shard_map/ppermute | solution.py:507
  213.5 82.9 %collective-permute-start.17 = (bf16[640,1024]{1,0:T(8,128)(2,1)}, bf16[640,1024]{1,0:T(8,128)(2,1)S(1)}, u32[]{:S(2)}, u32[]{:S(2)}) collective-permute-start(bf16[640,1024]{1,0:T(8,128)(2,1)} %convolution_convert_fusion.11), channel_id=1, source_target_pairs={{0,2},{1,3},{2,0},{3,1},{4,6},{5,7},{6,4},{7,5},{8,10},{9,11},{10,... | collective-permute-start | bytes 3932168 | tf_op jit(solution)/shard_map/ppermute | solution.py:507
  214.0 83.4 %collective-permute-start.18 = (bf16[640,1024]{1,0:T(8,128)(2,1)}, bf16[640,1024]{1,0:T(8,128)(2,1)S(1)}, u32[]{:S(2)}, u32[]{:S(2)}) collective-permute-start(bf16[640,1024]{1,0:T(8,128)(2,1)} %convolution_convert_fusion.10), channel_id=1, source_target_pairs={{0,3},{1,2},{2,1},{3,0},{4,7},{5,6},{6,5},{7,4},{8,11},{9,10},{10,... | collective-permute-start | bytes 3932168 | tf_op jit(solution)/shard_map/ppermute | solution.py:507
  298.5 90.9 %all-to-all-start = ((bf16[8,256,512]{2,1,0:T(8,128)(2,1)}), bf16[8,256,512]{2,1,0:T(8,128)(2,1)}, u32[]{:S(2)}, u32[]{:S(2)}) async-start(bf16[8,256,512]{2,1,0:T(8,128)(2,1)} %bitcast.39), calls=%async_computation | async-start | bytes 4194304 | tf_op jit(solution)/shard_map/all_to_all | solution.py:789
  304.1 64.4 %collective-permute-start.20 = (bf16[128,5632]{1,0:T(8,128)(2,1)}, bf16[128,5632]{1,0:T(8,128)(2,1)S(1)}, u32[]{:S(2)}, u32[]{:S(2)}) collective-permute-start(bf16[128,5632]{1,0:T(8,128)(2,1)} %copy-done.66), channel_id=1, source_target_pairs={{8,0},{16,8},{24,16},{28,24},{20,28},{12,20},{4,12},{0,4},{9,1},{1... | collective-permute-start | bytes 4325384 | tf_op jit(solution)/shard_map/ppermute | solution.py:583
  329.9 58.3 %collective-permute-start.21 = (bf16[128,5632]{1,0:T(8,128)(2,1)}, bf16[128,5632]{1,0:T(8,128)(2,1)S(1)}, u32[]{:S(2)}, u32[]{:S(2)}) collective-permute-start(bf16[128,5632]{1,0:T(8,128)(2,1)} %collective-permute-done.19), channel_id=1, source_target_pairs={{0,8},{8,16},{16,24},{24,28},{28,20},{20,12},{12,4},{4,0},{1,9},{9... | collective-permute-start | bytes 4325384 | tf_op jit(solution)/shard_map/ppermute | solution.py:580
  413.0 94.9 %collective-permute-start.22 = (bf16[656,1024]{1,0:T(8,128)(2,1)}, bf16[656,1024]{1,0:T(8,128)(2,1)S(1)}, u32[]{:S(2)}, u32[]{:S(2)}) collective-permute-start(bf16[656,1024]{1,0:T(8,128)(2,1)} %pad_maximum_fusion.8), channel_id=1, source_target_pairs={{0,1},{1,0},{2,3},{3,2},{4,5},{5,4},{6,7},{7,6},{8,9},{9,8},{10,11... | collective-permute-start | bytes 4030472 | tf_op jit(solution)/shard_map/ppermute | solution.py:507
  415.7 64.1 %collective-permute-start.25 = (bf16[656,1024]{1,0:T(8,128)(2,1)}, bf16[656,1024]{1,0:T(8,128)(2,1)}, u32[]{:S(2)}, u32[]{:S(2)}) collective-permute-start(bf16[656,1024]{1,0:T(8,128)(2,1)} %pad_maximum_fusion.10), channel_id=1, source_target_pairs={{0,3},{1,2},{2,1},{3,0},{4,7},{5,6},{6,5},{7,4},{8,11},{9,10},{10,... | collective-permute-start | bytes 4030472 | tf_op jit(solution)/shard_map/ppermute | solution.py:507
  578.8 62.2 %all-to-all-start.1 = ((bf16[8,256,512]{2,1,0:T(8,128)(2,1)}), bf16[8,256,512]{2,1,0:T(8,128)(2,1)S(1)}, u32[]{:S(2)}, u32[]{:S(2)}) async-start(bf16[8,256,512]{2,1,0:T(8,128)(2,1)} %bitcast.294), calls=%async_computation.1 | async-start | bytes 4194304 | tf_op jit(solution)/shard_map/all_to_all | solution.py:789
  592.0 331.3 %reduce-scatter.2.cloned.1.call-start = ((), (), s32[]{:S(2)}) async-start(), calls=%async_computation.8 | async-start | bytes 6488064 | tf_op jit(solution)/shard_map/reduce_scatter | solution.py:869
  718.5 73.6 %collective-permute-start.34 = (bf16[128,2816]{1,0:T(8,128)(2,1)S(1)}, bf16[128,2816]{1,0:T(8,128)(2,1)S(1)}, u32[]{:S(2)}, u32[]{:S(2)}) collective-permute-start(bf16[128,2816]{1,0:T(8,128)(2,1)S(1)} %get-tuple-element.319), channel_id=1, source_target_pairs={{8,0},{16,8},{24,16},{28,24},{20,28},{12,20},{4,12},{0,4},{9,1},{1... | collective-permute-start | bytes 2162696 | tf_op jit(solution)/shard_map/ppermute | solution.py:633
  795.1 76.2 %collective-permute-start.37 = (bf16[128,2816]{1,0:T(8,128)(2,1)}, bf16[128,2816]{1,0:T(8,128)(2,1)}, u32[]{:S(2)}, u32[]{:S(2)}) collective-permute-start(bf16[128,2816]{1,0:T(8,128)(2,1)} %get-tuple-element.314), channel_id=1, source_target_pairs={{0,8},{8,16},{16,24},{24,28},{28,20},{20,12},{12,4},{4,0},{1,9},{9... | collective-permute-start | bytes 2162696 | tf_op jit(solution)/shard_map/ppermute | solution.py:630
  796.7 74.5 %collective-permute-start.39 = (bf16[128,2816]{1,0:T(8,128)(2,1)}, bf16[128,2816]{1,0:T(8,128)(2,1)}, u32[]{:S(2)}, u32[]{:S(2)}) collective-permute-start(bf16[128,2816]{1,0:T(8,128)(2,1)} %get-tuple-element.313), channel_id=1, source_target_pairs={{8,0},{16,8},{24,16},{28,24},{20,28},{12,20},{4,12},{0,4},{9,1},{1... | collective-permute-start | bytes 2162696 | tf_op jit(solution)/shard_map/ppermute | solution.py:633
  818.3 104.9 %all-to-all-start.2 = ((bf16[4,640,1024]{2,1,0:T(8,128)(2,1)}), bf16[4,640,1024]{2,1,0:T(8,128)(2,1)}, u32[]{:S(2)}, u32[]{:S(2)}) async-start(bf16[4,640,1024]{2,1,0:T(8,128)(2,1)} %pad_maximum_fusion.1), calls=%async_computation.2 | async-start | bytes 10485760 | tf_op jit(solution)/shard_map/all_to_all | solution.py:894
  873.7 49.6 %collective-permute-start.41 = (bf16[128,2816]{1,0:T(8,128)(2,1)}, bf16[128,2816]{1,0:T(8,128)(2,1)}, u32[]{:S(2)}, u32[]{:S(2)}) collective-permute-start(bf16[128,2816]{1,0:T(8,128)(2,1)} %add_convert_fusion.1), channel_id=1, source_target_pairs={{0,8},{8,16},{16,24},{24,28},{28,20},{20,12},{12,4},{4,0},{1,9},{9... | collective-permute-start | bytes 2162696 | tf_op jit(solution)/shard_map/ppermute | solution.py:630
  (143 other events, 4396.8 us)
Sparse Core Ops, SparseCore 0:
  155.2 137.1 all-gather.1
  711.1 161.7 reduce-scatter.1

commit v9 on v8

--- a/solution.py
+++ b/solution.py
@@ -906,37 +906,27 @@
     def through(grads, part):
         return dot_nt(grads, qkv_w[:, part * head_width : (part + 1) * head_width])
 
+    normed_part = through(query_back, 0) + through(key_back, 1) + through(value_back, 2)
+    normed_part = normed_part.reshape(groups, split, local_len, width)
+    sides = [normed_part[:, rx].astype(LOW) for rx in range(1, split)]
+    sides, query_back, key_back, value_back = lax.optimization_barrier((sides, query_back, key_back, value_back))
+    sides = [partner(side, "x", rx) for rx, side in enumerate(sides, 1)]
     out_parts = width // head_width
     weight_sum = jnp.stack(
         [dot_tn(normed_one, grads).astype(LOW) for grads in (query_back, key_back, value_back)]
         + [out_sum[:, i * head_width : (i + 1) * head_width] for i in range(out_parts)]
     )
-    weight_sum, query_back, key_back, value_back = lax.optimization_barrier(
-        (weight_sum, query_back, key_back, value_back)
-    )
-    normed_part = through(query_back, 0) + through(key_back, 1) + through(value_back, 2)
-    half = width // 2
-    normed_part = normed_part.reshape(groups, split, local_len, width)
-
-    sides = [normed_part[:, rx].astype(LOW) for rx in range(1, split)]
-    first = [partner(side[:, :, :half], "x", rx) for rx, side in enumerate(sides, 1)]
-    first, rest = lax.optimization_barrier((first, [side[:, :, half:] for side in sides]))
-
-    def send_back(own_part, coming):
-        total = own_part + sum(part.astype(jnp.float32) for part in coming)
-        total = reorder(total.astype(LOW), z_at)
-        return lax.all_to_all(total, "z", split_axis=0, concat_axis=0, tiled=True)
-
-    normed_first = send_back(normed_part[:, 0, :, :half], first)
-    rest = [partner(side, "x", rx) for rx, side in enumerate(rest, 1)]
-    normed_second = send_back(normed_part[:, 0, :, half:], rest)
     weight_part = scatter_halve(
-        weight_sum.reshape((3 + out_parts,) + (2,) * (nz + nx + ne) + (rows_own, head_width)), halving[:ne]
-    )
-    weight_part = scatter_halve(weight_part, halving[ne:]).reshape(3 + out_parts, split, rows_own, head_width)
+        weight_sum.reshape((3 + out_parts,) + (2,) * (nz + nx + ne) + (rows_own, head_width)), halving[:1]
+    )
+    normed_back = normed_part[:, 0] + sum(side.astype(jnp.float32) for side in sides)
+    normed_back = lax.all_to_all(
+        reorder(normed_back.astype(LOW), z_at), "z", split_axis=0, concat_axis=0, tiled=True
+    )
+    weight_part = scatter_halve(weight_part, halving[1:]).reshape(3 + out_parts, split, rows_own, head_width)
     weight_own = [lax.dynamic_index_in_dim(weight_part, x_at ^ r, 1, keepdims=False) for r in range(split)]
     weight_own = [weight_own[0]] + [partner(weight_own[r], "x", r) for r in range(1, split)]
-    normed_second, weight_own = lax.optimization_barrier((normed_second, weight_own))
+    normed_back, weight_own = lax.optimization_barrier((normed_back, weight_own))
     block_out = (mid + dot32(table, reorder(returned, e_at).reshape(slot_count, width))).astype(LOW)
 
     block_out = block_out.reshape(groups, local_len, width)
@@ -945,7 +935,7 @@
     qkv_own = reorder(jnp.stack([part[:3] for part in weight_own]), x_at)
     qkv_own = qkv_own.transpose(1, 2, 0, 3).reshape(3, rows_own, hd).astype(jnp.float32)
 
-    normed_one_grad = jnp.concatenate([normed_first, normed_second], axis=2).astype(jnp.float32).reshape(tokens, width)
+    normed_one_grad = normed_back.astype(jnp.float32).reshape(tokens, width)
     scale_one = norm_scale(inputs)
     unit_one = inputs * scale_one
     gain_one_sum = jnp.sum(normed_one_grad * unit_one, axis=0)

time: 1120 us -> 1130 us (level)
  waiting for transfers between devices: 290 us -> 321 us
  Pallas kernels: 324 us -> 295 us
  starting transfers between devices: 87.4 us -> 99.6 us
    pallas_call x4, Pallas kernels: 147 us -> 127 us  [attend_backward(): pl.pallas_call(bwd_kernel, name='attend_backward', out_shape=(low, low, l...]
    ppermute x28 -> x27, waiting for transfers between devices: 137 us -> 151 us  [partner(): return lax.ppermute(value, axis, [(i, i ^ offset) for i in range(count)])]
    ppermute x8, waiting for transfers between devices: 5.2 us -> 17.7 us  [step(): self.forward = [lax.ppermute(part, SEQ, self.ahead) for part in parts]]
    ppermute x28 -> x27, starting transfers between devices: 26.2 us -> 38 us  [partner(): return lax.ppermute(value, axis, [(i, i ^ offset) for i in range(count)])]
    unnamed x240 -> x259, local copies, waits for them, and re-layouts: 42.5 us -> 39.5 us
  transfers between devices with their start and end apart: 57 -> 55, of which waited for: 21 -> 20; matrix products, arithmetic and copies ran while one was open for 25% -> 22% of each run, Pallas kernels for 29% -> 26%
where the time goes in v9:
time: 1130 us; the launch traced here: 1120 us
  waiting for transfers between devices  321 us (28%)
  Pallas kernels  295 us (26%)
  matrix products  192 us (17%)
  starting transfers between devices  99.6 us (9%)
  local copies, waits for them, and re-layouts  94.7 us (8%)
  other arithmetic  90.1 us (8%)
  between operations  28.3 us (3%)
    ppermute x27, waiting for transfers between devices, partner(): return lax.ppermute(value, axis, [(i, i ^ offset) for i in range(count)])  151 us
    pallas_call x4, Pallas kernels, attend_backward(): pl.pallas_call(bwd_kernel, name='attend_backward', out_shape=(low, low, l...  127 us
    pallas_call x4, Pallas kernels, expert_block(): pl.pallas_call(expert_kernel, name='expert_block', out_shape=(whole, whol...  109 us
    dot_general x16, matrix products, dot_tn(): lax.dot_general(a, b, (((0,), (0,)), ((), ())), preferred_element_type=jn...  102 us
    ppermute x4, waiting for transfers between devices, step(): self.forward = lax.ppermute(self.forward, SEQ, self.ahead)  68.9 us
    dot_general x9, matrix products, dot32(): return jnp.dot(a, b, preferred_element_type=jnp.float32)  62.8 us
    pallas_call x1, Pallas kernels, attend_forward(): pl.pallas_call(fwd_kernel, name='attend_forward', out_shape=(jax.ShapeDty...  59.1 us
    ppermute x3, waiting for transfers between devices, step(): lax.ppermute(self.backward, SEQ, [(b, a) for a, b in self.ahead])  51.8 us
  transfers between devices with their start and end apart: 55, of which 20 were waited for; matrix products, arithmetic and copies ran while one was open for 22% of the time, Pallas kernels for 26%

profile of v9, /device:TPU:0, one launch (start us, length us, event | category | flops | bytes accessed | tf_op | source)
XLA Modules:
  0.0 1121.0 jit_solution(6584643362622534302)
XLA Ops:
  59.5 24.4 %collective-permute-done.1 = bf16[2,32,2688]{2,1,0:T(8,128)(2,1)} collective-permute-done((bf16[2,32,2688]{2,1,0:T(8,128)(2,1)S(1)}, bf16[2,32,2688]{2,1,0:T(8,128)(2,1)}, u32[]{:S(2)}, u32[]{:S(2)}) %collective-permute-start.1) | collective-permute-done | bytes 344096 | tf_op jit(solution)/shard_map/ppermute | solution.py:507
  109.8 24.1 %collective-permute-done.6 = bf16[2,2,2,32,2688]{4,3,2,1,0:T(8,128)(2,1)S(1)} collective-permute-done((bf16[2,2,2,32,2688]{4,3,2,1,0:T(8,128)(2,1)S(1)}, bf16[2,2,2,32,2688]{4,3,2,1,0:T(8,128)(2,1)S(1)}, u32[]{:S(2)}, u32[]{:S(2)}) %collective-permute-start.6) | collective-permute-done | bytes 1376288 | tf_op jit(solution)/shard_map/ppermute | solution.py:507
  178.9 29.1 %collective-permute-done.12 = bf16[128,5632]{1,0:T(8,128)(2,1)} collective-permute-done((bf16[128,5632]{1,0:T(8,128)(2,1)}, bf16[128,5632]{1,0:T(8,128)(2,1)}, u32[]{:S(2)}, u32[]{:S(2)}) %collective-permute-start.12) | collective-permute-done | bytes 1441824 | tf_op jit(solution)/shard_map/ppermute | solution.py:580
  215.5 59.1 %attend_forward.1 = (bf16[2048,512]{1,0:T(8,128)(2,1)}, f32[4,2,2048]{2,1,0:T(2,128)S(1)}) custom-call(s32[2,8]{1,0:T(2,128)S(1)} %pad_add_fusion.ranges, f32[8,2]{1,0:T(8,128)S(1)} %maximum_convert_fusion.ends, s32[1]{0:T(128)} %bitcast.23.own, bf16[2048,1536]{1,0:T(8,128)(2,1)} %convolution_convert_fusion.q_ref.k_ref.v_ref, ...), custom_call_target="tpu_custom_call" | custom-call | flops 8589934592 | bytes 8388608 | tf_op jit(solution)/shard_map/attend_forward/pallas_call | solution.py:168
  277.2 15.0 %collective-permute-done.15 = bf16[128,5632]{1,0:T(8,128)(2,1)S(1)} collective-permute-done((bf16[128,5632]{1,0:T(8,128)(2,1)}, bf16[128,5632]{1,0:T(8,128)(2,1)S(1)}, u32[]{:S(2)}, u32[]{:S(2)}) %collective-permute-start.15) | collective-permute-done | bytes 1441824 | tf_op jit(solution)/shard_map/ppermute | solution.py:583
  308.7 21.5 %collective-permute-done.19 = bf16[128,5632]{1,0:T(8,128)(2,1)} collective-permute-done((bf16[128,5632]{1,0:T(8,128)(2,1)}, bf16[128,5632]{1,0:T(8,128)(2,1)}, u32[]{:S(2)}, u32[]{:S(2)}) %collective-permute-start.19) | collective-permute-done | bytes 1441824 | tf_op jit(solution)/shard_map/ppermute | solution.py:580
  334.5 34.1 %collective-permute-done.20 = bf16[128,5632]{1,0:T(8,128)(2,1)S(1)} collective-permute-done((bf16[128,5632]{1,0:T(8,128)(2,1)}, bf16[128,5632]{1,0:T(8,128)(2,1)S(1)}, u32[]{:S(2)}, u32[]{:S(2)}) %collective-permute-start.20) | collective-permute-done | bytes 1441824 | tf_op jit(solution)/shard_map/ppermute | solution.py:583
  369.8 18.4 %collective-permute-done.21 = bf16[128,5632]{1,0:T(8,128)(2,1)S(1)} collective-permute-done((bf16[128,5632]{1,0:T(8,128)(2,1)}, bf16[128,5632]{1,0:T(8,128)(2,1)S(1)}, u32[]{:S(2)}, u32[]{:S(2)}) %collective-permute-start.21) | collective-permute-done | bytes 1441824 | tf_op jit(solution)/shard_map/ppermute | solution.py:580
  424.1 27.2 %expert_block.4 = (bf16[2560,2816]{1,0:T(8,128)(2,1)}, bf16[2560,2816]{1,0:T(8,128)(2,1)}, bf16[2560,2816]{1,0:T(8,128)(2,1)}, bf16[656,1024]{1,0:T(8,128)(2,1)S(1)}) custom-call(s32[1]{0:T(128)} %constant.361.clone.1.own_ref, bf16[656,1024]{1,0:T(8,128)(2,1)S(1)} %copy-done.26, bf16[640,1024]{1,0:T(8,128)(2,1)S(1)} %copy-done.42, ...), custom_call_target="tpu_custom_call" | custom-call | flops 18454937600 | bytes 28114944 | tf_op jit(solution)/shard_map/expert_block/pallas_call | solution.py:468
  451.3 27.0 %expert_block.5 = (bf16[2560,2816]{1,0:T(8,128)(2,1)}, bf16[2560,2816]{1,0:T(8,128)(2,1)}, bf16[2560,2816]{1,0:T(8,128)(2,1)}, bf16[656,1024]{1,0:T(8,128)(2,1)S(1)}) custom-call(s32[1]{0:T(128)} %constant.361.clone.1.own_ref, bf16[656,1024]{1,0:T(8,128)(2,1)S(1)} %collective-permute-done.23.x_ref, ...), custom_call_target="tpu_custom_call", output_to_operand_aliasing={{0}: (6, {}), {1}: (7, {}), {2}: (8, {})} | custom-call | flops 18454937600 | bytes 28114944 | tf_op jit(solution)/shard_map/expert_block/pallas_call | solution.py:468
  479.6 28.0 %expert_block.6 = (bf16[2560,2816]{1,0:T(8,128)(2,1)}, bf16[2560,2816]{1,0:T(8,128)(2,1)}, bf16[2560,2816]{1,0:T(8,128)(2,1)}, bf16[656,1024]{1,0:T(8,128)(2,1)S(1)}) custom-call(s32[1]{0:T(128)} %constant.361.clone.1.own_ref, bf16[656,1024]{1,0:T(8,128)(2,1)} %collective-permute-done.25.x_ref, ...), custom_call_target="tpu_custom_call", output_to_operand_aliasing={{0}: (6, {}), {1}: (7, {}), {2}: (8, {})} | custom-call | flops 18454937600 | bytes 28114944 | tf_op jit(solution)/shard_map/expert_block/pallas_call | solution.py:468
  509.7 27.3 %expert_block.7 = (bf16[2560,2816]{1,0:T(8,128)(2,1)}, bf16[2560,2816]{1,0:T(8,128)(2,1)}, bf16[2560,2816]{1,0:T(8,128)(2,1)}, bf16[656,1024]{1,0:T(8,128)(2,1)S(1)}) custom-call(s32[1]{0:T(128)} %constant.361.clone.1.own_ref, bf16[656,1024]{1,0:T(8,128)(2,1)S(1)} %collective-permute-done.22.x_ref, ...), custom_call_target="tpu_custom_call", output_to_operand_aliasing={{0}: (6, {}), {1}: (7, {}), {2}: (8, {})} | custom-call | flops 18454937600 | bytes 28114944 | tf_op jit(solution)/shard_map/expert_block/pallas_call | solution.py:468
  592.9 22.6 %convolution_convert_fusion.2 = bf16[1024,2816]{1,0:T(8,128)(2,1)} fusion(bf16[2560,2816]{1,0:T(8,128)(2,1)} %get-tuple-element.207, bf16[640,1024]{1,0:T(8,128)(2,1)} %slice.247, bf16[640,1024]{1,0:T(8,128)(2,1)} %slice.246, bf16[640,1024]{1,0:T(8,128)(2,1)} %slice.245, bf16[640,1024]{1,0:T(8,128)(2,1)S(1)} %copy-done.71), kind=kOutput, calls=%fused_computation.21 | convolution fusion | flops 14787805184 | bytes 25427968 | tf_op jit(solution)/shard_map/dot_general | solution.py:502
  615.5 20.9 %convolution_convert_fusion.3 = bf16[1024,2816]{1,0:T(8,128)(2,1)} fusion(bf16[2560,2816]{1,0:T(8,128)(2,1)} %get-tuple-element.206, bf16[640,1024]{1,0:T(8,128)(2,1)S(1)} %copy-done.74, bf16[640,1024]{1,0:T(8,128)(2,1)S(1)} %copy-done.73, bf16[640,1024]{1,0:T(8,128)(2,1)S(1)} %copy-done.72, bf16[640,1024]{1,0:T(8,128)(2,1)S(1)} %copy-done.71), kind=kOutput, calls=%fused_computation.22 | convolution fusion | flops 14787805184 | bytes 25427968 | tf_op jit(solution)/shard_map/dot_general | solution.py:502
  649.6 31.9 %attend_backward.4 = (bf16[2048,512]{1,0:T(8,128)(2,1)S(1)}, bf16[2048,512]{1,0:T(8,128)(2,1)S(1)}, bf16[2048,512]{1,0:T(8,128)(2,1)S(1)}, f32[2,3,512]{2,1,0:T(4,128)S(1)}, f32[2,2,256]{2,1,0:T(2,128)S(1)}) custom-call(s32[2,8]{1,0:T(2,128)S(1)} %copy-done.41, f32[8,2]{1,0:T(8,128)S(1)} %copy-done.39, s32[2]{0:T(128)S(1)} %get-tuple-element.407.own, ...), custom_call_target="tpu_custom_call" | custom-call | flops 5368709120 | bytes 4194304 | tf_op jit(solution)/shard_map/attend_backward/pallas_call | solution.py:347
  685.7 20.9 %convolution_convert_fusion.1 = bf16[2816,1024]{1,0:T(8,128)(2,1)} fusion(bf16[2560,2816]{1,0:T(8,128)(2,1)} %get-tuple-element.246, bf16[640,1024]{1,0:T(8,128)(2,1)S(1)} %copy-done.37, bf16[640,1024]{1,0:T(8,128)(2,1)S(1)} %copy-done.34, bf16[640,1024]{1,0:T(8,128)(2,1)S(1)} %copy-done.31, bf16[640,1024]{1,0:T(8,128)(2,1)S(1)} %copy-done.43, ...), kind=kOutput, calls=%fused_computation.20 | convolution fusion | flops 14793048064 | bytes 25438208 | tf_op jit(solution)/shard_map/dot_general | solution.py:502
  718.6 31.7 %attend_backward.5 = (bf16[2048,512]{1,0:T(8,128)(2,1)S(1)}, bf16[2048,512]{1,0:T(8,128)(2,1)S(1)}, bf16[2048,512]{1,0:T(8,128)(2,1)S(1)}, f32[2,3,512]{2,1,0:T(4,128)S(1)}, f32[2,2,256]{2,1,0:T(2,128)S(1)}) custom-call(s32[2,8]{1,0:T(2,128)S(1)} %copy-done.41, f32[8,2]{1,0:T(8,128)S(1)} %copy-done.39, ...), custom_call_target="tpu_custom_call", output_to_operand_aliasing={{0}: (12, {}), {1}: (13, {}), {2}: (14, {})} | custom-call | flops 5368709120 | bytes 4194304 | tf_op jit(solution)/shard_map/attend_backward/pallas_call | solution.py:347
  755.5 17.7 %collective-permute-done.32 = bf16[128,2816]{1,0:T(8,128)(2,1)S(1)} collective-permute-done((bf16[128,2816]{1,0:T(8,128)(2,1)S(1)}, bf16[128,2816]{1,0:T(8,128)(2,1)S(1)}, u32[]{:S(2)}, u32[]{:S(2)}) %collective-permute-start.32) | collective-permute-done | bytes 720928 | tf_op jit(solution)/shard_map/ppermute | solution.py:630
  773.2 18.9 %collective-permute-done.34 = bf16[128,2816]{1,0:T(8,128)(2,1)S(1)} collective-permute-done((bf16[128,2816]{1,0:T(8,128)(2,1)S(1)}, bf16[128,2816]{1,0:T(8,128)(2,1)S(1)}, u32[]{:S(2)}, u32[]{:S(2)}) %collective-permute-start.34) | collective-permute-done | bytes 720928 | tf_op jit(solution)/shard_map/ppermute | solution.py:633
  797.1 17.6 %multiply_convert_fusion = bf16[2560,1024]{1,0:T(8,128)(2,1)S(1)} fusion(bf16[2560,2816]{1,0:T(8,128)(2,1)} %get-tuple-element.246, bf16[2816,1024]{1,0:T(8,128)(2,1)S(1)} %bitcast.258, f32[2560]{0:T(1024)S(1)} %pad_maximum_fusion.21), kind=kOutput, calls=%fused_computation.7 | convolution fusion | flops 14769192960 | bytes 25438208 | tf_op jit(solution)/shard_map/dot_general | solution.py:494
  832.0 31.4 %attend_backward.6 = (bf16[2048,512]{1,0:T(8,128)(2,1)S(1)}, bf16[2048,512]{1,0:T(8,128)(2,1)S(1)}, bf16[2048,512]{1,0:T(8,128)(2,1)S(1)}, f32[2,3,512]{2,1,0:T(4,128)S(1)}, f32[2,2,256]{2,1,0:T(2,128)S(1)}) custom-call(s32[2,8]{1,0:T(2,128)S(1)} %copy-done.41, f32[8,2]{1,0:T(8,128)S(1)} %copy-done.39, ...), custom_call_target="tpu_custom_call", output_to_operand_aliasing={{0}: (12, {}), {1}: (13, {}), {2}: (14, {})} | custom-call | flops 5368709120 | bytes 4194304 | tf_op jit(solution)/shard_map/attend_backward/pallas_call | solution.py:347
  873.8 31.6 %attend_backward.7 = (bf16[2048,512]{1,0:T(8,128)(2,1)S(1)}, bf16[2048,512]{1,0:T(8,128)(2,1)S(1)}, bf16[2048,512]{1,0:T(8,128)(2,1)S(1)}, f32[2,3,512]{2,1,0:T(4,128)S(1)}, f32[2,2,256]{2,1,0:T(2,128)S(1)}) custom-call(s32[2,8]{1,0:T(2,128)S(1)} %copy-done.41, f32[8,2]{1,0:T(8,128)S(1)} %copy-done.39, ...), custom_call_target="tpu_custom_call", output_to_operand_aliasing={{0}: (12, {}), {1}: (13, {}), {2}: (14, {})} | custom-call | flops 5368709120 | bytes 4194304 | tf_op jit(solution)/shard_map/attend_backward/pallas_call | solution.py:347
  979.2 33.1 %collective-permute-done.42 = bf16[4,256,1024]{2,1,0:T(8,128)(2,1)S(1)} collective-permute-done((bf16[4,256,1024]{2,1,0:T(8,128)(2,1)}, bf16[4,256,1024]{2,1,0:T(8,128)(2,1)S(1)}, u32[]{:S(2)}, u32[]{:S(2)}) %collective-permute-start.42) | collective-permute-done | bytes 2097184 | tf_op jit(solution)/shard_map/ppermute | solution.py:507
  1028.5 40.8 %collective-permute-done.45 = bf16[5,2,2,32,512]{4,3,0,2,1:T(8,128)(2,1)S(1)} collective-permute-done((bf16[5,2,2,32,512]{4,3,0,2,1:T(8,128)(2,1)S(1)}, bf16[5,2,2,32,512]{4,3,0,2,1:T(8,128)(2,1)S(1)}, u32[]{:S(2)}, u32[]{:S(2)}) %collective-permute-start.45) | collective-permute-done | bytes 655392 | tf_op jit(solution)/shard_map/ppermute | solution.py:507
  (582 shorter events, 438.4 us)
Async XLA Ops:
  7.2 411.6 %all-gather.2.cloned.1.call-start = ((), (), s32[]{:S(2)}) async-start(), calls=%async_computation.6 | async-start | bytes 6488064 | tf_op jit(solution)/shard_map/all_gather | solution.py:738
  19.5 84.7 %collective-permute-start.3 = (bf16[256,1024]{1,0:T(8,128)(2,1)}, bf16[256,1024]{1,0:T(8,128)(2,1)}, u32[]{:S(2)}, u32[]{:S(2)}) collective-permute-start(bf16[256,1024]{1,0:T(8,128)(2,1)} %get-tuple-element.341), channel_id=1, source_target_pairs={{0,8},{8,0},{16,24},{24,16},{1,9},{9,1},{17,25},{25,17},{2,10},{10... | collective-permute-start | bytes 1572872 | tf_op jit(solution)/shard_map/ppermute | solution.py:507
  21.1 83.2 %collective-permute-start.4 = (bf16[256,1024]{1,0:T(8,128)(2,1)}, bf16[256,1024]{1,0:T(8,128)(2,1)}, u32[]{:S(2)}, u32[]{:S(2)}) collective-permute-start(bf16[256,1024]{1,0:T(8,128)(2,1)} %get-tuple-element.340), channel_id=1, source_target_pairs={{0,16},{8,24},{16,0},{24,8},{1,17},{9,25},{17,1},{25,9},{2,18},{10... | collective-permute-start | bytes 1572872 | tf_op jit(solution)/shard_map/ppermute | solution.py:507
  23.7 80.6 %collective-permute-start.5 = (bf16[256,1024]{1,0:T(8,128)(2,1)}, bf16[256,1024]{1,0:T(8,128)(2,1)}, u32[]{:S(2)}, u32[]{:S(2)}) collective-permute-start(bf16[256,1024]{1,0:T(8,128)(2,1)} %get-tuple-element.342), channel_id=1, source_target_pairs={{0,24},{8,16},{16,8},{24,0},{1,25},{9,17},{17,9},{25,1},{2,26},{10... | collective-permute-start | bytes 1572872 | tf_op jit(solution)/shard_map/ppermute | solution.py:507
  23.9 112.1 %collective-permute-start.7 = (bf16[256,1024]{1,0:T(8,128)(2,1)}, bf16[256,1024]{1,0:T(8,128)(2,1)}, u32[]{:S(2)}, u32[]{:S(2)}) collective-permute-start(bf16[256,1024]{1,0:T(8,128)(2,1)} %get-tuple-element.155), channel_id=1, source_target_pairs={{0,4},{4,0},{1,5},{5,1},{2,6},{6,2},{3,7},{7,3},{8,12},{12,8},{9,1... | collective-permute-start | bytes 1572872 | tf_op jit(solution)/shard_map/ppermute | solution.py:507
  153.4 57.4 %collective-permute-start.13 = (bf16[128,5632]{1,0:T(8,128)(2,1)}, bf16[128,5632]{1,0:T(8,128)(2,1)}, u32[]{:S(2)}, u32[]{:S(2)}) collective-permute-start(bf16[128,5632]{1,0:T(8,128)(2,1)} %pad_maximum_fusion.5), channel_id=1, source_target_pairs={{8,0},{16,8},{24,16},{28,24},{20,28},{12,20},{4,12},{0,4},{9,1},{1... | collective-permute-start | bytes 4325384 | tf_op jit(solution)/shard_map/ppermute | solution.py:583
  211.2 66.0 %collective-permute-start.14 = (bf16[128,5632]{1,0:T(8,128)(2,1)}, bf16[128,5632]{1,0:T(8,128)(2,1)}, u32[]{:S(2)}, u32[]{:S(2)}) collective-permute-start(bf16[128,5632]{1,0:T(8,128)(2,1)} %collective-permute-done.12), channel_id=1, source_target_pairs={{0,8},{8,16},{16,24},{24,28},{28,20},{20,12},{12,4},{4,0},{1,9},{9... | collective-permute-start | bytes 4325384 | tf_op jit(solution)/shard_map/ppermute | solution.py:580
  212.8 79.3 %collective-permute-start.15 = (bf16[128,5632]{1,0:T(8,128)(2,1)}, bf16[128,5632]{1,0:T(8,128)(2,1)S(1)}, u32[]{:S(2)}, u32[]{:S(2)}) collective-permute-start(bf16[128,5632]{1,0:T(8,128)(2,1)} %collective-permute-done.13), channel_id=1, source_target_pairs={{8,0},{16,8},{24,16},{28,24},{20,28},{12,20},{4,12},{0,4},{9,1},{1... | collective-permute-start | bytes 4325384 | tf_op jit(solution)/shard_map/ppermute | solution.py:583
  213.5 81.7 %collective-permute-start.16 = (bf16[640,1024]{1,0:T(8,128)(2,1)}, bf16[640,1024]{1,0:T(8,128)(2,1)S(1)}, u32[]{:S(2)}, u32[]{:S(2)}) collective-permute-start(bf16[640,1024]{1,0:T(8,128)(2,1)} %convolution_convert_fusion.12), channel_id=1, source_target_pairs={{0,1},{1,0},{2,3},{3,2},{4,5},{5,4},{6,7},{7,6},{8,9},{9,8},{10,11... | collective-permute-start | bytes 3932168 | tf_op jit(solution)/shard_map/ppermute | solution.py:507
  213.5 82.9 %collective-permute-start.17 = (bf16[640,1024]{1,0:T(8,128)(2,1)}, bf16[640,1024]{1,0:T(8,128)(2,1)S(1)}, u32[]{:S(2)}, u32[]{:S(2)}) collective-permute-start(bf16[640,1024]{1,0:T(8,128)(2,1)} %convolution_convert_fusion.11), channel_id=1, source_target_pairs={{0,2},{1,3},{2,0},{3,1},{4,6},{5,7},{6,4},{7,5},{8,10},{9,11},{10,... | collective-permute-start | bytes 3932168 | tf_op jit(solution)/shard_map/ppermute | solution.py:507
  214.0 83.5 %collective-permute-start.18 = (bf16[640,1024]{1,0:T(8,128)(2,1)}, bf16[640,1024]{1,0:T(8,128)(2,1)S(1)}, u32[]{:S(2)}, u32[]{:S(2)}) collective-permute-start(bf16[640,1024]{1,0:T(8,128)(2,1)} %convolution_convert_fusion.10), channel_id=1, source_target_pairs={{0,3},{1,2},{2,1},{3,0},{4,7},{5,6},{6,5},{7,4},{8,11},{9,10},{10,... | collective-permute-start | bytes 3932168 | tf_op jit(solution)/shard_map/ppermute | solution.py:507
  298.6 90.8 %all-to-all-start = ((bf16[8,256,512]{2,1,0:T(8,128)(2,1)}), bf16[8,256,512]{2,1,0:T(8,128)(2,1)}, u32[]{:S(2)}, u32[]{:S(2)}) async-start(bf16[8,256,512]{2,1,0:T(8,128)(2,1)} %bitcast.39), calls=%async_computation | async-start | bytes 4194304 | tf_op jit(solution)/shard_map/all_to_all | solution.py:789
  304.2 64.4 %collective-permute-start.20 = (bf16[128,5632]{1,0:T(8,128)(2,1)}, bf16[128,5632]{1,0:T(8,128)(2,1)S(1)}, u32[]{:S(2)}, u32[]{:S(2)}) collective-permute-start(bf16[128,5632]{1,0:T(8,128)(2,1)} %copy-done.69), channel_id=1, source_target_pairs={{8,0},{16,8},{24,16},{28,24},{20,28},{12,20},{4,12},{0,4},{9,1},{1... | collective-permute-start | bytes 4325384 | tf_op jit(solution)/shard_map/ppermute | solution.py:583
  330.2 58.0 %collective-permute-start.21 = (bf16[128,5632]{1,0:T(8,128)(2,1)}, bf16[128,5632]{1,0:T(8,128)(2,1)S(1)}, u32[]{:S(2)}, u32[]{:S(2)}) collective-permute-start(bf16[128,5632]{1,0:T(8,128)(2,1)} %collective-permute-done.19), channel_id=1, source_target_pairs={{0,8},{8,16},{16,24},{24,28},{28,20},{20,12},{12,4},{4,0},{1,9},{9... | collective-permute-start | bytes 4325384 | tf_op jit(solution)/shard_map/ppermute | solution.py:580
  412.5 95.2 %collective-permute-start.22 = (bf16[656,1024]{1,0:T(8,128)(2,1)}, bf16[656,1024]{1,0:T(8,128)(2,1)S(1)}, u32[]{:S(2)}, u32[]{:S(2)}) collective-permute-start(bf16[656,1024]{1,0:T(8,128)(2,1)} %pad_maximum_fusion.8), channel_id=1, source_target_pairs={{0,1},{1,0},{2,3},{3,2},{4,5},{5,4},{6,7},{7,6},{8,9},{9,8},{10,11... | collective-permute-start | bytes 4030472 | tf_op jit(solution)/shard_map/ppermute | solution.py:507
  415.2 64.3 %collective-permute-start.25 = (bf16[656,1024]{1,0:T(8,128)(2,1)}, bf16[656,1024]{1,0:T(8,128)(2,1)}, u32[]{:S(2)}, u32[]{:S(2)}) collective-permute-start(bf16[656,1024]{1,0:T(8,128)(2,1)} %pad_maximum_fusion.10), channel_id=1, source_target_pairs={{0,3},{1,2},{2,1},{3,0},{4,7},{5,6},{6,5},{7,4},{8,11},{9,10},{10,... | collective-permute-start | bytes 4030472 | tf_op jit(solution)/shard_map/ppermute | solution.py:507
  579.5 62.2 %all-to-all-start.1 = ((bf16[8,256,512]{2,1,0:T(8,128)(2,1)}), bf16[8,256,512]{2,1,0:T(8,128)(2,1)S(1)}, u32[]{:S(2)}, u32[]{:S(2)}) async-start(bf16[8,256,512]{2,1,0:T(8,128)(2,1)} %bitcast.273), calls=%async_computation.1 | async-start | bytes 4194304 | tf_op jit(solution)/shard_map/all_to_all | solution.py:789
  592.8 317.8 %reduce-scatter.2.cloned.1.call-start = ((), (), s32[]{:S(2)}) async-start(), calls=%async_computation.7 | async-start | bytes 6488064 | tf_op jit(solution)/shard_map/reduce_scatter | solution.py:869
  716.0 57.2 %collective-permute-start.32 = (bf16[128,2816]{1,0:T(8,128)(2,1)S(1)}, bf16[128,2816]{1,0:T(8,128)(2,1)S(1)}, u32[]{:S(2)}, u32[]{:S(2)}) collective-permute-start(bf16[128,2816]{1,0:T(8,128)(2,1)S(1)} %get-tuple-element.314), channel_id=1, source_target_pairs={{0,8},{8,16},{16,24},{24,28},{28,20},{20,12},{12,4},{4,0},{1,9},{9... | collective-permute-start | bytes 2162696 | tf_op jit(solution)/shard_map/ppermute | solution.py:630
  718.1 74.0 %collective-permute-start.34 = (bf16[128,2816]{1,0:T(8,128)(2,1)S(1)}, bf16[128,2816]{1,0:T(8,128)(2,1)S(1)}, u32[]{:S(2)}, u32[]{:S(2)}) collective-permute-start(bf16[128,2816]{1,0:T(8,128)(2,1)S(1)} %get-tuple-element.313), channel_id=1, source_target_pairs={{8,0},{16,8},{24,16},{28,24},{20,28},{12,20},{4,12},{0,4},{9,1},{1... | collective-permute-start | bytes 2162696 | tf_op jit(solution)/shard_map/ppermute | solution.py:633
  795.1 68.4 %collective-permute-start.37 = (bf16[128,2816]{1,0:T(8,128)(2,1)}, bf16[128,2816]{1,0:T(8,128)(2,1)}, u32[]{:S(2)}, u32[]{:S(2)}) collective-permute-start(bf16[128,2816]{1,0:T(8,128)(2,1)} %get-tuple-element.308), channel_id=1, source_target_pairs={{0,8},{8,16},{16,24},{24,28},{28,20},{20,12},{12,4},{4,0},{1,9},{9... | collective-permute-start | bytes 2162696 | tf_op jit(solution)/shard_map/ppermute | solution.py:630
  795.1 68.4 %collective-permute-start.39 = (bf16[128,2816]{1,0:T(8,128)(2,1)}, bf16[128,2816]{1,0:T(8,128)(2,1)}, u32[]{:S(2)}, u32[]{:S(2)}) collective-permute-start(bf16[128,2816]{1,0:T(8,128)(2,1)} %get-tuple-element.307), channel_id=1, source_target_pairs={{8,0},{16,8},{24,16},{28,24},{20,28},{12,20},{4,12},{0,4},{9,1},{1... | collective-permute-start | bytes 2162696 | tf_op jit(solution)/shard_map/ppermute | solution.py:633
  818.4 92.2 %all-to-all-start.2 = ((bf16[4,640,1024]{2,1,0:T(8,128)(2,1)}), bf16[4,640,1024]{2,1,0:T(8,128)(2,1)}, u32[]{:S(2)}, u32[]{:S(2)}) async-start(bf16[4,640,1024]{2,1,0:T(8,128)(2,1)} %pad_maximum_fusion.1), calls=%async_computation.2 | async-start | bytes 10485760 | tf_op jit(solution)/shard_map/all_to_all | solution.py:894
  1015.0 76.7 %all-to-all-start.3 = ((bf16[4,256,1024]{2,1,0:T(8,128)(2,1)}), bf16[4,256,1024]{2,1,0:T(8,128)(2,1)}, u32[]{:S(2)}, u32[]{:S(2)}) async-start(bf16[4,256,1024]{2,1,0:T(8,128)(2,1)} %pad_maximum_fusion.4), calls=%async_computation.4 | async-start | bytes 4194304 | tf_op jit(solution)/shard_map/all_to_all | solution.py:923
  (149 other events, 4373.3 us)
Sparse Core Ops, SparseCore 0:
  155.2 137.1 all-gather.1
  706.7 162.2 reduce-scatter.1

commit v10 on v8

--- a/solution.py
+++ b/solution.py
@@ -99,7 +99,7 @@
             for h in range(heads):
                 kx = jnp.concatenate([k_ref[keys, h // 2 * LANES : (h // 2 + 1) * LANES], ks], axis=1)
                 scores.append(lax.dot_general(kx, queries[h], NT, preferred_element_type=jnp.float32))
-            out = []
+            kept = []
             for h in range(heads):
                 peak, total, acc = carry[h]
                 s = scores[h]
@@ -109,8 +109,12 @@
                 p = jnp.exp(s - new)
                 scale = jnp.exp(peak - new)
                 total = total * scale + jnp.sum(p, axis=0, keepdims=True)
+                kept.append((new, total, acc, scale, p.astype(jnp.bfloat16)))
+            out = []
+            for h in range(heads):
+                new, total, acc, scale, p = kept[h]
                 vt = vt_ref[h * HEAD_DIM : (h + 1) * HEAD_DIM, keys]
-                acc = acc * scale + jnp.dot(vt, p.astype(jnp.bfloat16), preferred_element_type=jnp.float32)
+                acc = acc * scale + jnp.dot(vt, p, preferred_element_type=jnp.float32)
                 out.append((new, total, acc))
             return tuple(out)
 
@@ -248,27 +252,29 @@
 
             def step(qb, carry):
                 at = block_at(qb, own, tile)
-                weights, grads = [], []
+                weights, grads, scores, products = [], [], [], []
                 for h in range(2):
-                    qx, dox = qx_ref[h, at, :], dox_ref[h, at, :]
-                    s = lax.dot_general(kx, qx, NT, preferred_element_type=jnp.float32)
+                    scores.append(lax.dot_general(kx, qx_ref[h, at, :], NT, preferred_element_type=jnp.float32))
+                    products.append(lax.dot_general(vx, dox_ref[h, at, :], NT, preferred_element_type=jnp.float32))
+                for h in range(2):
+                    s = scores[h]
                     if which == 1:
                         s = s + bias_ref[h, kb - qb + 1]
                     p = jnp.exp(s)
-                    dp = lax.dot_general(vx, dox, NT, preferred_element_type=jnp.float32)
-                    ds = p * dp
+                    ds = p * products[h]
                     if which == 1:
                         dsum_ref[h, kb - qb + 1] += ds
                     else:
                         fsum_ref[h, which // 2] += jnp.sum(ds.reshape(tile // 8, 8, tile), axis=0)
                     weights.append(p.astype(jnp.bfloat16))
                     grads.append(ds.astype(jnp.bfloat16))
-                    rows = slice(h * HEAD_DIM, (h + 1) * HEAD_DIM)
-                    dqt_ref[rows, at] += jnp.dot(kt_ref[rows, keys], grads[h], preferred_element_type=jnp.float32)
                 both_do = jnp.concatenate([dox_ref[0, at, :LANES], dox_ref[1, at, :LANES]], axis=0)
                 both_q = jnp.concatenate([qx_ref[0, at, :LANES], qx_ref[1, at, :LANES]], axis=0)
                 dva_ref[...] += jnp.dot(jnp.concatenate(weights, axis=1), both_do, preferred_element_type=jnp.float32)
                 dka_ref[...] += jnp.dot(jnp.concatenate(grads, axis=1), both_q, preferred_element_type=jnp.float32)
+                for h in range(2):
+                    part = slice(h * HEAD_DIM, (h + 1) * HEAD_DIM)
+                    dqt_ref[part, at] += jnp.dot(kt_ref[part, keys], grads[h], preferred_element_type=jnp.float32)
                 return carry
 
             return step

time: 1120 us -> 1100 us (0.982)
  Pallas kernels: 324 us -> 251 us
  waiting for transfers between devices: 290 us -> 326 us
  starting transfers between devices: 87.4 us -> 100 us
    pallas_call x4, Pallas kernels: 147 us -> 99.4 us  [attend_backward(): pl.pallas_call(bwd_kernel, name='attend_backward', out_shape=(low, low, l...]
    pallas_call x1, Pallas kernels: 67.4 us -> 42.3 us  [attend_forward(): pl.pallas_call(fwd_kernel, name='attend_forward', out_shape=(jax.ShapeDty...]
    ppermute x4, waiting for transfers between devices: 69.2 us -> 82.9 us  [step(): self.forward = lax.ppermute(self.forward, SEQ, self.ahead)]
    ppermute x3, waiting for transfers between devices: 43.3 us -> 54.8 us  [step(): lax.ppermute(self.backward, SEQ, [(b, a) for a, b in self.ahead])]
  transfers between devices with their start and end apart: 57 -> 57, of which waited for: 21 -> 24; matrix products, arithmetic and copies ran while one was open for 25% -> 25% of each run, Pallas kernels for 29% -> 23%
where the time goes in v10:
time: 1100 us; the launch traced here: 1090 us
  waiting for transfers between devices  326 us (30%)
  Pallas kernels  251 us (23%)
  matrix products  193 us (18%)
  starting transfers between devices  100 us (9%)
  local copies, waits for them, and re-layouts  97.3 us (9%)
  other arithmetic  96.8 us (9%)
  between operations  28.3 us (3%)
    ppermute x28, waiting for transfers between devices, partner(): return lax.ppermute(value, axis, [(i, i ^ offset) for i in range(count)])  135 us
    pallas_call x4, Pallas kernels, expert_block(): pl.pallas_call(expert_kernel, name='expert_block', out_shape=(whole, whol...  109 us
    dot_general x16, matrix products, dot_tn(): lax.dot_general(a, b, (((0,), (0,)), ((), ())), preferred_element_type=jn...  101 us
    pallas_call x4, Pallas kernels, attend_backward(): pl.pallas_call(bwd_kernel, name='attend_backward', out_shape=(low, low, l...  99.4 us
    ppermute x4, waiting for transfers between devices, step(): self.forward = lax.ppermute(self.forward, SEQ, self.ahead)  82.9 us
    dot_general x9, matrix products, dot32(): return jnp.dot(a, b, preferred_element_type=jnp.float32)  63.1 us
    ppermute x3, waiting for transfers between devices, step(): lax.ppermute(self.backward, SEQ, [(b, a) for a, b in self.ahead])  54.8 us
    unnamed x240, local copies, waits for them, and re-layouts  42.4 us
  transfers between devices with their start and end apart: 57, of which 24 were waited for; matrix products, arithmetic and copies ran while one was open for 25% of the time, Pallas kernels for 23%

profile of v10, /device:TPU:0, one launch (start us, length us, event | category | flops | bytes accessed | tf_op | source)
XLA Modules:
  0.0 1093.2 jit_solution(16244179062822659289)
XLA Ops:
  62.0 21.9 %collective-permute-done.1 = bf16[2,32,2688]{2,1,0:T(8,128)(2,1)} collective-permute-done((bf16[2,32,2688]{2,1,0:T(8,128)(2,1)S(1)}, bf16[2,32,2688]{2,1,0:T(8,128)(2,1)}, u32[]{:S(2)}, u32[]{:S(2)}) %collective-permute-start.1) | collective-permute-done | bytes 344096 | tf_op jit(solution)/shard_map/ppermute | solution.py:513
  109.8 24.1 %collective-permute-done.6 = bf16[2,2,2,32,2688]{4,3,2,1,0:T(8,128)(2,1)S(1)} collective-permute-done((bf16[2,2,2,32,2688]{4,3,2,1,0:T(8,128)(2,1)S(1)}, bf16[2,2,2,32,2688]{4,3,2,1,0:T(8,128)(2,1)S(1)}, u32[]{:S(2)}, u32[]{:S(2)}) %collective-permute-start.6) | collective-permute-done | bytes 1376288 | tf_op jit(solution)/shard_map/ppermute | solution.py:513
  178.9 29.5 %collective-permute-done.12 = bf16[128,5632]{1,0:T(8,128)(2,1)} collective-permute-done((bf16[128,5632]{1,0:T(8,128)(2,1)}, bf16[128,5632]{1,0:T(8,128)(2,1)}, u32[]{:S(2)}, u32[]{:S(2)}) %collective-permute-start.12) | collective-permute-done | bytes 1441824 | tf_op jit(solution)/shard_map/ppermute | solution.py:586
  215.5 42.3 %attend_forward.1 = (bf16[2048,512]{1,0:T(8,128)(2,1)}, f32[4,2,2048]{2,1,0:T(2,128)S(1)}) custom-call(s32[2,8]{1,0:T(2,128)S(1)} %pad_add_fusion.ranges, f32[8,2]{1,0:T(8,128)S(1)} %maximum_convert_fusion.ends, s32[1]{0:T(128)} %bitcast.23.own, bf16[2048,1536]{1,0:T(8,128)(2,1)} %convolution_convert_fusion.q_ref.k_ref.v_ref, ...), custom_call_target="tpu_custom_call" | custom-call | flops 8589934592 | bytes 8388608 | tf_op jit(solution)/shard_map/attend_forward/pallas_call | solution.py:172
  274.1 18.1 %collective-permute-done.15 = bf16[128,5632]{1,0:T(8,128)(2,1)S(1)} collective-permute-done((bf16[128,5632]{1,0:T(8,128)(2,1)}, bf16[128,5632]{1,0:T(8,128)(2,1)S(1)}, u32[]{:S(2)}, u32[]{:S(2)}) %collective-permute-start.15) | collective-permute-done | bytes 1441824 | tf_op jit(solution)/shard_map/ppermute | solution.py:589
  308.7 21.2 %collective-permute-done.19 = bf16[128,5632]{1,0:T(8,128)(2,1)} collective-permute-done((bf16[128,5632]{1,0:T(8,128)(2,1)}, bf16[128,5632]{1,0:T(8,128)(2,1)}, u32[]{:S(2)}, u32[]{:S(2)}) %collective-permute-start.19) | collective-permute-done | bytes 1441824 | tf_op jit(solution)/shard_map/ppermute | solution.py:586
  334.2 34.4 %collective-permute-done.20 = bf16[128,5632]{1,0:T(8,128)(2,1)S(1)} collective-permute-done((bf16[128,5632]{1,0:T(8,128)(2,1)}, bf16[128,5632]{1,0:T(8,128)(2,1)S(1)}, u32[]{:S(2)}, u32[]{:S(2)}) %collective-permute-start.20) | collective-permute-done | bytes 1441824 | tf_op jit(solution)/shard_map/ppermute | solution.py:589
  369.8 18.4 %collective-permute-done.21 = bf16[128,5632]{1,0:T(8,128)(2,1)S(1)} collective-permute-done((bf16[128,5632]{1,0:T(8,128)(2,1)}, bf16[128,5632]{1,0:T(8,128)(2,1)S(1)}, u32[]{:S(2)}, u32[]{:S(2)}) %collective-permute-start.21) | collective-permute-done | bytes 1441824 | tf_op jit(solution)/shard_map/ppermute | solution.py:586
  424.1 26.9 %expert_block.4 = (bf16[2560,2816]{1,0:T(8,128)(2,1)}, bf16[2560,2816]{1,0:T(8,128)(2,1)}, bf16[2560,2816]{1,0:T(8,128)(2,1)}, bf16[656,1024]{1,0:T(8,128)(2,1)S(1)}) custom-call(s32[1]{0:T(128)} %constant.371.clone.1.own_ref, bf16[656,1024]{1,0:T(8,128)(2,1)S(1)} %copy-done.26, bf16[640,1024]{1,0:T(8,128)(2,1)S(1)} %copy-done.42, ...), custom_call_target="tpu_custom_call" | custom-call | flops 18454937600 | bytes 28114944 | tf_op jit(solution)/shard_map/expert_block/pallas_call | solution.py:474
  451.0 27.0 %expert_block.5 = (bf16[2560,2816]{1,0:T(8,128)(2,1)}, bf16[2560,2816]{1,0:T(8,128)(2,1)}, bf16[2560,2816]{1,0:T(8,128)(2,1)}, bf16[656,1024]{1,0:T(8,128)(2,1)S(1)}) custom-call(s32[1]{0:T(128)} %constant.371.clone.1.own_ref, bf16[656,1024]{1,0:T(8,128)(2,1)S(1)} %collective-permute-done.23.x_ref, ...), custom_call_target="tpu_custom_call", output_to_operand_aliasing={{0}: (6, {}), {1}: (7, {}), {2}: (8, {})} | custom-call | flops 18454937600 | bytes 28114944 | tf_op jit(solution)/shard_map/expert_block/pallas_call | solution.py:474
  479.3 28.0 %expert_block.6 = (bf16[2560,2816]{1,0:T(8,128)(2,1)}, bf16[2560,2816]{1,0:T(8,128)(2,1)}, bf16[2560,2816]{1,0:T(8,128)(2,1)}, bf16[656,1024]{1,0:T(8,128)(2,1)S(1)}) custom-call(s32[1]{0:T(128)} %constant.371.clone.1.own_ref, bf16[656,1024]{1,0:T(8,128)(2,1)} %collective-permute-done.25.x_ref, ...), custom_call_target="tpu_custom_call", output_to_operand_aliasing={{0}: (6, {}), {1}: (7, {}), {2}: (8, {})} | custom-call | flops 18454937600 | bytes 28114944 | tf_op jit(solution)/shard_map/expert_block/pallas_call | solution.py:474
  509.4 27.4 %expert_block.7 = (bf16[2560,2816]{1,0:T(8,128)(2,1)}, bf16[2560,2816]{1,0:T(8,128)(2,1)}, bf16[2560,2816]{1,0:T(8,128)(2,1)}, bf16[656,1024]{1,0:T(8,128)(2,1)S(1)}) custom-call(s32[1]{0:T(128)} %constant.371.clone.1.own_ref, bf16[656,1024]{1,0:T(8,128)(2,1)S(1)} %collective-permute-done.22.x_ref, ...), custom_call_target="tpu_custom_call", output_to_operand_aliasing={{0}: (6, {}), {1}: (7, {}), {2}: (8, {})} | custom-call | flops 18454937600 | bytes 28114944 | tf_op jit(solution)/shard_map/expert_block/pallas_call | solution.py:474
  592.1 22.6 %convolution_convert_fusion.2 = bf16[1024,2816]{1,0:T(8,128)(2,1)} fusion(bf16[2560,2816]{1,0:T(8,128)(2,1)} %get-tuple-element.209, bf16[640,1024]{1,0:T(8,128)(2,1)} %slice.256, bf16[640,1024]{1,0:T(8,128)(2,1)} %slice.255, bf16[640,1024]{1,0:T(8,128)(2,1)} %slice.254, bf16[640,1024]{1,0:T(8,128)(2,1)S(1)} %copy-done.68), kind=kOutput, calls=%fused_computation.21 | convolution fusion | flops 14787805184 | bytes 25427968 | tf_op jit(solution)/shard_map/dot_general | solution.py:508
  614.7 20.8 %convolution_convert_fusion.3 = bf16[1024,2816]{1,0:T(8,128)(2,1)} fusion(bf16[2560,2816]{1,0:T(8,128)(2,1)} %get-tuple-element.208, bf16[640,1024]{1,0:T(8,128)(2,1)S(1)} %copy-done.71, bf16[640,1024]{1,0:T(8,128)(2,1)S(1)} %copy-done.70, bf16[640,1024]{1,0:T(8,128)(2,1)S(1)} %copy-done.69, bf16[640,1024]{1,0:T(8,128)(2,1)S(1)} %copy-done.68), kind=kOutput, calls=%fused_computation.22 | convolution fusion | flops 14787805184 | bytes 25427968 | tf_op jit(solution)/shard_map/dot_general | solution.py:508
  648.9 25.2 %attend_backward.4 = (bf16[2048,512]{1,0:T(8,128)(2,1)S(1)}, bf16[2048,512]{1,0:T(8,128)(2,1)S(1)}, bf16[2048,512]{1,0:T(8,128)(2,1)S(1)}, f32[2,3,512]{2,1,0:T(4,128)S(1)}, f32[2,2,256]{2,1,0:T(2,128)S(1)}) custom-call(s32[2,8]{1,0:T(2,128)S(1)} %copy-done.41, f32[8,2]{1,0:T(8,128)S(1)} %copy-done.39, s32[2]{0:T(128)S(1)} %get-tuple-element.417.own, ...), custom_call_target="tpu_custom_call" | custom-call | flops 5368709120 | bytes 4194304 | tf_op jit(solution)/shard_map/attend_backward/pallas_call | solution.py:353
  678.2 20.9 %convolution_convert_fusion.1 = bf16[2816,1024]{1,0:T(8,128)(2,1)} fusion(bf16[2560,2816]{1,0:T(8,128)(2,1)} %get-tuple-element.248, bf16[640,1024]{1,0:T(8,128)(2,1)S(1)} %copy-done.37, bf16[640,1024]{1,0:T(8,128)(2,1)S(1)} %copy-done.34, bf16[640,1024]{1,0:T(8,128)(2,1)S(1)} %copy-done.31, bf16[640,1024]{1,0:T(8,128)(2,1)S(1)} %copy-done.43, ...), kind=kOutput, calls=%fused_computation.20 | convolution fusion | flops 14793048064 | bytes 25438208 | tf_op jit(solution)/shard_map/dot_general | solution.py:508
  714.1 24.8 %attend_backward.5 = (bf16[2048,512]{1,0:T(8,128)(2,1)S(1)}, bf16[2048,512]{1,0:T(8,128)(2,1)S(1)}, bf16[2048,512]{1,0:T(8,128)(2,1)S(1)}, f32[2,3,512]{2,1,0:T(4,128)S(1)}, f32[2,2,256]{2,1,0:T(2,128)S(1)}) custom-call(s32[2,8]{1,0:T(2,128)S(1)} %copy-done.41, f32[8,2]{1,0:T(8,128)S(1)} %copy-done.39, ...), custom_call_target="tpu_custom_call", output_to_operand_aliasing={{0}: (12, {}), {1}: (13, {}), {2}: (14, {})} | custom-call | flops 5368709120 | bytes 4194304 | tf_op jit(solution)/shard_map/attend_backward/pallas_call | solution.py:353
  748.2 16.3 %collective-permute-done.32 = bf16[128,2816]{1,0:T(8,128)(2,1)S(1)} collective-permute-done((bf16[128,2816]{1,0:T(8,128)(2,1)S(1)}, bf16[128,2816]{1,0:T(8,128)(2,1)S(1)}, u32[]{:S(2)}, u32[]{:S(2)}) %collective-permute-start.32) | collective-permute-done | bytes 720928 | tf_op jit(solution)/shard_map/ppermute | solution.py:636
  784.6 17.6 %multiply_convert_fusion = bf16[2560,1024]{1,0:T(8,128)(2,1)S(1)} fusion(bf16[2560,2816]{1,0:T(8,128)(2,1)} %get-tuple-element.248, bf16[2816,1024]{1,0:T(8,128)(2,1)S(1)} %bitcast.278, f32[2560]{0:T(1024)S(1)} %pad_maximum_fusion.23), kind=kOutput, calls=%fused_computation.7 | convolution fusion | flops 14769192960 | bytes 25438208 | tf_op jit(solution)/shard_map/dot_general | solution.py:500
  822.2 24.5 %attend_backward.6 = (bf16[2048,512]{1,0:T(8,128)(2,1)S(1)}, bf16[2048,512]{1,0:T(8,128)(2,1)S(1)}, bf16[2048,512]{1,0:T(8,128)(2,1)S(1)}, f32[2,3,512]{2,1,0:T(4,128)S(1)}, f32[2,2,256]{2,1,0:T(2,128)S(1)}) custom-call(s32[2,8]{1,0:T(2,128)S(1)} %copy-done.41, f32[8,2]{1,0:T(8,128)S(1)} %copy-done.39, ...), custom_call_target="tpu_custom_call", output_to_operand_aliasing={{0}: (12, {}), {1}: (13, {}), {2}: (14, {})} | custom-call | flops 5368709120 | bytes 4194304 | tf_op jit(solution)/shard_map/attend_backward/pallas_call | solution.py:353
  865.2 24.9 %attend_backward.7 = (bf16[2048,512]{1,0:T(8,128)(2,1)S(1)}, bf16[2048,512]{1,0:T(8,128)(2,1)S(1)}, bf16[2048,512]{1,0:T(8,128)(2,1)S(1)}, f32[2,3,512]{2,1,0:T(4,128)S(1)}, f32[2,2,256]{2,1,0:T(2,128)S(1)}) custom-call(s32[2,8]{1,0:T(2,128)S(1)} %copy-done.41, f32[8,2]{1,0:T(8,128)S(1)} %copy-done.39, ...), custom_call_target="tpu_custom_call", output_to_operand_aliasing={{0}: (12, {}), {1}: (13, {}), {2}: (14, {})} | custom-call | flops 5368709120 | bytes 4194304 | tf_op jit(solution)/shard_map/attend_backward/pallas_call | solution.py:353
  946.3 16.2 %collective-permute-done.42 = bf16[4,256,512]{2,1,0:T(8,128)(2,1)S(1)} collective-permute-done((bf16[4,256,512]{2,1,0:T(8,128)(2,1)S(1)}, bf16[4,256,512]{2,1,0:T(8,128)(2,1)S(1)}, u32[]{:S(2)}, u32[]{:S(2)}) %collective-permute-start.42) | collective-permute-done | bytes 1048608 | tf_op jit(solution)/shard_map/ppermute | solution.py:513
  972.9 13.8 %collective-permute-done.43 = bf16[4,256,512]{2,1,0:T(8,128)(2,1)S(1)} collective-permute-done((bf16[4,256,512]{2,1,0:T(8,128)(2,1)S(1)}, bf16[4,256,512]{2,1,0:T(8,128)(2,1)S(1)}, u32[]{:S(2)}, u32[]{:S(2)}) %collective-permute-start.43) | collective-permute-done | bytes 1048608 | tf_op jit(solution)/shard_map/ppermute | solution.py:513
  1036.0 20.2 %collective-permute-done.47 = bf16[5,2,32,512]{3,2,0,1:T(8,128)(2,1)S(1)} collective-permute-done((bf16[5,2,32,512]{3,2,0,1:T(8,128)(2,1)S(1)}, bf16[5,2,32,512]{3,2,0,1:T(8,128)(2,1)S(1)}, u32[]{:S(2)}, u32[]{:S(2)}) %collective-permute-start.47) | collective-permute-done | bytes 327712 | tf_op jit(solution)/shard_map/ppermute | solution.py:513
  (571 shorter events, 497.9 us)
Async XLA Ops:
  7.2 411.6 %all-gather.2.cloned.1.call-start = ((), (), s32[]{:S(2)}) async-start(), calls=%async_computation.7 | async-start | bytes 6488064 | tf_op jit(solution)/shard_map/all_gather | solution.py:744
  19.5 84.7 %collective-permute-start.3 = (bf16[256,1024]{1,0:T(8,128)(2,1)}, bf16[256,1024]{1,0:T(8,128)(2,1)}, u32[]{:S(2)}, u32[]{:S(2)}) collective-permute-start(bf16[256,1024]{1,0:T(8,128)(2,1)} %get-tuple-element.343), channel_id=1, source_target_pairs={{0,8},{8,0},{16,24},{24,16},{1,9},{9,1},{17,25},{25,17},{2,10},{10... | collective-permute-start | bytes 1572872 | tf_op jit(solution)/shard_map/ppermute | solution.py:513
  21.1 83.2 %collective-permute-start.4 = (bf16[256,1024]{1,0:T(8,128)(2,1)}, bf16[256,1024]{1,0:T(8,128)(2,1)}, u32[]{:S(2)}, u32[]{:S(2)}) collective-permute-start(bf16[256,1024]{1,0:T(8,128)(2,1)} %get-tuple-element.342), channel_id=1, source_target_pairs={{0,16},{8,24},{16,0},{24,8},{1,17},{9,25},{17,1},{25,9},{2,18},{10... | collective-permute-start | bytes 1572872 | tf_op jit(solution)/shard_map/ppermute | solution.py:513
  23.7 80.6 %collective-permute-start.5 = (bf16[256,1024]{1,0:T(8,128)(2,1)}, bf16[256,1024]{1,0:T(8,128)(2,1)}, u32[]{:S(2)}, u32[]{:S(2)}) collective-permute-start(bf16[256,1024]{1,0:T(8,128)(2,1)} %get-tuple-element.344), channel_id=1, source_target_pairs={{0,24},{8,16},{16,8},{24,0},{1,25},{9,17},{17,9},{25,1},{2,26},{10... | collective-permute-start | bytes 1572872 | tf_op jit(solution)/shard_map/ppermute | solution.py:513
  23.9 112.1 %collective-permute-start.7 = (bf16[256,1024]{1,0:T(8,128)(2,1)}, bf16[256,1024]{1,0:T(8,128)(2,1)}, u32[]{:S(2)}, u32[]{:S(2)}) collective-permute-start(bf16[256,1024]{1,0:T(8,128)(2,1)} %get-tuple-element.157), channel_id=1, source_target_pairs={{0,4},{4,0},{1,5},{5,1},{2,6},{6,2},{3,7},{7,3},{8,12},{12,8},{9,1... | collective-permute-start | bytes 1572872 | tf_op jit(solution)/shard_map/ppermute | solution.py:513
  152.8 55.6 %collective-permute-start.12 = (bf16[128,5632]{1,0:T(8,128)(2,1)}, bf16[128,5632]{1,0:T(8,128)(2,1)}, u32[]{:S(2)}, u32[]{:S(2)}) collective-permute-start(bf16[128,5632]{1,0:T(8,128)(2,1)} %pad_maximum_fusion.5), channel_id=1, source_target_pairs={{0,8},{8,16},{16,24},{24,28},{28,20},{20,12},{12,4},{4,0},{1,9},{9... | collective-permute-start | bytes 4325384 | tf_op jit(solution)/shard_map/ppermute | solution.py:586
  153.6 57.2 %collective-permute-start.13 = (bf16[128,5632]{1,0:T(8,128)(2,1)}, bf16[128,5632]{1,0:T(8,128)(2,1)}, u32[]{:S(2)}, u32[]{:S(2)}) collective-permute-start(bf16[128,5632]{1,0:T(8,128)(2,1)} %pad_maximum_fusion.5), channel_id=1, source_target_pairs={{8,0},{16,8},{24,16},{28,24},{20,28},{12,20},{4,12},{0,4},{9,1},{1... | collective-permute-start | bytes 4325384 | tf_op jit(solution)/shard_map/ppermute | solution.py:589
  211.2 62.9 %collective-permute-start.14 = (bf16[128,5632]{1,0:T(8,128)(2,1)}, bf16[128,5632]{1,0:T(8,128)(2,1)}, u32[]{:S(2)}, u32[]{:S(2)}) collective-permute-start(bf16[128,5632]{1,0:T(8,128)(2,1)} %collective-permute-done.12), channel_id=1, source_target_pairs={{0,8},{8,16},{16,24},{24,28},{28,20},{20,12},{12,4},{4,0},{1,9},{9... | collective-permute-start | bytes 4325384 | tf_op jit(solution)/shard_map/ppermute | solution.py:586
  212.8 79.3 %collective-permute-start.15 = (bf16[128,5632]{1,0:T(8,128)(2,1)}, bf16[128,5632]{1,0:T(8,128)(2,1)S(1)}, u32[]{:S(2)}, u32[]{:S(2)}) collective-permute-start(bf16[128,5632]{1,0:T(8,128)(2,1)} %collective-permute-done.13), channel_id=1, source_target_pairs={{8,0},{16,8},{24,16},{28,24},{20,28},{12,20},{4,12},{0,4},{9,1},{1... | collective-permute-start | bytes 4325384 | tf_op jit(solution)/shard_map/ppermute | solution.py:589
  213.5 81.7 %collective-permute-start.16 = (bf16[640,1024]{1,0:T(8,128)(2,1)}, bf16[640,1024]{1,0:T(8,128)(2,1)S(1)}, u32[]{:S(2)}, u32[]{:S(2)}) collective-permute-start(bf16[640,1024]{1,0:T(8,128)(2,1)} %convolution_convert_fusion.12), channel_id=1, source_target_pairs={{0,1},{1,0},{2,3},{3,2},{4,5},{5,4},{6,7},{7,6},{8,9},{9,8},{10,11... | collective-permute-start | bytes 3932168 | tf_op jit(solution)/shard_map/ppermute | solution.py:513
  213.5 82.9 %collective-permute-start.17 = (bf16[640,1024]{1,0:T(8,128)(2,1)}, bf16[640,1024]{1,0:T(8,128)(2,1)S(1)}, u32[]{:S(2)}, u32[]{:S(2)}) collective-permute-start(bf16[640,1024]{1,0:T(8,128)(2,1)} %convolution_convert_fusion.11), channel_id=1, source_target_pairs={{0,2},{1,3},{2,0},{3,1},{4,6},{5,7},{6,4},{7,5},{8,10},{9,11},{10,... | collective-permute-start | bytes 3932168 | tf_op jit(solution)/shard_map/ppermute | solution.py:513
  214.0 83.4 %collective-permute-start.18 = (bf16[640,1024]{1,0:T(8,128)(2,1)}, bf16[640,1024]{1,0:T(8,128)(2,1)S(1)}, u32[]{:S(2)}, u32[]{:S(2)}) collective-permute-start(bf16[640,1024]{1,0:T(8,128)(2,1)} %convolution_convert_fusion.10), channel_id=1, source_target_pairs={{0,3},{1,2},{2,1},{3,0},{4,7},{5,6},{6,5},{7,4},{8,11},{9,10},{10,... | collective-permute-start | bytes 3932168 | tf_op jit(solution)/shard_map/ppermute | solution.py:513
  298.5 90.9 %all-to-all-start = ((bf16[8,256,512]{2,1,0:T(8,128)(2,1)}), bf16[8,256,512]{2,1,0:T(8,128)(2,1)}, u32[]{:S(2)}, u32[]{:S(2)}) async-start(bf16[8,256,512]{2,1,0:T(8,128)(2,1)} %bitcast.39), calls=%async_computation | async-start | bytes 4194304 | tf_op jit(solution)/shard_map/all_to_all | solution.py:795
  304.1 64.4 %collective-permute-start.20 = (bf16[128,5632]{1,0:T(8,128)(2,1)}, bf16[128,5632]{1,0:T(8,128)(2,1)S(1)}, u32[]{:S(2)}, u32[]{:S(2)}) collective-permute-start(bf16[128,5632]{1,0:T(8,128)(2,1)} %copy-done.66), channel_id=1, source_target_pairs={{8,0},{16,8},{24,16},{28,24},{20,28},{12,20},{4,12},{0,4},{9,1},{1... | collective-permute-start | bytes 4325384 | tf_op jit(solution)/shard_map/ppermute | solution.py:589
  329.9 58.3 %collective-permute-start.21 = (bf16[128,5632]{1,0:T(8,128)(2,1)}, bf16[128,5632]{1,0:T(8,128)(2,1)S(1)}, u32[]{:S(2)}, u32[]{:S(2)}) collective-permute-start(bf16[128,5632]{1,0:T(8,128)(2,1)} %collective-permute-done.19), channel_id=1, source_target_pairs={{0,8},{8,16},{16,24},{24,28},{28,20},{20,12},{12,4},{4,0},{1,9},{9... | collective-permute-start | bytes 4325384 | tf_op jit(solution)/shard_map/ppermute | solution.py:586
  412.5 94.9 %collective-permute-start.22 = (bf16[656,1024]{1,0:T(8,128)(2,1)}, bf16[656,1024]{1,0:T(8,128)(2,1)S(1)}, u32[]{:S(2)}, u32[]{:S(2)}) collective-permute-start(bf16[656,1024]{1,0:T(8,128)(2,1)} %pad_maximum_fusion.8), channel_id=1, source_target_pairs={{0,1},{1,0},{2,3},{3,2},{4,5},{5,4},{6,7},{7,6},{8,9},{9,8},{10,11... | collective-permute-start | bytes 4030472 | tf_op jit(solution)/shard_map/ppermute | solution.py:513
  415.2 64.1 %collective-permute-start.25 = (bf16[656,1024]{1,0:T(8,128)(2,1)}, bf16[656,1024]{1,0:T(8,128)(2,1)}, u32[]{:S(2)}, u32[]{:S(2)}) collective-permute-start(bf16[656,1024]{1,0:T(8,128)(2,1)} %pad_maximum_fusion.10), channel_id=1, source_target_pairs={{0,3},{1,2},{2,1},{3,0},{4,7},{5,6},{6,5},{7,4},{8,11},{9,10},{10,... | collective-permute-start | bytes 4030472 | tf_op jit(solution)/shard_map/ppermute | solution.py:513
  578.6 62.3 %all-to-all-start.1 = ((bf16[8,256,512]{2,1,0:T(8,128)(2,1)}), bf16[8,256,512]{2,1,0:T(8,128)(2,1)S(1)}, u32[]{:S(2)}, u32[]{:S(2)}) async-start(bf16[8,256,512]{2,1,0:T(8,128)(2,1)} %bitcast.294), calls=%async_computation.1 | async-start | bytes 4194304 | tf_op jit(solution)/shard_map/all_to_all | solution.py:795
  592.0 303.1 %reduce-scatter.2.cloned.1.call-start = ((), (), s32[]{:S(2)}) async-start(), calls=%async_computation.8 | async-start | bytes 6488064 | tf_op jit(solution)/shard_map/reduce_scatter | solution.py:875
  708.0 56.4 %collective-permute-start.32 = (bf16[128,2816]{1,0:T(8,128)(2,1)S(1)}, bf16[128,2816]{1,0:T(8,128)(2,1)S(1)}, u32[]{:S(2)}, u32[]{:S(2)}) collective-permute-start(bf16[128,2816]{1,0:T(8,128)(2,1)S(1)} %get-tuple-element.320), channel_id=1, source_target_pairs={{0,8},{8,16},{16,24},{24,28},{28,20},{20,12},{12,4},{4,0},{1,9},{9... | collective-permute-start | bytes 2162696 | tf_op jit(solution)/shard_map/ppermute | solution.py:636
  710.1 67.6 %collective-permute-start.34 = (bf16[128,2816]{1,0:T(8,128)(2,1)S(1)}, bf16[128,2816]{1,0:T(8,128)(2,1)S(1)}, u32[]{:S(2)}, u32[]{:S(2)}) collective-permute-start(bf16[128,2816]{1,0:T(8,128)(2,1)S(1)} %get-tuple-element.319), channel_id=1, source_target_pairs={{8,0},{16,8},{24,16},{28,24},{20,28},{12,20},{4,12},{0,4},{9,1},{1... | collective-permute-start | bytes 2162696 | tf_op jit(solution)/shard_map/ppermute | solution.py:639
  780.7 66.0 %collective-permute-start.37 = (bf16[128,2816]{1,0:T(8,128)(2,1)}, bf16[128,2816]{1,0:T(8,128)(2,1)}, u32[]{:S(2)}, u32[]{:S(2)}) collective-permute-start(bf16[128,2816]{1,0:T(8,128)(2,1)} %get-tuple-element.314), channel_id=1, source_target_pairs={{0,8},{8,16},{16,24},{24,28},{28,20},{20,12},{12,4},{4,0},{1,9},{9... | collective-permute-start | bytes 2162696 | tf_op jit(solution)/shard_map/ppermute | solution.py:636
  780.7 66.0 %collective-permute-start.39 = (bf16[128,2816]{1,0:T(8,128)(2,1)}, bf16[128,2816]{1,0:T(8,128)(2,1)}, u32[]{:S(2)}, u32[]{:S(2)}) collective-permute-start(bf16[128,2816]{1,0:T(8,128)(2,1)} %get-tuple-element.313), channel_id=1, source_target_pairs={{8,0},{16,8},{24,16},{28,24},{20,28},{12,20},{4,12},{0,4},{9,1},{1... | collective-permute-start | bytes 2162696 | tf_op jit(solution)/shard_map/ppermute | solution.py:639
  805.9 89.2 %all-to-all-start.2 = ((bf16[4,640,1024]{2,1,0:T(8,128)(2,1)}), bf16[4,640,1024]{2,1,0:T(8,128)(2,1)}, u32[]{:S(2)}, u32[]{:S(2)}) async-start(bf16[4,640,1024]{2,1,0:T(8,128)(2,1)} %pad_maximum_fusion.1), calls=%async_computation.2 | async-start | bytes 10485760 | tf_op jit(solution)/shard_map/all_to_all | solution.py:900
  (143 other events, 4168.3 us)
Sparse Core Ops, SparseCore 0:
  155.2 137.1 all-gather.1
  699.2 161.2 reduce-scatter.1

commit v11 on v10

--- a/solution.py
+++ b/solution.py
@@ -926,16 +926,19 @@
 
     sides = [normed_part[:, rx].astype(LOW) for rx in range(1, split)]
     first = [partner(side[:, :, :half], "x", rx) for rx, side in enumerate(sides, 1)]
+
+    def add_up(own_part, coming):
+        total = own_part + sum(part.astype(jnp.float32) for part in coming)
+        return reorder(total.astype(LOW), z_at)
+
+    def send_back(total):
+        return lax.all_to_all(total, "z", split_axis=0, concat_axis=0, tiled=True)
+
+    first = add_up(normed_part[:, 0, :, :half], first)
     first, rest = lax.optimization_barrier((first, [side[:, :, half:] for side in sides]))
-
-    def send_back(own_part, coming):
-        total = own_part + sum(part.astype(jnp.float32) for part in coming)
-        total = reorder(total.astype(LOW), z_at)
-        return lax.all_to_all(total, "z", split_axis=0, concat_axis=0, tiled=True)
-
-    normed_first = send_back(normed_part[:, 0, :, :half], first)
+    normed_first = send_back(first)
     rest = [partner(side, "x", rx) for rx, side in enumerate(rest, 1)]
-    normed_second = send_back(normed_part[:, 0, :, half:], rest)
+    normed_second = send_back(add_up(normed_part[:, 0, :, half:], rest))
     weight_part = scatter_halve(
         weight_sum.reshape((3 + out_parts,) + (2,) * (nz + nx + ne) + (rows_own, head_width)), halving[:ne]
     )

time: 1100 us -> 1070 us (0.973)
  waiting for transfers between devices: 326 us -> 280 us
  Pallas kernels: 251 us -> 277 us
  starting transfers between devices: 100 us -> 86.1 us
    ppermute x28, waiting for transfers between devices: 135 us -> 99.6 us  [partner(): return lax.ppermute(value, axis, [(i, i ^ offset) for i in range(count)])]
    all_to_all x2, waiting for transfers between devices: 3.6 us -> 33.9 us  [send_back(): return lax.all_to_all(total, 'z', split_axis=0, concat_axis=0, tiled=True)]
    ppermute x6, waiting for transfers between devices: 28.6 us -> 8.49 us  [step(): lax.ppermute(part, SEQ, [(b, a) for a, b in self.ahead])]
    pallas_call x4, Pallas kernels: 99.4 us -> 117 us  [attend_backward(): pl.pallas_call(bwd_kernel, name='attend_backward', out_shape=(low, low, l...]
    ppermute x8, starting transfers between devices: 14.5 us -> 0.39 us  [step(): self.forward = [lax.ppermute(part, SEQ, self.ahead) for part in parts]]
    ppermute x8, waiting for transfers between devices: 16.3 us -> 4 us  [step(): self.forward = [lax.ppermute(part, SEQ, self.ahead) for part in parts]]
    unnamed x240 -> x224, local copies, waits for them, and re-layouts: 42.4 us -> 41.4 us
  transfers between devices with their start and end apart: 57 -> 57, of which waited for: 24 -> 22; matrix products, arithmetic and copies ran while one was open for 25% -> 28% of each run, Pallas kernels for 23% -> 26%
where the time goes in v11:
time: 1070 us; the launch traced here: 1060 us
  waiting for transfers between devices  280 us (26%)
  Pallas kernels  277 us (26%)
  matrix products  197 us (18%)
  other arithmetic  96.1 us (9%)
  local copies, waits for them, and re-layouts  94.8 us (9%)
  starting transfers between devices  86.1 us (8%)
  between operations  28.3 us (3%)
    pallas_call x4, Pallas kernels, attend_backward(): pl.pallas_call(bwd_kernel, name='attend_backward', out_shape=(low, low, l...  117 us
    pallas_call x4, Pallas kernels, expert_block(): pl.pallas_call(expert_kernel, name='expert_block', out_shape=(whole, whol...  109 us
    dot_general x16, matrix products, dot_tn(): lax.dot_general(a, b, (((0,), (0,)), ((), ())), preferred_element_type=jn...  102 us
    ppermute x28, waiting for transfers between devices, partner(): return lax.ppermute(value, axis, [(i, i ^ offset) for i in range(count)])  99.6 us
    ppermute x4, waiting for transfers between devices, step(): self.forward = lax.ppermute(self.forward, SEQ, self.ahead)  73.9 us
    dot_general x9, matrix products, dot32(): return jnp.dot(a, b, preferred_element_type=jnp.float32)  65.3 us
    ppermute x3, waiting for transfers between devices, step(): lax.ppermute(self.backward, SEQ, [(b, a) for a, b in self.ahead])  54.8 us
    pallas_call x1, Pallas kernels, attend_forward(): pl.pallas_call(fwd_kernel, name='attend_forward', out_shape=(jax.ShapeDty...  51.2 us
  transfers between devices with their start and end apart: 57, of which 22 were waited for; matrix products, arithmetic and copies ran while one was open for 28% of the time, Pallas kernels for 26%

profile of v11, /device:TPU:0, one launch (start us, length us, event | category | flops | bytes accessed | tf_op | source)
XLA Modules:
  0.0 1059.9 jit_solution(2808833470411080195)
XLA Ops:
  62.2 21.7 %collective-permute-done.1 = bf16[2,32,2688]{2,1,0:T(8,128)(2,1)} collective-permute-done((bf16[2,32,2688]{2,1,0:T(8,128)(2,1)S(1)}, bf16[2,32,2688]{2,1,0:T(8,128)(2,1)}, u32[]{:S(2)}, u32[]{:S(2)}) %collective-permute-start.1) | collective-permute-done | bytes 344096 | tf_op jit(solution)/shard_map/ppermute | solution.py:513
  89.5 13.2 %collective-permute-done.2 = bf16[2,2,32,2688]{3,2,1,0:T(8,128)(2,1)} collective-permute-done((bf16[2,2,32,2688]{3,2,1,0:T(8,128)(2,1)}, bf16[2,2,32,2688]{3,2,1,0:T(8,128)(2,1)}, u32[]{:S(2)}, u32[]{:S(2)}) %collective-permute-start.2) | collective-permute-done | bytes 688160 | tf_op jit(solution)/shard_map/ppermute | solution.py:513
  109.8 24.1 %collective-permute-done.6 = bf16[2,2,2,32,2688]{4,3,2,1,0:T(8,128)(2,1)S(1)} collective-permute-done((bf16[2,2,2,32,2688]{4,3,2,1,0:T(8,128)(2,1)S(1)}, bf16[2,2,2,32,2688]{4,3,2,1,0:T(8,128)(2,1)S(1)}, u32[]{:S(2)}, u32[]{:S(2)}) %collective-permute-start.6) | collective-permute-done | bytes 1376288 | tf_op jit(solution)/shard_map/ppermute | solution.py:513
  178.9 29.5 %collective-permute-done.12 = bf16[128,5632]{1,0:T(8,128)(2,1)} collective-permute-done((bf16[128,5632]{1,0:T(8,128)(2,1)}, bf16[128,5632]{1,0:T(8,128)(2,1)}, u32[]{:S(2)}, u32[]{:S(2)}) %collective-permute-start.12) | collective-permute-done | bytes 1441824 | tf_op jit(solution)/shard_map/ppermute | solution.py:586
  215.4 51.2 %attend_forward.1 = (bf16[2048,512]{1,0:T(8,128)(2,1)}, f32[4,2,2048]{2,1,0:T(2,128)S(1)}) custom-call(s32[2,8]{1,0:T(2,128)S(1)} %pad_add_fusion.ranges, f32[8,2]{1,0:T(8,128)S(1)} %maximum_convert_fusion.ends, s32[1]{0:T(128)} %bitcast.23.own, bf16[2048,1536]{1,0:T(8,128)(2,1)} %convolution_convert_fusion.q_ref.k_ref.v_ref, ...), custom_call_target="tpu_custom_call" | custom-call | flops 8589934592 | bytes 8388608 | tf_op jit(solution)/shard_map/attend_forward/pallas_call | solution.py:172
  274.1 18.1 %collective-permute-done.15 = bf16[128,5632]{1,0:T(8,128)(2,1)S(1)} collective-permute-done((bf16[128,5632]{1,0:T(8,128)(2,1)}, bf16[128,5632]{1,0:T(8,128)(2,1)S(1)}, u32[]{:S(2)}, u32[]{:S(2)}) %collective-permute-start.15) | collective-permute-done | bytes 1441824 | tf_op jit(solution)/shard_map/ppermute | solution.py:589
  308.7 21.2 %collective-permute-done.19 = bf16[128,5632]{1,0:T(8,128)(2,1)} collective-permute-done((bf16[128,5632]{1,0:T(8,128)(2,1)}, bf16[128,5632]{1,0:T(8,128)(2,1)}, u32[]{:S(2)}, u32[]{:S(2)}) %collective-permute-start.19) | collective-permute-done | bytes 1441824 | tf_op jit(solution)/shard_map/ppermute | solution.py:586
  334.1 34.4 %collective-permute-done.20 = bf16[128,5632]{1,0:T(8,128)(2,1)S(1)} collective-permute-done((bf16[128,5632]{1,0:T(8,128)(2,1)}, bf16[128,5632]{1,0:T(8,128)(2,1)S(1)}, u32[]{:S(2)}, u32[]{:S(2)}) %collective-permute-start.20) | collective-permute-done | bytes 1441824 | tf_op jit(solution)/shard_map/ppermute | solution.py:589
  369.7 18.4 %collective-permute-done.21 = bf16[128,5632]{1,0:T(8,128)(2,1)S(1)} collective-permute-done((bf16[128,5632]{1,0:T(8,128)(2,1)}, bf16[128,5632]{1,0:T(8,128)(2,1)S(1)}, u32[]{:S(2)}, u32[]{:S(2)}) %collective-permute-start.21) | collective-permute-done | bytes 1441824 | tf_op jit(solution)/shard_map/ppermute | solution.py:586
  424.1 27.2 %expert_block.4 = (bf16[2560,2816]{1,0:T(8,128)(2,1)}, bf16[2560,2816]{1,0:T(8,128)(2,1)}, bf16[2560,2816]{1,0:T(8,128)(2,1)}, bf16[656,1024]{1,0:T(8,128)(2,1)S(1)}) custom-call(s32[1]{0:T(128)} %constant.371.clone.1.own_ref, bf16[656,1024]{1,0:T(8,128)(2,1)S(1)} %copy-done.26, bf16[640,1024]{1,0:T(8,128)(2,1)S(1)} %copy-done.42, ...), custom_call_target="tpu_custom_call" | custom-call | flops 18454937600 | bytes 28114944 | tf_op jit(solution)/shard_map/expert_block/pallas_call | solution.py:474
  451.3 26.9 %expert_block.5 = (bf16[2560,2816]{1,0:T(8,128)(2,1)}, bf16[2560,2816]{1,0:T(8,128)(2,1)}, bf16[2560,2816]{1,0:T(8,128)(2,1)}, bf16[656,1024]{1,0:T(8,128)(2,1)S(1)}) custom-call(s32[1]{0:T(128)} %constant.371.clone.1.own_ref, bf16[656,1024]{1,0:T(8,128)(2,1)S(1)} %collective-permute-done.23.x_ref, ...), custom_call_target="tpu_custom_call", output_to_operand_aliasing={{0}: (6, {}), {1}: (7, {}), {2}: (8, {})} | custom-call | flops 18454937600 | bytes 28114944 | tf_op jit(solution)/shard_map/expert_block/pallas_call | solution.py:474
  479.5 28.0 %expert_block.6 = (bf16[2560,2816]{1,0:T(8,128)(2,1)}, bf16[2560,2816]{1,0:T(8,128)(2,1)}, bf16[2560,2816]{1,0:T(8,128)(2,1)}, bf16[656,1024]{1,0:T(8,128)(2,1)S(1)}) custom-call(s32[1]{0:T(128)} %constant.371.clone.1.own_ref, bf16[656,1024]{1,0:T(8,128)(2,1)} %collective-permute-done.25.x_ref, ...), custom_call_target="tpu_custom_call", output_to_operand_aliasing={{0}: (6, {}), {1}: (7, {}), {2}: (8, {})} | custom-call | flops 18454937600 | bytes 28114944 | tf_op jit(solution)/shard_map/expert_block/pallas_call | solution.py:474
  509.6 27.3 %expert_block.7 = (bf16[2560,2816]{1,0:T(8,128)(2,1)}, bf16[2560,2816]{1,0:T(8,128)(2,1)}, bf16[2560,2816]{1,0:T(8,128)(2,1)}, bf16[656,1024]{1,0:T(8,128)(2,1)S(1)}) custom-call(s32[1]{0:T(128)} %constant.371.clone.1.own_ref, bf16[656,1024]{1,0:T(8,128)(2,1)S(1)} %collective-permute-done.22.x_ref, ...), custom_call_target="tpu_custom_call", output_to_operand_aliasing={{0}: (6, {}), {1}: (7, {}), {2}: (8, {})} | custom-call | flops 18454937600 | bytes 28114944 | tf_op jit(solution)/shard_map/expert_block/pallas_call | solution.py:474
  578.7 13.4 %all-to-all-start.1 = ((bf16[8,256,512]{2,1,0:T(8,128)(2,1)}), bf16[8,256,512]{2,1,0:T(8,128)(2,1)S(1)}, u32[]{:S(2)}, u32[]{:S(2)}) async-start(bf16[8,256,512]{2,1,0:T(8,128)(2,1)} %bitcast.294), calls=%async_computation.1 | async-start | bytes 4194304 | tf_op jit(solution)/shard_map/all_to_all | solution.py:795
  592.2 22.6 %convolution_convert_fusion.2 = bf16[1024,2816]{1,0:T(8,128)(2,1)} fusion(bf16[2560,2816]{1,0:T(8,128)(2,1)} %get-tuple-element.209, bf16[640,1024]{1,0:T(8,128)(2,1)} %slice.256, bf16[640,1024]{1,0:T(8,128)(2,1)} %slice.255, bf16[640,1024]{1,0:T(8,128)(2,1)} %slice.254, bf16[640,1024]{1,0:T(8,128)(2,1)S(1)} %copy-done.64), kind=kOutput, calls=%fused_computation.21 | convolution fusion | flops 14787805184 | bytes 25427968 | tf_op jit(solution)/shard_map/dot_general | solution.py:508
  614.9 20.9 %convolution_convert_fusion.3 = bf16[1024,2816]{1,0:T(8,128)(2,1)} fusion(bf16[2560,2816]{1,0:T(8,128)(2,1)} %get-tuple-element.208, bf16[640,1024]{1,0:T(8,128)(2,1)S(1)} %copy-done.67, bf16[640,1024]{1,0:T(8,128)(2,1)S(1)} %copy-done.66, bf16[640,1024]{1,0:T(8,128)(2,1)S(1)} %copy-done.65, bf16[640,1024]{1,0:T(8,128)(2,1)S(1)} %copy-done.64), kind=kOutput, calls=%fused_computation.22 | convolution fusion | flops 14787805184 | bytes 25427968 | tf_op jit(solution)/shard_map/dot_general | solution.py:508
  649.0 29.4 %attend_backward.4 = (bf16[2048,512]{1,0:T(8,128)(2,1)S(1)}, bf16[2048,512]{1,0:T(8,128)(2,1)S(1)}, bf16[2048,512]{1,0:T(8,128)(2,1)S(1)}, f32[2,3,512]{2,1,0:T(4,128)S(1)}, f32[2,2,256]{2,1,0:T(2,128)S(1)}) custom-call(s32[2,8]{1,0:T(2,128)S(1)} %copy-done.41, f32[8,2]{1,0:T(8,128)S(1)} %copy-done.39, s32[2]{0:T(128)S(1)} %get-tuple-element.417.own, ...), custom_call_target="tpu_custom_call" | custom-call | flops 5368709120 | bytes 4194304 | tf_op jit(solution)/shard_map/attend_backward/pallas_call | solution.py:353
  687.4 20.9 %convolution_convert_fusion.1 = bf16[2816,1024]{1,0:T(8,128)(2,1)} fusion(bf16[2560,2816]{1,0:T(8,128)(2,1)} %get-tuple-element.248, bf16[640,1024]{1,0:T(8,128)(2,1)S(1)} %copy-done.37, bf16[640,1024]{1,0:T(8,128)(2,1)S(1)} %copy-done.34, bf16[640,1024]{1,0:T(8,128)(2,1)S(1)} %copy-done.31, bf16[640,1024]{1,0:T(8,128)(2,1)S(1)} %copy-done.43, ...), kind=kOutput, calls=%fused_computation.20 | convolution fusion | flops 14793048064 | bytes 25438208 | tf_op jit(solution)/shard_map/dot_general | solution.py:508
  718.7 29.0 %attend_backward.5 = (bf16[2048,512]{1,0:T(8,128)(2,1)S(1)}, bf16[2048,512]{1,0:T(8,128)(2,1)S(1)}, bf16[2048,512]{1,0:T(8,128)(2,1)S(1)}, f32[2,3,512]{2,1,0:T(4,128)S(1)}, f32[2,2,256]{2,1,0:T(2,128)S(1)}) custom-call(s32[2,8]{1,0:T(2,128)S(1)} %copy-done.41, f32[8,2]{1,0:T(8,128)S(1)} %copy-done.39, ...), custom_call_target="tpu_custom_call", output_to_operand_aliasing={{0}: (12, {}), {1}: (13, {}), {2}: (14, {})} | custom-call | flops 5368709120 | bytes 4194304 | tf_op jit(solution)/shard_map/attend_backward/pallas_call | solution.py:353
  766.3 17.6 %multiply_convert_fusion = bf16[2560,1024]{1,0:T(8,128)(2,1)S(1)} fusion(bf16[2560,2816]{1,0:T(8,128)(2,1)} %get-tuple-element.248, bf16[2816,1024]{1,0:T(8,128)(2,1)S(1)} %bitcast.278, f32[2560]{0:T(1024)S(1)} %pad_maximum_fusion.23), kind=kOutput, calls=%fused_computation.7 | convolution fusion | flops 14769192960 | bytes 25438208 | tf_op jit(solution)/shard_map/dot_general | solution.py:500
  799.7 29.0 %attend_backward.6 = (bf16[2048,512]{1,0:T(8,128)(2,1)S(1)}, bf16[2048,512]{1,0:T(8,128)(2,1)S(1)}, bf16[2048,512]{1,0:T(8,128)(2,1)S(1)}, f32[2,3,512]{2,1,0:T(4,128)S(1)}, f32[2,2,256]{2,1,0:T(2,128)S(1)}) custom-call(s32[2,8]{1,0:T(2,128)S(1)} %copy-done.41, f32[8,2]{1,0:T(8,128)S(1)} %copy-done.39, ...), custom_call_target="tpu_custom_call", output_to_operand_aliasing={{0}: (12, {}), {1}: (13, {}), {2}: (14, {})} | custom-call | flops 5368709120 | bytes 4194304 | tf_op jit(solution)/shard_map/attend_backward/pallas_call | solution.py:353
  833.5 29.4 %attend_backward.7 = (bf16[2048,512]{1,0:T(8,128)(2,1)S(1)}, bf16[2048,512]{1,0:T(8,128)(2,1)S(1)}, bf16[2048,512]{1,0:T(8,128)(2,1)S(1)}, f32[2,3,512]{2,1,0:T(4,128)S(1)}, f32[2,2,256]{2,1,0:T(2,128)S(1)}) custom-call(s32[2,8]{1,0:T(2,128)S(1)} %copy-done.41, f32[8,2]{1,0:T(8,128)S(1)} %copy-done.39, ...), custom_call_target="tpu_custom_call", output_to_operand_aliasing={{0}: (12, {}), {1}: (13, {}), {2}: (14, {})} | custom-call | flops 5368709120 | bytes 4194304 | tf_op jit(solution)/shard_map/attend_backward/pallas_call | solution.py:353
  987.4 18.4 %all-to-all-done.4 = bf16[4,256,512]{2,1,0:T(8,128)(2,1)S(1)} async-done(((bf16[4,256,512]{2,1,0:T(8,128)(2,1)}), bf16[4,256,512]{2,1,0:T(8,128)(2,1)S(1)}, u32[]{:S(2)}, u32[]{:S(2)}) %all-to-all-start.4) | async-done | bytes 1048608 | tf_op jit(solution)/shard_map/all_to_all | solution.py:935
  1018.9 15.5 %all-to-all-done.3 = bf16[4,256,512]{2,1,0:T(8,128)(2,1)} async-done(((bf16[4,256,512]{2,1,0:T(8,128)(2,1)}), bf16[4,256,512]{2,1,0:T(8,128)(2,1)}, u32[]{:S(2)}, u32[]{:S(2)}) %all-to-all-start.3) | async-done | bytes 1048608 | tf_op jit(solution)/shard_map/all_to_all | solution.py:935
  (555 shorter events, 444.5 us)
Async XLA Ops:
  7.2 411.6 %all-gather.2.cloned.1.call-start = ((), (), s32[]{:S(2)}) async-start(), calls=%async_computation.7 | async-start | bytes 6488064 | tf_op jit(solution)/shard_map/all_gather | solution.py:744
  19.5 84.8 %collective-permute-start.3 = (bf16[256,1024]{1,0:T(8,128)(2,1)}, bf16[256,1024]{1,0:T(8,128)(2,1)}, u32[]{:S(2)}, u32[]{:S(2)}) collective-permute-start(bf16[256,1024]{1,0:T(8,128)(2,1)} %get-tuple-element.343), channel_id=1, source_target_pairs={{0,8},{8,0},{16,24},{24,16},{1,9},{9,1},{17,25},{25,17},{2,10},{10... | collective-permute-start | bytes 1572872 | tf_op jit(solution)/shard_map/ppermute | solution.py:513
  21.1 83.2 %collective-permute-start.4 = (bf16[256,1024]{1,0:T(8,128)(2,1)}, bf16[256,1024]{1,0:T(8,128)(2,1)}, u32[]{:S(2)}, u32[]{:S(2)}) collective-permute-start(bf16[256,1024]{1,0:T(8,128)(2,1)} %get-tuple-element.342), channel_id=1, source_target_pairs={{0,16},{8,24},{16,0},{24,8},{1,17},{9,25},{17,1},{25,9},{2,18},{10... | collective-permute-start | bytes 1572872 | tf_op jit(solution)/shard_map/ppermute | solution.py:513
  23.6 80.6 %collective-permute-start.5 = (bf16[256,1024]{1,0:T(8,128)(2,1)}, bf16[256,1024]{1,0:T(8,128)(2,1)}, u32[]{:S(2)}, u32[]{:S(2)}) collective-permute-start(bf16[256,1024]{1,0:T(8,128)(2,1)} %get-tuple-element.344), channel_id=1, source_target_pairs={{0,24},{8,16},{16,8},{24,0},{1,25},{9,17},{17,9},{25,1},{2,26},{10... | collective-permute-start | bytes 1572872 | tf_op jit(solution)/shard_map/ppermute | solution.py:513
  23.9 112.1 %collective-permute-start.7 = (bf16[256,1024]{1,0:T(8,128)(2,1)}, bf16[256,1024]{1,0:T(8,128)(2,1)}, u32[]{:S(2)}, u32[]{:S(2)}) collective-permute-start(bf16[256,1024]{1,0:T(8,128)(2,1)} %get-tuple-element.157), channel_id=1, source_target_pairs={{0,4},{4,0},{1,5},{5,1},{2,6},{6,2},{3,7},{7,3},{8,12},{12,8},{9,1... | collective-permute-start | bytes 1572872 | tf_op jit(solution)/shard_map/ppermute | solution.py:513
  211.2 62.9 %collective-permute-start.14 = (bf16[128,5632]{1,0:T(8,128)(2,1)}, bf16[128,5632]{1,0:T(8,128)(2,1)}, u32[]{:S(2)}, u32[]{:S(2)}) collective-permute-start(bf16[128,5632]{1,0:T(8,128)(2,1)} %collective-permute-done.12), channel_id=1, source_target_pairs={{0,8},{8,16},{16,24},{24,28},{28,20},{20,12},{12,4},{4,0},{1,9},{9... | collective-permute-start | bytes 4325384 | tf_op jit(solution)/shard_map/ppermute | solution.py:586
  212.8 79.3 %collective-permute-start.15 = (bf16[128,5632]{1,0:T(8,128)(2,1)}, bf16[128,5632]{1,0:T(8,128)(2,1)S(1)}, u32[]{:S(2)}, u32[]{:S(2)}) collective-permute-start(bf16[128,5632]{1,0:T(8,128)(2,1)} %collective-permute-done.13), channel_id=1, source_target_pairs={{8,0},{16,8},{24,16},{28,24},{20,28},{12,20},{4,12},{0,4},{9,1},{1... | collective-permute-start | bytes 4325384 | tf_op jit(solution)/shard_map/ppermute | solution.py:589
  213.5 81.7 %collective-permute-start.16 = (bf16[640,1024]{1,0:T(8,128)(2,1)}, bf16[640,1024]{1,0:T(8,128)(2,1)S(1)}, u32[]{:S(2)}, u32[]{:S(2)}) collective-permute-start(bf16[640,1024]{1,0:T(8,128)(2,1)} %convolution_convert_fusion.12), channel_id=1, source_target_pairs={{0,1},{1,0},{2,3},{3,2},{4,5},{5,4},{6,7},{7,6},{8,9},{9,8},{10,11... | collective-permute-start | bytes 3932168 | tf_op jit(solution)/shard_map/ppermute | solution.py:513
  213.5 82.9 %collective-permute-start.17 = (bf16[640,1024]{1,0:T(8,128)(2,1)}, bf16[640,1024]{1,0:T(8,128)(2,1)S(1)}, u32[]{:S(2)}, u32[]{:S(2)}) collective-permute-start(bf16[640,1024]{1,0:T(8,128)(2,1)} %convolution_convert_fusion.11), channel_id=1, source_target_pairs={{0,2},{1,3},{2,0},{3,1},{4,6},{5,7},{6,4},{7,5},{8,10},{9,11},{10,... | collective-permute-start | bytes 3932168 | tf_op jit(solution)/shard_map/ppermute | solution.py:513
  214.0 83.5 %collective-permute-start.18 = (bf16[640,1024]{1,0:T(8,128)(2,1)}, bf16[640,1024]{1,0:T(8,128)(2,1)S(1)}, u32[]{:S(2)}, u32[]{:S(2)}) collective-permute-start(bf16[640,1024]{1,0:T(8,128)(2,1)} %convolution_convert_fusion.10), channel_id=1, source_target_pairs={{0,3},{1,2},{2,1},{3,0},{4,7},{5,6},{6,5},{7,4},{8,11},{9,10},{10,... | collective-permute-start | bytes 3932168 | tf_op jit(solution)/shard_map/ppermute | solution.py:513
  298.5 90.8 %all-to-all-start = ((bf16[8,256,512]{2,1,0:T(8,128)(2,1)}), bf16[8,256,512]{2,1,0:T(8,128)(2,1)}, u32[]{:S(2)}, u32[]{:S(2)}) async-start(bf16[8,256,512]{2,1,0:T(8,128)(2,1)} %bitcast.39), calls=%async_computation | async-start | bytes 4194304 | tf_op jit(solution)/shard_map/all_to_all | solution.py:795
  304.1 64.4 %collective-permute-start.20 = (bf16[128,5632]{1,0:T(8,128)(2,1)}, bf16[128,5632]{1,0:T(8,128)(2,1)S(1)}, u32[]{:S(2)}, u32[]{:S(2)}) collective-permute-start(bf16[128,5632]{1,0:T(8,128)(2,1)} %copy-done.62), channel_id=1, source_target_pairs={{8,0},{16,8},{24,16},{28,24},{20,28},{12,20},{4,12},{0,4},{9,1},{1... | collective-permute-start | bytes 4325384 | tf_op jit(solution)/shard_map/ppermute | solution.py:589
  329.9 58.3 %collective-permute-start.21 = (bf16[128,5632]{1,0:T(8,128)(2,1)}, bf16[128,5632]{1,0:T(8,128)(2,1)S(1)}, u32[]{:S(2)}, u32[]{:S(2)}) collective-permute-start(bf16[128,5632]{1,0:T(8,128)(2,1)} %collective-permute-done.19), channel_id=1, source_target_pairs={{0,8},{8,16},{16,24},{24,28},{28,20},{20,12},{12,4},{4,0},{1,9},{9... | collective-permute-start | bytes 4325384 | tf_op jit(solution)/shard_map/ppermute | solution.py:586
  412.5 95.2 %collective-permute-start.22 = (bf16[656,1024]{1,0:T(8,128)(2,1)}, bf16[656,1024]{1,0:T(8,128)(2,1)S(1)}, u32[]{:S(2)}, u32[]{:S(2)}) collective-permute-start(bf16[656,1024]{1,0:T(8,128)(2,1)} %pad_maximum_fusion.8), channel_id=1, source_target_pairs={{0,1},{1,0},{2,3},{3,2},{4,5},{5,4},{6,7},{7,6},{8,9},{9,8},{10,11... | collective-permute-start | bytes 4030472 | tf_op jit(solution)/shard_map/ppermute | solution.py:513
  415.2 64.3 %collective-permute-start.25 = (bf16[656,1024]{1,0:T(8,128)(2,1)}, bf16[656,1024]{1,0:T(8,128)(2,1)}, u32[]{:S(2)}, u32[]{:S(2)}) collective-permute-start(bf16[656,1024]{1,0:T(8,128)(2,1)} %pad_maximum_fusion.10), channel_id=1, source_target_pairs={{0,3},{1,2},{2,1},{3,0},{4,7},{5,6},{6,5},{7,4},{8,11},{9,10},{10,... | collective-permute-start | bytes 4030472 | tf_op jit(solution)/shard_map/ppermute | solution.py:513
  578.7 62.3 %all-to-all-start.1 = ((bf16[8,256,512]{2,1,0:T(8,128)(2,1)}), bf16[8,256,512]{2,1,0:T(8,128)(2,1)S(1)}, u32[]{:S(2)}, u32[]{:S(2)}) async-start(bf16[8,256,512]{2,1,0:T(8,128)(2,1)} %bitcast.294), calls=%async_computation.1 | async-start | bytes 4194304 | tf_op jit(solution)/shard_map/all_to_all | solution.py:795
  592.1 282.6 %reduce-scatter.2.cloned.1.call-start = ((), (), s32[]{:S(2)}) async-start(), calls=%async_computation.8 | async-start | bytes 6488064 | tf_op jit(solution)/shard_map/reduce_scatter | solution.py:875
  685.4 62.4 %collective-permute-start.33 = (bf16[128,2816]{1,0:T(8,128)(2,1)}, bf16[128,2816]{1,0:T(8,128)(2,1)}, u32[]{:S(2)}, u32[]{:S(2)}) collective-permute-start(bf16[128,2816]{1,0:T(8,128)(2,1)} %get-tuple-element.318), channel_id=1, source_target_pairs={{0,8},{8,16},{16,24},{24,28},{28,20},{20,12},{12,4},{4,0},{1,9},{9... | collective-permute-start | bytes 2162696 | tf_op jit(solution)/shard_map/ppermute | solution.py:636
  685.4 62.4 %collective-permute-start.35 = (bf16[128,2816]{1,0:T(8,128)(2,1)}, bf16[128,2816]{1,0:T(8,128)(2,1)}, u32[]{:S(2)}, u32[]{:S(2)}) collective-permute-start(bf16[128,2816]{1,0:T(8,128)(2,1)} %get-tuple-element.317), channel_id=1, source_target_pairs={{8,0},{16,8},{24,16},{28,24},{20,28},{12,20},{4,12},{0,4},{9,1},{1... | collective-permute-start | bytes 2162696 | tf_op jit(solution)/shard_map/ppermute | solution.py:639
  759.5 69.2 %collective-permute-start.37 = (bf16[128,2816]{1,0:T(8,128)(2,1)}, bf16[128,2816]{1,0:T(8,128)(2,1)}, u32[]{:S(2)}, u32[]{:S(2)}) collective-permute-start(bf16[128,2816]{1,0:T(8,128)(2,1)} %get-tuple-element.314), channel_id=1, source_target_pairs={{0,8},{8,16},{16,24},{24,28},{28,20},{20,12},{12,4},{4,0},{1,9},{9... | collective-permute-start | bytes 2162696 | tf_op jit(solution)/shard_map/ppermute | solution.py:636
  759.5 69.2 %collective-permute-start.39 = (bf16[128,2816]{1,0:T(8,128)(2,1)}, bf16[128,2816]{1,0:T(8,128)(2,1)}, u32[]{:S(2)}, u32[]{:S(2)}) collective-permute-start(bf16[128,2816]{1,0:T(8,128)(2,1)} %get-tuple-element.313), channel_id=1, source_target_pairs={{8,0},{16,8},{24,16},{28,24},{20,28},{12,20},{4,12},{0,4},{9,1},{1... | collective-permute-start | bytes 2162696 | tf_op jit(solution)/shard_map/ppermute | solution.py:639
  764.2 64.4 %collective-permute-start.36 = (bf16[128,2816]{1,0:T(8,128)(2,1)}, bf16[128,2816]{1,0:T(8,128)(2,1)}, u32[]{:S(2)}, u32[]{:S(2)}) collective-permute-start(bf16[128,2816]{1,0:T(8,128)(2,1)} %get-tuple-element.316), channel_id=1, source_target_pairs={{0,8},{8,16},{16,24},{24,28},{28,20},{20,12},{12,4},{4,0},{1,9},{9... | collective-permute-start | bytes 2162696 | tf_op jit(solution)/shard_map/ppermute | solution.py:636
  764.3 64.4 %collective-permute-start.38 = (bf16[128,2816]{1,0:T(8,128)(2,1)}, bf16[128,2816]{1,0:T(8,128)(2,1)}, u32[]{:S(2)}, u32[]{:S(2)}) collective-permute-start(bf16[128,2816]{1,0:T(8,128)(2,1)} %get-tuple-element.315), channel_id=1, source_target_pairs={{8,0},{16,8},{24,16},{28,24},{20,28},{12,20},{4,12},{0,4},{9,1},{1... | collective-permute-start | bytes 2162696 | tf_op jit(solution)/shard_map/ppermute | solution.py:639
  787.5 87.2 %all-to-all-start.2 = ((bf16[4,640,1024]{2,1,0:T(8,128)(2,1)}), bf16[4,640,1024]{2,1,0:T(8,128)(2,1)}, u32[]{:S(2)}, u32[]{:S(2)}) async-start(bf16[4,640,1024]{2,1,0:T(8,128)(2,1)} %pad_maximum_fusion.1), calls=%async_computation.2 | async-start | bytes 10485760 | tf_op jit(solution)/shard_map/all_to_all | solution.py:900
  (135 other events, 3853.7 us)
Sparse Core Ops, SparseCore 0:
  155.1 137.1 all-gather.1
  708.4 142.3 reduce-scatter.1
